TPU v7x, 256 devices: a whole 4x4x8 slice. The times are simulated.
256 devices in a mesh: ctx: 64 (over y, z, core), tp: 4 (over x).
Axes of the slice: x: 4, y: 4, z: 8, core: 2. Of those that a mesh axis runs over, the one named last changes fastest.
Arguments:
- outer_gate: bfloat16 [8192, 1024], P('ctx', 'tp'), may hold values from -6 to 6
- inner_gate: bfloat16 [8192, 1024], P('ctx', 'tp'), may hold values from -6 to 6
- values: bfloat16 [8192, 1024], P('ctx', 'tp'), may hold values from -6 to 6
- residues: float32 [16, 1024], P(None, 'tp'), may hold values from -4 to 4
- log_decay: float32 [16, 1024], P(None, 'tp'), may hold values from -16 to -2, as said below
- skip_gain: float32 [1024], P('tp'), may hold values from 0.5 to 1.5
- out_weight: bfloat16 [1024, 8192], P('tp'), may hold values from -0.25 to 0.25
- out_grad: bfloat16 [8192, 8192], P('ctx', 'tp'), may hold values from -4 to 4
Outputs:
- mixed: bfloat16 [8192, 8192], P('ctx', 'tp')
- grad_outer: bfloat16 [8192, 1024], P('ctx', 'tp')
- grad_inner: bfloat16 [8192, 1024], P('ctx', 'tp')
- grad_values: bfloat16 [8192, 1024], P('ctx', 'tp')
- grad_weight: float32 [1024, 8192], P('tp', 'ctx')
- grad_skip: float32 [1024], P('tp')
- grad_residues: float32 [16, 1024], P(None, 'tp')
- grad_decay: float32 [16, 1024], P(None, 'tp')
Inputs may be any that keep to these rules, and one draw needn't show every extreme that they name: exp(log_decay) is a decay rate per position between 0.3 / 8192 and 0.12.
All inputs are finite; a program needn't handle non-finite values.
Results may differ from a plain program's by a relative error of at most 0.015.
Values may be sent and summed in bfloat16 or wider, within the bound.
No kernel may reach another device: no remote copies, remote signals or barrier semaphores. Data moves between devices by JAX's collectives and lax.ppermute only.
A program may use at most 128 MiB of HBM per device.

v0:
```python
import jax
import jax.numpy as jnp
import numpy as np
from jax import lax
from jax.sharding import PartitionSpec as P

F32 = jnp.float32
BF16 = jnp.bfloat16
EXACT = lax.Precision.HIGHEST


def dft_tables(block):
    size = 2 * block
    freqs = np.arange(block + 1)
    rows = np.arange(block)
    angles = 2.0 * np.pi * (freqs[:, None] * rows[None, :] % size) / size
    forward = np.concatenate([np.cos(angles), -np.sin(angles)], axis=0)
    weight = np.where((freqs == 0) | (freqs == block), 1.0, 2.0)[:, None] / size
    inverse = np.concatenate([weight * np.cos(angles), -weight * np.sin(angles)], axis=0).T
    return jnp.asarray(forward, F32), jnp.asarray(inverse, F32)


def spectrum(forward, rows):
    both = jnp.dot(forward, rows, precision=EXACT, preferred_element_type=F32)
    half = both.shape[0] // 2
    return both[:half], both[half:]


def back(inverse, real_part, imag_part):
    return jnp.dot(
        inverse, jnp.concatenate([real_part, imag_part], 0), precision=EXACT, preferred_element_type=F32
    )


def body(outer_gate, inner_gate, values, residues, log_decay, skip_gain, out_weight, out_grad):
    ctx = lax.axis_size("ctx")
    tps = lax.axis_size("tp")
    dev = lax.axis_index("ctx")
    tp = lax.axis_index("tp")
    block, chans = outer_gate.shape
    modes = residues.shape[0]
    feats = out_grad.shape[1]
    ny = tps
    nz = ctx // (2 * ny)
    pairs = ctx // 2
    core = dev % 2
    pair = dev // 2
    yy = dev // (2 * nz)
    width = feats // (2 * nz)

    def swap_core(a):
        return lax.ppermute(a, "ctx", [(i, i ^ 1) for i in range(ctx)])

    def shift_tp(a, k):
        return lax.ppermute(a, "tp", [(i, (i + k) % tps) for i in range(tps)])

    def shift_y(a, k):
        per = 2 * nz
        return lax.ppermute(a, "ctx", [(i, (i // per + k) % ny * per + i % per) for i in range(ctx)])

    def of_pairs(a):
        copies = jnp.broadcast_to(a[None], (pairs, *a.shape))
        groups = [[2 * i + j for i in range(pairs)] for j in range(2)]
        return lax.all_to_all(copies, "ctx", 0, 0, tiled=True, axis_index_groups=groups)

    og = out_grad.reshape(block, nz, 2, width)
    og_mine = lax.dynamic_index_in_dim(og, core, 2, keepdims=False)
    og_other = lax.dynamic_index_in_dim(og, 1 - core, 2, keepdims=False)
    pg0 = jnp.concatenate([og_mine, swap_core(og_other)], 0).reshape(2 * block, nz * width)
    pgs = [pg0] + [shift_tp(pg0, k) for k in range(1, tps)]

    u = inner_gate.astype(F32) * values.astype(F32)
    rate = jnp.exp(log_decay)
    rows = jnp.arange(block, dtype=F32)[None, :, None]
    rate3 = rate[:, None, :]
    rise = jnp.exp(-rate3 * (block - rows))
    fall_block = jnp.exp(-rate * block)

    lead = rise * u[None]
    st = jnp.sum(lead, 1)
    st_lag = jnp.sum(lead * (block - rows), 1)
    mine = jnp.concatenate([st, st_lag], 0)
    theirs = swap_core(mine)
    first = jnp.where(core == 0, mine, theirs)
    second = jnp.where(core == 0, theirs, mine)
    half = chans // 2

    def my_half(a):
        return lax.dynamic_slice_in_dim(a, core * half, half, a.ndim - 1)

    def both_halves(a):
        other = swap_core(a)
        return jnp.concatenate(
            [jnp.where(core == 0, a, other), jnp.where(core == 0, other, a)], a.ndim - 1
        )

    rate_h = my_half(rate)
    decay_h = jnp.exp(-rate_h * block)
    f_h, s_h = my_half(first), my_half(second)
    total = decay_h * f_h[:modes] + s_h[:modes]
    total_lag = decay_h * (block * f_h[:modes] + f_h[modes:]) + s_h[modes:]
    to_send = jnp.concatenate([total, total_lag], 0).astype(BF16)
    gathered = of_pairs(to_send).astype(F32)
    place = jnp.arange(pairs, dtype=jnp.int32)
    gap = (2 * block) * jnp.maximum(pair - 1 - place, 0).astype(F32)[:, None, None]
    weight = jnp.where(
        (place < pair)[:, None, None], jnp.exp(-rate_h[None] * gap), 0.0
    )
    in_h = jnp.sum(weight * gathered[:, :modes], 0)
    in_lag_h = jnp.sum(weight * (gap * gathered[:, :modes] + gathered[:, modes:]), 0)
    incoming = both_halves(jnp.concatenate([in_h, in_lag_h], 0))
    in_pair, in_pair_lag = incoming[:modes], incoming[modes:]
    x_in = jnp.where(core == 0, in_pair, fall_block * in_pair + first[:modes])
    x_lag = jnp.where(
        core == 0, in_pair_lag, fall_block * (in_pair_lag + block * in_pair) + first[modes:]
    )

    outer_gate, inner_gate, values, residues, log_decay, x_in, x_lag = lax.optimization_barrier(
        (outer_gate, inner_gate, values, residues, log_decay, x_in, x_lag)
    )
    rate = jnp.exp(log_decay)
    gain = residues * jnp.sqrt(-jnp.expm1(-2.0 * rate))
    fall = jnp.exp(-rate[:, None, :] * rows)
    outer_f = outer_gate.astype(F32)
    u = inner_gate.astype(F32) * values.astype(F32)

    forward, inverse = dft_tables(block)
    response = jnp.sum(gain[:, None, :] * fall, 0)
    h_re, h_im = spectrum(forward, response)
    u_re, u_im = spectrum(forward, u)
    conv_local = back(inverse, h_re * u_re - h_im * u_im, h_re * u_im + h_im * u_re)
    conv_out = conv_local + jnp.sum((gain * x_in)[:, None, :] * fall, 0)
    gated = conv_out + skip_gain[None, :] * u
    result = (outer_f * gated).astype(BF16)

    result_pair = jnp.concatenate([result, swap_core(result)], 0)
    parts = [
        lax.dot_general(result_pair, pg, (((0,), (0,)), ((), ())), preferred_element_type=F32)
        .astype(BF16)
        .reshape(chans, nz, width)
        .swapaxes(0, 1)
        for pg in pgs
    ]
    parts = jnp.stack(parts, 0)

    def part_for(s):
        return lax.dynamic_index_in_dim(parts, (tp - yy - s) % tps, 0, keepdims=False)

    y_parts = [part_for(s) for s in range(ny)]
    over_y = [y_parts[0]] + [shift_y(y_parts[s], s) for s in range(1, ny)]
    summed_y = sum(a.astype(F32) for a in over_y).astype(BF16)

    w_blocks = out_weight.reshape(chans, tps, feats)

    def projected(k):
        w_block = lax.dynamic_index_in_dim(w_blocks, (tp + k) % tps, 1, keepdims=False)
        return jnp.dot(result, w_block, preferred_element_type=F32)

    mixed = projected(0)
    for k in range(1, tps):
        piece = projected(k).astype(BF16)
        piece = shift_tp(piece, k)
        mixed = mixed + piece.astype(F32)
    mixed = mixed.astype(BF16)

    w_half = lax.dynamic_index_in_dim(
        out_weight.reshape(chans, tps, nz, 2, width), core, 3, keepdims=False
    ).reshape(chans, tps, nz * width)
    grad_pair = 0.0
    for k in range(tps):
        w_block = lax.dynamic_index_in_dim(w_half, (tp - k) % tps, 1, keepdims=False)
        grad_pair = grad_pair + lax.dot_general(
            pgs[k], w_block, (((1,), (1,)), ((), ())), preferred_element_type=F32
        )
    grad_gated = grad_pair[:block] + swap_core(grad_pair[block:])
    outer_gate, inner_gate, values, residues, log_decay, grad_gated = lax.optimization_barrier(
        (outer_gate, inner_gate, values, residues, log_decay, grad_gated)
    )
    outer_f = outer_gate.astype(F32)
    inner_f = inner_gate.astype(F32)
    value_f = values.astype(F32)
    u = inner_f * value_f
    rate = jnp.exp(log_decay)
    norm = jnp.sqrt(-jnp.expm1(-2.0 * rate))
    gain = residues * norm
    fall = jnp.exp(-rate[:, None, :] * rows)
    rise = jnp.exp(-rate[:, None, :] * (block - rows))
    fall_block = jnp.exp(-rate * block)
    gc = grad_gated * outer_f
    grad_outer = (grad_gated * gated).astype(BF16)

    g_re, g_im = spectrum(forward, gc)
    corr_local = back(inverse, h_re * g_re + h_im * g_im, h_re * g_im - h_im * g_re)
    lags = back(inverse, u_re * g_re + u_im * g_im, u_re * g_im - u_im * g_re)
    fg = fall * gc[None]
    g_st = jnp.sum(fg, 1)
    g_lag = jnp.sum(fg * rows, 1)
    fl = fall * lags[None]
    sum_a = g_st * x_in + jnp.sum(fl, 1)
    sum_b = g_lag * x_in + g_st * x_lag + jnp.sum(fl * rows, 1)
    sum_skip = jnp.sum(gc * u, 0, keepdims=True)
    mine_g = jnp.concatenate([g_st, sum_a, sum_b, sum_skip], 0)
    theirs_g = swap_core(mine_g)
    later = jnp.where(core == 0, theirs_g[:modes], mine_g[:modes])
    mine_h, theirs_h = my_half(mine_g), my_half(theirs_g)
    early_h = jnp.where(core == 0, mine_h[:modes], theirs_h[:modes])
    total_g = early_h + decay_h * my_half(later)
    sent = jnp.concatenate([total_g, mine_h[modes:] + theirs_h[modes:]], 0).astype(BF16)
    got = of_pairs(sent).astype(F32)
    gap_g = (2 * block) * jnp.maximum(place - pair - 1, 0).astype(F32)[:, None, None]
    weight_g = jnp.where((place > pair)[:, None, None], jnp.exp(-rate_h[None] * gap_g), 0.0)
    h_half = jnp.sum(weight_g * got[:, :modes], 0)
    sums_half = jnp.sum(got[:, modes:], 0)
    final = both_halves(jnp.concatenate([h_half, sums_half], 0))
    h_pair = final[:modes]
    h_in = jnp.where(core == 0, later + fall_block * h_pair, h_pair)
    tot_a, tot_b = final[modes : 2 * modes], final[2 * modes : 3 * modes]
    grad_skip = final[3 * modes]
    grad_residues = norm * tot_a
    grad_decay = rate * residues * (jnp.exp(-2.0 * rate) / norm * tot_a - norm * tot_b)
    corr_in = corr_local + jnp.sum((gain * h_in)[:, None, :] * rise, 0)
    grad_mixed = corr_in + skip_gain[None, :] * gc
    grad_inner = (grad_mixed * value_f).astype(BF16)
    grad_values = (grad_mixed * inner_f).astype(BF16)

    z_groups = [[i * 2 * nz + j * 2 + k for j in range(nz)] for i in range(ny) for k in range(2)]
    over_z = lax.all_to_all(summed_y, "ctx", 0, 0, tiled=True, axis_index_groups=z_groups)
    grad_weight = jnp.sum(over_z.astype(F32), 0)
    return (
        mixed,
        grad_outer,
        grad_inner,
        grad_values,
        grad_weight,
        grad_skip,
        grad_residues,
        grad_decay,
    )


def solution(mesh):
    placed = (
        P("ctx", "tp"),
        P("ctx", "tp"),
        P("ctx", "tp"),
        P(None, "tp"),
        P(None, "tp"),
        P("tp"),
        P("tp", None),
        P("ctx", "tp"),
    )

    return jax.shard_map(
        body,
        mesh=mesh,
        in_specs=placed,
        out_specs=(
            P("ctx", "tp"),
            P("ctx", "tp"),
            P("ctx", "tp"),
            P("ctx", "tp"),
            P("tp", "ctx"),
            P("tp"),
            P(None, "tp"),
            P(None, "tp"),
        ),
        check_vma=False,
    )
```

profile of v0, /device:TPU:2, one launch (start us, length us, event | category | flops | bytes accessed | tf_op | source)
XLA Modules:
  0.0 144.3 jit_solution(17471091518042728026)
XLA Ops:
  0.7 0.7 fusion.121
  1.4 0.9 convert_multiply_fusion.5
  2.3 0.7 fusion.4
  3.1 1.3 copy.94
  4.7 0.6 collective-permute-start.5
  5.4 0.7 broadcast_in_dim.26
  6.1 11.5 %all-to-all-start = ((bf16[32,32,128]{2,1,0:T(8,128)(2,1)}), bf16[32,32,128]{2,1,0:T(8,128)(2,1)S(1)}, u32[]{:S(2)}, u32[]{:S(2)}) async-start(bf16[32,32,128]{2,1,0:T(8,128)(2,1)} %broadcast_in_dim.26), calls=%async_computation | async-start | bytes 524288 | tf_op jit(solution)/shard_map/all_to_all | solution.py:64
  17.7 6.4 %copy.89 = bf16[256,8192]{0,1:T(8,128)(2,1)} copy(bf16[256,8192]{1,0:T(8,128)(2,1)} %param.16) | data formatting | bytes 8388608 | tf_op args[6]
  24.1 0.5 convert_multiply_fusion.7
  24.6 0.6 iota_compare_fusion
  25.2 1.7 %constant_dynamic-slice_fusion = bf16[256,4,8,1,128]{0,4,3,2,1:T(8,128)(2,1)S(1)} fusion(bf16[256,4,8,2,128]{0,4,3,2,1:T(8,128)(2,1)} %bitcast.119, s32[]{:T(128)S(6)} %select_n.206), kind=kLoop, calls=%fused_computation.202 | loop fusion | bytes 4194308 | tf_op jit(solution)/shard_map/jit(dynamic_index_in_dim)/dynamic_slice | solution.py:166
  27.3 3.0 %all-to-all-done = bf16[32,32,128]{2,1,0:T(8,128)(2,1)S(1)} async-done(((bf16[32,32,128]{2,1,0:T(8,128)(2,1)}), bf16[32,32,128]{2,1,0:T(8,128)(2,1)S(1)}, u32[]{:S(2)}, u32[]{:S(2)}) %all-to-all-start) | async-done | bytes 262176 | tf_op jit(solution)/shard_map/all_to_all | solution.py:64
  30.7 0.6 collective-permute-start.8
  31.4 1.5 %collective-permute-start.6 = (bf16[256,1024]{0,1:T(8,128)(2,1)S(1)}, bf16[256,1024]{0,1:T(8,128)(2,1)S(1)}, u32[]{:S(2)}, u32[]{:S(2)}) collective-permute-start(bf16[256,1024]{0,1:T(8,128)(2,1)S(1)} %pad_maximum_fusion.1), channel_id=1, source_target_pairs={{0,1},{1,2},{2,3},{3,0},{4,5},{5,6},{6,7},{7,4},{8,9},{9,10},{10,1... | collective-permute-start | bytes 1572872 | tf_op jit(solution)/shard_map/ppermute | solution.py:55
  32.8 3.3 %collective-permute-start.7 = (bf16[256,1024]{0,1:T(8,128)(2,1)S(1)}, bf16[256,1024]{0,1:T(8,128)(2,1)S(1)}, u32[]{:S(2)}, u32[]{:S(2)}) collective-permute-start(bf16[256,1024]{0,1:T(8,128)(2,1)S(1)} %pad_maximum_fusion.1), channel_id=1, source_target_pairs={{0,2},{1,3},{2,0},{3,1},{4,6},{5,7},{6,4},{7,5},{8,10},{9,11},{10,... | collective-permute-start | bytes 1572872 | tf_op jit(solution)/shard_map/ppermute | solution.py:55
  36.2 0.6 fusion.103
  36.9 0.5 multiply_reduce_fusion.4
  38.5 8.4 %collective-permute-done.6 = bf16[256,1024]{0,1:T(8,128)(2,1)S(1)} collective-permute-done((bf16[256,1024]{0,1:T(8,128)(2,1)S(1)}, bf16[256,1024]{0,1:T(8,128)(2,1)S(1)}, u32[]{:S(2)}, u32[]{:S(2)}) %collective-permute-start.6) | collective-permute-done | bytes 524320 | tf_op jit(solution)/shard_map/ppermute | solution.py:55
  48.0 9.3 %collective-permute-done.7 = bf16[256,1024]{0,1:T(8,128)(2,1)S(1)} collective-permute-done((bf16[256,1024]{0,1:T(8,128)(2,1)S(1)}, bf16[256,1024]{0,1:T(8,128)(2,1)S(1)}, u32[]{:S(2)}, u32[]{:S(2)}) %collective-permute-start.7) | collective-permute-done | bytes 524320 | tf_op jit(solution)/shard_map/ppermute | solution.py:55
  58.1 1.0 collective-permute-done.9
  59.2 0.7 fusion.67
  60.2 0.6 fusion.47
  61.6 1.3 convolution_convert_fusion
  62.9 4.5 %collective-permute-start.4 = (bf16[128,2048]{1,0:T(8,128)(2,1)}, bf16[128,2048]{1,0:T(8,128)(2,1)}, u32[]{:S(2)}, u32[]{:S(2)}) collective-permute-start(bf16[128,2048]{1,0:T(8,128)(2,1)} %convolution_convert_fusion), channel_id=1, source_target_pairs={{0,3},{1,0},{2,1},{3,2},{4,7},{5,4},{6,5},{7,6},{8,11},{9,8},{10,9... | collective-permute-start | bytes 1572872 | tf_op jit(solution)/shard_map/ppermute | solution.py:55
  67.3 1.3 convolution_convert_fusion.1
  68.6 0.6 fusion.10
  69.4 1.1 fusion.3
  70.8 2.5 %convolution_convert_fusion.2 = bf16[128,2048]{1,0:T(8,128)(2,1)} fusion(bf16[128,256]{1,0:T(8,128)(2,1)S(1)} %get-tuple-element.58, bf16[256,4,2048]{0,2,1:T(8,128)(2,1)} %bitcast.120, s32[]{:T(128)S(6)} %select_n.201), kind=kOutput, calls=%fused_computation.2 | convolution fusion | flops 134479872 | bytes 1638404 | tf_op jit(solution)/shard_map/dot_general | solution.py:157
  73.3 1.5 %collective-permute-start.2 = (bf16[128,2048]{1,0:T(8,128)(2,1)}, bf16[128,2048]{1,0:T(8,128)(2,1)}, u32[]{:S(2)}, u32[]{:S(2)}) collective-permute-start(bf16[128,2048]{1,0:T(8,128)(2,1)} %convolution_convert_fusion.2), channel_id=1, source_target_pairs={{0,1},{1,2},{2,3},{3,0},{4,5},{5,6},{6,7},{7,4},{8,9},{9,10},{10,1... | collective-permute-start | bytes 1572872 | tf_op jit(solution)/shard_map/ppermute | solution.py:55
  74.9 0.9 broadcast_in_dim.29
  75.7 6.9 %all-to-all-start.1 = ((bf16[32,49,128]{2,1,0:T(8,128)(2,1)}), bf16[32,49,128]{2,1,0:T(8,128)(2,1)}, u32[]{:S(2)}, u32[]{:S(2)}) async-start(bf16[32,49,128]{2,1,0:T(8,128)(2,1)} %broadcast_in_dim.29), calls=%async_computation.1 | async-start | bytes 917504 | tf_op jit(solution)/shard_map/all_to_all | solution.py:64
  84.9 1.2 dynamic-slice_bitcast_fusion.2
  86.1 3.0 %collective-permute-start.15 = (bf16[8,256,128]{2,1,0:T(8,128)(2,1)}, bf16[8,256,128]{2,1,0:T(8,128)(2,1)}, u32[]{:S(2)}, u32[]{:S(2)}) collective-permute-start(bf16[8,256,128]{2,1,0:T(8,128)(2,1)} %get-tuple-element.51), channel_id=1, source_target_pairs={{0,192},{4,196},{8,200},{12,204},{16,208},{20,212},{24,216},{28,22... | collective-permute-start | bytes 1572872 | tf_op jit(solution)/shard_map/ppermute | solution.py:59
  89.1 0.8 collective-permute-start.14
  90.0 0.9 collective-permute-start.13
  90.9 1.8 %collective-permute-done.2 = bf16[128,2048]{1,0:T(8,128)(2,1)} collective-permute-done((bf16[128,2048]{1,0:T(8,128)(2,1)}, bf16[128,2048]{1,0:T(8,128)(2,1)}, u32[]{:S(2)}, u32[]{:S(2)}) %collective-permute-start.2) | collective-permute-done | bytes 524320 | tf_op jit(solution)/shard_map/ppermute | solution.py:55
  92.7 3.0 %add_convert_fusion = bf16[128,2048]{1,0:T(8,128)(2,1)} fusion(bf16[128,2048]{1,0:T(8,128)(2,1)} %collective-permute-done.4, bf16[128,2048]{1,0:T(8,128)(2,1)} %collective-permute-done.3, bf16[128,2048]{1,0:T(8,128)(2,1)} %collective-permute-done.2, bf16[128,256]{1,0:T(8,128)(2,1)S(1)} %get-tuple-element.58, bf16[256,4,2048]{0,2,1:T(8,128)(2,1)} %bitcast.121, ...), kind=kOutput, calls=%fused_computation.49 | convolution fusion | flops 136052736 | bytes 3211268 | tf_op jit(solution)/shard_map/dot_general | solution.py:157
  95.7 2.6 %all-to-all-done.1 = bf16[32,49,128]{2,1,0:T(8,128)(2,1)} async-done(((bf16[32,49,128]{2,1,0:T(8,128)(2,1)}), bf16[32,49,128]{2,1,0:T(8,128)(2,1)}, u32[]{:S(2)}, u32[]{:S(2)}) %all-to-all-start.1) | async-done | bytes 401440 | tf_op jit(solution)/shard_map/all_to_all | solution.py:64
  98.2 1.1 convert_element_type.140
  99.8 14.9 %collective-permute-done.15 = bf16[8,256,128]{2,1,0:T(8,128)(2,1)} collective-permute-done((bf16[8,256,128]{2,1,0:T(8,128)(2,1)}, bf16[8,256,128]{2,1,0:T(8,128)(2,1)}, u32[]{:S(2)}, u32[]{:S(2)}) %collective-permute-start.15) | collective-permute-done | bytes 524320 | tf_op jit(solution)/shard_map/ppermute | solution.py:59
  114.6 3.1 %collective-permute-done.13 = bf16[8,256,128]{2,1,0:T(8,128)(2,1)} collective-permute-done((bf16[8,256,128]{2,1,0:T(8,128)(2,1)}, bf16[8,256,128]{2,1,0:T(8,128)(2,1)}, u32[]{:S(2)}, u32[]{:S(2)}) %collective-permute-start.13) | collective-permute-done | bytes 524320 | tf_op jit(solution)/shard_map/ppermute | solution.py:59
  117.7 2.4 %fusion.24 = bf16[8,256,128]{2,1,0:T(8,128)(2,1)} fusion(bf16[8,256,128]{2,1,0:T(8,128)(2,1)} %collective-permute-done.15, bf16[8,256,128]{2,1,0:T(8,128)(2,1)} %collective-permute-done.14, bf16[8,256,128]{2,1,0:T(8,128)(2,1)} %collective-permute-done.13, bf16[4,8,256,128]{3,2,1,0:T(8,128)(2,1)S(1)} %pad_maximum_fusion, s32[]{:T(128)S(6)} %select_n.224), kind=kLoop, calls=%fused_computation.47 | loop fusion | flops 2097152 | bytes 2621444 | tf_op jit(solution)/shard_map/convert_element_type | solution.py:151
  120.2 5.6 %all-to-all-start.2 = ((bf16[8,256,128]{2,1,0:T(8,128)(2,1)}), bf16[8,256,128]{2,1,0:T(8,128)(2,1)S(1)}, u32[]{:S(2)}, u32[]{:S(2)}) async-start(bf16[8,256,128]{2,1,0:T(8,128)(2,1)} %fusion.24), calls=%async_computation.2 | async-start | bytes 1048576 | tf_op jit(solution)/shard_map/all_to_all | solution.py:227
  125.8 0.6 fusion.119
  126.4 0.7 fusion.102
  127.5 1.0 fusion.65
  128.5 15.1 %all-to-all-done.2 = bf16[8,256,128]{2,1,0:T(8,128)(2,1)S(1)} async-done(((bf16[8,256,128]{2,1,0:T(8,128)(2,1)}), bf16[8,256,128]{2,1,0:T(8,128)(2,1)S(1)}, u32[]{:S(2)}, u32[]{:S(2)}) %all-to-all-start.2) | async-done | bytes 524320 | tf_op jit(solution)/shard_map/all_to_all | solution.py:227
  143.5 0.7 convert_reduce_fusion
  (144 shorter events, 8.4 us)
Async XLA Ops:
  3.0 2.3 %collective-permute-start = (f32[32,256]{1,0:T(8,128)S(1)}, f32[32,256]{1,0:T(8,128)S(1)}, u32[]{:S(2)}, u32[]{:S(2)}) collective-permute-start(f32[32,256]{1,0:T(8,128)S(1)} %pad_maximum_fusion.4), channel_id=1, source_target_pairs={{0,4},{4,0},{8,12},{12,8},{16,20},{20,16},{24,28},{28,24},{32,36},... | collective-permute-start | bytes 98312 | tf_op jit(solution)/shard_map/ppermute | solution.py:52
  4.5 42.8 %copy-start.13 = (bf16[128,8,1,128]{0,3,2,1:T(8,128)(2,1)}, bf16[128,8,1,128]{0,3,2,1:T(8,128)(2,1)S(1)}, u32[]{:S(2)}) copy-start(bf16[128,8,1,128]{0,3,2,1:T(8,128)(2,1)S(1)} %get-tuple-element.53) | copy-start | bytes 786436
  4.7 22.3 %collective-permute-start.5 = (bf16[128,8,128]{2,1,0:T(8,128)(2,1)S(1)}, bf16[128,8,128]{2,1,0:T(8,128)(2,1)S(1)}, u32[]{:S(2)}, u32[]{:S(2)}) collective-permute-start(bf16[128,8,128]{2,1,0:T(8,128)(2,1)S(1)} %bitcast.135), channel_id=1, source_target_pairs={{0,4},{4,0},{8,12},{12,8},{16,20},{20,16},{24,28},{28,24},{32,36},... | collective-permute-start | bytes 786440 | tf_op jit(solution)/shard_map/ppermute | solution.py:52
  5.3 25.0 %copy-start.23 = (f32[16,128]{1,0:T(8,128)}, f32[16,128]{1,0:T(8,128)S(1)}, u32[]{:S(2)}) copy-start(f32[16,128]{1,0:T(8,128)S(1)} %get-tuple-element.73) | copy-start | bytes 24580
  6.1 24.2 %all-to-all-start = ((bf16[32,32,128]{2,1,0:T(8,128)(2,1)}), bf16[32,32,128]{2,1,0:T(8,128)(2,1)S(1)}, u32[]{:S(2)}, u32[]{:S(2)}) async-start(bf16[32,32,128]{2,1,0:T(8,128)(2,1)} %broadcast_in_dim.26), calls=%async_computation | async-start | bytes 524288 | tf_op jit(solution)/shard_map/all_to_all | solution.py:64
  27.0 9.2 %copy-start.18 = (f32[16,256]{1,0:T(8,128)S(1)}, f32[16,256]{1,0:T(8,128)}, u32[]{:S(2)}) copy-start(f32[16,256]{1,0:T(8,128)} %param.14) | copy-start | bytes 49156
  27.0 9.9 %copy-start.27 = (f32[16,256]{1,0:T(8,128)S(1)}, f32[16,256]{1,0:T(8,128)}, u32[]{:S(2)}) copy-start(f32[16,256]{1,0:T(8,128)} %param.13) | copy-start | bytes 49156
  27.0 10.4 %copy-start.7 = (f32[258,128]{1,0:T(8,128)S(1)}, f32[258,128]{1,0:T(8,128)}, u32[]{:S(2)}) copy-start(f32[258,128]{1,0:T(8,128)} %constant.169.clone) | copy-start | bytes 396292
  27.2 10.5 %copy-start.5 = (bf16[128,256]{1,0:T(8,128)(2,1)S(1)}, bf16[128,256]{1,0:T(8,128)(2,1)}, u32[]{:S(2)}) copy-start(bf16[128,256]{1,0:T(8,128)(2,1)} %param.12) | copy-start | bytes 196612
  27.3 10.5 %copy-start.6 = (bf16[128,256]{1,0:T(8,128)(2,1)S(1)}, bf16[128,256]{1,0:T(8,128)(2,1)}, u32[]{:S(2)}) copy-start(bf16[128,256]{1,0:T(8,128)(2,1)} %param.11) | copy-start | bytes 196612
  30.4 7.8 %copy-start.12 = (f32[128,129]{1,0:T(8,128)S(1)}, f32[128,129]{1,0:T(8,128)}, u32[]{:S(2)}) copy-start(f32[128,129]{1,0:T(8,128)} %constant.171) | copy-start | bytes 198148
  30.6 5.6 %collective-permute-start.1 = (f32[32,128]{1,0:T(8,128)S(1)}, f32[32,128]{1,0:T(8,128)S(1)}, u32[]{:S(2)}, u32[]{:S(2)}) collective-permute-start(f32[32,128]{1,0:T(8,128)S(1)} %pad_maximum_fusion.8), channel_id=1, source_target_pairs={{0,4},{4,0},{8,12},{12,8},{16,20},{20,16},{24,28},{28,24},{32,36},... | collective-permute-start | bytes 49160 | tf_op jit(solution)/shard_map/ppermute | solution.py:52
  30.7 16.9 %collective-permute-start.8 = (bf16[256,1024]{0,1:T(8,128)(2,1)S(1)}, bf16[256,1024]{0,1:T(8,128)(2,1)S(1)}, u32[]{:S(2)}, u32[]{:S(2)}) collective-permute-start(bf16[256,1024]{0,1:T(8,128)(2,1)S(1)} %pad_maximum_fusion.1), channel_id=1, source_target_pairs={{0,3},{1,0},{2,1},{3,2},{4,7},{5,4},{6,5},{7,6},{8,11},{9,8},{10,9... | collective-permute-start | bytes 1572872 | tf_op jit(solution)/shard_map/ppermute | solution.py:55
  31.4 15.9 %copy-start.16 = (bf16[128,8,128]{0,2,1:T(8,128)(2,1)S(1)}, bf16[128,8,128]{0,2,1:T(8,128)(2,1)}, u32[]{:S(2)}) copy-start(bf16[128,8,128]{0,2,1:T(8,128)(2,1)} %copy-done.15) | copy-start | bytes 786436
  31.4 15.5 %collective-permute-start.6 = (bf16[256,1024]{0,1:T(8,128)(2,1)S(1)}, bf16[256,1024]{0,1:T(8,128)(2,1)S(1)}, u32[]{:S(2)}, u32[]{:S(2)}) collective-permute-start(bf16[256,1024]{0,1:T(8,128)(2,1)S(1)} %pad_maximum_fusion.1), channel_id=1, source_target_pairs={{0,1},{1,2},{2,3},{3,0},{4,5},{5,6},{6,7},{7,4},{8,9},{9,10},{10,1... | collective-permute-start | bytes 1572872 | tf_op jit(solution)/shard_map/ppermute | solution.py:55
  32.8 24.5 %collective-permute-start.7 = (bf16[256,1024]{0,1:T(8,128)(2,1)S(1)}, bf16[256,1024]{0,1:T(8,128)(2,1)S(1)}, u32[]{:S(2)}, u32[]{:S(2)}) collective-permute-start(bf16[256,1024]{0,1:T(8,128)(2,1)S(1)} %pad_maximum_fusion.1), channel_id=1, source_target_pairs={{0,2},{1,3},{2,0},{3,1},{4,6},{5,7},{6,4},{7,5},{8,10},{9,11},{10,... | collective-permute-start | bytes 1572872 | tf_op jit(solution)/shard_map/ppermute | solution.py:55
  47.6 10.2 %copy-start.8 = (f32[128,129]{1,0:T(8,128)S(1)}, f32[128,129]{1,0:T(8,128)}, u32[]{:S(2)}) copy-start(f32[128,129]{1,0:T(8,128)} %constant.172) | copy-start | bytes 198148
  47.6 10.2 %copy-start.33 = (f32[256]{0:T(256)S(1)}, f32[256]{0:T(256)}, u32[]{:S(2)}) copy-start(f32[256]{0:T(256)} %param.15) | copy-start | bytes 3076
  47.6 11.5 %copy-start.30 = (bf16[128,256]{1,0:T(8,128)(2,1)S(1)}, bf16[128,256]{1,0:T(8,128)(2,1)}, u32[]{:S(2)}) copy-start(bf16[128,256]{1,0:T(8,128)(2,1)} %param.10) | copy-start | bytes 196612
  47.7 10.5 %copy-start.1 = (bf16[256,1024]{0,1:T(8,128)(2,1)}, bf16[256,1024]{0,1:T(8,128)(2,1)S(1)}, u32[]{:S(2)}) copy-start(bf16[256,1024]{0,1:T(8,128)(2,1)S(1)} %collective-permute-done.8) | copy-start | bytes 1572868
  57.7 1.4 collective-permute-start.9
  59.8 9.5 %copy-start.10 = (f32[128,256]{1,0:T(8,128)}, f32[128,256]{1,0:T(8,128)S(1)}, u32[]{:S(2)}) copy-start(f32[128,256]{1,0:T(8,128)S(1)} %get-tuple-element.47) | copy-start | bytes 393220
  61.2 21.4 %collective-permute-start.12 = (bf16[128,256]{1,0:T(8,128)(2,1)S(1)}, bf16[128,256]{1,0:T(8,128)(2,1)S(1)}, u32[]{:S(2)}, u32[]{:S(2)}) collective-permute-start(bf16[128,256]{1,0:T(8,128)(2,1)S(1)} %get-tuple-element.58), channel_id=1, source_target_pairs={{0,4},{4,0},{8,12},{12,8},{16,20},{20,16},{24,28},{28,24},{32,36},... | collective-permute-start | bytes 196616 | tf_op jit(solution)/shard_map/ppermute | solution.py:52
  61.6 7.8 %copy-start.19 = (f32[16,256]{1,0:T(8,128)S(1)}, f32[16,256]{1,0:T(8,128)}, u32[]{:S(2)}) copy-start(f32[16,256]{1,0:T(8,128)} %param.14) | copy-start | bytes 49156
  62.9 27.1 %collective-permute-start.4 = (bf16[128,2048]{1,0:T(8,128)(2,1)}, bf16[128,2048]{1,0:T(8,128)(2,1)}, u32[]{:S(2)}, u32[]{:S(2)}) collective-permute-start(bf16[128,2048]{1,0:T(8,128)(2,1)} %convolution_convert_fusion), channel_id=1, source_target_pairs={{0,3},{1,0},{2,1},{3,2},{4,7},{5,4},{6,5},{7,6},{8,11},{9,8},{10,9... | collective-permute-start | bytes 1572872 | tf_op jit(solution)/shard_map/ppermute | solution.py:55
  68.6 22.3 %collective-permute-start.3 = (bf16[128,2048]{1,0:T(8,128)(2,1)}, bf16[128,2048]{1,0:T(8,128)(2,1)}, u32[]{:S(2)}, u32[]{:S(2)}) collective-permute-start(bf16[128,2048]{1,0:T(8,128)(2,1)} %convolution_convert_fusion.1), channel_id=1, source_target_pairs={{0,2},{1,3},{2,0},{3,1},{4,6},{5,7},{6,4},{7,5},{8,10},{9,11},{10,... | collective-permute-start | bytes 1572872 | tf_op jit(solution)/shard_map/ppermute | solution.py:55
  69.4 13.2 %copy-start.2 = (bf16[256,1024]{0,1:T(8,128)(2,1)S(1)}, bf16[256,1024]{0,1:T(8,128)(2,1)}, u32[]{:S(2)}) copy-start(bf16[256,1024]{0,1:T(8,128)(2,1)} %copy-done.1) | copy-start | bytes 1572868
  70.6 12.4 %copy-start.4 = (bf16[256,1024]{0,1:T(8,128)(2,1)S(1)}, bf16[256,1024]{0,1:T(8,128)(2,1)}, u32[]{:S(2)}) copy-start(bf16[256,1024]{0,1:T(8,128)(2,1)} %copy-done.3) | copy-start | bytes 1572868
  70.6 4.2 %collective-permute-start.10 = (f32[49,256]{1,0:T(8,128)S(1)}, f32[49,256]{1,0:T(8,128)S(1)}, u32[]{:S(2)}, u32[]{:S(2)}) collective-permute-start(f32[49,256]{1,0:T(8,128)S(1)} %pad_maximum_fusion.3), channel_id=1, source_target_pairs={{0,4},{4,0},{8,12},{12,8},{16,20},{20,16},{24,28},{28,24},{32,36},... | collective-permute-start | bytes 150536 | tf_op jit(solution)/shard_map/ppermute | solution.py:52
  73.3 19.3 %collective-permute-start.2 = (bf16[128,2048]{1,0:T(8,128)(2,1)}, bf16[128,2048]{1,0:T(8,128)(2,1)}, u32[]{:S(2)}, u32[]{:S(2)}) collective-permute-start(bf16[128,2048]{1,0:T(8,128)(2,1)} %convolution_convert_fusion.2), channel_id=1, source_target_pairs={{0,1},{1,2},{2,3},{3,0},{4,5},{5,6},{6,7},{7,4},{8,9},{9,10},{10,1... | collective-permute-start | bytes 1572872 | tf_op jit(solution)/shard_map/ppermute | solution.py:55
  74.8 7.8 %copy-start.21 = (f32[16,256]{1,0:T(8,128)}, f32[16,256]{1,0:T(8,128)S(1)}, u32[]{:S(2)}) copy-start(f32[16,256]{1,0:T(8,128)S(1)} %slice_select_fusion) | copy-start | bytes 49156
  75.7 22.5 %all-to-all-start.1 = ((bf16[32,49,128]{2,1,0:T(8,128)(2,1)}), bf16[32,49,128]{2,1,0:T(8,128)(2,1)}, u32[]{:S(2)}, u32[]{:S(2)}) async-start(bf16[32,49,128]{2,1,0:T(8,128)(2,1)} %broadcast_in_dim.29), calls=%async_computation.1 | async-start | bytes 917504 | tf_op jit(solution)/shard_map/all_to_all | solution.py:64
  86.1 28.5 %collective-permute-start.15 = (bf16[8,256,128]{2,1,0:T(8,128)(2,1)}, bf16[8,256,128]{2,1,0:T(8,128)(2,1)}, u32[]{:S(2)}, u32[]{:S(2)}) collective-permute-start(bf16[8,256,128]{2,1,0:T(8,128)(2,1)} %get-tuple-element.51), channel_id=1, source_target_pairs={{0,192},{4,196},{8,200},{12,204},{16,208},{20,212},{24,216},{28,22... | collective-permute-start | bytes 1572872 | tf_op jit(solution)/shard_map/ppermute | solution.py:59
  89.1 25.5 %collective-permute-start.14 = (bf16[8,256,128]{2,1,0:T(8,128)(2,1)}, bf16[8,256,128]{2,1,0:T(8,128)(2,1)}, u32[]{:S(2)}, u32[]{:S(2)}) collective-permute-start(bf16[8,256,128]{2,1,0:T(8,128)(2,1)} %get-tuple-element.52), channel_id=1, source_target_pairs={{0,128},{4,132},{8,136},{12,140},{16,144},{20,148},{24,152},{28,15... | collective-permute-start | bytes 1572872 | tf_op jit(solution)/shard_map/ppermute | solution.py:59
  89.9 9.4 %copy-start.24 = (f32[16,128]{1,0:T(8,128)S(1)}, f32[16,128]{1,0:T(8,128)}, u32[]{:S(2)}) copy-start(f32[16,128]{1,0:T(8,128)} %copy-done.23) | copy-start | bytes 24580
  90.0 9.4 %copy-start.35 = (f32[32]{0:T(128)S(1)}, f32[32]{0:T(128)}, u32[]{:S(2)}) copy-start(f32[32]{0:T(128)} %convert_multiply_fusion.7) | copy-start | bytes 388
  90.0 9.4 %copy-start.36 = (pred[32]{0:T(512)(128)(4,1)S(1)}, pred[32]{0:T(512)(128)(4,1)}, u32[]{:S(2)}) copy-start(pred[32]{0:T(512)(128)(4,1)} %iota_compare_fusion) | copy-start | bytes 100
  90.0 27.8 %collective-permute-start.13 = (bf16[8,256,128]{2,1,0:T(8,128)(2,1)}, bf16[8,256,128]{2,1,0:T(8,128)(2,1)}, u32[]{:S(2)}, u32[]{:S(2)}) collective-permute-start(bf16[8,256,128]{2,1,0:T(8,128)(2,1)} %get-tuple-element.50), channel_id=1, source_target_pairs={{0,64},{4,68},{8,72},{12,76},{16,80},{20,84},{24,88},{28,92},{32,9... | collective-permute-start | bytes 1572872 | tf_op jit(solution)/shard_map/ppermute | solution.py:59
  99.6 26.8 %copy-start.20 = (f32[16,256]{1,0:T(8,128)S(1)}, f32[16,256]{1,0:T(8,128)}, u32[]{:S(2)}) copy-start(f32[16,256]{1,0:T(8,128)} %param.14) | copy-start | bytes 49156
  99.6 26.8 %copy-start.22 = (f32[16,256]{1,0:T(8,128)S(1)}, f32[16,256]{1,0:T(8,128)}, u32[]{:S(2)}) copy-start(f32[16,256]{1,0:T(8,128)} %copy-done.21) | copy-start | bytes 49156
  99.6 26.8 %copy-start.28 = (f32[16,256]{1,0:T(8,128)S(1)}, f32[16,256]{1,0:T(8,128)}, u32[]{:S(2)}) copy-start(f32[16,256]{1,0:T(8,128)} %param.13) | copy-start | bytes 49156
  99.6 27.4 %copy-start.32 = (f32[16,256]{1,0:T(8,128)S(1)}, f32[16,256]{1,0:T(8,128)}, u32[]{:S(2)}) copy-start(f32[16,256]{1,0:T(8,128)} %copy-done.31) | copy-start | bytes 49156
  99.6 27.4 %copy-start.38 = (f32[128]{0:T(128)S(1)}, f32[128]{0:T(128)}, u32[]{:S(2)}) copy-start(f32[128]{0:T(128)} %copy-done.37) | copy-start | bytes 1540
  99.6 27.8 %copy-start.9 = (f32[128,129]{1,0:T(8,128)S(1)}, f32[128,129]{1,0:T(8,128)}, u32[]{:S(2)}) copy-start(f32[128,129]{1,0:T(8,128)} %constant.172) | copy-start | bytes 198148
  99.6 27.8 %copy-start.11 = (f32[128,256]{1,0:T(8,128)S(1)}, f32[128,256]{1,0:T(8,128)}, u32[]{:S(2)}) copy-start(f32[128,256]{1,0:T(8,128)} %copy-done.10) | copy-start | bytes 393220
  99.7 27.8 %copy-start.34 = (f32[256]{0:T(256)S(1)}, f32[256]{0:T(256)}, u32[]{:S(2)}) copy-start(f32[256]{0:T(256)} %param.15) | copy-start | bytes 3076
  99.7 26.1 %collective-permute-start.11 = (f32[49,128]{1,0:T(8,128)S(1)}, f32[49,128]{1,0:T(8,128)S(1)}, u32[]{:S(2)}, u32[]{:S(2)}) collective-permute-start(f32[49,128]{1,0:T(8,128)S(1)} %pad_maximum_fusion.5), channel_id=1, source_target_pairs={{0,4},{4,0},{8,12},{12,8},{16,20},{20,16},{24,28},{28,24},{32,36},... | collective-permute-start | bytes 75272 | tf_op jit(solution)/shard_map/ppermute | solution.py:52
  120.2 23.4 %all-to-all-start.2 = ((bf16[8,256,128]{2,1,0:T(8,128)(2,1)}), bf16[8,256,128]{2,1,0:T(8,128)(2,1)S(1)}, u32[]{:S(2)}, u32[]{:S(2)}) async-start(bf16[8,256,128]{2,1,0:T(8,128)(2,1)} %fusion.24), calls=%async_computation.2 | async-start | bytes 1048576 | tf_op jit(solution)/shard_map/all_to_all | solution.py:227
  (10 other events, 36.3 us)
where the time goes:
time: 146 us; the launch traced here: 144 us
  waiting for transfers between devices  59.1 us (40%)
  starting transfers between devices  41.6 us (28%)
  matrix products  15.1 us (10%)
  local copies, waits for them, and re-layouts  13.5 us (9%)
  other arithmetic  13.1 us (9%)
  between operations  1.75 us (1%)
    ppermute x6, waiting for transfers between devices, shift_tp(): return lax.ppermute(a, 'tp', [(i, (i + k) % tps) for i in range(tps)])  19.4 us
    all_to_all x2, starting transfers between devices, of_pairs(): lax.all_to_all(copies, 'ctx', 0, 0, tiled=True, axis_index_groups=groups)  18.4 us
    ppermute x3, waiting for transfers between devices, shift_y(): lax.ppermute(a, 'ctx', [(i, (i // per + k) % ny * per + i % per) for i in...  18 us
    all_to_all x1, waiting for transfers between devices, body(): lax.all_to_all(summed_y, 'ctx', 0, 0, tiled=True, axis_index_groups=z_gro...  15.1 us
    ppermute x6, starting transfers between devices, shift_tp(): return lax.ppermute(a, 'tp', [(i, (i + k) % tps) for i in range(tps)])  11.4 us
    dot_general x4, matrix products, projected(): return jnp.dot(result, w_block, preferred_element_type=F32)  8.09 us
    unnamed x80, local copies, waits for them, and re-layouts  7.93 us
    all_to_all x2, waiting for transfers between devices, of_pairs(): lax.all_to_all(copies, 'ctx', 0, 0, tiled=True, axis_index_groups=groups)  5.63 us
  transfers between devices with their start and end apart: 19, of which 9 were waited for; matrix products, arithmetic and copies ran while one was open for 25% of the time, Pallas kernels for 0%

commit v1 on v0

--- a/solution.py
+++ b/solution.py
@@ -2,6 +2,9 @@
 import jax.numpy as jnp
 import numpy as np
 from jax import lax
+from jax.experimental import pallas as pl
+from jax.experimental.layout import Layout, with_layout_constraint
+from jax.experimental.pallas import tpu as pltpu
 from jax.sharding import PartitionSpec as P
 
 F32 = jnp.float32
@@ -32,12 +35,71 @@
     )
 
 
+def row_major(a):
+    return with_layout_constraint(a, Layout(major_to_minor=tuple(range(a.ndim))))
+
+
+def in_vmem(count):
+    return [pl.BlockSpec(memory_space=pltpu.VMEM)] * count
+
+
+def given_half(turns, rows, width):
+    count = rows.shape[1] // (2 * width)
+
+    def kernel(turns_ref, rows_ref, out_ref):
+        other = 1 - turns_ref[0]
+        for i in range(count):
+            at = pl.multiple_of((2 * i + other) * width, width)
+            out_ref[:, i * width : (i + 1) * width] = rows_ref[:, pl.ds(at, width)]
+
+    return pl.pallas_call(
+        kernel,
+        out_shape=jax.ShapeDtypeStruct((rows.shape[0], count * width), rows.dtype),
+        in_specs=[pl.BlockSpec(memory_space=pltpu.SMEM)] + in_vmem(1),
+        out_specs=in_vmem(1)[0],
+    )(turns, rows)
+
+
+def weight_parts(turns, result, result_other, blocks, taken, width):
+    count = len(blocks)
+    tokens, chans = result.shape
+    tiles = blocks[0].shape[1] // (2 * width)
+
+    def kernel(turns_ref, *refs):
+        mine_ref, other_ref = refs[:2]
+        block_refs, taken_refs = refs[2 : 2 + count], refs[2 + count : 2 + 2 * count]
+        out_refs, all_ref = refs[2 + 2 * count : -1], refs[-1]
+        core = turns_ref[0]
+        for k in range(count):
+            for i in range(tiles):
+                at = pl.multiple_of((2 * i + core) * width, width)
+                lanes = slice(i * width, (i + 1) * width)
+                all_ref[k, :tokens, lanes] = block_refs[k][:, pl.ds(at, width)]
+            all_ref[k, tokens:, :] = taken_refs[k][...]
+        left = jnp.concatenate([mine_ref[...], other_ref[...]], 0).T
+        for s in range(count):
+            part = jnp.dot(
+                left, all_ref[(turns_ref[1] - s + count) % count], preferred_element_type=F32
+            ).astype(BF16)
+            for i in range(tiles):
+                out_refs[s][i] = part[:, i * width : (i + 1) * width]
+
+    return pl.pallas_call(
+        kernel,
+        out_shape=[jax.ShapeDtypeStruct((tiles, chans, width), BF16)] * count,
+        in_specs=[pl.BlockSpec(memory_space=pltpu.SMEM)] + in_vmem(2 + 2 * count),
+        out_specs=in_vmem(count),
+        scratch_shapes=[pltpu.VMEM((count, 2 * tokens, tiles * width), BF16)],
+    )(turns, result, result_other, *blocks, *taken)
+
+
 def body(outer_gate, inner_gate, values, residues, log_decay, skip_gain, out_weight, out_grad):
     ctx = lax.axis_size("ctx")
     tps = lax.axis_size("tp")
     dev = lax.axis_index("ctx")
     tp = lax.axis_index("tp")
     block, chans = outer_gate.shape
+    first_weight = row_major(out_weight)
     modes = residues.shape[0]
     feats = out_grad.shape[1]
     ny = tps
@@ -63,11 +125,7 @@
         groups = [[2 * i + j for i in range(pairs)] for j in range(2)]
         return lax.all_to_all(copies, "ctx", 0, 0, tiled=True, axis_index_groups=groups)
 
-    og = out_grad.reshape(block, nz, 2, width)
-    og_mine = lax.dynamic_index_in_dim(og, core, 2, keepdims=False)
-    og_other = lax.dynamic_index_in_dim(og, 1 - core, 2, keepdims=False)
-    pg0 = jnp.concatenate([og_mine, swap_core(og_other)], 0).reshape(2 * block, nz * width)
-    pgs = [pg0] + [shift_tp(pg0, k) for k in range(1, tps)]
+    og = [out_grad] + [row_major(shift_tp(out_grad, k)) for k in range(1, tps)]
 
     u = inner_gate.astype(F32) * values.astype(F32)
     rate = jnp.exp(log_decay)
@@ -131,29 +189,21 @@
     conv_local = back(inverse, h_re * u_re - h_im * u_im, h_re * u_im + h_im * u_re)
     conv_out = conv_local + jnp.sum((gain * x_in)[:, None, :] * fall, 0)
     gated = conv_out + skip_gain[None, :] * u
-    result = (outer_f * gated).astype(BF16)
-
-    result_pair = jnp.concatenate([result, swap_core(result)], 0)
-    parts = [
-        lax.dot_general(result_pair, pg, (((0,), (0,)), ((), ())), preferred_element_type=F32)
-        .astype(BF16)
-        .reshape(chans, nz, width)
-        .swapaxes(0, 1)
-        for pg in pgs
-    ]
-    parts = jnp.stack(parts, 0)
-
-    def part_for(s):
-        return lax.dynamic_index_in_dim(parts, (tp - yy - s) % tps, 0, keepdims=False)
-
-    y_parts = [part_for(s) for s in range(ny)]
+    result = row_major((outer_f * gated).astype(BF16))
+
+    turns = jnp.stack([core, (tp - yy) % tps]).astype(jnp.int32)
+    given = [given_half(turns, a, width) for a in og]
+    taken = [swap_core(a) for a in given]
+    result_other = swap_core(result)
+    y_parts = weight_parts(turns, result, result_other, og, taken, width)
     over_y = [y_parts[0]] + [shift_y(y_parts[s], s) for s in range(1, ny)]
     summed_y = sum(a.astype(F32) for a in over_y).astype(BF16)
 
-    w_blocks = out_weight.reshape(chans, tps, feats)
+    late = lax.optimization_barrier((result, gated, out_weight, *y_parts))
+    result, gated, out_weight = late[:3]
 
     def projected(k):
-        w_block = lax.dynamic_index_in_dim(w_blocks, (tp + k) % tps, 1, keepdims=False)
+        w_block = lax.dynamic_slice_in_dim(out_weight, (tp + k) % tps * feats, feats, 1)
         return jnp.dot(result, w_block, preferred_element_type=F32)
 
     mixed = projected(0)
@@ -163,19 +213,16 @@
         mixed = mixed + piece.astype(F32)
     mixed = mixed.astype(BF16)
 
-    w_half = lax.dynamic_index_in_dim(
-        out_weight.reshape(chans, tps, nz, 2, width), core, 3, keepdims=False
-    ).reshape(chans, tps, nz * width)
-    grad_pair = 0.0
+    grad_gated = 0.0
     for k in range(tps):
-        w_block = lax.dynamic_index_in_dim(w_half, (tp - k) % tps, 1, keepdims=False)
-        grad_pair = grad_pair + lax.dot_general(
-            pgs[k], w_block, (((1,), (1,)), ((), ())), preferred_element_type=F32
+        w_block = lax.dynamic_slice_in_dim(first_weight, (tp - k) % tps * feats, feats, 1)
+        grad_gated = grad_gated + lax.dot_general(
+            og[k], w_block, (((1,), (1,)), ((), ())), preferred_element_type=F32
         )
-    grad_gated = grad_pair[:block] + swap_core(grad_pair[block:])
-    outer_gate, inner_gate, values, residues, log_decay, grad_gated = lax.optimization_barrier(
-        (outer_gate, inner_gate, values, residues, log_decay, grad_gated)
-    )
+    late = lax.optimization_barrier(
+        (outer_gate, inner_gate, values, residues, log_decay, grad_gated, *y_parts)
+    )
+    outer_gate, inner_gate, values, residues, log_decay, grad_gated = late[:6]
     outer_f = outer_gate.astype(F32)
     inner_f = inner_gate.astype(F32)
     value_f = values.astype(F32)

time: 146 us -> 109 us (0.75)
  the two profiles are of different devices: /device:TPU:2 before, /device:TPU:25 now
where the time goes in v1:
time: 109 us; the launch traced here: 108 us
  starting transfers between devices  44.4 us (41%)
  matrix products  21.3 us (20%)
  waiting for transfers between devices  14.3 us (13%)
  Pallas kernels  11.2 us (10%)
  other arithmetic  10.4 us (10%)
  local copies, waits for them, and re-layouts  4.87 us (4%)
  between operations  1.37 us (1%)
    all_to_all x2, starting transfers between devices, of_pairs(): lax.all_to_all(copies, 'ctx', 0, 0, tiled=True, axis_index_groups=groups)  21.3 us
    dot_general x4, matrix products, projected(): return jnp.dot(result, w_block, preferred_element_type=F32)  10 us
    ppermute x6, starting transfers between devices, shift_tp(): return lax.ppermute(a, 'tp', [(i, (i + k) % tps) for i in range(tps)])  7.88 us
    pallas_call x4, Pallas kernels, given_half(): pl.pallas_call(kernel, out_shape=jax.ShapeDtypeStruct((rows.shape[0], cou...  7.35 us
    all_to_all x1, starting transfers between devices, body(): lax.all_to_all(summed_y, 'ctx', 0, 0, tiled=True, axis_index_groups=z_gro...  7.2 us
    ppermute x6, waiting for transfers between devices, shift_tp(): return lax.ppermute(a, 'tp', [(i, (i + k) % tps) for i in range(tps)])  7.14 us
    dot_general x4, matrix products, body(): lax.dot_general(og[k], w_block, (((1,), (1,)), ((), ())), preferred_eleme...  7.02 us
    ppermute x9, starting transfers between devices, swap_core(): return lax.ppermute(a, 'ctx', [(i, i ^ 1) for i in range(ctx)])  5.72 us
  transfers between devices with their start and end apart: 21, of which 4 were waited for; matrix products, arithmetic and copies ran while one was open for 30% of the time, Pallas kernels for 7%

profile of v1, /device:TPU:25, one launch (start us, length us, event | category | flops | bytes accessed | tf_op | source)
XLA Modules:
  0.0 108.0 jit_solution(13728464864353225353)
XLA Ops:
  0.6 1.3 %collective-permute-start.3 = (bf16[128,2048]{1,0:T(8,128)(2,1)}, bf16[128,2048]{1,0:T(8,128)(2,1)S(1)}, u32[]{:S(2)}, u32[]{:S(2)}) collective-permute-start(bf16[128,2048]{1,0:T(8,128)(2,1)} %refs_2_.1), channel_id=1, source_target_pairs={{0,1},{1,2},{2,3},{3,0},{4,5},{5,6},{6,7},{7,4},{8,9},{9,10},{10,1... | collective-permute-start | bytes 1572872 | tf_op jit(solution)/shard_map/ppermute | solution.py:117
  1.9 2.5 %collective-permute-start.4 = (bf16[128,2048]{1,0:T(8,128)(2,1)}, bf16[128,2048]{1,0:T(8,128)(2,1)S(1)}, u32[]{:S(2)}, u32[]{:S(2)}) collective-permute-start(bf16[128,2048]{1,0:T(8,128)(2,1)} %refs_2_.1), channel_id=1, source_target_pairs={{0,2},{1,3},{2,0},{3,1},{4,6},{5,7},{6,4},{7,5},{8,10},{9,11},{10,... | collective-permute-start | bytes 1572872 | tf_op jit(solution)/shard_map/ppermute | solution.py:117
  4.4 1.2 %collective-permute-start.5 = (bf16[128,2048]{1,0:T(8,128)(2,1)}, bf16[128,2048]{1,0:T(8,128)(2,1)S(1)}, u32[]{:S(2)}, u32[]{:S(2)}) collective-permute-start(bf16[128,2048]{1,0:T(8,128)(2,1)} %refs_2_.1), channel_id=1, source_target_pairs={{0,3},{1,0},{2,1},{3,2},{4,7},{5,4},{6,5},{7,6},{8,11},{9,8},{10,9... | collective-permute-start | bytes 1572872 | tf_op jit(solution)/shard_map/ppermute | solution.py:117
  5.5 0.7 fusion.107
  6.3 0.9 convert_multiply_fusion.5
  7.2 0.7 fusion.4
  7.9 1.6 %collective-permute-start = (f32[32,256]{1,0:T(8,128)S(1)}, f32[32,256]{1,0:T(8,128)S(1)}, u32[]{:S(2)}, u32[]{:S(2)}) collective-permute-start(f32[32,256]{1,0:T(8,128)S(1)} %pad_maximum_fusion.1), channel_id=1, source_target_pairs={{0,4},{4,0},{8,12},{12,8},{16,20},{20,16},{24,28},{28,24},{32,36},... | collective-permute-start | bytes 98312 | tf_op jit(solution)/shard_map/ppermute | solution.py:114
  9.5 0.6 pad_add_fusion.turns_ref
  10.1 1.9 %shard_map.161 = bf16[128,1024]{1,0:T(8,128)(2,1)} custom-call(s32[2]{0:T(128)} %pad_add_fusion.turns_ref, bf16[128,2048]{1,0:T(8,128)(2,1)} %refs_2_.1), custom_call_target="tpu_custom_call" | custom-call | tf_op jit(solution)/shard_map/pallas_call | solution.py:55
  12.1 0.8 broadcast_in_dim.26
  12.9 11.0 %all-to-all-start = ((bf16[32,32,128]{2,1,0:T(8,128)(2,1)}), bf16[32,32,128]{2,1,0:T(8,128)(2,1)S(1)}, u32[]{:S(2)}, u32[]{:S(2)}) async-start(bf16[32,32,128]{2,1,0:T(8,128)(2,1)} %broadcast_in_dim.26), calls=%async_computation | async-start | bytes 524288 | tf_op jit(solution)/shard_map/all_to_all | solution.py:126
  24.0 1.7 %fusion.18 = f32[256,128]{0,1:T(8,128)S(1)} fusion(bf16[128,2048]{1,0:T(8,128)(2,1)S(1)} %copy-done.2, bf16[256,8192]{1,0:T(8,128)(2,1)} %param.16, s32[]{:T(128)S(6)} %select_n.165), kind=kOutput, calls=%fused_computation.37 | convolution fusion | flops 134217728 | bytes 1703940 | tf_op jit(solution)/shard_map/dot_general | solution.py:219
  25.7 0.8 copy-done.5
  26.5 1.8 %shard_map.162 = bf16[128,1024]{1,0:T(8,128)(2,1)} custom-call(s32[2]{0:T(128)} %pad_add_fusion.turns_ref, bf16[128,2048]{1,0:T(8,128)(2,1)} %copy-done.5), custom_call_target="tpu_custom_call" | custom-call | tf_op jit(solution)/shard_map/pallas_call | solution.py:55
  28.3 1.0 collective-permute-start.7
  29.3 0.8 copy-done
  30.1 1.8 %shard_map.163 = bf16[128,1024]{1,0:T(8,128)(2,1)} custom-call(s32[2]{0:T(128)} %pad_add_fusion.turns_ref, bf16[128,2048]{1,0:T(8,128)(2,1)} %copy-done), custom_call_target="tpu_custom_call" | custom-call | tf_op jit(solution)/shard_map/pallas_call | solution.py:55
  32.0 0.8 copy-done.3
  32.8 1.8 %shard_map.164 = bf16[128,1024]{1,0:T(8,128)(2,1)} custom-call(s32[2]{0:T(128)} %pad_add_fusion.turns_ref, bf16[128,2048]{1,0:T(8,128)(2,1)} %copy-done.3), custom_call_target="tpu_custom_call" | custom-call | tf_op jit(solution)/shard_map/pallas_call | solution.py:55
  35.1 1.8 %convolution_add_fusion.3 = f32[256,128]{0,1:T(8,128)S(1)} fusion(f32[256,128]{0,1:T(8,128)S(1)} %fusion.18, bf16[128,2048]{1,0:T(8,128)(2,1)} %copy-done.5, bf16[256,8192]{1,0:T(8,128)(2,1)} %param.16, s32[]{:T(128)S(6)} %select_n.173), kind=kOutput, calls=%fused_computation.26 | convolution fusion | flops 134250496 | bytes 1835012 | tf_op jit(solution)/shard_map/dot_general | solution.py:219
  37.5 1.7 %fusion.14 = f32[256,128]{0,1:T(8,128)S(1)} fusion(bf16[128,2048]{1,0:T(8,128)(2,1)S(1)} %copy-done.4, bf16[256,8192]{1,0:T(8,128)(2,1)} %param.16, s32[]{:T(128)S(6)} %select_n.177), kind=kOutput, calls=%fused_computation.33 | convolution fusion | flops 134217728 | bytes 1703940 | tf_op jit(solution)/shard_map/dot_general | solution.py:219
  41.4 0.7 collective-permute-start.2
  42.1 1.7 %fusion.10 = f32[128,256]{1,0:T(8,128)S(1)} fusion(f32[256,128]{0,1:T(8,128)S(1)} %fusion.14, f32[256,128]{0,1:T(8,128)S(1)} %convolution_add_fusion.3, bf16[128,2048]{1,0:T(8,128)(2,1)S(1)} %copy-done.1, bf16[256,8192]{1,0:T(8,128)(2,1)} %param.16, s32[]{:T(128)S(6)} %select_n.175), kind=kOutput, calls=%fused_computation.25 | convolution fusion | flops 134283264 | bytes 1966084 | tf_op jit(solution)/shard_map/dot_general | solution.py:219
  43.9 0.6 copy-done.16
  44.6 3.9 %shard_map.165 = (bf16[8,256,128]{2,1,0:T(8,128)(2,1)}, bf16[8,256,128]{2,1,0:T(8,128)(2,1)}, bf16[8,256,128]{2,1,0:T(8,128)(2,1)}, bf16[8,256,128]{2,1,0:T(8,128)(2,1)}) custom-call(s32[2]{0:T(128)} %pad_add_fusion.turns_ref, bf16[128,256]{1,0:T(8,128)(2,1)} %copy-done.6, bf16[128,256]{1,0:T(8,128)(2,1)} %copy-done.18, bf16[128,2048]{1,0:T(8,128)(2,1)} %refs_2_.1, ...), custom_call_target="tpu_custom_call" | custom-call | tf_op jit(solution)/shard_map/pallas_call | solution.py:87
  48.5 2.3 %collective-permute-start.16 = (bf16[8,256,128]{2,1,0:T(8,128)(2,1)}, bf16[8,256,128]{2,1,0:T(8,128)(2,1)S(1)}, u32[]{:S(2)}, u32[]{:S(2)}) collective-permute-start(bf16[8,256,128]{2,1,0:T(8,128)(2,1)} %get-tuple-element.36), channel_id=1, source_target_pairs={{0,128},{4,132},{8,136},{12,140},{16,144},{20,148},{24,152},{28,15... | collective-permute-start | bytes 1572872 | tf_op jit(solution)/shard_map/ppermute | solution.py:121
  50.8 0.7 fusion.53
  51.9 0.6 fusion.33
  52.5 0.6 fusion.5
  53.3 1.1 %fusion.3 = (f32[16,256]{1,0:T(8,128)S(1)}, f32[16,256]{1,0:T(8,128)S(1)}, f32[16,256]{1,0:T(8,128)S(1)}, f32[16,256]{1,0:T(8,128)S(1)}) fusion(f32[128,256]{1,0:T(8,128)S(1)} %copy.47, f32[16,256]{1,0:T(8,128)S(1)} %exponential_negate_fusion.1, f32[128,256]{1,0:T(8,128)S(1)} %get-tuple-element.61), kind=kLoop, calls=%fused_computation.10 | loop fusion | flops 4702208 | bytes 344064 | tf_op jit(solution)/shard_map/reduce_sum | solution.py:246
  54.4 0.7 collective-permute-start.13
  55.2 2.3 %convolution_convert_fusion.2 = bf16[128,2048]{1,0:T(8,128)(2,1)} fusion(bf16[128,256]{1,0:T(8,128)(2,1)S(1)} %copy-done.7, bf16[256,8192]{1,0:T(8,128)(2,1)} %param.16, s32[]{:T(128)S(6)} %select_n.167), kind=kOutput, calls=%fused_computation.2 | convolution fusion | flops 134479872 | bytes 1638404 | tf_op jit(solution)/shard_map/dot_general | solution.py:207
  57.9 0.8 broadcast_in_dim.29
  58.7 10.4 %all-to-all-start.1 = ((bf16[32,49,128]{2,1,0:T(8,128)(2,1)}), bf16[32,49,128]{2,1,0:T(8,128)(2,1)S(1)}, u32[]{:S(2)}, u32[]{:S(2)}) async-start(bf16[32,49,128]{2,1,0:T(8,128)(2,1)} %broadcast_in_dim.29), calls=%async_computation.1 | async-start | bytes 917504 | tf_op jit(solution)/shard_map/all_to_all | solution.py:126
  69.1 2.4 %convolution_convert_fusion.1 = bf16[128,2048]{1,0:T(8,128)(2,1)} fusion(bf16[128,256]{1,0:T(8,128)(2,1)S(1)} %copy-done.7, bf16[256,8192]{1,0:T(8,128)(2,1)} %param.16, s32[]{:T(128)S(6)} %select_n.169), kind=kOutput, calls=%fused_computation.1 | convolution fusion | flops 134479872 | bytes 1638404 | tf_op jit(solution)/shard_map/dot_general | solution.py:207
  72.4 2.3 %convolution_convert_fusion = bf16[128,2048]{1,0:T(8,128)(2,1)} fusion(bf16[128,256]{1,0:T(8,128)(2,1)S(1)} %copy-done.7, bf16[256,8192]{1,0:T(8,128)(2,1)} %param.16, s32[]{:T(128)S(6)} %select_n.171), kind=kOutput, calls=%fused_computation | convolution fusion | flops 134479872 | bytes 1638404 | tf_op jit(solution)/shard_map/dot_general | solution.py:207
  74.7 2.1 %collective-permute-start.12 = (bf16[128,2048]{1,0:T(8,128)(2,1)}, bf16[128,2048]{1,0:T(8,128)(2,1)}, u32[]{:S(2)}, u32[]{:S(2)}) collective-permute-start(bf16[128,2048]{1,0:T(8,128)(2,1)} %convolution_convert_fusion), channel_id=1, source_target_pairs={{0,3},{1,0},{2,1},{3,2},{4,7},{5,4},{6,5},{7,6},{8,11},{9,8},{10,9... | collective-permute-start | bytes 1572872 | tf_op jit(solution)/shard_map/ppermute | solution.py:117
  76.8 0.9 collective-permute-done.17
  77.7 2.1 %add_convert_fusion = bf16[8,256,128]{2,1,0:T(8,128)(2,1)} fusion(bf16[8,256,128]{2,1,0:T(8,128)(2,1)} %collective-permute-done.17, bf16[8,256,128]{2,1,0:T(8,128)(2,1)S(1)} %collective-permute-done.16, bf16[8,256,128]{2,1,0:T(8,128)(2,1)S(1)} %collective-permute-done.15, bf16[8,256,128]{2,1,0:T(8,128)(2,1)S(1)} %copy-done.13), kind=kLoop, calls=%fused_computation.32 | loop fusion | flops 2097152 | bytes 2621440 | tf_op jit(solution)/shard_map/convert_element_type | solution.py:200
  79.8 2.2 %all-to-all-done.1 = bf16[32,49,128]{2,1,0:T(8,128)(2,1)S(1)} async-done(((bf16[32,49,128]{2,1,0:T(8,128)(2,1)}), bf16[32,49,128]{2,1,0:T(8,128)(2,1)S(1)}, u32[]{:S(2)}, u32[]{:S(2)}) %all-to-all-start.1) | async-done | bytes 401440 | tf_op jit(solution)/shard_map/all_to_all | solution.py:126
  82.1 7.2 %all-to-all-start.2 = ((bf16[8,256,128]{2,1,0:T(8,128)(2,1)}), bf16[8,256,128]{2,1,0:T(8,128)(2,1)S(1)}, u32[]{:S(2)}, u32[]{:S(2)}) async-start(bf16[8,256,128]{2,1,0:T(8,128)(2,1)} %add_convert_fusion), calls=%async_computation.2 | async-start | bytes 1048576 | tf_op jit(solution)/shard_map/all_to_all | solution.py:274
  89.5 1.0 collective-permute-start.14
  90.5 7.1 %collective-permute-done.12 = bf16[128,2048]{1,0:T(8,128)(2,1)} collective-permute-done((bf16[128,2048]{1,0:T(8,128)(2,1)}, bf16[128,2048]{1,0:T(8,128)(2,1)}, u32[]{:S(2)}, u32[]{:S(2)}) %collective-permute-start.12) | collective-permute-done | bytes 524320 | tf_op jit(solution)/shard_map/ppermute | solution.py:117
  97.6 2.9 %add_convert_fusion.1 = bf16[128,2048]{1,0:T(8,128)(2,1)} fusion(bf16[128,2048]{1,0:T(8,128)(2,1)} %collective-permute-done.12, bf16[128,2048]{1,0:T(8,128)(2,1)} %collective-permute-done.11, bf16[128,2048]{1,0:T(8,128)(2,1)} %collective-permute-done.10, bf16[128,256]{1,0:T(8,128)(2,1)S(1)} %copy-done.7, bf16[256,8192]{1,0:T(8,128)(2,1)} %param.16, ...), kind=kOutput, calls=%fused_computation.39 | convolution fusion | flops 136052736 | bytes 3211268 | tf_op jit(solution)/shard_map/dot_general | solution.py:207
  101.1 0.6 fusion.88
  102.2 1.0 fusion.51
  103.2 4.0 %all-to-all-done.2 = bf16[8,256,128]{2,1,0:T(8,128)(2,1)S(1)} async-done(((bf16[8,256,128]{2,1,0:T(8,128)(2,1)}), bf16[8,256,128]{2,1,0:T(8,128)(2,1)S(1)}, u32[]{:S(2)}, u32[]{:S(2)}) %all-to-all-start.2) | async-done | bytes 524320 | tf_op jit(solution)/shard_map/all_to_all | solution.py:274
  107.2 0.7 convert_reduce_fusion
  (101 shorter events, 6.2 us)
Async XLA Ops:
  0.6 23.3 %copy-start.2 = (bf16[128,2048]{1,0:T(8,128)(2,1)S(1)}, bf16[128,2048]{1,0:T(8,128)(2,1)}, u32[]{:S(2)}) copy-start(bf16[128,2048]{1,0:T(8,128)(2,1)} %refs_2_.1) | copy-start | bytes 1572868
  0.6 25.1 %collective-permute-start.3 = (bf16[128,2048]{1,0:T(8,128)(2,1)}, bf16[128,2048]{1,0:T(8,128)(2,1)S(1)}, u32[]{:S(2)}, u32[]{:S(2)}) collective-permute-start(bf16[128,2048]{1,0:T(8,128)(2,1)} %refs_2_.1), channel_id=1, source_target_pairs={{0,1},{1,2},{2,3},{3,0},{4,5},{5,6},{6,7},{7,4},{8,9},{9,10},{10,1... | collective-permute-start | bytes 1572872 | tf_op jit(solution)/shard_map/ppermute | solution.py:117
  1.9 27.4 %collective-permute-start.4 = (bf16[128,2048]{1,0:T(8,128)(2,1)}, bf16[128,2048]{1,0:T(8,128)(2,1)S(1)}, u32[]{:S(2)}, u32[]{:S(2)}) collective-permute-start(bf16[128,2048]{1,0:T(8,128)(2,1)} %refs_2_.1), channel_id=1, source_target_pairs={{0,2},{1,3},{2,0},{3,1},{4,6},{5,7},{6,4},{7,5},{8,10},{9,11},{10,... | collective-permute-start | bytes 1572872 | tf_op jit(solution)/shard_map/ppermute | solution.py:117
  4.4 27.6 %collective-permute-start.5 = (bf16[128,2048]{1,0:T(8,128)(2,1)}, bf16[128,2048]{1,0:T(8,128)(2,1)S(1)}, u32[]{:S(2)}, u32[]{:S(2)}) collective-permute-start(bf16[128,2048]{1,0:T(8,128)(2,1)} %refs_2_.1), channel_id=1, source_target_pairs={{0,3},{1,0},{2,1},{3,2},{4,7},{5,4},{6,5},{7,6},{8,11},{9,8},{10,9... | collective-permute-start | bytes 1572872 | tf_op jit(solution)/shard_map/ppermute | solution.py:117
  7.9 4.1 %collective-permute-start = (f32[32,256]{1,0:T(8,128)S(1)}, f32[32,256]{1,0:T(8,128)S(1)}, u32[]{:S(2)}, u32[]{:S(2)}) collective-permute-start(f32[32,256]{1,0:T(8,128)S(1)} %pad_maximum_fusion.1), channel_id=1, source_target_pairs={{0,4},{4,0},{8,12},{12,8},{16,20},{20,16},{24,28},{28,24},{32,36},... | collective-permute-start | bytes 98312 | tf_op jit(solution)/shard_map/ppermute | solution.py:114
  11.9 31.9 %collective-permute-start.6 = (bf16[128,1024]{1,0:T(8,128)(2,1)}, bf16[128,1024]{1,0:T(8,128)(2,1)S(1)}, u32[]{:S(2)}, u32[]{:S(2)}) collective-permute-start(bf16[128,1024]{1,0:T(8,128)(2,1)} %shard_map.161), channel_id=1, source_target_pairs={{0,4},{4,0},{8,12},{12,8},{16,20},{20,16},{24,28},{28,24},{32,36},... | collective-permute-start | bytes 786440 | tf_op jit(solution)/shard_map/ppermute | solution.py:114
  12.9 24.1 %all-to-all-start = ((bf16[32,32,128]{2,1,0:T(8,128)(2,1)}), bf16[32,32,128]{2,1,0:T(8,128)(2,1)S(1)}, u32[]{:S(2)}, u32[]{:S(2)}) async-start(bf16[32,32,128]{2,1,0:T(8,128)(2,1)} %broadcast_in_dim.26), calls=%async_computation | async-start | bytes 524288 | tf_op jit(solution)/shard_map/all_to_all | solution.py:126
  25.7 0.8 copy-start.5
  28.3 15.5 %collective-permute-start.7 = (bf16[128,1024]{1,0:T(8,128)(2,1)}, bf16[128,1024]{1,0:T(8,128)(2,1)S(1)}, u32[]{:S(2)}, u32[]{:S(2)}) collective-permute-start(bf16[128,1024]{1,0:T(8,128)(2,1)} %shard_map.162), channel_id=1, source_target_pairs={{0,4},{4,0},{8,12},{12,8},{16,20},{20,16},{24,28},{28,24},{32,36},... | collective-permute-start | bytes 786440 | tf_op jit(solution)/shard_map/ppermute | solution.py:114
  29.3 0.8 copy-start
  32.0 11.9 %collective-permute-start.8 = (bf16[128,1024]{1,0:T(8,128)(2,1)}, bf16[128,1024]{1,0:T(8,128)(2,1)}, u32[]{:S(2)}, u32[]{:S(2)}) collective-permute-start(bf16[128,1024]{1,0:T(8,128)(2,1)} %shard_map.163), channel_id=1, source_target_pairs={{0,4},{4,0},{8,12},{12,8},{16,20},{20,16},{24,28},{28,24},{32,36},... | collective-permute-start | bytes 786440 | tf_op jit(solution)/shard_map/ppermute | solution.py:114
  32.0 0.8 copy-start.3
  34.6 2.9 %copy-start.4 = (bf16[128,2048]{1,0:T(8,128)(2,1)S(1)}, bf16[128,2048]{1,0:T(8,128)(2,1)}, u32[]{:S(2)}) copy-start(bf16[128,2048]{1,0:T(8,128)(2,1)} %copy-done.3) | copy-start | bytes 1572868
  34.6 4.6 %copy-start.14 = (f32[16,256]{1,0:T(8,128)S(1)}, f32[16,256]{1,0:T(8,128)}, u32[]{:S(2)}) copy-start(f32[16,256]{1,0:T(8,128)} %param.14) | copy-start | bytes 49156
  34.6 4.7 %copy-start.19 = (f32[16,256]{1,0:T(8,128)S(1)}, f32[16,256]{1,0:T(8,128)}, u32[]{:S(2)}) copy-start(f32[16,256]{1,0:T(8,128)} %param.13) | copy-start | bytes 49156
  34.6 9.2 %collective-permute-start.9 = (bf16[128,1024]{1,0:T(8,128)(2,1)}, bf16[128,1024]{1,0:T(8,128)(2,1)}, u32[]{:S(2)}, u32[]{:S(2)}) collective-permute-start(bf16[128,1024]{1,0:T(8,128)(2,1)} %shard_map.164), channel_id=1, source_target_pairs={{0,4},{4,0},{8,12},{12,8},{16,20},{20,16},{24,28},{28,24},{32,36},... | collective-permute-start | bytes 786440 | tf_op jit(solution)/shard_map/ppermute | solution.py:114
  37.0 2.9 %copy-start.10 = (f32[258,128]{1,0:T(8,128)S(1)}, f32[258,128]{1,0:T(8,128)}, u32[]{:S(2)}) copy-start(f32[258,128]{1,0:T(8,128)} %constant.117.clone) | copy-start | bytes 396292
  37.1 3.2 %copy-start.8 = (bf16[128,256]{1,0:T(8,128)(2,1)S(1)}, bf16[128,256]{1,0:T(8,128)(2,1)}, u32[]{:S(2)}) copy-start(bf16[128,256]{1,0:T(8,128)(2,1)} %param.12) | copy-start | bytes 196612
  37.1 3.2 %copy-start.9 = (bf16[128,256]{1,0:T(8,128)(2,1)S(1)}, bf16[128,256]{1,0:T(8,128)(2,1)}, u32[]{:S(2)}) copy-start(bf16[128,256]{1,0:T(8,128)(2,1)} %param.11) | copy-start | bytes 196612
  37.3 3.4 %copy-start.12 = (f32[128,129]{1,0:T(8,128)S(1)}, f32[128,129]{1,0:T(8,128)}, u32[]{:S(2)}) copy-start(f32[128,129]{1,0:T(8,128)} %constant.119) | copy-start | bytes 198148
  37.3 3.7 %copy-start.11 = (f32[128,129]{1,0:T(8,128)S(1)}, f32[128,129]{1,0:T(8,128)}, u32[]{:S(2)}) copy-start(f32[128,129]{1,0:T(8,128)} %constant.120) | copy-start | bytes 198148
  37.3 3.7 %copy-start.15 = (bf16[128,256]{1,0:T(8,128)(2,1)S(1)}, bf16[128,256]{1,0:T(8,128)(2,1)}, u32[]{:S(2)}) copy-start(bf16[128,256]{1,0:T(8,128)(2,1)} %param.10) | copy-start | bytes 196612
  37.3 3.7 %copy-start.20 = (f32[256]{0:T(256)S(1)}, f32[256]{0:T(256)}, u32[]{:S(2)}) copy-start(f32[256]{0:T(256)} %param.15) | copy-start | bytes 3076
  37.3 1.9 %collective-permute-start.1 = (f32[32,128]{1,0:T(8,128)S(1)}, f32[32,128]{1,0:T(8,128)S(1)}, u32[]{:S(2)}, u32[]{:S(2)}) collective-permute-start(f32[32,128]{1,0:T(8,128)S(1)} %pad_maximum_fusion.5), channel_id=1, source_target_pairs={{0,4},{4,0},{8,12},{12,8},{16,20},{20,16},{24,28},{28,24},{32,36},... | collective-permute-start | bytes 49160 | tf_op jit(solution)/shard_map/ppermute | solution.py:114
  39.2 2.8 %copy-start.1 = (bf16[128,2048]{1,0:T(8,128)(2,1)S(1)}, bf16[128,2048]{1,0:T(8,128)(2,1)}, u32[]{:S(2)}) copy-start(bf16[128,2048]{1,0:T(8,128)(2,1)} %copy-done) | copy-start | bytes 1572868
  41.3 2.5 %copy-start.6 = (bf16[128,256]{1,0:T(8,128)(2,1)}, bf16[128,256]{1,0:T(8,128)(2,1)S(1)}, u32[]{:S(2)}) copy-start(bf16[128,256]{1,0:T(8,128)(2,1)S(1)} %get-tuple-element.38.refs_0_) | copy-start | bytes 196612
  41.4 2.5 %collective-permute-start.2 = (bf16[128,256]{1,0:T(8,128)(2,1)S(1)}, bf16[128,256]{1,0:T(8,128)(2,1)S(1)}, u32[]{:S(2)}, u32[]{:S(2)}) collective-permute-start(bf16[128,256]{1,0:T(8,128)(2,1)S(1)} %get-tuple-element.38.refs_0_), channel_id=1, source_target_pairs={{0,4},{4,0},{8,12},{12,8},{16,20},{20,16},{24,28},{28,24},{32,36},... | collective-permute-start | bytes 196616 | tf_op jit(solution)/shard_map/ppermute | solution.py:114
  43.8 0.7 copy-start.16
  43.8 0.7 copy-start.18
  43.8 0.8 copy-start.17
  48.5 6.7 %copy-start.7 = (bf16[128,256]{1,0:T(8,128)(2,1)S(1)}, bf16[128,256]{1,0:T(8,128)(2,1)}, u32[]{:S(2)}) copy-start(bf16[128,256]{1,0:T(8,128)(2,1)} %copy-done.6) | copy-start | bytes 196612
  48.5 26.2 %collective-permute-start.15 = (bf16[8,256,128]{2,1,0:T(8,128)(2,1)}, bf16[8,256,128]{2,1,0:T(8,128)(2,1)S(1)}, u32[]{:S(2)}, u32[]{:S(2)}) collective-permute-start(bf16[8,256,128]{2,1,0:T(8,128)(2,1)} %get-tuple-element.35), channel_id=1, source_target_pairs={{0,64},{4,68},{8,72},{12,76},{16,80},{20,84},{24,88},{28,92},{32,9... | collective-permute-start | bytes 1572872 | tf_op jit(solution)/shard_map/ppermute | solution.py:121
  48.5 28.3 %collective-permute-start.16 = (bf16[8,256,128]{2,1,0:T(8,128)(2,1)}, bf16[8,256,128]{2,1,0:T(8,128)(2,1)S(1)}, u32[]{:S(2)}, u32[]{:S(2)}) collective-permute-start(bf16[8,256,128]{2,1,0:T(8,128)(2,1)} %get-tuple-element.36), channel_id=1, source_target_pairs={{0,128},{4,132},{8,136},{12,140},{16,144},{20,148},{24,152},{28,15... | collective-permute-start | bytes 1572872 | tf_op jit(solution)/shard_map/ppermute | solution.py:121
  50.8 26.9 %collective-permute-start.17 = (bf16[8,256,128]{2,1,0:T(8,128)(2,1)}, bf16[8,256,128]{2,1,0:T(8,128)(2,1)}, u32[]{:S(2)}, u32[]{:S(2)}) collective-permute-start(bf16[8,256,128]{2,1,0:T(8,128)(2,1)} %get-tuple-element.37), channel_id=1, source_target_pairs={{0,192},{4,196},{8,200},{12,204},{16,208},{20,212},{24,216},{28,22... | collective-permute-start | bytes 1572872 | tf_op jit(solution)/shard_map/ppermute | solution.py:121
  54.4 3.4 %collective-permute-start.13 = (f32[49,256]{1,0:T(8,128)S(1)}, f32[49,256]{1,0:T(8,128)S(1)}, u32[]{:S(2)}, u32[]{:S(2)}) collective-permute-start(f32[49,256]{1,0:T(8,128)S(1)} %pad_maximum_fusion), channel_id=1, source_target_pairs={{0,4},{4,0},{8,12},{12,8},{16,20},{20,16},{24,28},{28,24},{32,36},... | collective-permute-start | bytes 150536 | tf_op jit(solution)/shard_map/ppermute | solution.py:114
  57.5 33.0 %collective-permute-start.10 = (bf16[128,2048]{1,0:T(8,128)(2,1)}, bf16[128,2048]{1,0:T(8,128)(2,1)}, u32[]{:S(2)}, u32[]{:S(2)}) collective-permute-start(bf16[128,2048]{1,0:T(8,128)(2,1)} %convolution_convert_fusion.2), channel_id=1, source_target_pairs={{0,1},{1,2},{2,3},{3,0},{4,5},{5,6},{6,7},{7,4},{8,9},{9,10},{10,1... | collective-permute-start | bytes 1572872 | tf_op jit(solution)/shard_map/ppermute | solution.py:117
  58.7 23.4 %all-to-all-start.1 = ((bf16[32,49,128]{2,1,0:T(8,128)(2,1)}), bf16[32,49,128]{2,1,0:T(8,128)(2,1)S(1)}, u32[]{:S(2)}, u32[]{:S(2)}) async-start(bf16[32,49,128]{2,1,0:T(8,128)(2,1)} %broadcast_in_dim.29), calls=%async_computation.1 | async-start | bytes 917504 | tf_op jit(solution)/shard_map/all_to_all | solution.py:126
  69.1 8.6 %copy-start.13 = (bf16[8,256,128]{2,1,0:T(8,128)(2,1)S(1)}, bf16[8,256,128]{2,1,0:T(8,128)(2,1)}, u32[]{:S(2)}) copy-start(bf16[8,256,128]{2,1,0:T(8,128)(2,1)} %get-tuple-element.34) | copy-start | bytes 1572868
  71.5 19.0 %collective-permute-start.11 = (bf16[128,2048]{1,0:T(8,128)(2,1)}, bf16[128,2048]{1,0:T(8,128)(2,1)}, u32[]{:S(2)}, u32[]{:S(2)}) collective-permute-start(bf16[128,2048]{1,0:T(8,128)(2,1)} %convolution_convert_fusion.1), channel_id=1, source_target_pairs={{0,2},{1,3},{2,0},{3,1},{4,6},{5,7},{6,4},{7,5},{8,10},{9,11},{10,... | collective-permute-start | bytes 1572872 | tf_op jit(solution)/shard_map/ppermute | solution.py:117
  74.7 22.9 %collective-permute-start.12 = (bf16[128,2048]{1,0:T(8,128)(2,1)}, bf16[128,2048]{1,0:T(8,128)(2,1)}, u32[]{:S(2)}, u32[]{:S(2)}) collective-permute-start(bf16[128,2048]{1,0:T(8,128)(2,1)} %convolution_convert_fusion), channel_id=1, source_target_pairs={{0,3},{1,0},{2,1},{3,2},{4,7},{5,4},{6,5},{7,6},{8,11},{9,8},{10,9... | collective-permute-start | bytes 1572872 | tf_op jit(solution)/shard_map/ppermute | solution.py:117
  82.1 25.2 %all-to-all-start.2 = ((bf16[8,256,128]{2,1,0:T(8,128)(2,1)}), bf16[8,256,128]{2,1,0:T(8,128)(2,1)S(1)}, u32[]{:S(2)}, u32[]{:S(2)}) async-start(bf16[8,256,128]{2,1,0:T(8,128)(2,1)} %add_convert_fusion), calls=%async_computation.2 | async-start | bytes 1048576 | tf_op jit(solution)/shard_map/all_to_all | solution.py:274
  89.5 11.0 %collective-permute-start.14 = (f32[49,128]{1,0:T(8,128)S(1)}, f32[49,128]{1,0:T(8,128)S(1)}, u32[]{:S(2)}, u32[]{:S(2)}) collective-permute-start(f32[49,128]{1,0:T(8,128)S(1)} %pad_maximum_fusion.2), channel_id=1, source_target_pairs={{0,4},{4,0},{8,12},{12,8},{16,20},{20,16},{24,28},{28,24},{32,36},... | collective-permute-start | bytes 75272 | tf_op jit(solution)/shard_map/ppermute | solution.py:114

commit v2 on v1

--- a/solution.py
+++ b/solution.py
@@ -41,23 +41,6 @@
 
 def in_vmem(count):
     return [pl.BlockSpec(memory_space=pltpu.VMEM)] * count
-
-
-def given_half(turns, rows, width):
-    count = rows.shape[1] // (2 * width)
-
-    def kernel(turns_ref, rows_ref, out_ref):
-        other = 1 - turns_ref[0]
-        for i in range(count):
-            at = pl.multiple_of((2 * i + other) * width, width)
-            out_ref[:, i * width : (i + 1) * width] = rows_ref[:, pl.ds(at, width)]
-
-    return pl.pallas_call(
-        kernel,
-        out_shape=jax.ShapeDtypeStruct((rows.shape[0], count * width), rows.dtype),
-        in_specs=[pl.BlockSpec(memory_space=pltpu.SMEM)] + in_vmem(1),
-        out_specs=in_vmem(1)[0],
-    )(turns, rows)
 
 
 def weight_parts(turns, result, result_other, blocks, taken, width):
@@ -75,7 +58,7 @@
                 at = pl.multiple_of((2 * i + core) * width, width)
                 lanes = slice(i * width, (i + 1) * width)
                 all_ref[k, :tokens, lanes] = block_refs[k][:, pl.ds(at, width)]
-            all_ref[k, tokens:, :] = taken_refs[k][...]
+                all_ref[k, tokens:, lanes] = taken_refs[k][:, pl.ds(at, width)]
         left = jnp.concatenate([mine_ref[...], other_ref[...]], 0).T
         for s in range(count):
             part = jnp.dot(
@@ -99,14 +82,12 @@
     dev = lax.axis_index("ctx")
     tp = lax.axis_index("tp")
     block, chans = outer_gate.shape
-    first_weight = row_major(out_weight)
     modes = residues.shape[0]
     feats = out_grad.shape[1]
     ny = tps
     nz = ctx // (2 * ny)
-    pairs = ctx // 2
     core = dev % 2
-    pair = dev // 2
+    zz = dev // 2 % nz
     yy = dev // (2 * nz)
     width = feats // (2 * nz)
 
@@ -120,10 +101,11 @@
         per = 2 * nz
         return lax.ppermute(a, "ctx", [(i, (i // per + k) % ny * per + i % per) for i in range(ctx)])
 
-    def of_pairs(a):
-        copies = jnp.broadcast_to(a[None], (pairs, *a.shape))
-        groups = [[2 * i + j for i in range(pairs)] for j in range(2)]
-        return lax.all_to_all(copies, "ctx", 0, 0, tiled=True, axis_index_groups=groups)
+    z_groups = [[i * 2 * nz + j * 2 + k for j in range(nz)] for i in range(ny) for k in range(2)]
+
+    def of_plane(a):
+        copies = jnp.broadcast_to(a[None], (nz, *a.shape))
+        return lax.all_to_all(copies, "ctx", 0, 0, tiled=True, axis_index_groups=z_groups)
 
     og = [out_grad] + [row_major(shift_tp(out_grad, k)) for k in range(1, tps)]
 
@@ -158,14 +140,36 @@
     total = decay_h * f_h[:modes] + s_h[:modes]
     total_lag = decay_h * (block * f_h[:modes] + f_h[modes:]) + s_h[modes:]
     to_send = jnp.concatenate([total, total_lag], 0).astype(BF16)
-    gathered = of_pairs(to_send).astype(F32)
-    place = jnp.arange(pairs, dtype=jnp.int32)
-    gap = (2 * block) * jnp.maximum(pair - 1 - place, 0).astype(F32)[:, None, None]
-    weight = jnp.where(
-        (place < pair)[:, None, None], jnp.exp(-rate_h[None] * gap), 0.0
-    )
-    in_h = jnp.sum(weight * gathered[:, :modes], 0)
-    in_lag_h = jnp.sum(weight * (gap * gathered[:, :modes] + gathered[:, modes:]), 0)
+    gathered = of_plane(to_send).astype(F32)
+    place = jnp.arange(nz, dtype=jnp.int32)
+    per_pair = 2 * block
+    per_plane = per_pair * nz
+
+    def weights(which, gap):
+        gap = jnp.where(which, gap, 0).astype(F32)[:, None, None] * per_pair
+        return jnp.where(which[:, None, None], jnp.exp(-rate_h[None] * gap), 0.0), gap
+
+    def carried(w, gap):
+        base = gathered[:, :modes]
+        return jnp.sum(w * base, 0), jnp.sum(w * (gap * base + gathered[:, modes:]), 0)
+
+    plane, plane_lag = carried(*weights(place >= 0, nz - 1 - place))
+    plane_all = jnp.concatenate([plane, plane_lag], 0)
+    in_h, in_lag_h = carried(*weights(place < zz, zz - 1 - place))
+    y_in, y_in_lag = 0.0, 0.0
+    for k in range(1, ny):
+        per = 2 * nz
+        came = lax.ppermute(
+            plane_all, "ctx", [(i, i + k * per) for i in range(ctx) if i + k * per < ctx]
+        )
+        gap = float(per_plane * (k - 1))
+        w = jnp.exp(-rate_h * gap)
+        y_in = y_in + w * came[:modes]
+        y_in_lag = y_in_lag + w * (gap * came[:modes] + came[modes:])
+    gap = (per_pair * zz).astype(F32)
+    w = jnp.exp(-rate_h * gap)
+    in_h = in_h + w * y_in
+    in_lag_h = in_lag_h + w * (gap * y_in + y_in_lag)
     incoming = both_halves(jnp.concatenate([in_h, in_lag_h], 0))
     in_pair, in_pair_lag = incoming[:modes], incoming[modes:]
     x_in = jnp.where(core == 0, in_pair, fall_block * in_pair + first[:modes])
@@ -192,8 +196,7 @@
     result = row_major((outer_f * gated).astype(BF16))
 
     turns = jnp.stack([core, (tp - yy) % tps]).astype(jnp.int32)
-    given = [given_half(turns, a, width) for a in og]
-    taken = [swap_core(a) for a in given]
+    taken = [row_major(swap_core(a)) for a in og]
     result_other = swap_core(result)
     y_parts = weight_parts(turns, result, result_other, og, taken, width)
     over_y = [y_parts[0]] + [shift_y(y_parts[s], s) for s in range(1, ny)]
@@ -215,7 +218,7 @@
 
     grad_gated = 0.0
     for k in range(tps):
-        w_block = lax.dynamic_slice_in_dim(first_weight, (tp - k) % tps * feats, feats, 1)
+        w_block = lax.dynamic_slice_in_dim(out_weight, (tp - k) % tps * feats, feats, 1)
         grad_gated = grad_gated + lax.dot_general(
             og[k], w_block, (((1,), (1,)), ((), ())), preferred_element_type=F32
         )
@@ -253,11 +256,18 @@
     early_h = jnp.where(core == 0, mine_h[:modes], theirs_h[:modes])
     total_g = early_h + decay_h * my_half(later)
     sent = jnp.concatenate([total_g, mine_h[modes:] + theirs_h[modes:]], 0).astype(BF16)
-    got = of_pairs(sent).astype(F32)
-    gap_g = (2 * block) * jnp.maximum(place - pair - 1, 0).astype(F32)[:, None, None]
-    weight_g = jnp.where((place > pair)[:, None, None], jnp.exp(-rate_h[None] * gap_g), 0.0)
-    h_half = jnp.sum(weight_g * got[:, :modes], 0)
-    sums_half = jnp.sum(got[:, modes:], 0)
+    got = of_plane(sent).astype(F32)
+    plane_h = jnp.sum(weights(place >= 0, place)[0] * got[:, :modes], 0)
+    plane_sums = jnp.sum(got[:, modes:], 0)
+    plane_g = jnp.concatenate([plane_h, plane_sums], 0)
+    h_half = jnp.sum(weights(place > zz, place - zz - 1)[0] * got[:, :modes], 0)
+    y_h, sums_half = 0.0, plane_sums
+    for k in range(1, ny):
+        came = shift_y(plane_g, -k)
+        w = jnp.exp(-rate_h * float(per_plane * (k - 1)))
+        y_h = y_h + jnp.where(yy + k < ny, w * came[:modes], 0.0)
+        sums_half = sums_half + came[modes:]
+    h_half = h_half + jnp.exp(-rate_h * (per_pair * (nz - 1 - zz)).astype(F32)) * y_h
     final = both_halves(jnp.concatenate([h_half, sums_half], 0))
     h_pair = final[:modes]
     h_in = jnp.where(core == 0, later + fall_block * h_pair, h_pair)
@@ -270,7 +280,6 @@
     grad_inner = (grad_mixed * value_f).astype(BF16)
     grad_values = (grad_mixed * inner_f).astype(BF16)
 
-    z_groups = [[i * 2 * nz + j * 2 + k for j in range(nz)] for i in range(ny) for k in range(2)]
     over_z = lax.all_to_all(summed_y, "ctx", 0, 0, tiled=True, axis_index_groups=z_groups)
     grad_weight = jnp.sum(over_z.astype(F32), 0)
     return (

time: 109 us -> 130 us (1.19)
  the two profiles are of different devices: /device:TPU:25 before, /device:TPU:1 now
where the time goes in v2:
time: 130 us
  starting transfers between devices  49.6 us (38%)
  waiting for transfers between devices  38.8 us (30%)
  matrix products  21.4 us (16%)
  other arithmetic  10.9 us (8%)
  Pallas kernels  4.42 us (3%)
  local copies, waits for them, and re-layouts  3.12 us (2%)
  between operations  1.34 us (1%)
    ppermute x6, waiting for transfers between devices, shift_tp(): return lax.ppermute(a, 'tp', [(i, (i + k) % tps) for i in range(tps)])  18 us
    all_to_all x2, waiting for transfers between devices, of_plane(): lax.all_to_all(copies, 'ctx', 0, 0, tiled=True, axis_index_groups=z_groups)  15.4 us
    ppermute x9, starting transfers between devices, swap_core(): return lax.ppermute(a, 'ctx', [(i, i ^ 1) for i in range(ctx)])  13.8 us
    all_to_all x2, starting transfers between devices, of_plane(): lax.all_to_all(copies, 'ctx', 0, 0, tiled=True, axis_index_groups=z_groups)  11.6 us
    dot_general x4, matrix products, projected(): return jnp.dot(result, w_block, preferred_element_type=F32)  9.89 us
    ppermute x3, starting transfers between devices, body(): lax.ppermute(plane_all, 'ctx', [(i, i + k * per) for i in range(ctx) if i...  8.41 us
    dot_general x4, matrix products, body(): lax.dot_general(og[k], w_block, (((1,), (1,)), ((), ())), preferred_eleme...  7.2 us
    ppermute x6, starting transfers between devices, shift_y(): lax.ppermute(a, 'ctx', [(i, (i // per + k) % ny * per + i % per) for i in...  6.56 us
  transfers between devices with their start and end apart: 27, of which 8 were waited for; matrix products, arithmetic and copies ran while one was open for 24% of the time, Pallas kernels for 0%

profile of v2, /device:TPU:1, one launch (start us, length us, event | category | flops | bytes accessed | tf_op | source)
XLA Modules:
  0.0 129.7 jit_solution(8989672046682757893)
XLA Ops:
  0.7 0.8 fusion.119
  1.4 0.9 convert_multiply_fusion.5
  2.4 0.7 fusion.4
  3.1 3.3 %collective-permute-start = (f32[32,256]{1,0:T(8,128)S(1)}, f32[32,256]{1,0:T(8,128)S(1)}, u32[]{:S(2)}, u32[]{:S(2)}) collective-permute-start(f32[32,256]{1,0:T(8,128)S(1)} %pad_maximum_fusion.1), channel_id=1, source_target_pairs={{0,4},{4,0},{8,12},{12,8},{16,20},{20,16},{24,28},{28,24},{32,36},... | collective-permute-start | bytes 98312 | tf_op jit(solution)/shard_map/ppermute | solution.py:95
  6.4 2.0 %collective-permute-start.7 = (bf16[128,2048]{1,0:T(8,128)(2,1)}, bf16[128,2048]{1,0:T(8,128)(2,1)S(1)}, u32[]{:S(2)}, u32[]{:S(2)}) collective-permute-start(bf16[128,2048]{1,0:T(8,128)(2,1)} %refs_2_.1), channel_id=1, source_target_pairs={{0,2},{1,3},{2,0},{3,1},{4,6},{5,7},{6,4},{7,5},{8,10},{9,11},{10,... | collective-permute-start | bytes 1572872 | tf_op jit(solution)/shard_map/ppermute | solution.py:98
  8.4 0.6 broadcast_in_dim.80
  9.1 8.2 %all-to-all-start = ((bf16[8,32,128]{2,1,0:T(8,128)(2,1)}), bf16[8,32,128]{2,1,0:T(8,128)(2,1)S(1)}, u32[]{:S(2)}, u32[]{:S(2)}) async-start(bf16[8,32,128]{2,1,0:T(8,128)(2,1)} %broadcast_in_dim.80), calls=%async_computation | async-start | bytes 131072 | tf_op jit(solution)/shard_map/all_to_all | solution.py:108
  17.3 7.3 %all-to-all-done = bf16[8,32,128]{2,1,0:T(8,128)(2,1)S(1)} async-done(((bf16[8,32,128]{2,1,0:T(8,128)(2,1)}), bf16[8,32,128]{2,1,0:T(8,128)(2,1)S(1)}, u32[]{:S(2)}, u32[]{:S(2)}) %all-to-all-start) | async-done | bytes 65568 | tf_op jit(solution)/shard_map/all_to_all | solution.py:108
  24.7 4.6 %collective-permute-start.3 = (f32[32,128]{1,0:T(8,128)S(1)}, f32[32,128]{1,0:T(8,128)S(1)}, u32[]{:S(2)}, u32[]{:S(2)}) collective-permute-start(f32[32,128]{1,0:T(8,128)S(1)} %pad_maximum_fusion.6), channel_id=1, source_target_pairs={{0,192},{4,196},{8,200},{12,204},{16,208},{20,212},{24,216},{28,22... | collective-permute-start | bytes 49160 | tf_op jit(solution)/shard_map/ppermute | solution.py:162
  29.4 1.3 collective-permute-start.2
  30.7 2.5 %collective-permute-start.1 = (f32[32,128]{1,0:T(8,128)S(1)}, f32[32,128]{1,0:T(8,128)S(1)}, u32[]{:S(2)}, u32[]{:S(2)}) collective-permute-start(f32[32,128]{1,0:T(8,128)S(1)} %pad_maximum_fusion.6), channel_id=1, source_target_pairs={{0,64},{4,68},{8,72},{12,76},{16,80},{20,84},{24,88},{28,92},{32,9... | collective-permute-start | bytes 49160 | tf_op jit(solution)/shard_map/ppermute | solution.py:162
  33.7 1.2 collective-permute-start.8
  34.8 2.8 %collective-permute-start.9 = (bf16[128,2048]{1,0:T(8,128)(2,1)}, bf16[128,2048]{1,0:T(8,128)(2,1)S(1)}, u32[]{:S(2)}, u32[]{:S(2)}) collective-permute-start(bf16[128,2048]{1,0:T(8,128)(2,1)} %refs_2_.1), channel_id=1, source_target_pairs={{0,4},{4,0},{8,12},{12,8},{16,20},{20,16},{24,28},{28,24},{32,36},... | collective-permute-start | bytes 1572872 | tf_op jit(solution)/shard_map/ppermute | solution.py:95
  38.4 1.0 collective-permute-done.4
  42.1 2.8 %collective-permute-done.8.refs_5_ = bf16[128,2048]{1,0:T(8,128)(2,1)S(1)} collective-permute-done((bf16[128,2048]{1,0:T(8,128)(2,1)}, bf16[128,2048]{1,0:T(8,128)(2,1)S(1)}, u32[]{:S(2)}, u32[]{:S(2)}) %collective-permute-start.8) | collective-permute-done | bytes 524320 | tf_op jit(solution)/shard_map/ppermute | solution.py:98
  44.8 3.4 %collective-permute-start.12 = (bf16[128,2048]{1,0:T(8,128)(2,1)S(1)}, bf16[128,2048]{1,0:T(8,128)(2,1)}, u32[]{:S(2)}, u32[]{:S(2)}) collective-permute-start(bf16[128,2048]{1,0:T(8,128)(2,1)S(1)} %collective-permute-done.8.refs_5_), channel_id=1, source_target_pairs={{0,4},{4,0},{8,12},{12,8},{16,20},{20,16},{24,28},{28,24},{32,36},... | collective-permute-start | bytes 1572872 | tf_op jit(solution)/shard_map/ppermute | solution.py:95
  49.6 0.7 collective-permute-done.5.refs_1_
  50.3 0.8 copy-done.14
  51.1 0.8 copy-done.15
  52.0 4.4 %shard_map.161 = (bf16[8,256,128]{2,1,0:T(8,128)(2,1)}, bf16[8,256,128]{2,1,0:T(8,128)(2,1)}, bf16[8,256,128]{2,1,0:T(8,128)(2,1)}, bf16[8,256,128]{2,1,0:T(8,128)(2,1)}) custom-call(s32[2]{0:T(128)} %pad_add_fusion.turns_ref, bf16[128,256]{1,0:T(8,128)(2,1)} %copy-done, bf16[128,256]{1,0:T(8,128)(2,1)} %copy-done.18, bf16[128,2048]{1,0:T(8,128)(2,1)} %refs_2_.1, ...), custom_call_target="tpu_custom_call" | custom-call | tf_op jit(solution)/shard_map/pallas_call | solution.py:70
  56.4 1.8 %collective-permute-start.22 = (bf16[8,256,128]{2,1,0:T(8,128)(2,1)}, bf16[8,256,128]{2,1,0:T(8,128)(2,1)S(1)}, u32[]{:S(2)}, u32[]{:S(2)}) collective-permute-start(bf16[8,256,128]{2,1,0:T(8,128)(2,1)} %get-tuple-element.36), channel_id=1, source_target_pairs={{0,128},{4,132},{8,136},{12,140},{16,144},{20,148},{24,152},{28,15... | collective-permute-start | bytes 1572872 | tf_op jit(solution)/shard_map/ppermute | solution.py:102
  58.2 1.8 %fusion.21 = f32[256,128]{0,1:T(8,128)S(1)} fusion(bf16[128,2048]{1,0:T(8,128)(2,1)} %refs_2_.1, bf16[256,8192]{1,0:T(8,128)(2,1)} %param.16, s32[]{:T(128)S(6)} %select_n.210), kind=kOutput, calls=%fused_computation.41 | convolution fusion | flops 134217728 | bytes 1703940 | tf_op jit(solution)/shard_map/dot_general | solution.py:222
  60.1 1.9 %fusion.14 = f32[256,128]{0,1:T(8,128)S(1)} fusion(bf16[128,2048]{1,0:T(8,128)(2,1)} %copy-done.4, bf16[256,8192]{1,0:T(8,128)(2,1)} %param.16, s32[]{:T(128)S(6)} %select_n.222), kind=kOutput, calls=%fused_computation.33 | convolution fusion | flops 134217728 | bytes 1703940 | tf_op jit(solution)/shard_map/dot_general | solution.py:222
  62.0 1.7 %convolution_add_fusion.3 = f32[256,128]{0,1:T(8,128)S(1)} fusion(f32[256,128]{0,1:T(8,128)S(1)} %fusion.21, bf16[128,2048]{1,0:T(8,128)(2,1)S(1)} %copy-done.6, bf16[256,8192]{1,0:T(8,128)(2,1)} %param.16, s32[]{:T(128)S(6)} %select_n.218), kind=kOutput, calls=%fused_computation.26 | convolution fusion | flops 134250496 | bytes 1835012 | tf_op jit(solution)/shard_map/dot_general | solution.py:222
  63.7 1.7 %fusion.10 = f32[128,256]{1,0:T(8,128)S(1)} fusion(f32[256,128]{0,1:T(8,128)S(1)} %fusion.14, f32[256,128]{0,1:T(8,128)S(1)} %convolution_add_fusion.3, bf16[128,2048]{1,0:T(8,128)(2,1)S(1)} %copy-done.3, bf16[256,8192]{1,0:T(8,128)(2,1)} %param.16, s32[]{:T(128)S(6)} %select_n.220), kind=kOutput, calls=%fused_computation.25 | convolution fusion | flops 134283264 | bytes 1966084 | tf_op jit(solution)/shard_map/dot_general | solution.py:222
  65.5 0.7 fusion.50
  66.5 0.6 fusion.30
  68.0 1.2 fusion.3
  69.1 0.8 collective-permute-start.16
  70.0 2.3 %convolution_convert_fusion = bf16[128,2048]{1,0:T(8,128)(2,1)} fusion(bf16[128,256]{1,0:T(8,128)(2,1)S(1)} %copy-done.1, bf16[256,8192]{1,0:T(8,128)(2,1)} %param.16, s32[]{:T(128)S(6)} %select_n.216), kind=kOutput, calls=%fused_computation | convolution fusion | flops 134479872 | bytes 1638404 | tf_op jit(solution)/shard_map/dot_general | solution.py:210
  72.3 0.7 broadcast_in_dim.83
  73.0 3.4 %all-to-all-start.1 = ((bf16[8,49,128]{2,1,0:T(8,128)(2,1)}), bf16[8,49,128]{2,1,0:T(8,128)(2,1)S(1)}, u32[]{:S(2)}, u32[]{:S(2)}) async-start(bf16[8,49,128]{2,1,0:T(8,128)(2,1)} %broadcast_in_dim.83), calls=%async_computation.1 | async-start | bytes 229376 | tf_op jit(solution)/shard_map/all_to_all | solution.py:108
  76.7 8.1 %all-to-all-done.1 = bf16[8,49,128]{2,1,0:T(8,128)(2,1)S(1)} async-done(((bf16[8,49,128]{2,1,0:T(8,128)(2,1)}), bf16[8,49,128]{2,1,0:T(8,128)(2,1)S(1)}, u32[]{:S(2)}, u32[]{:S(2)}) %all-to-all-start.1) | async-done | bytes 100384 | tf_op jit(solution)/shard_map/all_to_all | solution.py:108
  85.1 3.2 %collective-permute-start.18 = (f32[49,128]{1,0:T(8,128)S(1)}, f32[49,128]{1,0:T(8,128)S(1)}, u32[]{:S(2)}, u32[]{:S(2)}) collective-permute-start(f32[49,128]{1,0:T(8,128)S(1)} %pad_maximum_fusion.2), channel_id=1, source_target_pairs={{0,128},{4,132},{8,136},{12,140},{16,144},{20,148},{24,152},{28,15... | collective-permute-start | bytes 75272 | tf_op jit(solution)/shard_map/ppermute | solution.py:102
  88.3 2.3 %convolution_convert_fusion.1 = bf16[128,2048]{1,0:T(8,128)(2,1)} fusion(bf16[128,256]{1,0:T(8,128)(2,1)S(1)} %copy-done.1, bf16[256,8192]{1,0:T(8,128)(2,1)} %param.16, s32[]{:T(128)S(6)} %select_n.214), kind=kOutput, calls=%fused_computation.1 | convolution fusion | flops 134479872 | bytes 1638404 | tf_op jit(solution)/shard_map/dot_general | solution.py:210
  90.6 1.5 %collective-permute-start.21 = (bf16[8,256,128]{2,1,0:T(8,128)(2,1)}, bf16[8,256,128]{2,1,0:T(8,128)(2,1)S(1)}, u32[]{:S(2)}, u32[]{:S(2)}) collective-permute-start(bf16[8,256,128]{2,1,0:T(8,128)(2,1)} %get-tuple-element.35), channel_id=1, source_target_pairs={{0,64},{4,68},{8,72},{12,76},{16,80},{20,84},{24,88},{28,92},{32,9... | collective-permute-start | bytes 1572872 | tf_op jit(solution)/shard_map/ppermute | solution.py:102
  92.1 2.4 %collective-permute-start.15 = (bf16[128,2048]{1,0:T(8,128)(2,1)}, bf16[128,2048]{1,0:T(8,128)(2,1)}, u32[]{:S(2)}, u32[]{:S(2)}) collective-permute-start(bf16[128,2048]{1,0:T(8,128)(2,1)} %convolution_convert_fusion), channel_id=1, source_target_pairs={{0,3},{1,0},{2,1},{3,2},{4,7},{5,4},{6,5},{7,6},{8,11},{9,8},{10,9... | collective-permute-start | bytes 1572872 | tf_op jit(solution)/shard_map/ppermute | solution.py:98
  94.5 2.6 %collective-permute-start.20 = (f32[49,128]{1,0:T(8,128)S(1)}, f32[49,128]{1,0:T(8,128)S(1)}, u32[]{:S(2)}, u32[]{:S(2)}) collective-permute-start(f32[49,128]{1,0:T(8,128)S(1)} %pad_maximum_fusion.3), channel_id=1, source_target_pairs={{0,4},{4,0},{8,12},{12,8},{16,20},{20,16},{24,28},{28,24},{32,36},... | collective-permute-start | bytes 75272 | tf_op jit(solution)/shard_map/ppermute | solution.py:95
  97.2 2.3 %convolution_convert_fusion.2 = bf16[128,2048]{1,0:T(8,128)(2,1)} fusion(bf16[128,256]{1,0:T(8,128)(2,1)S(1)} %copy-done.1, bf16[256,8192]{1,0:T(8,128)(2,1)} %param.16, s32[]{:T(128)S(6)} %select_n.212), kind=kOutput, calls=%fused_computation.2 | convolution fusion | flops 134479872 | bytes 1638404 | tf_op jit(solution)/shard_map/dot_general | solution.py:210
  99.9 3.7 %collective-permute-done.21 = bf16[8,256,128]{2,1,0:T(8,128)(2,1)S(1)} collective-permute-done((bf16[8,256,128]{2,1,0:T(8,128)(2,1)}, bf16[8,256,128]{2,1,0:T(8,128)(2,1)S(1)}, u32[]{:S(2)}, u32[]{:S(2)}) %collective-permute-start.21) | collective-permute-done | bytes 524320 | tf_op jit(solution)/shard_map/ppermute | solution.py:102
  103.6 1.1 add_convert_fusion
  104.6 3.5 %all-to-all-start.2 = ((bf16[8,256,128]{2,1,0:T(8,128)(2,1)}), bf16[8,256,128]{2,1,0:T(8,128)(2,1)S(1)}, u32[]{:S(2)}, u32[]{:S(2)}) async-start(bf16[8,256,128]{2,1,0:T(8,128)(2,1)} %add_convert_fusion), calls=%async_computation.2 | async-start | bytes 1048576 | tf_op jit(solution)/shard_map/all_to_all | solution.py:283
  108.1 0.7 fusion.85
  109.8 1.0 fusion.48
  110.8 4.1 %collective-permute-done.14 = bf16[128,2048]{1,0:T(8,128)(2,1)} collective-permute-done((bf16[128,2048]{1,0:T(8,128)(2,1)}, bf16[128,2048]{1,0:T(8,128)(2,1)}, u32[]{:S(2)}, u32[]{:S(2)}) %collective-permute-start.14) | collective-permute-done | bytes 524320 | tf_op jit(solution)/shard_map/ppermute | solution.py:98
  114.8 11.2 %collective-permute-done.13 = bf16[128,2048]{1,0:T(8,128)(2,1)} collective-permute-done((bf16[128,2048]{1,0:T(8,128)(2,1)}, bf16[128,2048]{1,0:T(8,128)(2,1)}, u32[]{:S(2)}, u32[]{:S(2)}) %collective-permute-start.13) | collective-permute-done | bytes 524320 | tf_op jit(solution)/shard_map/ppermute | solution.py:98
  126.0 2.9 %add_convert_fusion.1 = bf16[128,2048]{1,0:T(8,128)(2,1)} fusion(bf16[128,2048]{1,0:T(8,128)(2,1)} %collective-permute-done.15, bf16[128,2048]{1,0:T(8,128)(2,1)} %collective-permute-done.14, bf16[128,2048]{1,0:T(8,128)(2,1)} %collective-permute-done.13, bf16[128,256]{1,0:T(8,128)(2,1)S(1)} %copy-done.1, bf16[256,8192]{1,0:T(8,128)(2,1)} %param.16, ...), kind=kOutput, calls=%fused_computation.37 | convolution fusion | flops 136052736 | bytes 3211268 | tf_op jit(solution)/shard_map/dot_general | solution.py:210
  129.0 0.7 convert_reduce_fusion
  (127 shorter events, 8.5 us)
Async XLA Ops:
  0.6 40.0 %copy-start.9 = (f32[258,128]{1,0:T(8,128)S(1)}, f32[258,128]{1,0:T(8,128)}, u32[]{:S(2)}) copy-start(f32[258,128]{1,0:T(8,128)} %constant.135.clone) | copy-start | bytes 396292
  0.6 38.8 %copy-start.16 = (f32[16,256]{1,0:T(8,128)S(1)}, f32[16,256]{1,0:T(8,128)}, u32[]{:S(2)}) copy-start(f32[16,256]{1,0:T(8,128)} %param.14) | copy-start | bytes 49156
  0.7 39.4 %copy-start.19 = (f32[16,256]{1,0:T(8,128)S(1)}, f32[16,256]{1,0:T(8,128)}, u32[]{:S(2)}) copy-start(f32[16,256]{1,0:T(8,128)} %param.13) | copy-start | bytes 49156
  2.3 38.7 %copy-start.7 = (bf16[128,256]{1,0:T(8,128)(2,1)S(1)}, bf16[128,256]{1,0:T(8,128)(2,1)}, u32[]{:S(2)}) copy-start(bf16[128,256]{1,0:T(8,128)(2,1)} %param.12) | copy-start | bytes 196612
  2.4 38.7 %copy-start.8 = (bf16[128,256]{1,0:T(8,128)(2,1)S(1)}, bf16[128,256]{1,0:T(8,128)(2,1)}, u32[]{:S(2)}) copy-start(bf16[128,256]{1,0:T(8,128)(2,1)} %param.11) | copy-start | bytes 196612
  3.1 45.2 %copy-start.11 = (f32[128,129]{1,0:T(8,128)S(1)}, f32[128,129]{1,0:T(8,128)}, u32[]{:S(2)}) copy-start(f32[128,129]{1,0:T(8,128)} %constant.137) | copy-start | bytes 198148
  3.1 5.3 %collective-permute-start = (f32[32,256]{1,0:T(8,128)S(1)}, f32[32,256]{1,0:T(8,128)S(1)}, u32[]{:S(2)}, u32[]{:S(2)}) collective-permute-start(f32[32,256]{1,0:T(8,128)S(1)} %pad_maximum_fusion.1), channel_id=1, source_target_pairs={{0,4},{4,0},{8,12},{12,8},{16,20},{20,16},{24,28},{28,24},{32,36},... | collective-permute-start | bytes 98312 | tf_op jit(solution)/shard_map/ppermute | solution.py:95
  6.4 35.1 %collective-permute-start.6 = (bf16[128,2048]{1,0:T(8,128)(2,1)}, bf16[128,2048]{1,0:T(8,128)(2,1)S(1)}, u32[]{:S(2)}, u32[]{:S(2)}) collective-permute-start(bf16[128,2048]{1,0:T(8,128)(2,1)} %refs_2_.1), channel_id=1, source_target_pairs={{0,1},{1,2},{2,3},{3,0},{4,5},{5,6},{6,7},{7,4},{8,9},{9,10},{10,1... | collective-permute-start | bytes 1572872 | tf_op jit(solution)/shard_map/ppermute | solution.py:98
  6.4 35.5 %collective-permute-start.7 = (bf16[128,2048]{1,0:T(8,128)(2,1)}, bf16[128,2048]{1,0:T(8,128)(2,1)S(1)}, u32[]{:S(2)}, u32[]{:S(2)}) collective-permute-start(bf16[128,2048]{1,0:T(8,128)(2,1)} %refs_2_.1), channel_id=1, source_target_pairs={{0,2},{1,3},{2,0},{3,1},{4,6},{5,7},{6,4},{7,5},{8,10},{9,11},{10,... | collective-permute-start | bytes 1572872 | tf_op jit(solution)/shard_map/ppermute | solution.py:98
  8.3 40.2 %copy-start.10 = (f32[128,129]{1,0:T(8,128)S(1)}, f32[128,129]{1,0:T(8,128)}, u32[]{:S(2)}) copy-start(f32[128,129]{1,0:T(8,128)} %constant.138) | copy-start | bytes 198148
  8.3 40.2 %copy-start.17 = (bf16[128,256]{1,0:T(8,128)(2,1)S(1)}, bf16[128,256]{1,0:T(8,128)(2,1)}, u32[]{:S(2)}) copy-start(bf16[128,256]{1,0:T(8,128)(2,1)} %param.10) | copy-start | bytes 196612
  8.3 40.3 %copy-start.21 = (f32[256]{0:T(256)S(1)}, f32[256]{0:T(256)}, u32[]{:S(2)}) copy-start(f32[256]{0:T(256)} %param.15) | copy-start | bytes 3076
  9.1 15.5 %all-to-all-start = ((bf16[8,32,128]{2,1,0:T(8,128)(2,1)}), bf16[8,32,128]{2,1,0:T(8,128)(2,1)S(1)}, u32[]{:S(2)}, u32[]{:S(2)}) async-start(bf16[8,32,128]{2,1,0:T(8,128)(2,1)} %broadcast_in_dim.80), calls=%async_computation | async-start | bytes 131072 | tf_op jit(solution)/shard_map/all_to_all | solution.py:108
  24.7 9.0 %collective-permute-start.3 = (f32[32,128]{1,0:T(8,128)S(1)}, f32[32,128]{1,0:T(8,128)S(1)}, u32[]{:S(2)}, u32[]{:S(2)}) collective-permute-start(f32[32,128]{1,0:T(8,128)S(1)} %pad_maximum_fusion.6), channel_id=1, source_target_pairs={{0,192},{4,196},{8,200},{12,204},{16,208},{20,212},{24,216},{28,22... | collective-permute-start | bytes 49160 | tf_op jit(solution)/shard_map/ppermute | solution.py:162
  29.4 5.5 %collective-permute-start.2 = (f32[32,128]{1,0:T(8,128)S(1)}, f32[32,128]{1,0:T(8,128)S(1)}, u32[]{:S(2)}, u32[]{:S(2)}) collective-permute-start(f32[32,128]{1,0:T(8,128)S(1)} %pad_maximum_fusion.6), channel_id=1, source_target_pairs={{0,128},{4,132},{8,136},{12,140},{16,144},{20,148},{24,152},{28,15... | collective-permute-start | bytes 49160 | tf_op jit(solution)/shard_map/ppermute | solution.py:162
  30.7 7.0 %collective-permute-start.1 = (f32[32,128]{1,0:T(8,128)S(1)}, f32[32,128]{1,0:T(8,128)S(1)}, u32[]{:S(2)}, u32[]{:S(2)}) collective-permute-start(f32[32,128]{1,0:T(8,128)S(1)} %pad_maximum_fusion.6), channel_id=1, source_target_pairs={{0,64},{4,68},{8,72},{12,76},{16,80},{20,84},{24,88},{28,92},{32,9... | collective-permute-start | bytes 49160 | tf_op jit(solution)/shard_map/ppermute | solution.py:162
  33.7 11.1 %collective-permute-start.8 = (bf16[128,2048]{1,0:T(8,128)(2,1)}, bf16[128,2048]{1,0:T(8,128)(2,1)S(1)}, u32[]{:S(2)}, u32[]{:S(2)}) collective-permute-start(bf16[128,2048]{1,0:T(8,128)(2,1)} %refs_2_.1), channel_id=1, source_target_pairs={{0,3},{1,0},{2,1},{3,2},{4,7},{5,4},{6,5},{7,6},{8,11},{9,8},{10,9... | collective-permute-start | bytes 1572872 | tf_op jit(solution)/shard_map/ppermute | solution.py:98
  34.8 15.4 %collective-permute-start.9 = (bf16[128,2048]{1,0:T(8,128)(2,1)}, bf16[128,2048]{1,0:T(8,128)(2,1)S(1)}, u32[]{:S(2)}, u32[]{:S(2)}) collective-permute-start(bf16[128,2048]{1,0:T(8,128)(2,1)} %refs_2_.1), channel_id=1, source_target_pairs={{0,4},{4,0},{8,12},{12,8},{16,20},{20,16},{24,28},{28,24},{32,36},... | collective-permute-start | bytes 1572872 | tf_op jit(solution)/shard_map/ppermute | solution.py:95
  37.7 1.7 %collective-permute-start.4 = (f32[32,128]{1,0:T(8,128)S(1)}, f32[32,128]{1,0:T(8,128)S(1)}, u32[]{:S(2)}, u32[]{:S(2)}) collective-permute-start(f32[32,128]{1,0:T(8,128)S(1)} %pad_maximum_fusion.7), channel_id=1, source_target_pairs={{0,4},{4,0},{8,12},{12,8},{16,20},{20,16},{24,28},{28,24},{32,36},... | collective-permute-start | bytes 49160 | tf_op jit(solution)/shard_map/ppermute | solution.py:95
  41.4 10.5 %copy-start.5 = (bf16[128,2048]{1,0:T(8,128)(2,1)}, bf16[128,2048]{1,0:T(8,128)(2,1)S(1)}, u32[]{:S(2)}) copy-start(bf16[128,2048]{1,0:T(8,128)(2,1)S(1)} %collective-permute-done.6.refs_3_) | copy-start | bytes 1572868
  41.5 8.8 %collective-permute-start.10 = (bf16[128,2048]{1,0:T(8,128)(2,1)S(1)}, bf16[128,2048]{1,0:T(8,128)(2,1)S(1)}, u32[]{:S(2)}, u32[]{:S(2)}) collective-permute-start(bf16[128,2048]{1,0:T(8,128)(2,1)S(1)} %collective-permute-done.6.refs_3_), channel_id=1, source_target_pairs={{0,4},{4,0},{8,12},{12,8},{16,20},{20,16},{24,28},{28,24},{32,36},... | collective-permute-start | bytes 1572872 | tf_op jit(solution)/shard_map/ppermute | solution.py:95
  41.9 10.0 %copy-start.2 = (bf16[128,2048]{1,0:T(8,128)(2,1)}, bf16[128,2048]{1,0:T(8,128)(2,1)S(1)}, u32[]{:S(2)}) copy-start(bf16[128,2048]{1,0:T(8,128)(2,1)S(1)} %collective-permute-done.7.refs_4_) | copy-start | bytes 1572868
  41.9 8.4 %collective-permute-start.11 = (bf16[128,2048]{1,0:T(8,128)(2,1)S(1)}, bf16[128,2048]{1,0:T(8,128)(2,1)S(1)}, u32[]{:S(2)}, u32[]{:S(2)}) collective-permute-start(bf16[128,2048]{1,0:T(8,128)(2,1)S(1)} %collective-permute-done.7.refs_4_), channel_id=1, source_target_pairs={{0,4},{4,0},{8,12},{12,8},{16,20},{20,16},{24,28},{28,24},{32,36},... | collective-permute-start | bytes 1572872 | tf_op jit(solution)/shard_map/ppermute | solution.py:95
  44.8 7.1 %copy-start.4 = (bf16[128,2048]{1,0:T(8,128)(2,1)}, bf16[128,2048]{1,0:T(8,128)(2,1)S(1)}, u32[]{:S(2)}) copy-start(bf16[128,2048]{1,0:T(8,128)(2,1)S(1)} %collective-permute-done.8.refs_5_) | copy-start | bytes 1572868
  44.8 7.1 %collective-permute-start.12 = (bf16[128,2048]{1,0:T(8,128)(2,1)S(1)}, bf16[128,2048]{1,0:T(8,128)(2,1)}, u32[]{:S(2)}, u32[]{:S(2)}) collective-permute-start(bf16[128,2048]{1,0:T(8,128)(2,1)S(1)} %collective-permute-done.8.refs_5_), channel_id=1, source_target_pairs={{0,4},{4,0},{8,12},{12,8},{16,20},{20,16},{24,28},{28,24},{32,36},... | collective-permute-start | bytes 1572872 | tf_op jit(solution)/shard_map/ppermute | solution.py:95
  48.9 1.3 %collective-permute-start.5 = (bf16[128,256]{1,0:T(8,128)(2,1)S(1)}, bf16[128,256]{1,0:T(8,128)(2,1)S(1)}, u32[]{:S(2)}, u32[]{:S(2)}) collective-permute-start(bf16[128,256]{1,0:T(8,128)(2,1)S(1)} %get-tuple-element.38.refs_0_), channel_id=1, source_target_pairs={{0,4},{4,0},{8,12},{12,8},{16,20},{20,16},{24,28},{28,24},{32,36},... | collective-permute-start | bytes 196616 | tf_op jit(solution)/shard_map/ppermute | solution.py:95
  56.4 5.6 %copy-start.6 = (bf16[128,2048]{1,0:T(8,128)(2,1)S(1)}, bf16[128,2048]{1,0:T(8,128)(2,1)}, u32[]{:S(2)}) copy-start(bf16[128,2048]{1,0:T(8,128)(2,1)} %copy-done.5) | copy-start | bytes 1572868
  56.4 43.1 %collective-permute-start.23 = (bf16[8,256,128]{2,1,0:T(8,128)(2,1)}, bf16[8,256,128]{2,1,0:T(8,128)(2,1)S(1)}, u32[]{:S(2)}, u32[]{:S(2)}) collective-permute-start(bf16[8,256,128]{2,1,0:T(8,128)(2,1)} %get-tuple-element.37), channel_id=1, source_target_pairs={{0,192},{4,196},{8,200},{12,204},{16,208},{20,212},{24,216},{28,22... | collective-permute-start | bytes 1572872 | tf_op jit(solution)/shard_map/ppermute | solution.py:102
  56.4 43.5 %collective-permute-start.22 = (bf16[8,256,128]{2,1,0:T(8,128)(2,1)}, bf16[8,256,128]{2,1,0:T(8,128)(2,1)S(1)}, u32[]{:S(2)}, u32[]{:S(2)}) collective-permute-start(bf16[8,256,128]{2,1,0:T(8,128)(2,1)} %get-tuple-element.36), channel_id=1, source_target_pairs={{0,128},{4,132},{8,136},{12,140},{16,144},{20,148},{24,152},{28,15... | collective-permute-start | bytes 1572872 | tf_op jit(solution)/shard_map/ppermute | solution.py:102
  60.0 3.7 %copy-start.3 = (bf16[128,2048]{1,0:T(8,128)(2,1)S(1)}, bf16[128,2048]{1,0:T(8,128)(2,1)}, u32[]{:S(2)}) copy-start(bf16[128,2048]{1,0:T(8,128)(2,1)} %copy-done.2) | copy-start | bytes 1572868
  65.5 3.6 %copy-start.20 = (f32[16,256]{1,0:T(8,128)S(1)}, f32[16,256]{1,0:T(8,128)}, u32[]{:S(2)}) copy-start(f32[16,256]{1,0:T(8,128)} %get-tuple-element.45) | copy-start | bytes 49156
  65.5 4.5 %copy-start.1 = (bf16[128,256]{1,0:T(8,128)(2,1)S(1)}, bf16[128,256]{1,0:T(8,128)(2,1)}, u32[]{:S(2)}) copy-start(bf16[128,256]{1,0:T(8,128)(2,1)} %copy-done) | copy-start | bytes 196612
  67.9 16.9 %copy-start.22 = (f32[8]{0:T(128)S(1)}, f32[8]{0:T(128)}, u32[]{:S(2)}) copy-start(f32[8]{0:T(128)} %get-tuple-element.95) | copy-start | bytes 100
  67.9 16.9 %copy-start.23 = (f32[8]{0:T(128)S(1)}, f32[8]{0:T(128)}, u32[]{:S(2)}) copy-start(f32[8]{0:T(128)} %get-tuple-element.96) | copy-start | bytes 100
  67.9 16.9 %copy-start.24 = (pred[8]{0:T(512)(128)(4,1)S(1)}, pred[8]{0:T(512)(128)(4,1)}, u32[]{:S(2)}) copy-start(pred[8]{0:T(512)(128)(4,1)} %iota_compare_fusion) | copy-start | bytes 28
  69.1 3.1 %collective-permute-start.16 = (f32[49,256]{1,0:T(8,128)S(1)}, f32[49,256]{1,0:T(8,128)S(1)}, u32[]{:S(2)}, u32[]{:S(2)}) collective-permute-start(f32[49,256]{1,0:T(8,128)S(1)} %pad_maximum_fusion), channel_id=1, source_target_pairs={{0,4},{4,0},{8,12},{12,8},{16,20},{20,16},{24,28},{28,24},{32,36},... | collective-permute-start | bytes 150536 | tf_op jit(solution)/shard_map/ppermute | solution.py:95
  73.0 11.8 %all-to-all-start.1 = ((bf16[8,49,128]{2,1,0:T(8,128)(2,1)}), bf16[8,49,128]{2,1,0:T(8,128)(2,1)S(1)}, u32[]{:S(2)}, u32[]{:S(2)}) async-start(bf16[8,49,128]{2,1,0:T(8,128)(2,1)} %broadcast_in_dim.83), calls=%async_computation.1 | async-start | bytes 229376 | tf_op jit(solution)/shard_map/all_to_all | solution.py:108
  76.7 26.9 %copy-start.13 = (bf16[8,256,128]{2,1,0:T(8,128)(2,1)S(1)}, bf16[8,256,128]{2,1,0:T(8,128)(2,1)}, u32[]{:S(2)}) copy-start(bf16[8,256,128]{2,1,0:T(8,128)(2,1)} %get-tuple-element.34) | copy-start | bytes 1572868
  85.0 5.6 %collective-permute-start.19 = (f32[49,128]{1,0:T(8,128)S(1)}, f32[49,128]{1,0:T(8,128)S(1)}, u32[]{:S(2)}, u32[]{:S(2)}) collective-permute-start(f32[49,128]{1,0:T(8,128)S(1)} %pad_maximum_fusion.2), channel_id=1, source_target_pairs={{0,64},{4,68},{8,72},{12,76},{16,80},{20,84},{24,88},{28,92},{32,9... | collective-permute-start | bytes 75272 | tf_op jit(solution)/shard_map/ppermute | solution.py:102
  85.1 7.0 %collective-permute-start.18 = (f32[49,128]{1,0:T(8,128)S(1)}, f32[49,128]{1,0:T(8,128)S(1)}, u32[]{:S(2)}, u32[]{:S(2)}) collective-permute-start(f32[49,128]{1,0:T(8,128)S(1)} %pad_maximum_fusion.2), channel_id=1, source_target_pairs={{0,128},{4,132},{8,136},{12,140},{16,144},{20,148},{24,152},{28,15... | collective-permute-start | bytes 75272 | tf_op jit(solution)/shard_map/ppermute | solution.py:102
  88.3 6.2 %collective-permute-start.17 = (f32[49,128]{1,0:T(8,128)S(1)}, f32[49,128]{1,0:T(8,128)S(1)}, u32[]{:S(2)}, u32[]{:S(2)}) collective-permute-start(f32[49,128]{1,0:T(8,128)S(1)} %pad_maximum_fusion.2), channel_id=1, source_target_pairs={{0,192},{4,196},{8,200},{12,204},{16,208},{20,212},{24,216},{28,22... | collective-permute-start | bytes 75272 | tf_op jit(solution)/shard_map/ppermute | solution.py:102
  90.6 12.9 %collective-permute-start.21 = (bf16[8,256,128]{2,1,0:T(8,128)(2,1)}, bf16[8,256,128]{2,1,0:T(8,128)(2,1)S(1)}, u32[]{:S(2)}, u32[]{:S(2)}) collective-permute-start(bf16[8,256,128]{2,1,0:T(8,128)(2,1)} %get-tuple-element.35), channel_id=1, source_target_pairs={{0,64},{4,68},{8,72},{12,76},{16,80},{20,84},{24,88},{28,92},{32,9... | collective-permute-start | bytes 1572872 | tf_op jit(solution)/shard_map/ppermute | solution.py:102
  92.1 18.7 %collective-permute-start.15 = (bf16[128,2048]{1,0:T(8,128)(2,1)}, bf16[128,2048]{1,0:T(8,128)(2,1)}, u32[]{:S(2)}, u32[]{:S(2)}) collective-permute-start(bf16[128,2048]{1,0:T(8,128)(2,1)} %convolution_convert_fusion), channel_id=1, source_target_pairs={{0,3},{1,0},{2,1},{3,2},{4,7},{5,4},{6,5},{7,6},{8,11},{9,8},{10,9... | collective-permute-start | bytes 1572872 | tf_op jit(solution)/shard_map/ppermute | solution.py:98
  94.5 5.0 %collective-permute-start.20 = (f32[49,128]{1,0:T(8,128)S(1)}, f32[49,128]{1,0:T(8,128)S(1)}, u32[]{:S(2)}, u32[]{:S(2)}) collective-permute-start(f32[49,128]{1,0:T(8,128)S(1)} %pad_maximum_fusion.3), channel_id=1, source_target_pairs={{0,4},{4,0},{8,12},{12,8},{16,20},{20,16},{24,28},{28,24},{32,36},... | collective-permute-start | bytes 75272 | tf_op jit(solution)/shard_map/ppermute | solution.py:95
  99.5 9.9 %copy-start.26 = (f32[128]{0:T(128)S(1)}, f32[128]{0:T(128)}, u32[]{:S(2)}) copy-start(f32[128]{0:T(128)} %copy-done.25) | copy-start | bytes 1540
  99.5 15.3 %collective-permute-start.14 = (bf16[128,2048]{1,0:T(8,128)(2,1)}, bf16[128,2048]{1,0:T(8,128)(2,1)}, u32[]{:S(2)}, u32[]{:S(2)}) collective-permute-start(bf16[128,2048]{1,0:T(8,128)(2,1)} %convolution_convert_fusion.1), channel_id=1, source_target_pairs={{0,2},{1,3},{2,0},{3,1},{4,6},{5,7},{6,4},{7,5},{8,10},{9,11},{10,... | collective-permute-start | bytes 1572872 | tf_op jit(solution)/shard_map/ppermute | solution.py:98
  99.5 26.5 %collective-permute-start.13 = (bf16[128,2048]{1,0:T(8,128)(2,1)}, bf16[128,2048]{1,0:T(8,128)(2,1)}, u32[]{:S(2)}, u32[]{:S(2)}) collective-permute-start(bf16[128,2048]{1,0:T(8,128)(2,1)} %convolution_convert_fusion.2), channel_id=1, source_target_pairs={{0,1},{1,2},{2,3},{3,0},{4,5},{5,6},{6,7},{7,4},{8,9},{9,10},{10,1... | collective-permute-start | bytes 1572872 | tf_op jit(solution)/shard_map/ppermute | solution.py:98
  104.6 24.3 %all-to-all-start.2 = ((bf16[8,256,128]{2,1,0:T(8,128)(2,1)}), bf16[8,256,128]{2,1,0:T(8,128)(2,1)S(1)}, u32[]{:S(2)}, u32[]{:S(2)}) async-start(bf16[8,256,128]{2,1,0:T(8,128)(2,1)} %add_convert_fusion), calls=%async_computation.2 | async-start | bytes 1048576 | tf_op jit(solution)/shard_map/all_to_all | solution.py:283
  (6 other events, 10.4 us)

commit v3 on v2

--- a/solution.py
+++ b/solution.py
@@ -87,7 +87,9 @@
     ny = tps
     nz = ctx // (2 * ny)
     core = dev % 2
-    zz = dev // 2 % nz
+    pair = dev // 2
+    zz = pair % nz
+    pairs = ctx // 2
     yy = dev // (2 * nz)
     width = feats // (2 * nz)
 
@@ -106,6 +108,11 @@
     def of_plane(a):
         copies = jnp.broadcast_to(a[None], (nz, *a.shape))
         return lax.all_to_all(copies, "ctx", 0, 0, tiled=True, axis_index_groups=z_groups)
+
+    def of_pairs(a):
+        copies = jnp.broadcast_to(a[None], (pairs, *a.shape))
+        groups = [[2 * i + j for i in range(pairs)] for j in range(2)]
+        return lax.all_to_all(copies, "ctx", 0, 0, tiled=True, axis_index_groups=groups)
 
     og = [out_grad] + [row_major(shift_tp(out_grad, k)) for k in range(1, tps)]
 
@@ -140,8 +147,9 @@
     total = decay_h * f_h[:modes] + s_h[:modes]
     total_lag = decay_h * (block * f_h[:modes] + f_h[modes:]) + s_h[modes:]
     to_send = jnp.concatenate([total, total_lag], 0).astype(BF16)
-    gathered = of_plane(to_send).astype(F32)
+    gathered = of_pairs(to_send).astype(F32)
     place = jnp.arange(nz, dtype=jnp.int32)
+    every = jnp.arange(pairs, dtype=jnp.int32)
     per_pair = 2 * block
     per_plane = per_pair * nz
 
@@ -149,27 +157,10 @@
         gap = jnp.where(which, gap, 0).astype(F32)[:, None, None] * per_pair
         return jnp.where(which[:, None, None], jnp.exp(-rate_h[None] * gap), 0.0), gap
 
-    def carried(w, gap):
-        base = gathered[:, :modes]
-        return jnp.sum(w * base, 0), jnp.sum(w * (gap * base + gathered[:, modes:]), 0)
-
-    plane, plane_lag = carried(*weights(place >= 0, nz - 1 - place))
-    plane_all = jnp.concatenate([plane, plane_lag], 0)
-    in_h, in_lag_h = carried(*weights(place < zz, zz - 1 - place))
-    y_in, y_in_lag = 0.0, 0.0
-    for k in range(1, ny):
-        per = 2 * nz
-        came = lax.ppermute(
-            plane_all, "ctx", [(i, i + k * per) for i in range(ctx) if i + k * per < ctx]
-        )
-        gap = float(per_plane * (k - 1))
-        w = jnp.exp(-rate_h * gap)
-        y_in = y_in + w * came[:modes]
-        y_in_lag = y_in_lag + w * (gap * came[:modes] + came[modes:])
-    gap = (per_pair * zz).astype(F32)
-    w = jnp.exp(-rate_h * gap)
-    in_h = in_h + w * y_in
-    in_lag_h = in_lag_h + w * (gap * y_in + y_in_lag)
+    w, gap = weights(every < pair, pair - 1 - every)
+    base = gathered[:, :modes]
+    in_h = jnp.sum(w * base, 0)
+    in_lag_h = jnp.sum(w * (gap * base + gathered[:, modes:]), 0)
     incoming = both_halves(jnp.concatenate([in_h, in_lag_h], 0))
     in_pair, in_pair_lag = incoming[:modes], incoming[modes:]
     x_in = jnp.where(core == 0, in_pair, fall_block * in_pair + first[:modes])
@@ -207,11 +198,11 @@
 
     def projected(k):
         w_block = lax.dynamic_slice_in_dim(out_weight, (tp + k) % tps * feats, feats, 1)
-        return jnp.dot(result, w_block, preferred_element_type=F32)
-
-    mixed = projected(0)
+        return jnp.dot(result, w_block, preferred_element_type=F32).astype(BF16)
+
+    mixed = projected(0).astype(F32)
     for k in range(1, tps):
-        piece = projected(k).astype(BF16)
+        piece = projected(k)
         piece = shift_tp(piece, k)
         mixed = mixed + piece.astype(F32)
     mixed = mixed.astype(BF16)

time: 130 us -> 134 us (1.031)
  waiting for transfers between devices: 38.8 us -> 40.9 us
    all_to_all x0 -> x1, starting transfers between devices: none -> 9.5 us  [of_pairs(): lax.all_to_all(copies, 'ctx', 0, 0, tiled=True, axis_index_groups=groups)]
    ppermute x3 -> x0, starting transfers between devices: 8.41 us -> none  [body(): lax.ppermute(plane_all, 'ctx', [(i, i + k * per) for i in range(ctx) if i...]
    all_to_all x2 -> x1, waiting for transfers between devices: 15.4 us -> 7.83 us  [of_plane(): lax.all_to_all(copies, 'ctx', 0, 0, tiled=True, axis_index_groups=z_groups)]
    ppermute x6, waiting for transfers between devices: 18 us -> 24.7 us  [shift_tp(): return lax.ppermute(a, 'tp', [(i, (i + k) % tps) for i in range(tps)])]
    all_to_all x2 -> x1, starting transfers between devices: 11.6 us -> 6.36 us  [of_plane(): lax.all_to_all(copies, 'ctx', 0, 0, tiled=True, axis_index_groups=z_groups)]
    all_to_all x0 -> x1, waiting for transfers between devices: none -> 2.66 us  [of_pairs(): lax.all_to_all(copies, 'ctx', 0, 0, tiled=True, axis_index_groups=groups)]
    ppermute x9, starting transfers between devices: 13.8 us -> 15.9 us  [swap_core(): return lax.ppermute(a, 'ctx', [(i, i ^ 1) for i in range(ctx)])]
    ppermute x6, starting transfers between devices: 5.84 us -> 7.91 us  [shift_tp(): return lax.ppermute(a, 'tp', [(i, (i + k) % tps) for i in range(tps)])]
  transfers between devices with their start and end apart: 27 -> 24, of which waited for: 8 -> 9; matrix products, arithmetic and copies ran while one was open for 24% -> 23% of each run, Pallas kernels for 0% -> 0%
where the time goes in v3:
time: 134 us; the launch traced here: 133 us
  starting transfers between devices  50.8 us (38%)
  waiting for transfers between devices  40.9 us (31%)
  matrix products  21.4 us (16%)
  other arithmetic  11 us (8%)
  Pallas kernels  4.44 us (3%)
  local copies, waits for them, and re-layouts  3.21 us (2%)
    ppermute x6, waiting for transfers between devices, shift_tp(): return lax.ppermute(a, 'tp', [(i, (i + k) % tps) for i in range(tps)])  24.7 us
    ppermute x9, starting transfers between devices, swap_core(): return lax.ppermute(a, 'ctx', [(i, i ^ 1) for i in range(ctx)])  15.9 us
    dot_general x4, matrix products, projected(): return jnp.dot(result, w_block, preferred_element_type=F32).astype(BF16)  9.9 us
    all_to_all x1, starting transfers between devices, of_pairs(): lax.all_to_all(copies, 'ctx', 0, 0, tiled=True, axis_index_groups=groups)  9.5 us
    ppermute x6, starting transfers between devices, shift_tp(): return lax.ppermute(a, 'tp', [(i, (i + k) % tps) for i in range(tps)])  7.91 us
    all_to_all x1, waiting for transfers between devices, of_plane(): lax.all_to_all(copies, 'ctx', 0, 0, tiled=True, axis_index_groups=z_groups)  7.83 us
    ppermute x6, starting transfers between devices, shift_y(): lax.ppermute(a, 'ctx', [(i, (i // per + k) % ny * per + i % per) for i in...  7.65 us
    dot_general x4, matrix products, body(): lax.dot_general(og[k], w_block, (((1,), (1,)), ((), ())), preferred_eleme...  7.21 us
  transfers between devices with their start and end apart: 24, of which 9 were waited for; matrix products, arithmetic and copies ran while one was open for 23% of the time, Pallas kernels for 0%

profile of v3, /device:TPU:1, one launch (start us, length us, event | category | flops | bytes accessed | tf_op | source)
XLA Modules:
  0.0 133.0 jit_solution(12597489926117450865)
XLA Ops:
  0.7 0.7 fusion.113
  1.4 0.9 convert_multiply_fusion.5
  2.3 0.7 fusion.5
  3.0 3.3 %collective-permute-start = (f32[32,256]{1,0:T(8,128)S(1)}, f32[32,256]{1,0:T(8,128)S(1)}, u32[]{:S(2)}, u32[]{:S(2)}) collective-permute-start(f32[32,256]{1,0:T(8,128)S(1)} %pad_maximum_fusion.1), channel_id=1, source_target_pairs={{0,4},{4,0},{8,12},{12,8},{16,20},{20,16},{24,28},{28,24},{32,36},... | collective-permute-start | bytes 98312 | tf_op jit(solution)/shard_map/ppermute | solution.py:97
  6.3 0.9 collective-permute-done
  7.3 0.7 broadcast_in_dim.49
  8.0 9.5 %all-to-all-start = ((bf16[32,32,128]{2,1,0:T(8,128)(2,1)}), bf16[32,32,128]{2,1,0:T(8,128)(2,1)S(1)}, u32[]{:S(2)}, u32[]{:S(2)}) async-start(bf16[32,32,128]{2,1,0:T(8,128)(2,1)} %broadcast_in_dim.49), calls=%async_computation | async-start | bytes 524288 | tf_op jit(solution)/shard_map/all_to_all | solution.py:115
  17.5 1.3 collective-permute-start.3
  18.8 2.5 %collective-permute-start.4 = (bf16[128,2048]{1,0:T(8,128)(2,1)}, bf16[128,2048]{1,0:T(8,128)(2,1)S(1)}, u32[]{:S(2)}, u32[]{:S(2)}) collective-permute-start(bf16[128,2048]{1,0:T(8,128)(2,1)} %refs_2_.1), channel_id=1, source_target_pairs={{0,2},{1,3},{2,0},{3,1},{4,6},{5,7},{6,4},{7,5},{8,10},{9,11},{10,... | collective-permute-start | bytes 1572872 | tf_op jit(solution)/shard_map/ppermute | solution.py:100
  21.3 1.2 collective-permute-start.5
  22.4 1.5 %collective-permute-start.6 = (bf16[128,2048]{1,0:T(8,128)(2,1)}, bf16[128,2048]{1,0:T(8,128)(2,1)S(1)}, u32[]{:S(2)}, u32[]{:S(2)}) collective-permute-start(bf16[128,2048]{1,0:T(8,128)(2,1)} %refs_2_.1), channel_id=1, source_target_pairs={{0,4},{4,0},{8,12},{12,8},{16,20},{20,16},{24,28},{28,24},{32,36},... | collective-permute-start | bytes 1572872 | tf_op jit(solution)/shard_map/ppermute | solution.py:97
  24.5 2.7 %all-to-all-done = bf16[32,32,128]{2,1,0:T(8,128)(2,1)S(1)} async-done(((bf16[32,32,128]{2,1,0:T(8,128)(2,1)}), bf16[32,32,128]{2,1,0:T(8,128)(2,1)S(1)}, u32[]{:S(2)}, u32[]{:S(2)}) %all-to-all-start) | async-done | bytes 262176 | tf_op jit(solution)/shard_map/all_to_all | solution.py:115
  27.4 3.8 %collective-permute-start.1 = (f32[32,128]{1,0:T(8,128)S(1)}, f32[32,128]{1,0:T(8,128)S(1)}, u32[]{:S(2)}, u32[]{:S(2)}) collective-permute-start(f32[32,128]{1,0:T(8,128)S(1)} %pad_maximum_fusion.6), channel_id=1, source_target_pairs={{0,4},{4,0},{8,12},{12,8},{16,20},{20,16},{24,28},{28,24},{32,36},... | collective-permute-start | bytes 49160 | tf_op jit(solution)/shard_map/ppermute | solution.py:97
  31.9 1.6 %collective-permute-start.7 = (bf16[128,2048]{1,0:T(8,128)(2,1)S(1)}, bf16[128,2048]{1,0:T(8,128)(2,1)S(1)}, u32[]{:S(2)}, u32[]{:S(2)}) collective-permute-start(bf16[128,2048]{1,0:T(8,128)(2,1)S(1)} %collective-permute-done.3.refs_3_), channel_id=1, source_target_pairs={{0,4},{4,0},{8,12},{12,8},{16,20},{20,16},{24,28},{28,24},{32,36},... | collective-permute-start | bytes 1572872 | tf_op jit(solution)/shard_map/ppermute | solution.py:97
  33.5 10.6 %collective-permute-done.4.refs_4_ = bf16[128,2048]{1,0:T(8,128)(2,1)S(1)} collective-permute-done((bf16[128,2048]{1,0:T(8,128)(2,1)}, bf16[128,2048]{1,0:T(8,128)(2,1)S(1)}, u32[]{:S(2)}, u32[]{:S(2)}) %collective-permute-start.4) | collective-permute-done | bytes 524320 | tf_op jit(solution)/shard_map/ppermute | solution.py:100
  44.1 1.5 %collective-permute-start.8 = (bf16[128,2048]{1,0:T(8,128)(2,1)S(1)}, bf16[128,2048]{1,0:T(8,128)(2,1)S(1)}, u32[]{:S(2)}, u32[]{:S(2)}) collective-permute-start(bf16[128,2048]{1,0:T(8,128)(2,1)S(1)} %collective-permute-done.4.refs_4_), channel_id=1, source_target_pairs={{0,4},{4,0},{8,12},{12,8},{16,20},{20,16},{24,28},{28,24},{32,36},... | collective-permute-start | bytes 1572872 | tf_op jit(solution)/shard_map/ppermute | solution.py:97
  49.8 0.8 copy-done.14
  50.6 0.8 copy-done.15
  51.5 4.4 %shard_map.161 = (bf16[8,256,128]{2,1,0:T(8,128)(2,1)}, bf16[8,256,128]{2,1,0:T(8,128)(2,1)}, bf16[8,256,128]{2,1,0:T(8,128)(2,1)}, bf16[8,256,128]{2,1,0:T(8,128)(2,1)}) custom-call(s32[2]{0:T(128)} %pad_add_fusion.turns_ref, bf16[128,256]{1,0:T(8,128)(2,1)} %copy-done, bf16[128,256]{1,0:T(8,128)(2,1)} %copy-done.18, bf16[128,2048]{1,0:T(8,128)(2,1)} %refs_2_.1, ...), custom_call_target="tpu_custom_call" | custom-call | tf_op jit(solution)/shard_map/pallas_call | solution.py:70
  55.9 2.5 %collective-permute-start.20 = (bf16[8,256,128]{2,1,0:T(8,128)(2,1)}, bf16[8,256,128]{2,1,0:T(8,128)(2,1)S(1)}, u32[]{:S(2)}, u32[]{:S(2)}) collective-permute-start(bf16[8,256,128]{2,1,0:T(8,128)(2,1)} %get-tuple-element.37), channel_id=1, source_target_pairs={{0,192},{4,196},{8,200},{12,204},{16,208},{20,212},{24,216},{28,22... | collective-permute-start | bytes 1572872 | tf_op jit(solution)/shard_map/ppermute | solution.py:104
  58.9 1.8 %fusion.22 = f32[256,128]{0,1:T(8,128)S(1)} fusion(bf16[128,2048]{1,0:T(8,128)(2,1)} %refs_2_.1, bf16[256,8192]{1,0:T(8,128)(2,1)} %param.16, s32[]{:T(128)S(6)} %select_n.209), kind=kOutput, calls=%fused_computation.43 | convolution fusion | flops 134217728 | bytes 1703940 | tf_op jit(solution)/shard_map/dot_general | solution.py:213
  60.8 1.9 %fusion.15 = f32[256,128]{0,1:T(8,128)S(1)} fusion(bf16[128,2048]{1,0:T(8,128)(2,1)} %copy-done.4, bf16[256,8192]{1,0:T(8,128)(2,1)} %param.16, s32[]{:T(128)S(6)} %select_n.221), kind=kOutput, calls=%fused_computation.35 | convolution fusion | flops 134217728 | bytes 1703940 | tf_op jit(solution)/shard_map/dot_general | solution.py:213
  62.7 1.7 %convolution_add_fusion.3 = f32[256,128]{0,1:T(8,128)S(1)} fusion(f32[256,128]{0,1:T(8,128)S(1)} %fusion.22, bf16[128,2048]{1,0:T(8,128)(2,1)S(1)} %copy-done.6, bf16[256,8192]{1,0:T(8,128)(2,1)} %param.16, s32[]{:T(128)S(6)} %select_n.217), kind=kOutput, calls=%fused_computation.28 | convolution fusion | flops 134250496 | bytes 1835012 | tf_op jit(solution)/shard_map/dot_general | solution.py:213
  64.5 1.7 %fusion.11 = f32[128,256]{1,0:T(8,128)S(1)} fusion(f32[256,128]{0,1:T(8,128)S(1)} %fusion.15, f32[256,128]{0,1:T(8,128)S(1)} %convolution_add_fusion.3, bf16[128,2048]{1,0:T(8,128)(2,1)S(1)} %copy-done.3, bf16[256,8192]{1,0:T(8,128)(2,1)} %param.16, s32[]{:T(128)S(6)} %select_n.219), kind=kOutput, calls=%fused_computation.27 | convolution fusion | flops 134283264 | bytes 1966084 | tf_op jit(solution)/shard_map/dot_general | solution.py:213
  66.2 0.7 fusion.52
  68.7 1.1 fusion.4
  69.9 1.0 collective-permute-start.13
  70.9 2.3 %convolution_convert_fusion = bf16[128,2048]{1,0:T(8,128)(2,1)} fusion(bf16[128,256]{1,0:T(8,128)(2,1)S(1)} %copy-done.1, bf16[256,8192]{1,0:T(8,128)(2,1)} %param.16, s32[]{:T(128)S(6)} %select_n.215), kind=kOutput, calls=%fused_computation | convolution fusion | flops 134479872 | bytes 1638404 | tf_op jit(solution)/shard_map/dot_general | solution.py:201
  73.3 0.7 broadcast_in_dim.86
  73.9 6.4 %all-to-all-start.1 = ((bf16[8,49,128]{2,1,0:T(8,128)(2,1)}), bf16[8,49,128]{2,1,0:T(8,128)(2,1)S(1)}, u32[]{:S(2)}, u32[]{:S(2)}) async-start(bf16[8,49,128]{2,1,0:T(8,128)(2,1)} %broadcast_in_dim.86), calls=%async_computation.1 | async-start | bytes 229376 | tf_op jit(solution)/shard_map/all_to_all | solution.py:110
  80.6 7.8 %all-to-all-done.1 = bf16[8,49,128]{2,1,0:T(8,128)(2,1)S(1)} async-done(((bf16[8,49,128]{2,1,0:T(8,128)(2,1)}), bf16[8,49,128]{2,1,0:T(8,128)(2,1)S(1)}, u32[]{:S(2)}, u32[]{:S(2)}) %all-to-all-start.1) | async-done | bytes 100384 | tf_op jit(solution)/shard_map/all_to_all | solution.py:110
  88.6 0.7 collective-permute-start.16
  89.3 2.0 %collective-permute-start.15 = (f32[49,128]{1,0:T(8,128)S(1)}, f32[49,128]{1,0:T(8,128)S(1)}, u32[]{:S(2)}, u32[]{:S(2)}) collective-permute-start(f32[49,128]{1,0:T(8,128)S(1)} %pad_maximum_fusion.2), channel_id=1, source_target_pairs={{0,128},{4,132},{8,136},{12,140},{16,144},{20,148},{24,152},{28,15... | collective-permute-start | bytes 75272 | tf_op jit(solution)/shard_map/ppermute | solution.py:104
  91.3 2.0 %collective-permute-start.14 = (f32[49,128]{1,0:T(8,128)S(1)}, f32[49,128]{1,0:T(8,128)S(1)}, u32[]{:S(2)}, u32[]{:S(2)}) collective-permute-start(f32[49,128]{1,0:T(8,128)S(1)} %pad_maximum_fusion.2), channel_id=1, source_target_pairs={{0,192},{4,196},{8,200},{12,204},{16,208},{20,212},{24,216},{28,22... | collective-permute-start | bytes 75272 | tf_op jit(solution)/shard_map/ppermute | solution.py:104
  93.3 2.3 %convolution_convert_fusion.1 = bf16[128,2048]{1,0:T(8,128)(2,1)} fusion(bf16[128,256]{1,0:T(8,128)(2,1)S(1)} %copy-done.1, bf16[256,8192]{1,0:T(8,128)(2,1)} %param.16, s32[]{:T(128)S(6)} %select_n.213), kind=kOutput, calls=%fused_computation.1 | convolution fusion | flops 134479872 | bytes 1638404 | tf_op jit(solution)/shard_map/dot_general | solution.py:201
  95.6 1.7 %collective-permute-start.12 = (bf16[128,2048]{1,0:T(8,128)(2,1)}, bf16[128,2048]{1,0:T(8,128)(2,1)}, u32[]{:S(2)}, u32[]{:S(2)}) collective-permute-start(bf16[128,2048]{1,0:T(8,128)(2,1)} %convolution_convert_fusion), channel_id=1, source_target_pairs={{0,3},{1,0},{2,1},{3,2},{4,7},{5,4},{6,5},{7,6},{8,11},{9,8},{10,9... | collective-permute-start | bytes 1572872 | tf_op jit(solution)/shard_map/ppermute | solution.py:100
  97.4 2.7 %collective-permute-start.17 = (f32[49,128]{1,0:T(8,128)S(1)}, f32[49,128]{1,0:T(8,128)S(1)}, u32[]{:S(2)}, u32[]{:S(2)}) collective-permute-start(f32[49,128]{1,0:T(8,128)S(1)} %pad_maximum_fusion.3), channel_id=1, source_target_pairs={{0,4},{4,0},{8,12},{12,8},{16,20},{20,16},{24,28},{28,24},{32,36},... | collective-permute-start | bytes 75272 | tf_op jit(solution)/shard_map/ppermute | solution.py:97
  100.1 2.3 %convolution_convert_fusion.2 = bf16[128,2048]{1,0:T(8,128)(2,1)} fusion(bf16[128,256]{1,0:T(8,128)(2,1)S(1)} %copy-done.1, bf16[256,8192]{1,0:T(8,128)(2,1)} %param.16, s32[]{:T(128)S(6)} %select_n.211), kind=kOutput, calls=%fused_computation.2 | convolution fusion | flops 134479872 | bytes 1638404 | tf_op jit(solution)/shard_map/dot_general | solution.py:201
  102.4 0.9 collective-permute-start.11
  103.8 4.5 %collective-permute-done.18 = bf16[8,256,128]{2,1,0:T(8,128)(2,1)S(1)} collective-permute-done((bf16[8,256,128]{2,1,0:T(8,128)(2,1)}, bf16[8,256,128]{2,1,0:T(8,128)(2,1)S(1)}, u32[]{:S(2)}, u32[]{:S(2)}) %collective-permute-start.18) | collective-permute-done | bytes 524320 | tf_op jit(solution)/shard_map/ppermute | solution.py:104
  108.3 1.1 add_convert_fusion
  109.3 3.5 %all-to-all-start.2 = ((bf16[8,256,128]{2,1,0:T(8,128)(2,1)}), bf16[8,256,128]{2,1,0:T(8,128)(2,1)S(1)}, u32[]{:S(2)}, u32[]{:S(2)}) async-start(bf16[8,256,128]{2,1,0:T(8,128)(2,1)} %add_convert_fusion), calls=%async_computation.2 | async-start | bytes 1048576 | tf_op jit(solution)/shard_map/all_to_all | solution.py:274
  112.8 0.7 fusion.87
  114.5 1.0 fusion.50
  115.5 2.3 %collective-permute-done.11 = bf16[128,2048]{1,0:T(8,128)(2,1)} collective-permute-done((bf16[128,2048]{1,0:T(8,128)(2,1)}, bf16[128,2048]{1,0:T(8,128)(2,1)}, u32[]{:S(2)}, u32[]{:S(2)}) %collective-permute-start.11) | collective-permute-done | bytes 524320 | tf_op jit(solution)/shard_map/ppermute | solution.py:100
  117.8 11.6 %collective-permute-done.10 = bf16[128,2048]{1,0:T(8,128)(2,1)} collective-permute-done((bf16[128,2048]{1,0:T(8,128)(2,1)}, bf16[128,2048]{1,0:T(8,128)(2,1)}, u32[]{:S(2)}, u32[]{:S(2)}) %collective-permute-start.10) | collective-permute-done | bytes 524320 | tf_op jit(solution)/shard_map/ppermute | solution.py:100
  129.4 2.9 %add_convert_fusion.1 = bf16[128,2048]{1,0:T(8,128)(2,1)} fusion(bf16[128,2048]{1,0:T(8,128)(2,1)} %collective-permute-done.12, bf16[128,2048]{1,0:T(8,128)(2,1)} %collective-permute-done.11, bf16[128,2048]{1,0:T(8,128)(2,1)} %collective-permute-done.10, bf16[128,256]{1,0:T(8,128)(2,1)S(1)} %copy-done.1, bf16[256,8192]{1,0:T(8,128)(2,1)} %param.16, ...), kind=kOutput, calls=%fused_computation.39 | convolution fusion | flops 136577024 | bytes 3211268 | tf_op jit(solution)/shard_map/dot_general | solution.py:201
  132.3 0.7 convert_reduce_fusion
  (119 shorter events, 10.0 us)
Async XLA Ops:
  0.6 6.5 %copy-start.25 = (f32[128]{0:T(128)}, f32[128]{0:T(128)S(1)}, u32[]{:S(2)}) copy-start(f32[128]{0:T(128)S(1)} %iota_subtract_fusion) | copy-start | bytes 1540
  1.4 44.3 %copy-start.16 = (f32[16,256]{1,0:T(8,128)S(1)}, f32[16,256]{1,0:T(8,128)}, u32[]{:S(2)}) copy-start(f32[16,256]{1,0:T(8,128)} %param.14) | copy-start | bytes 49156
  1.4 45.0 %copy-start.19 = (f32[16,256]{1,0:T(8,128)S(1)}, f32[16,256]{1,0:T(8,128)}, u32[]{:S(2)}) copy-start(f32[16,256]{1,0:T(8,128)} %param.13) | copy-start | bytes 49156
  3.0 43.9 %copy-start.9 = (f32[258,128]{1,0:T(8,128)S(1)}, f32[258,128]{1,0:T(8,128)}, u32[]{:S(2)}) copy-start(f32[258,128]{1,0:T(8,128)} %constant.135.clone) | copy-start | bytes 396292
  3.0 4.1 %collective-permute-start = (f32[32,256]{1,0:T(8,128)S(1)}, f32[32,256]{1,0:T(8,128)S(1)}, u32[]{:S(2)}, u32[]{:S(2)}) collective-permute-start(f32[32,256]{1,0:T(8,128)S(1)} %pad_maximum_fusion.1), channel_id=1, source_target_pairs={{0,4},{4,0},{8,12},{12,8},{16,20},{20,16},{24,28},{28,24},{32,36},... | collective-permute-start | bytes 98312 | tf_op jit(solution)/shard_map/ppermute | solution.py:97
  7.3 40.1 %copy-start.7 = (bf16[128,256]{1,0:T(8,128)(2,1)S(1)}, bf16[128,256]{1,0:T(8,128)(2,1)}, u32[]{:S(2)}) copy-start(bf16[128,256]{1,0:T(8,128)(2,1)} %param.12) | copy-start | bytes 196612
  7.3 40.1 %copy-start.8 = (bf16[128,256]{1,0:T(8,128)(2,1)S(1)}, bf16[128,256]{1,0:T(8,128)(2,1)}, u32[]{:S(2)}) copy-start(bf16[128,256]{1,0:T(8,128)(2,1)} %param.11) | copy-start | bytes 196612
  8.0 19.2 %all-to-all-start = ((bf16[32,32,128]{2,1,0:T(8,128)(2,1)}), bf16[32,32,128]{2,1,0:T(8,128)(2,1)S(1)}, u32[]{:S(2)}, u32[]{:S(2)}) async-start(bf16[32,32,128]{2,1,0:T(8,128)(2,1)} %broadcast_in_dim.49), calls=%async_computation | async-start | bytes 524288 | tf_op jit(solution)/shard_map/all_to_all | solution.py:115
  17.5 30.2 %copy-start.11 = (f32[128,129]{1,0:T(8,128)S(1)}, f32[128,129]{1,0:T(8,128)}, u32[]{:S(2)}) copy-start(f32[128,129]{1,0:T(8,128)} %constant.137) | copy-start | bytes 198148
  17.5 14.4 %collective-permute-start.3 = (bf16[128,2048]{1,0:T(8,128)(2,1)}, bf16[128,2048]{1,0:T(8,128)(2,1)S(1)}, u32[]{:S(2)}, u32[]{:S(2)}) collective-permute-start(bf16[128,2048]{1,0:T(8,128)(2,1)} %refs_2_.1), channel_id=1, source_target_pairs={{0,1},{1,2},{2,3},{3,0},{4,5},{5,6},{6,7},{7,4},{8,9},{9,10},{10,1... | collective-permute-start | bytes 1572872 | tf_op jit(solution)/shard_map/ppermute | solution.py:100
  18.8 25.3 %collective-permute-start.4 = (bf16[128,2048]{1,0:T(8,128)(2,1)}, bf16[128,2048]{1,0:T(8,128)(2,1)S(1)}, u32[]{:S(2)}, u32[]{:S(2)}) collective-permute-start(bf16[128,2048]{1,0:T(8,128)(2,1)} %refs_2_.1), channel_id=1, source_target_pairs={{0,2},{1,3},{2,0},{3,1},{4,6},{5,7},{6,4},{7,5},{8,10},{9,11},{10,... | collective-permute-start | bytes 1572872 | tf_op jit(solution)/shard_map/ppermute | solution.py:100
  21.3 24.3 %collective-permute-start.5 = (bf16[128,2048]{1,0:T(8,128)(2,1)}, bf16[128,2048]{1,0:T(8,128)(2,1)S(1)}, u32[]{:S(2)}, u32[]{:S(2)}) collective-permute-start(bf16[128,2048]{1,0:T(8,128)(2,1)} %refs_2_.1), channel_id=1, source_target_pairs={{0,3},{1,0},{2,1},{3,2},{4,7},{5,4},{6,5},{7,6},{8,11},{9,8},{10,9... | collective-permute-start | bytes 1572872 | tf_op jit(solution)/shard_map/ppermute | solution.py:100
  22.4 27.1 %collective-permute-start.6 = (bf16[128,2048]{1,0:T(8,128)(2,1)}, bf16[128,2048]{1,0:T(8,128)(2,1)S(1)}, u32[]{:S(2)}, u32[]{:S(2)}) collective-permute-start(bf16[128,2048]{1,0:T(8,128)(2,1)} %refs_2_.1), channel_id=1, source_target_pairs={{0,4},{4,0},{8,12},{12,8},{16,20},{20,16},{24,28},{28,24},{32,36},... | collective-permute-start | bytes 1572872 | tf_op jit(solution)/shard_map/ppermute | solution.py:97
  24.5 23.5 %copy-start.10 = (f32[128,129]{1,0:T(8,128)S(1)}, f32[128,129]{1,0:T(8,128)}, u32[]{:S(2)}) copy-start(f32[128,129]{1,0:T(8,128)} %constant.138) | copy-start | bytes 198148
  24.5 23.5 %copy-start.17 = (bf16[128,256]{1,0:T(8,128)(2,1)S(1)}, bf16[128,256]{1,0:T(8,128)(2,1)}, u32[]{:S(2)}) copy-start(bf16[128,256]{1,0:T(8,128)(2,1)} %param.10) | copy-start | bytes 196612
  24.5 23.5 %copy-start.21 = (f32[256]{0:T(256)S(1)}, f32[256]{0:T(256)}, u32[]{:S(2)}) copy-start(f32[256]{0:T(256)} %param.15) | copy-start | bytes 3076
  27.4 18.3 %collective-permute-start.1 = (f32[32,128]{1,0:T(8,128)S(1)}, f32[32,128]{1,0:T(8,128)S(1)}, u32[]{:S(2)}, u32[]{:S(2)}) collective-permute-start(f32[32,128]{1,0:T(8,128)S(1)} %pad_maximum_fusion.6), channel_id=1, source_target_pairs={{0,4},{4,0},{8,12},{12,8},{16,20},{20,16},{24,28},{28,24},{32,36},... | collective-permute-start | bytes 49160 | tf_op jit(solution)/shard_map/ppermute | solution.py:97
  31.9 19.5 %copy-start.5 = (bf16[128,2048]{1,0:T(8,128)(2,1)}, bf16[128,2048]{1,0:T(8,128)(2,1)S(1)}, u32[]{:S(2)}) copy-start(bf16[128,2048]{1,0:T(8,128)(2,1)S(1)} %collective-permute-done.3.refs_3_) | copy-start | bytes 1572868
  31.9 17.9 %collective-permute-start.7 = (bf16[128,2048]{1,0:T(8,128)(2,1)S(1)}, bf16[128,2048]{1,0:T(8,128)(2,1)S(1)}, u32[]{:S(2)}, u32[]{:S(2)}) collective-permute-start(bf16[128,2048]{1,0:T(8,128)(2,1)S(1)} %collective-permute-done.3.refs_3_), channel_id=1, source_target_pairs={{0,4},{4,0},{8,12},{12,8},{16,20},{20,16},{24,28},{28,24},{32,36},... | collective-permute-start | bytes 1572872 | tf_op jit(solution)/shard_map/ppermute | solution.py:97
  44.1 7.3 %copy-start.2 = (bf16[128,2048]{1,0:T(8,128)(2,1)}, bf16[128,2048]{1,0:T(8,128)(2,1)S(1)}, u32[]{:S(2)}) copy-start(bf16[128,2048]{1,0:T(8,128)(2,1)S(1)} %collective-permute-done.4.refs_4_) | copy-start | bytes 1572868
  44.1 5.7 %collective-permute-start.8 = (bf16[128,2048]{1,0:T(8,128)(2,1)S(1)}, bf16[128,2048]{1,0:T(8,128)(2,1)S(1)}, u32[]{:S(2)}, u32[]{:S(2)}) collective-permute-start(bf16[128,2048]{1,0:T(8,128)(2,1)S(1)} %collective-permute-done.4.refs_4_), channel_id=1, source_target_pairs={{0,4},{4,0},{8,12},{12,8},{16,20},{20,16},{24,28},{28,24},{32,36},... | collective-permute-start | bytes 1572872 | tf_op jit(solution)/shard_map/ppermute | solution.py:97
  45.6 5.8 %copy-start.4 = (bf16[128,2048]{1,0:T(8,128)(2,1)}, bf16[128,2048]{1,0:T(8,128)(2,1)S(1)}, u32[]{:S(2)}) copy-start(bf16[128,2048]{1,0:T(8,128)(2,1)S(1)} %collective-permute-done.5.refs_5_) | copy-start | bytes 1572868
  45.6 5.8 %collective-permute-start.9 = (bf16[128,2048]{1,0:T(8,128)(2,1)S(1)}, bf16[128,2048]{1,0:T(8,128)(2,1)}, u32[]{:S(2)}, u32[]{:S(2)}) collective-permute-start(bf16[128,2048]{1,0:T(8,128)(2,1)S(1)} %collective-permute-done.5.refs_5_), channel_id=1, source_target_pairs={{0,4},{4,0},{8,12},{12,8},{16,20},{20,16},{24,28},{28,24},{32,36},... | collective-permute-start | bytes 1572872 | tf_op jit(solution)/shard_map/ppermute | solution.py:97
  48.4 3.0 %copy-start = (bf16[128,256]{1,0:T(8,128)(2,1)}, bf16[128,256]{1,0:T(8,128)(2,1)S(1)}, u32[]{:S(2)}) copy-start(bf16[128,256]{1,0:T(8,128)(2,1)S(1)} %get-tuple-element.38.refs_0_) | copy-start | bytes 196612
  48.4 1.4 %collective-permute-start.2 = (bf16[128,256]{1,0:T(8,128)(2,1)S(1)}, bf16[128,256]{1,0:T(8,128)(2,1)S(1)}, u32[]{:S(2)}, u32[]{:S(2)}) collective-permute-start(bf16[128,256]{1,0:T(8,128)(2,1)S(1)} %get-tuple-element.38.refs_0_), channel_id=1, source_target_pairs={{0,4},{4,0},{8,12},{12,8},{16,20},{20,16},{24,28},{28,24},{32,36},... | collective-permute-start | bytes 196616 | tf_op jit(solution)/shard_map/ppermute | solution.py:97
  49.5 2.0 %copy-start.12 = (bf16[128,2048]{1,0:T(8,128)(2,1)}, bf16[128,2048]{1,0:T(8,128)(2,1)S(1)}, u32[]{:S(2)}) copy-start(bf16[128,2048]{1,0:T(8,128)(2,1)S(1)} %collective-permute-done.6.refs_6_) | copy-start | bytes 1572868
  55.9 6.8 %copy-start.6 = (bf16[128,2048]{1,0:T(8,128)(2,1)S(1)}, bf16[128,2048]{1,0:T(8,128)(2,1)}, u32[]{:S(2)}) copy-start(bf16[128,2048]{1,0:T(8,128)(2,1)} %copy-done.5) | copy-start | bytes 1572868
  55.9 47.4 %collective-permute-start.20 = (bf16[8,256,128]{2,1,0:T(8,128)(2,1)}, bf16[8,256,128]{2,1,0:T(8,128)(2,1)S(1)}, u32[]{:S(2)}, u32[]{:S(2)}) collective-permute-start(bf16[8,256,128]{2,1,0:T(8,128)(2,1)} %get-tuple-element.37), channel_id=1, source_target_pairs={{0,192},{4,196},{8,200},{12,204},{16,208},{20,212},{24,216},{28,22... | collective-permute-start | bytes 1572872 | tf_op jit(solution)/shard_map/ppermute | solution.py:104
  58.4 45.4 %collective-permute-start.19 = (bf16[8,256,128]{2,1,0:T(8,128)(2,1)}, bf16[8,256,128]{2,1,0:T(8,128)(2,1)S(1)}, u32[]{:S(2)}, u32[]{:S(2)}) collective-permute-start(bf16[8,256,128]{2,1,0:T(8,128)(2,1)} %get-tuple-element.36), channel_id=1, source_target_pairs={{0,128},{4,132},{8,136},{12,140},{16,144},{20,148},{24,152},{28,15... | collective-permute-start | bytes 1572872 | tf_op jit(solution)/shard_map/ppermute | solution.py:104
  60.8 3.7 %copy-start.3 = (bf16[128,2048]{1,0:T(8,128)(2,1)S(1)}, bf16[128,2048]{1,0:T(8,128)(2,1)}, u32[]{:S(2)}) copy-start(bf16[128,2048]{1,0:T(8,128)(2,1)} %copy-done.2) | copy-start | bytes 1572868
  66.2 3.6 %copy-start.20 = (f32[16,256]{1,0:T(8,128)S(1)}, f32[16,256]{1,0:T(8,128)}, u32[]{:S(2)}) copy-start(f32[16,256]{1,0:T(8,128)} %get-tuple-element.45) | copy-start | bytes 49156
  66.2 4.7 %copy-start.1 = (bf16[128,256]{1,0:T(8,128)(2,1)S(1)}, bf16[128,256]{1,0:T(8,128)(2,1)}, u32[]{:S(2)}) copy-start(bf16[128,256]{1,0:T(8,128)(2,1)} %copy-done) | copy-start | bytes 196612
  68.7 19.8 %copy-start.22 = (f32[8]{0:T(128)S(1)}, f32[8]{0:T(128)}, u32[]{:S(2)}) copy-start(f32[8]{0:T(128)} %get-tuple-element.87) | copy-start | bytes 100
  68.7 19.8 %copy-start.23 = (f32[8]{0:T(128)S(1)}, f32[8]{0:T(128)}, u32[]{:S(2)}) copy-start(f32[8]{0:T(128)} %get-tuple-element.88) | copy-start | bytes 100
  68.7 19.8 %copy-start.24 = (pred[8]{0:T(512)(128)(4,1)S(1)}, pred[8]{0:T(512)(128)(4,1)}, u32[]{:S(2)}) copy-start(pred[8]{0:T(512)(128)(4,1)} %iota_compare_fusion) | copy-start | bytes 28
  69.9 3.3 %collective-permute-start.13 = (f32[49,256]{1,0:T(8,128)S(1)}, f32[49,256]{1,0:T(8,128)S(1)}, u32[]{:S(2)}, u32[]{:S(2)}) collective-permute-start(f32[49,256]{1,0:T(8,128)S(1)} %pad_maximum_fusion), channel_id=1, source_target_pairs={{0,4},{4,0},{8,12},{12,8},{16,20},{20,16},{24,28},{28,24},{32,36},... | collective-permute-start | bytes 150536 | tf_op jit(solution)/shard_map/ppermute | solution.py:97
  73.9 14.5 %all-to-all-start.1 = ((bf16[8,49,128]{2,1,0:T(8,128)(2,1)}), bf16[8,49,128]{2,1,0:T(8,128)(2,1)S(1)}, u32[]{:S(2)}, u32[]{:S(2)}) async-start(bf16[8,49,128]{2,1,0:T(8,128)(2,1)} %broadcast_in_dim.86), calls=%async_computation.1 | async-start | bytes 229376 | tf_op jit(solution)/shard_map/all_to_all | solution.py:110
  80.6 27.6 %copy-start.13 = (bf16[8,256,128]{2,1,0:T(8,128)(2,1)S(1)}, bf16[8,256,128]{2,1,0:T(8,128)(2,1)}, u32[]{:S(2)}) copy-start(bf16[8,256,128]{2,1,0:T(8,128)(2,1)} %get-tuple-element.34) | copy-start | bytes 1572868
  88.6 7.0 %collective-permute-start.16 = (f32[49,128]{1,0:T(8,128)S(1)}, f32[49,128]{1,0:T(8,128)S(1)}, u32[]{:S(2)}, u32[]{:S(2)}) collective-permute-start(f32[49,128]{1,0:T(8,128)S(1)} %pad_maximum_fusion.2), channel_id=1, source_target_pairs={{0,64},{4,68},{8,72},{12,76},{16,80},{20,84},{24,88},{28,92},{32,9... | collective-permute-start | bytes 75272 | tf_op jit(solution)/shard_map/ppermute | solution.py:104
  89.3 6.3 %collective-permute-start.15 = (f32[49,128]{1,0:T(8,128)S(1)}, f32[49,128]{1,0:T(8,128)S(1)}, u32[]{:S(2)}, u32[]{:S(2)}) collective-permute-start(f32[49,128]{1,0:T(8,128)S(1)} %pad_maximum_fusion.2), channel_id=1, source_target_pairs={{0,128},{4,132},{8,136},{12,140},{16,144},{20,148},{24,152},{28,15... | collective-permute-start | bytes 75272 | tf_op jit(solution)/shard_map/ppermute | solution.py:104
  91.3 6.0 %collective-permute-start.14 = (f32[49,128]{1,0:T(8,128)S(1)}, f32[49,128]{1,0:T(8,128)S(1)}, u32[]{:S(2)}, u32[]{:S(2)}) collective-permute-start(f32[49,128]{1,0:T(8,128)S(1)} %pad_maximum_fusion.2), channel_id=1, source_target_pairs={{0,192},{4,196},{8,200},{12,204},{16,208},{20,212},{24,216},{28,22... | collective-permute-start | bytes 75272 | tf_op jit(solution)/shard_map/ppermute | solution.py:104
  95.6 12.7 %collective-permute-start.18 = (bf16[8,256,128]{2,1,0:T(8,128)(2,1)}, bf16[8,256,128]{2,1,0:T(8,128)(2,1)S(1)}, u32[]{:S(2)}, u32[]{:S(2)}) collective-permute-start(bf16[8,256,128]{2,1,0:T(8,128)(2,1)} %get-tuple-element.35), channel_id=1, source_target_pairs={{0,64},{4,68},{8,72},{12,76},{16,80},{20,84},{24,88},{28,92},{32,9... | collective-permute-start | bytes 1572872 | tf_op jit(solution)/shard_map/ppermute | solution.py:104
  95.6 19.9 %collective-permute-start.12 = (bf16[128,2048]{1,0:T(8,128)(2,1)}, bf16[128,2048]{1,0:T(8,128)(2,1)}, u32[]{:S(2)}, u32[]{:S(2)}) collective-permute-start(bf16[128,2048]{1,0:T(8,128)(2,1)} %convolution_convert_fusion), channel_id=1, source_target_pairs={{0,3},{1,0},{2,1},{3,2},{4,7},{5,4},{6,5},{7,6},{8,11},{9,8},{10,9... | collective-permute-start | bytes 1572872 | tf_op jit(solution)/shard_map/ppermute | solution.py:100
  97.4 5.1 %collective-permute-start.17 = (f32[49,128]{1,0:T(8,128)S(1)}, f32[49,128]{1,0:T(8,128)S(1)}, u32[]{:S(2)}, u32[]{:S(2)}) collective-permute-start(f32[49,128]{1,0:T(8,128)S(1)} %pad_maximum_fusion.3), channel_id=1, source_target_pairs={{0,4},{4,0},{8,12},{12,8},{16,20},{20,16},{24,28},{28,24},{32,36},... | collective-permute-start | bytes 75272 | tf_op jit(solution)/shard_map/ppermute | solution.py:97
  102.4 11.6 %copy-start.26 = (f32[128]{0:T(128)S(1)}, f32[128]{0:T(128)}, u32[]{:S(2)}) copy-start(f32[128]{0:T(128)} %copy-done.25) | copy-start | bytes 1540
  102.4 15.3 %collective-permute-start.11 = (bf16[128,2048]{1,0:T(8,128)(2,1)}, bf16[128,2048]{1,0:T(8,128)(2,1)}, u32[]{:S(2)}, u32[]{:S(2)}) collective-permute-start(bf16[128,2048]{1,0:T(8,128)(2,1)} %convolution_convert_fusion.1), channel_id=1, source_target_pairs={{0,2},{1,3},{2,0},{3,1},{4,6},{5,7},{6,4},{7,5},{8,10},{9,11},{10,... | collective-permute-start | bytes 1572872 | tf_op jit(solution)/shard_map/ppermute | solution.py:100
  103.3 26.1 %collective-permute-start.10 = (bf16[128,2048]{1,0:T(8,128)(2,1)}, bf16[128,2048]{1,0:T(8,128)(2,1)}, u32[]{:S(2)}, u32[]{:S(2)}) collective-permute-start(bf16[128,2048]{1,0:T(8,128)(2,1)} %convolution_convert_fusion.2), channel_id=1, source_target_pairs={{0,1},{1,2},{2,3},{3,0},{4,5},{5,6},{6,7},{7,4},{8,9},{9,10},{10,1... | collective-permute-start | bytes 1572872 | tf_op jit(solution)/shard_map/ppermute | solution.py:100
  109.3 22.9 %all-to-all-start.2 = ((bf16[8,256,128]{2,1,0:T(8,128)(2,1)}), bf16[8,256,128]{2,1,0:T(8,128)(2,1)S(1)}, u32[]{:S(2)}, u32[]{:S(2)}) async-start(bf16[8,256,128]{2,1,0:T(8,128)(2,1)} %add_convert_fusion), calls=%async_computation.2 | async-start | bytes 1048576 | tf_op jit(solution)/shard_map/all_to_all | solution.py:274
  (3 other events, 3.3 us)

commit v4 on v3

--- a/solution.py
+++ b/solution.py
@@ -51,29 +51,88 @@
     def kernel(turns_ref, *refs):
         mine_ref, other_ref = refs[:2]
         block_refs, taken_refs = refs[2 : 2 + count], refs[2 + count : 2 + 2 * count]
-        out_refs, all_ref = refs[2 + 2 * count : -1], refs[-1]
+        out_refs = refs[2 + 2 * count : 2 + 3 * count]
+        all_ref, part_ref, in_sems, out_sems = refs[2 + 3 * count :]
         core = turns_ref[0]
         for k in range(count):
             for i in range(tiles):
                 at = pl.multiple_of((2 * i + core) * width, width)
-                lanes = slice(i * width, (i + 1) * width)
-                all_ref[k, :tokens, lanes] = block_refs[k][:, pl.ds(at, width)]
-                all_ref[k, tokens:, lanes] = taken_refs[k][:, pl.ds(at, width)]
+                lanes = pl.ds(i * width, width)
+                for half, source in enumerate((block_refs[k], taken_refs[k])):
+                    pltpu.make_async_copy(
+                        source.at[:, pl.ds(at, width)],
+                        all_ref.at[k, pl.ds(half * tokens, tokens), lanes],
+                        in_sems.at[k],
+                    ).start()
         left = jnp.concatenate([mine_ref[...], other_ref[...]], 0).T
+        for k in range(count):
+            pltpu.make_async_copy(all_ref.at[k], all_ref.at[k], in_sems.at[k]).wait()
         for s in range(count):
             part = jnp.dot(
                 left, all_ref[(turns_ref[1] - s + count) % count], preferred_element_type=F32
             ).astype(BF16)
             for i in range(tiles):
-                out_refs[s][i] = part[:, i * width : (i + 1) * width]
+                part_ref[s, i] = part[:, i * width : (i + 1) * width]
+            pltpu.make_async_copy(part_ref.at[s], out_refs[s], out_sems.at[s]).start()
+        for s in range(count):
+            pltpu.make_async_copy(part_ref.at[s], out_refs[s], out_sems.at[s]).wait()
 
     return pl.pallas_call(
         kernel,
         out_shape=[jax.ShapeDtypeStruct((tiles, chans, width), BF16)] * count,
-        in_specs=[pl.BlockSpec(memory_space=pltpu.SMEM)] + in_vmem(2 + 2 * count),
-        out_specs=in_vmem(count),
-        scratch_shapes=[pltpu.VMEM((count, 2 * tokens, tiles * width), BF16)],
+        in_specs=[pl.BlockSpec(memory_space=pltpu.SMEM)]
+        + in_vmem(2)
+        + [pl.BlockSpec(memory_space=pl.ANY)] * (2 * count),
+        out_specs=[pl.BlockSpec(memory_space=pl.ANY)] * count,
+        scratch_shapes=[
+            pltpu.VMEM((count, 2 * tokens, tiles * width), BF16),
+            pltpu.VMEM((count, tiles, chans, width), BF16),
+            pltpu.SemaphoreType.DMA((count,)),
+            pltpu.SemaphoreType.DMA((count,)),
+        ],
     )(turns, result, result_other, *blocks, *taken)
+
+
+def projections(turns, result, blocks, weight):
+    count = len(blocks)
+    tokens, feats = blocks[0].shape
+    chans = result.shape[1]
+
+    def kernel(turns_ref, result_ref, *refs):
+        block_refs, weight_ref = refs[:count], refs[count]
+        grad_ref, piece_refs = refs[count + 1], refs[count + 2 :]
+        for j in range(count):
+
+            @pl.when(pl.program_id(0) == j)
+            def _():
+                w = weight_ref[...]
+                piece_refs[j][...] = jnp.dot(
+                    result_ref[...], w, preferred_element_type=F32
+                ).astype(BF16)
+                term = lax.dot_general(
+                    block_refs[-j % count][...],
+                    w,
+                    (((1,), (1,)), ((), ())),
+                    preferred_element_type=F32,
+                )
+                grad_ref[...] = term if j == 0 else grad_ref[...] + term
+
+    def whole(shape):
+        return pl.BlockSpec(shape, lambda j, turns_ref: (0, 0))
+
+    return pl.pallas_call(
+        kernel,
+        out_shape=[jax.ShapeDtypeStruct((tokens, chans), F32)]
+        + [jax.ShapeDtypeStruct((tokens, feats), BF16)] * count,
+        grid_spec=pltpu.PrefetchScalarGridSpec(
+            num_scalar_prefetch=1,
+            grid=(count,),
+            in_specs=[whole((tokens, chans))]
+            + [whole((tokens, feats))] * count
+            + [pl.BlockSpec((chans, feats), lambda j, turns_ref: (0, (turns_ref[2] + j) % count))],
+            out_specs=[whole((tokens, chans))] + [whole((tokens, feats))] * count,
+        ),
+    )(turns, result, *blocks, weight)
 
 
 def body(outer_gate, inner_gate, values, residues, log_decay, skip_gain, out_weight, out_grad):
@@ -186,33 +245,22 @@
     gated = conv_out + skip_gain[None, :] * u
     result = row_major((outer_f * gated).astype(BF16))
 
-    turns = jnp.stack([core, (tp - yy) % tps]).astype(jnp.int32)
+    turns = jnp.stack([core, (tp - yy) % tps, tp]).astype(jnp.int32)
     taken = [row_major(swap_core(a)) for a in og]
     result_other = swap_core(result)
     y_parts = weight_parts(turns, result, result_other, og, taken, width)
     over_y = [y_parts[0]] + [shift_y(y_parts[s], s) for s in range(1, ny)]
     summed_y = sum(a.astype(F32) for a in over_y).astype(BF16)
 
-    late = lax.optimization_barrier((result, gated, out_weight, *y_parts))
-    result, gated, out_weight = late[:3]
-
-    def projected(k):
-        w_block = lax.dynamic_slice_in_dim(out_weight, (tp + k) % tps * feats, feats, 1)
-        return jnp.dot(result, w_block, preferred_element_type=F32).astype(BF16)
-
-    mixed = projected(0).astype(F32)
+    late = lax.optimization_barrier((result, gated, *y_parts))
+    result, gated = late[:2]
+    grad_gated, *pieces = projections(turns, result, og, out_weight)
+    mixed = pieces[0].astype(F32)
     for k in range(1, tps):
-        piece = projected(k)
-        piece = shift_tp(piece, k)
+        piece = shift_tp(pieces[k], k)
         mixed = mixed + piece.astype(F32)
     mixed = mixed.astype(BF16)
 
-    grad_gated = 0.0
-    for k in range(tps):
-        w_block = lax.dynamic_slice_in_dim(out_weight, (tp - k) % tps * feats, feats, 1)
-        grad_gated = grad_gated + lax.dot_general(
-            og[k], w_block, (((1,), (1,)), ((), ())), preferred_element_type=F32
-        )
     late = lax.optimization_barrier(
         (outer_gate, inner_gate, values, residues, log_decay, grad_gated, *y_parts)
     )

time: 134 us -> 138 us (1.030)
  the two profiles are of different devices: /device:TPU:1 before, /device:TPU:2 now
where the time goes in v4:
time: 138 us; the launch traced here: 136 us
  waiting for transfers between devices  60.8 us (44%)
  starting transfers between devices  41.6 us (30%)
  other arithmetic  13.3 us (10%)
  Pallas kernels  11.4 us (8%)
  matrix products  4.3 us (3%)
  local copies, waits for them, and re-layouts  3.19 us (2%)
    ppermute x6, waiting for transfers between devices, shift_y(): lax.ppermute(a, 'ctx', [(i, (i // per + k) % ny * per + i % per) for i in...  15.4 us
    ppermute x6, waiting for transfers between devices, shift_tp(): return lax.ppermute(a, 'tp', [(i, (i + k) % tps) for i in range(tps)])  15.3 us
    all_to_all x1, starting transfers between devices, of_pairs(): lax.all_to_all(copies, 'ctx', 0, 0, tiled=True, axis_index_groups=groups)  11.6 us
    all_to_all x1, waiting for transfers between devices, body(): lax.all_to_all(summed_y, 'ctx', 0, 0, tiled=True, axis_index_groups=z_gro...  10.7 us
    all_to_all x1, waiting for transfers between devices, of_plane(): lax.all_to_all(copies, 'ctx', 0, 0, tiled=True, axis_index_groups=z_groups)  9.21 us
    ppermute x6, starting transfers between devices, shift_y(): lax.ppermute(a, 'ctx', [(i, (i // per + k) % ny * per + i % per) for i in...  8.99 us
    ppermute x6, starting transfers between devices, shift_tp(): return lax.ppermute(a, 'tp', [(i, (i + k) % tps) for i in range(tps)])  8.75 us
    all_to_all x1, waiting for transfers between devices, of_pairs(): lax.all_to_all(copies, 'ctx', 0, 0, tiled=True, axis_index_groups=groups)  7.83 us
  transfers between devices with their start and end apart: 24, of which 12 were waited for; matrix products, arithmetic and copies ran while one was open for 7% of the time, Pallas kernels for 0%

profile of v4, /device:TPU:2, one launch (start us, length us, event | category | flops | bytes accessed | tf_op | source)
XLA Modules:
  0.0 135.8 jit_solution(1349768465438419938)
XLA Ops:
  0.7 0.8 fusion.90
  1.5 0.9 convert_multiply_fusion.5
  2.4 0.7 fusion.4
  3.2 1.2 collective-permute-done
  4.5 0.7 broadcast_in_dim.49
  5.2 11.6 %all-to-all-start = ((bf16[32,32,128]{2,1,0:T(8,128)(2,1)}), bf16[32,32,128]{2,1,0:T(8,128)(2,1)S(1)}, u32[]{:S(2)}, u32[]{:S(2)}) async-start(bf16[32,32,128]{2,1,0:T(8,128)(2,1)} %broadcast_in_dim.49), calls=%async_computation | async-start | bytes 524288 | tf_op jit(solution)/shard_map/all_to_all | solution.py:174
  16.8 1.6 %collective-permute-start.3 = (bf16[128,2048]{1,0:T(8,128)(2,1)S(1)}, bf16[128,2048]{1,0:T(8,128)(2,1)S(1)}, u32[]{:S(2)}, u32[]{:S(2)}) collective-permute-start(bf16[128,2048]{1,0:T(8,128)(2,1)S(1)} %copy-done), channel_id=1, source_target_pairs={{0,1},{1,2},{2,3},{3,0},{4,5},{5,6},{6,7},{7,4},{8,9},{9,10},{10,1... | collective-permute-start | bytes 1572872 | tf_op jit(solution)/shard_map/ppermute | solution.py:159
  18.4 1.1 collective-permute-start.4
  19.5 2.2 %collective-permute-start.5 = (bf16[128,2048]{1,0:T(8,128)(2,1)S(1)}, bf16[128,2048]{1,0:T(8,128)(2,1)S(1)}, u32[]{:S(2)}, u32[]{:S(2)}) collective-permute-start(bf16[128,2048]{1,0:T(8,128)(2,1)S(1)} %copy-done), channel_id=1, source_target_pairs={{0,3},{1,0},{2,1},{3,2},{4,7},{5,4},{6,5},{7,6},{8,11},{9,8},{10,9... | collective-permute-start | bytes 1572872 | tf_op jit(solution)/shard_map/ppermute | solution.py:159
  21.7 7.8 %all-to-all-done = bf16[32,32,128]{2,1,0:T(8,128)(2,1)S(1)} async-done(((bf16[32,32,128]{2,1,0:T(8,128)(2,1)}), bf16[32,32,128]{2,1,0:T(8,128)(2,1)S(1)}, u32[]{:S(2)}, u32[]{:S(2)}) %all-to-all-start) | async-done | bytes 262176 | tf_op jit(solution)/shard_map/all_to_all | solution.py:174
  30.4 1.3 collective-permute-done.3.refs_3_.refs_1_
  31.7 3.0 %collective-permute-done.4.refs_4_.refs_2_ = bf16[128,2048]{1,0:T(8,128)(2,1)S(1)} collective-permute-done((bf16[128,2048]{1,0:T(8,128)(2,1)S(1)}, bf16[128,2048]{1,0:T(8,128)(2,1)S(1)}, u32[]{:S(2)}, u32[]{:S(2)}) %collective-permute-start.4) | collective-permute-done | bytes 524320 | tf_op jit(solution)/shard_map/ppermute | solution.py:159
  34.7 9.2 %collective-permute-done.5.refs_5_.refs_3_ = bf16[128,2048]{1,0:T(8,128)(2,1)S(1)} collective-permute-done((bf16[128,2048]{1,0:T(8,128)(2,1)S(1)}, bf16[128,2048]{1,0:T(8,128)(2,1)S(1)}, u32[]{:S(2)}, u32[]{:S(2)}) %collective-permute-start.5) | collective-permute-done | bytes 524320 | tf_op jit(solution)/shard_map/ppermute | solution.py:159
  43.9 0.7 fusion.73
  46.7 0.7 collective-permute-start.2
  47.4 0.6 pad_add_fusion.turns_ref
  48.3 0.8 copy-done.12
  49.1 0.8 copy-done.13
  49.9 4.1 %shard_map.161 = (bf16[8,256,128]{2,1,0:T(8,128)(2,1)}, bf16[8,256,128]{2,1,0:T(8,128)(2,1)}, bf16[8,256,128]{2,1,0:T(8,128)(2,1)}, bf16[8,256,128]{2,1,0:T(8,128)(2,1)}) custom-call(s32[3]{0:T(128)} %pad_add_fusion.turns_ref, bf16[128,256]{1,0:T(8,128)(2,1)} %copy-done.9, bf16[128,256]{1,0:T(8,128)(2,1)} %copy-done.16, bf16[128,2048]{1,0:T(8,128)(2,1)} %refs_0_.1, ...), custom_call_target="tpu_custom_call" | custom-call | tf_op jit(solution)/shard_map/pallas_call | solution.py:80
  54.1 7.3 %shard_map.162 = (f32[128,256]{1,0:T(8,128)}, bf16[128,2048]{1,0:T(8,128)(2,1)}, bf16[128,2048]{1,0:T(8,128)(2,1)}, bf16[128,2048]{1,0:T(8,128)(2,1)}, bf16[128,2048]{1,0:T(8,128)(2,1)}) custom-call(s32[3]{0:T(128)} %pad_add_fusion.turns_ref, bf16[128,256]{1,0:T(8,128)(2,1)} %copy-done.9, bf16[128,2048]{1,0:T(8,128)(2,1)} %refs_0_.1, ...), custom_call_target="tpu_custom_call" | custom-call | tf_op jit(solution)/shard_map/pallas_call | solution.py:123
  61.3 1.6 %fusion.37 = (f32[256]{0:T(256)S(1)}, f32[128,256]{1,0:T(8,128)S(1)}, bf16[128,256]{1,0:T(8,128)(2,1)}) fusion(bf16[128,256]{1,0:T(8,128)(2,1)S(1)} %copy-done.4, bf16[128,256]{1,0:T(8,128)(2,1)S(1)} %copy-done.5, f32[128,256]{1,0:T(8,128)} %get-tuple-element.48, bf16[128,256]{1,0:T(8,128)(2,1)S(1)} %copy-done.15, f32[128,256]{1,0:T(8,128)S(1)} %get-tuple-element.49), kind=kLoop, calls=%fused_computation.59 | loop fusion | flops 294656 | bytes 656384 | tf_op jit(solution)/shard_map/reduce_sum | solution.py:290
  63.3 0.6 fusion.17
  63.9 0.6 fusion.5
  64.7 1.2 fusion.3
  66.3 0.9 collective-permute-done.13
  67.3 0.7 broadcast_in_dim.86
  67.9 6.7 %all-to-all-start.1 = ((bf16[8,49,128]{2,1,0:T(8,128)(2,1)}), bf16[8,49,128]{2,1,0:T(8,128)(2,1)S(1)}, u32[]{:S(2)}, u32[]{:S(2)}) async-start(bf16[8,49,128]{2,1,0:T(8,128)(2,1)} %broadcast_in_dim.86), calls=%async_computation.1 | async-start | bytes 229376 | tf_op jit(solution)/shard_map/all_to_all | solution.py:169
  74.7 9.2 %all-to-all-done.1 = bf16[8,49,128]{2,1,0:T(8,128)(2,1)S(1)} async-done(((bf16[8,49,128]{2,1,0:T(8,128)(2,1)}), bf16[8,49,128]{2,1,0:T(8,128)(2,1)S(1)}, u32[]{:S(2)}, u32[]{:S(2)}) %all-to-all-start.1) | async-done | bytes 100384 | tf_op jit(solution)/shard_map/all_to_all | solution.py:169
  84.1 2.8 %collective-permute-start.14 = (f32[49,128]{1,0:T(8,128)S(1)}, f32[49,128]{1,0:T(8,128)S(1)}, u32[]{:S(2)}, u32[]{:S(2)}) collective-permute-start(f32[49,128]{1,0:T(8,128)S(1)} %pad_maximum_fusion.2), channel_id=1, source_target_pairs={{0,192},{4,196},{8,200},{12,204},{16,208},{20,212},{24,216},{28,22... | collective-permute-start | bytes 75272 | tf_op jit(solution)/shard_map/ppermute | solution.py:163
  86.9 0.8 collective-permute-start.15
  87.7 0.9 collective-permute-start.16
  88.5 1.8 %collective-permute-start.18 = (bf16[8,256,128]{2,1,0:T(8,128)(2,1)}, bf16[8,256,128]{2,1,0:T(8,128)(2,1)S(1)}, u32[]{:S(2)}, u32[]{:S(2)}) collective-permute-start(bf16[8,256,128]{2,1,0:T(8,128)(2,1)} %get-tuple-element.39), channel_id=1, source_target_pairs={{0,64},{4,68},{8,72},{12,76},{16,80},{20,84},{24,88},{28,92},{32,9... | collective-permute-start | bytes 1572872 | tf_op jit(solution)/shard_map/ppermute | solution.py:163
  90.3 2.0 %collective-permute-start.19 = (bf16[8,256,128]{2,1,0:T(8,128)(2,1)}, bf16[8,256,128]{2,1,0:T(8,128)(2,1)S(1)}, u32[]{:S(2)}, u32[]{:S(2)}) collective-permute-start(bf16[8,256,128]{2,1,0:T(8,128)(2,1)} %get-tuple-element.40), channel_id=1, source_target_pairs={{0,128},{4,132},{8,136},{12,140},{16,144},{20,148},{24,152},{28,15... | collective-permute-start | bytes 1572872 | tf_op jit(solution)/shard_map/ppermute | solution.py:163
  92.4 0.7 collective-permute-start.20
  93.6 1.4 %collective-permute-start.10 = (bf16[128,2048]{1,0:T(8,128)(2,1)}, bf16[128,2048]{1,0:T(8,128)(2,1)S(1)}, u32[]{:S(2)}, u32[]{:S(2)}) collective-permute-start(bf16[128,2048]{1,0:T(8,128)(2,1)} %get-tuple-element.44), channel_id=1, source_target_pairs={{0,1},{1,2},{2,3},{3,0},{4,5},{5,6},{6,7},{7,4},{8,9},{9,10},{10,1... | collective-permute-start | bytes 1572872 | tf_op jit(solution)/shard_map/ppermute | solution.py:159
  94.9 1.6 %collective-permute-start.11 = (bf16[128,2048]{1,0:T(8,128)(2,1)}, bf16[128,2048]{1,0:T(8,128)(2,1)}, u32[]{:S(2)}, u32[]{:S(2)}) collective-permute-start(bf16[128,2048]{1,0:T(8,128)(2,1)} %get-tuple-element.45), channel_id=1, source_target_pairs={{0,2},{1,3},{2,0},{3,1},{4,6},{5,7},{6,4},{7,5},{8,10},{9,11},{10,... | collective-permute-start | bytes 1572872 | tf_op jit(solution)/shard_map/ppermute | solution.py:159
  96.6 0.6 fusion.88
  97.2 0.6 fusion.72
  97.8 6.3 %collective-permute-done.18 = bf16[8,256,128]{2,1,0:T(8,128)(2,1)S(1)} collective-permute-done((bf16[8,256,128]{2,1,0:T(8,128)(2,1)}, bf16[8,256,128]{2,1,0:T(8,128)(2,1)S(1)}, u32[]{:S(2)}, u32[]{:S(2)}) %collective-permute-start.18) | collective-permute-done | bytes 524320 | tf_op jit(solution)/shard_map/ppermute | solution.py:163
  104.1 0.9 collective-permute-start.12
  105.0 9.1 %collective-permute-done.19 = bf16[8,256,128]{2,1,0:T(8,128)(2,1)S(1)} collective-permute-done((bf16[8,256,128]{2,1,0:T(8,128)(2,1)}, bf16[8,256,128]{2,1,0:T(8,128)(2,1)S(1)}, u32[]{:S(2)}, u32[]{:S(2)}) %collective-permute-start.19) | collective-permute-done | bytes 524320 | tf_op jit(solution)/shard_map/ppermute | solution.py:163
  114.1 1.1 add_convert_fusion
  115.2 3.6 %all-to-all-start.2 = ((bf16[8,256,128]{2,1,0:T(8,128)(2,1)}), bf16[8,256,128]{2,1,0:T(8,128)(2,1)S(1)}, u32[]{:S(2)}, u32[]{:S(2)}) async-start(bf16[8,256,128]{2,1,0:T(8,128)(2,1)} %add_convert_fusion), calls=%async_computation.2 | async-start | bytes 1048576 | tf_op jit(solution)/shard_map/all_to_all | solution.py:322
  119.3 1.0 fusion.35
  120.3 1.8 %collective-permute-done.12 = bf16[128,2048]{1,0:T(8,128)(2,1)} collective-permute-done((bf16[128,2048]{1,0:T(8,128)(2,1)S(1)}, bf16[128,2048]{1,0:T(8,128)(2,1)}, u32[]{:S(2)}, u32[]{:S(2)}) %collective-permute-start.12) | collective-permute-done | bytes 524320 | tf_op jit(solution)/shard_map/ppermute | solution.py:159
  122.0 2.3 %add_convert_fusion.1 = bf16[128,2048]{1,0:T(8,128)(2,1)} fusion(bf16[128,2048]{1,0:T(8,128)(2,1)} %collective-permute-done.12, bf16[128,2048]{1,0:T(8,128)(2,1)} %collective-permute-done.11, bf16[128,2048]{1,0:T(8,128)(2,1)S(1)} %collective-permute-done.10, bf16[128,2048]{1,0:T(8,128)(2,1)S(1)} %copy-done.10), kind=kLoop, calls=%fused_computation.26 | loop fusion | flops 2097152 | bytes 2621440 | tf_op jit(solution)/shard_map/convert_element_type | solution.py:262
  124.4 10.7 %all-to-all-done.2 = bf16[8,256,128]{2,1,0:T(8,128)(2,1)S(1)} async-done(((bf16[8,256,128]{2,1,0:T(8,128)(2,1)}), bf16[8,256,128]{2,1,0:T(8,128)(2,1)S(1)}, u32[]{:S(2)}, u32[]{:S(2)}) %all-to-all-start.2) | async-done | bytes 524320 | tf_op jit(solution)/shard_map/all_to_all | solution.py:322
  135.0 0.7 convert_reduce_fusion
  (105 shorter events, 5.4 us)
Async XLA Ops:
  0.6 43.3 %copy-start.14 = (f32[16,256]{1,0:T(8,128)S(1)}, f32[16,256]{1,0:T(8,128)}, u32[]{:S(2)}) copy-start(f32[16,256]{1,0:T(8,128)} %param.14) | copy-start | bytes 49156
  0.6 16.2 %copy-start = (bf16[128,2048]{1,0:T(8,128)(2,1)S(1)}, bf16[128,2048]{1,0:T(8,128)(2,1)}, u32[]{:S(2)}) copy-start(bf16[128,2048]{1,0:T(8,128)(2,1)} %refs_0_.1) | copy-start | bytes 1572868
  0.7 44.0 %copy-start.17 = (f32[16,256]{1,0:T(8,128)S(1)}, f32[16,256]{1,0:T(8,128)}, u32[]{:S(2)}) copy-start(f32[16,256]{1,0:T(8,128)} %param.13) | copy-start | bytes 49156
  3.0 42.2 %copy-start.6 = (f32[258,128]{1,0:T(8,128)S(1)}, f32[258,128]{1,0:T(8,128)}, u32[]{:S(2)}) copy-start(f32[258,128]{1,0:T(8,128)} %constant.96.clone) | copy-start | bytes 396292
  3.1 1.3 collective-permute-start
  4.4 41.2 %copy-start.4 = (bf16[128,256]{1,0:T(8,128)(2,1)S(1)}, bf16[128,256]{1,0:T(8,128)(2,1)}, u32[]{:S(2)}) copy-start(bf16[128,256]{1,0:T(8,128)(2,1)} %param.12) | copy-start | bytes 196612
  4.4 41.2 %copy-start.5 = (bf16[128,256]{1,0:T(8,128)(2,1)S(1)}, bf16[128,256]{1,0:T(8,128)(2,1)}, u32[]{:S(2)}) copy-start(bf16[128,256]{1,0:T(8,128)(2,1)} %param.11) | copy-start | bytes 196612
  5.2 40.8 %copy-start.8 = (f32[128,129]{1,0:T(8,128)S(1)}, f32[128,129]{1,0:T(8,128)}, u32[]{:S(2)}) copy-start(f32[128,129]{1,0:T(8,128)} %constant.98) | copy-start | bytes 198148
  5.2 24.4 %all-to-all-start = ((bf16[32,32,128]{2,1,0:T(8,128)(2,1)}), bf16[32,32,128]{2,1,0:T(8,128)(2,1)S(1)}, u32[]{:S(2)}, u32[]{:S(2)}) async-start(bf16[32,32,128]{2,1,0:T(8,128)(2,1)} %broadcast_in_dim.49), calls=%async_computation | async-start | bytes 524288 | tf_op jit(solution)/shard_map/all_to_all | solution.py:174
  16.8 14.9 %collective-permute-start.3 = (bf16[128,2048]{1,0:T(8,128)(2,1)S(1)}, bf16[128,2048]{1,0:T(8,128)(2,1)S(1)}, u32[]{:S(2)}, u32[]{:S(2)}) collective-permute-start(bf16[128,2048]{1,0:T(8,128)(2,1)S(1)} %copy-done), channel_id=1, source_target_pairs={{0,1},{1,2},{2,3},{3,0},{4,5},{5,6},{6,7},{7,4},{8,9},{9,10},{10,1... | collective-permute-start | bytes 1572872 | tf_op jit(solution)/shard_map/ppermute | solution.py:159
  18.4 16.3 %collective-permute-start.4 = (bf16[128,2048]{1,0:T(8,128)(2,1)S(1)}, bf16[128,2048]{1,0:T(8,128)(2,1)S(1)}, u32[]{:S(2)}, u32[]{:S(2)}) collective-permute-start(bf16[128,2048]{1,0:T(8,128)(2,1)S(1)} %copy-done), channel_id=1, source_target_pairs={{0,2},{1,3},{2,0},{3,1},{4,6},{5,7},{6,4},{7,5},{8,10},{9,11},{10,... | collective-permute-start | bytes 1572872 | tf_op jit(solution)/shard_map/ppermute | solution.py:159
  19.5 24.4 %collective-permute-start.5 = (bf16[128,2048]{1,0:T(8,128)(2,1)S(1)}, bf16[128,2048]{1,0:T(8,128)(2,1)S(1)}, u32[]{:S(2)}, u32[]{:S(2)}) collective-permute-start(bf16[128,2048]{1,0:T(8,128)(2,1)S(1)} %copy-done), channel_id=1, source_target_pairs={{0,3},{1,0},{2,1},{3,2},{4,7},{5,4},{6,5},{7,6},{8,11},{9,8},{10,9... | collective-permute-start | bytes 1572872 | tf_op jit(solution)/shard_map/ppermute | solution.py:159
  21.7 24.6 %copy-start.7 = (f32[128,129]{1,0:T(8,128)S(1)}, f32[128,129]{1,0:T(8,128)}, u32[]{:S(2)}) copy-start(f32[128,129]{1,0:T(8,128)} %constant.99) | copy-start | bytes 198148
  21.7 24.6 %copy-start.15 = (bf16[128,256]{1,0:T(8,128)(2,1)S(1)}, bf16[128,256]{1,0:T(8,128)(2,1)}, u32[]{:S(2)}) copy-start(bf16[128,256]{1,0:T(8,128)(2,1)} %param.10) | copy-start | bytes 196612
  21.7 24.6 %copy-start.20 = (f32[256]{0:T(256)S(1)}, f32[256]{0:T(256)}, u32[]{:S(2)}) copy-start(f32[256]{0:T(256)} %param.15) | copy-start | bytes 3076
  29.8 14.1 %collective-permute-start.1 = (f32[32,128]{1,0:T(8,128)S(1)}, f32[32,128]{1,0:T(8,128)S(1)}, u32[]{:S(2)}, u32[]{:S(2)}) collective-permute-start(f32[32,128]{1,0:T(8,128)S(1)} %pad_maximum_fusion.6), channel_id=1, source_target_pairs={{0,4},{4,0},{8,12},{12,8},{16,20},{20,16},{24,28},{28,24},{32,36},... | collective-permute-start | bytes 49160 | tf_op jit(solution)/shard_map/ppermute | solution.py:156
  29.9 18.1 %collective-permute-start.6 = (bf16[128,2048]{1,0:T(8,128)(2,1)S(1)}, bf16[128,2048]{1,0:T(8,128)(2,1)}, u32[]{:S(2)}, u32[]{:S(2)}) collective-permute-start(bf16[128,2048]{1,0:T(8,128)(2,1)S(1)} %copy-done), channel_id=1, source_target_pairs={{0,4},{4,0},{8,12},{12,8},{16,20},{20,16},{24,28},{28,24},{32,36},... | collective-permute-start | bytes 1572872 | tf_op jit(solution)/shard_map/ppermute | solution.py:156
  31.7 18.2 %copy-start.1 = (bf16[128,2048]{1,0:T(8,128)(2,1)}, bf16[128,2048]{1,0:T(8,128)(2,1)S(1)}, u32[]{:S(2)}) copy-start(bf16[128,2048]{1,0:T(8,128)(2,1)S(1)} %collective-permute-done.3.refs_3_.refs_1_) | copy-start | bytes 1572868
  31.7 16.6 %collective-permute-start.7 = (bf16[128,2048]{1,0:T(8,128)(2,1)S(1)}, bf16[128,2048]{1,0:T(8,128)(2,1)S(1)}, u32[]{:S(2)}, u32[]{:S(2)}) collective-permute-start(bf16[128,2048]{1,0:T(8,128)(2,1)S(1)} %collective-permute-done.3.refs_3_.refs_1_), channel_id=1, source_target_pairs={{0,4},{4,0},{8,12},{12,8},{16,20},{20,16},{24,28},{28,24},{32,36},... | collective-permute-start | bytes 1572872 | tf_op jit(solution)/shard_map/ppermute | solution.py:156
  34.7 15.2 %copy-start.2 = (bf16[128,2048]{1,0:T(8,128)(2,1)}, bf16[128,2048]{1,0:T(8,128)(2,1)S(1)}, u32[]{:S(2)}) copy-start(bf16[128,2048]{1,0:T(8,128)(2,1)S(1)} %collective-permute-done.4.refs_4_.refs_2_) | copy-start | bytes 1572868
  34.7 13.6 %collective-permute-start.8 = (bf16[128,2048]{1,0:T(8,128)(2,1)S(1)}, bf16[128,2048]{1,0:T(8,128)(2,1)S(1)}, u32[]{:S(2)}, u32[]{:S(2)}) collective-permute-start(bf16[128,2048]{1,0:T(8,128)(2,1)S(1)} %collective-permute-done.4.refs_4_.refs_2_), channel_id=1, source_target_pairs={{0,4},{4,0},{8,12},{12,8},{16,20},{20,16},{24,28},{28,24},{32,36},... | collective-permute-start | bytes 1572872 | tf_op jit(solution)/shard_map/ppermute | solution.py:156
  43.9 6.0 %copy-start.3 = (bf16[128,2048]{1,0:T(8,128)(2,1)}, bf16[128,2048]{1,0:T(8,128)(2,1)S(1)}, u32[]{:S(2)}) copy-start(bf16[128,2048]{1,0:T(8,128)(2,1)S(1)} %collective-permute-done.5.refs_5_.refs_3_) | copy-start | bytes 1572868
  43.9 6.0 %collective-permute-start.9 = (bf16[128,2048]{1,0:T(8,128)(2,1)S(1)}, bf16[128,2048]{1,0:T(8,128)(2,1)}, u32[]{:S(2)}, u32[]{:S(2)}) collective-permute-start(bf16[128,2048]{1,0:T(8,128)(2,1)S(1)} %collective-permute-done.5.refs_5_.refs_3_), channel_id=1, source_target_pairs={{0,4},{4,0},{8,12},{12,8},{16,20},{20,16},{24,28},{28,24},{32,36},... | collective-permute-start | bytes 1572872 | tf_op jit(solution)/shard_map/ppermute | solution.py:156
  46.7 3.2 %copy-start.9 = (bf16[128,256]{1,0:T(8,128)(2,1)}, bf16[128,256]{1,0:T(8,128)(2,1)S(1)}, u32[]{:S(2)}) copy-start(bf16[128,256]{1,0:T(8,128)(2,1)S(1)} %get-tuple-element.42.refs_0_.result_ref) | copy-start | bytes 196612
  46.7 1.6 %collective-permute-start.2 = (bf16[128,256]{1,0:T(8,128)(2,1)S(1)}, bf16[128,256]{1,0:T(8,128)(2,1)S(1)}, u32[]{:S(2)}, u32[]{:S(2)}) collective-permute-start(bf16[128,256]{1,0:T(8,128)(2,1)S(1)} %get-tuple-element.42.refs_0_.result_ref), channel_id=1, source_target_pairs={{0,4},{4,0},{8,12},{12,8},{16,20},{20,16},{24,28},{28,24},{32,36},... | collective-permute-start | bytes 196616 | tf_op jit(solution)/shard_map/ppermute | solution.py:156
  48.3 1.6 %copy-start.16 = (bf16[128,256]{1,0:T(8,128)(2,1)}, bf16[128,256]{1,0:T(8,128)(2,1)S(1)}, u32[]{:S(2)}) copy-start(bf16[128,256]{1,0:T(8,128)(2,1)S(1)} %collective-permute-done.2.refs_1_) | copy-start | bytes 196612
  48.3 0.8 copy-start.12
  49.1 0.8 copy-start.13
  61.3 4.5 %copy-start.19 = (f32[16,256]{1,0:T(8,128)S(1)}, f32[16,256]{1,0:T(8,128)}, u32[]{:S(2)}) copy-start(f32[16,256]{1,0:T(8,128)} %get-tuple-element.53) | copy-start | bytes 49156
  63.3 29.1 %copy-start.22 = (bf16[8,256,128]{2,1,0:T(8,128)(2,1)S(1)}, bf16[8,256,128]{2,1,0:T(8,128)(2,1)}, u32[]{:S(2)}) copy-start(bf16[8,256,128]{2,1,0:T(8,128)(2,1)} %get-tuple-element.41) | copy-start | bytes 1572868
  63.9 33.2 %copy-start.18 = (f32[16,256]{1,0:T(8,128)S(1)}, f32[16,256]{1,0:T(8,128)}, u32[]{:S(2)}) copy-start(f32[16,256]{1,0:T(8,128)} %param.13) | copy-start | bytes 49156
  64.6 39.5 %copy-start.21 = (bf16[128,2048]{1,0:T(8,128)(2,1)S(1)}, bf16[128,2048]{1,0:T(8,128)(2,1)}, u32[]{:S(2)}) copy-start(bf16[128,2048]{1,0:T(8,128)(2,1)} %get-tuple-element.46) | copy-start | bytes 1572868
  64.6 49.6 %copy-start.11 = (bf16[8,256,128]{2,1,0:T(8,128)(2,1)S(1)}, bf16[8,256,128]{2,1,0:T(8,128)(2,1)}, u32[]{:S(2)}) copy-start(bf16[8,256,128]{2,1,0:T(8,128)(2,1)} %get-tuple-element.38) | copy-start | bytes 1572868
  65.9 1.3 collective-permute-start.13
  67.9 15.9 %all-to-all-start.1 = ((bf16[8,49,128]{2,1,0:T(8,128)(2,1)}), bf16[8,49,128]{2,1,0:T(8,128)(2,1)S(1)}, u32[]{:S(2)}, u32[]{:S(2)}) async-start(bf16[8,49,128]{2,1,0:T(8,128)(2,1)} %broadcast_in_dim.86), calls=%async_computation.1 | async-start | bytes 229376 | tf_op jit(solution)/shard_map/all_to_all | solution.py:169
  84.1 8.3 %collective-permute-start.14 = (f32[49,128]{1,0:T(8,128)S(1)}, f32[49,128]{1,0:T(8,128)S(1)}, u32[]{:S(2)}, u32[]{:S(2)}) collective-permute-start(f32[49,128]{1,0:T(8,128)S(1)} %pad_maximum_fusion.2), channel_id=1, source_target_pairs={{0,192},{4,196},{8,200},{12,204},{16,208},{20,212},{24,216},{28,22... | collective-permute-start | bytes 75272 | tf_op jit(solution)/shard_map/ppermute | solution.py:163
  86.9 6.2 %collective-permute-start.15 = (f32[49,128]{1,0:T(8,128)S(1)}, f32[49,128]{1,0:T(8,128)S(1)}, u32[]{:S(2)}, u32[]{:S(2)}) collective-permute-start(f32[49,128]{1,0:T(8,128)S(1)} %pad_maximum_fusion.2), channel_id=1, source_target_pairs={{0,128},{4,132},{8,136},{12,140},{16,144},{20,148},{24,152},{28,15... | collective-permute-start | bytes 75272 | tf_op jit(solution)/shard_map/ppermute | solution.py:163
  87.7 5.4 %collective-permute-start.16 = (f32[49,128]{1,0:T(8,128)S(1)}, f32[49,128]{1,0:T(8,128)S(1)}, u32[]{:S(2)}, u32[]{:S(2)}) collective-permute-start(f32[49,128]{1,0:T(8,128)S(1)} %pad_maximum_fusion.2), channel_id=1, source_target_pairs={{0,64},{4,68},{8,72},{12,76},{16,80},{20,84},{24,88},{28,92},{32,9... | collective-permute-start | bytes 75272 | tf_op jit(solution)/shard_map/ppermute | solution.py:163
  88.5 15.6 %collective-permute-start.18 = (bf16[8,256,128]{2,1,0:T(8,128)(2,1)}, bf16[8,256,128]{2,1,0:T(8,128)(2,1)S(1)}, u32[]{:S(2)}, u32[]{:S(2)}) collective-permute-start(bf16[8,256,128]{2,1,0:T(8,128)(2,1)} %get-tuple-element.39), channel_id=1, source_target_pairs={{0,64},{4,68},{8,72},{12,76},{16,80},{20,84},{24,88},{28,92},{32,9... | collective-permute-start | bytes 1572872 | tf_op jit(solution)/shard_map/ppermute | solution.py:163
  90.3 23.8 %collective-permute-start.19 = (bf16[8,256,128]{2,1,0:T(8,128)(2,1)}, bf16[8,256,128]{2,1,0:T(8,128)(2,1)S(1)}, u32[]{:S(2)}, u32[]{:S(2)}) collective-permute-start(bf16[8,256,128]{2,1,0:T(8,128)(2,1)} %get-tuple-element.40), channel_id=1, source_target_pairs={{0,128},{4,132},{8,136},{12,140},{16,144},{20,148},{24,152},{28,15... | collective-permute-start | bytes 1572872 | tf_op jit(solution)/shard_map/ppermute | solution.py:163
  92.4 21.8 %collective-permute-start.20 = (bf16[8,256,128]{2,1,0:T(8,128)(2,1)S(1)}, bf16[8,256,128]{2,1,0:T(8,128)(2,1)S(1)}, u32[]{:S(2)}, u32[]{:S(2)}) collective-permute-start(bf16[8,256,128]{2,1,0:T(8,128)(2,1)S(1)} %copy-done.22), channel_id=1, source_target_pairs={{0,192},{4,196},{8,200},{12,204},{16,208},{20,212},{24,216},{28,22... | collective-permute-start | bytes 1572872 | tf_op jit(solution)/shard_map/ppermute | solution.py:163
  93.1 1.8 %collective-permute-start.17 = (f32[49,128]{1,0:T(8,128)S(1)}, f32[49,128]{1,0:T(8,128)S(1)}, u32[]{:S(2)}, u32[]{:S(2)}) collective-permute-start(f32[49,128]{1,0:T(8,128)S(1)} %pad_maximum_fusion.3), channel_id=1, source_target_pairs={{0,4},{4,0},{8,12},{12,8},{16,20},{20,16},{24,28},{28,24},{32,36},... | collective-permute-start | bytes 75272 | tf_op jit(solution)/shard_map/ppermute | solution.py:156
  93.6 26.7 %collective-permute-start.10 = (bf16[128,2048]{1,0:T(8,128)(2,1)}, bf16[128,2048]{1,0:T(8,128)(2,1)S(1)}, u32[]{:S(2)}, u32[]{:S(2)}) collective-permute-start(bf16[128,2048]{1,0:T(8,128)(2,1)} %get-tuple-element.44), channel_id=1, source_target_pairs={{0,1},{1,2},{2,3},{3,0},{4,5},{5,6},{6,7},{7,4},{8,9},{9,10},{10,1... | collective-permute-start | bytes 1572872 | tf_op jit(solution)/shard_map/ppermute | solution.py:159
  94.9 25.3 %collective-permute-start.11 = (bf16[128,2048]{1,0:T(8,128)(2,1)}, bf16[128,2048]{1,0:T(8,128)(2,1)}, u32[]{:S(2)}, u32[]{:S(2)}) collective-permute-start(bf16[128,2048]{1,0:T(8,128)(2,1)} %get-tuple-element.45), channel_id=1, source_target_pairs={{0,2},{1,3},{2,0},{3,1},{4,6},{5,7},{6,4},{7,5},{8,10},{9,11},{10,... | collective-permute-start | bytes 1572872 | tf_op jit(solution)/shard_map/ppermute | solution.py:159
  104.1 17.9 %collective-permute-start.12 = (bf16[128,2048]{1,0:T(8,128)(2,1)S(1)}, bf16[128,2048]{1,0:T(8,128)(2,1)}, u32[]{:S(2)}, u32[]{:S(2)}) collective-permute-start(bf16[128,2048]{1,0:T(8,128)(2,1)S(1)} %copy-done.21), channel_id=1, source_target_pairs={{0,3},{1,0},{2,1},{3,2},{4,7},{5,4},{6,5},{7,6},{8,11},{9,8},{10,9... | collective-permute-start | bytes 1572872 | tf_op jit(solution)/shard_map/ppermute | solution.py:159
  115.2 6.8 %copy-start.10 = (bf16[128,2048]{1,0:T(8,128)(2,1)S(1)}, bf16[128,2048]{1,0:T(8,128)(2,1)}, u32[]{:S(2)}) copy-start(bf16[128,2048]{1,0:T(8,128)(2,1)} %get-tuple-element.43) | copy-start | bytes 1572868
  115.2 19.8 %all-to-all-start.2 = ((bf16[8,256,128]{2,1,0:T(8,128)(2,1)}), bf16[8,256,128]{2,1,0:T(8,128)(2,1)S(1)}, u32[]{:S(2)}, u32[]{:S(2)}) async-start(bf16[8,256,128]{2,1,0:T(8,128)(2,1)} %add_convert_fusion), calls=%async_computation.2 | async-start | bytes 1048576 | tf_op jit(solution)/shard_map/all_to_all | solution.py:322

commit v5 on v4

--- a/solution.py
+++ b/solution.py
@@ -90,6 +90,7 @@
             pltpu.SemaphoreType.DMA((count,)),
             pltpu.SemaphoreType.DMA((count,)),
         ],
+        compiler_params=pltpu.CompilerParams(vmem_limit_bytes=12 * 2**20),
     )(turns, result, result_other, *blocks, *taken)
 
 
@@ -101,37 +102,29 @@
     def kernel(turns_ref, result_ref, *refs):
         block_refs, weight_ref = refs[:count], refs[count]
         grad_ref, piece_refs = refs[count + 1], refs[count + 2 :]
+        grad = None
         for j in range(count):
-
-            @pl.when(pl.program_id(0) == j)
-            def _():
-                w = weight_ref[...]
-                piece_refs[j][...] = jnp.dot(
-                    result_ref[...], w, preferred_element_type=F32
-                ).astype(BF16)
-                term = lax.dot_general(
-                    block_refs[-j % count][...],
-                    w,
-                    (((1,), (1,)), ((), ())),
-                    preferred_element_type=F32,
-                )
-                grad_ref[...] = term if j == 0 else grad_ref[...] + term
-
-    def whole(shape):
-        return pl.BlockSpec(shape, lambda j, turns_ref: (0, 0))
+            at = pl.multiple_of((turns_ref[2] + j) % count * feats, feats)
+            w = weight_ref[:, pl.ds(at, feats)]
+            piece_refs[j][...] = jnp.dot(result_ref[...], w, preferred_element_type=F32).astype(
+                BF16
+            )
+            term = lax.dot_general(
+                block_refs[-j % count][...],
+                w,
+                (((1,), (1,)), ((), ())),
+                preferred_element_type=F32,
+            )
+            grad = term if j == 0 else grad + term
+        grad_ref[...] = grad
 
     return pl.pallas_call(
         kernel,
         out_shape=[jax.ShapeDtypeStruct((tokens, chans), F32)]
         + [jax.ShapeDtypeStruct((tokens, feats), BF16)] * count,
-        grid_spec=pltpu.PrefetchScalarGridSpec(
-            num_scalar_prefetch=1,
-            grid=(count,),
-            in_specs=[whole((tokens, chans))]
-            + [whole((tokens, feats))] * count
-            + [pl.BlockSpec((chans, feats), lambda j, turns_ref: (0, (turns_ref[2] + j) % count))],
-            out_specs=[whole((tokens, chans))] + [whole((tokens, feats))] * count,
-        ),
+        in_specs=[pl.BlockSpec(memory_space=pltpu.SMEM)] + in_vmem(2 + count),
+        out_specs=in_vmem(1 + count),
+        compiler_params=pltpu.CompilerParams(vmem_limit_bytes=24 * 2**20),
     )(turns, result, *blocks, weight)
 
 

time: 138 us -> 146 us (1.058)
  other arithmetic: 13.3 us -> 26.7 us
  waiting for transfers between devices: 60.8 us -> 54.5 us
  Pallas kernels: 11.4 us -> 5.37 us
  matrix products: 4.3 us -> 7.83 us
  local copies, waits for them, and re-layouts: 3.19 us -> 6.29 us
    pallas_call x1, Pallas kernels: 7.25 us -> 2.64 us  [projections(): pl.pallas_call(kernel, out_shape=[jax.ShapeDtypeStruct((tokens, chans), F...]
    ppermute x6, waiting for transfers between devices: 15.4 us -> 11.7 us  [shift_y(): lax.ppermute(a, 'ctx', [(i, (i // per + k) % ny * per + i % per) for i in...]
    dot_general x6, matrix products: 3.18 us -> 6.72 us  [back(): jnp.dot(inverse, jnp.concatenate([real_part, imag_part], 0), precision=EX...]
    all_to_all x1, waiting for transfers between devices: 10.7 us -> 7.21 us  [body(): lax.all_to_all(summed_y, 'ctx', 0, 0, tiled=True, axis_index_groups=z_gro...]
    dot_general x1, local copies, waits for them, and re-layouts: 0.09 us -> 1.77 us  [back(): jnp.dot(inverse, jnp.concatenate([real_part, imag_part], 0), precision=EX...]
    unnamed x46 -> x72, local copies, waits for them, and re-layouts: 1.7 us -> 3.13 us
  transfers between devices with their start and end apart: 24 -> 24, of which waited for: 12 -> 13; matrix products, arithmetic and copies ran while one was open for 7% -> 12% of each run, Pallas kernels for 0% -> 0%
where the time goes in v5:
time: 146 us; the launch traced here: 143 us
  waiting for transfers between devices  54.5 us (37%)
  starting transfers between devices  41.2 us (28%)
  other arithmetic  26.7 us (18%)
  matrix products  7.83 us (5%)
  local copies, waits for them, and re-layouts  6.29 us (4%)
  Pallas kernels  5.37 us (4%)
    ppermute x6, waiting for transfers between devices, shift_tp(): return lax.ppermute(a, 'tp', [(i, (i + k) % tps) for i in range(tps)])  16.2 us
    ppermute x6, waiting for transfers between devices, shift_y(): lax.ppermute(a, 'ctx', [(i, (i // per + k) % ny * per + i % per) for i in...  11.7 us
    all_to_all x1, starting transfers between devices, of_pairs(): lax.all_to_all(copies, 'ctx', 0, 0, tiled=True, axis_index_groups=groups)  11.6 us
    ppermute x6, starting transfers between devices, shift_y(): lax.ppermute(a, 'ctx', [(i, (i // per + k) % ny * per + i % per) for i in...  8.93 us
    ppermute x6, starting transfers between devices, shift_tp(): return lax.ppermute(a, 'tp', [(i, (i + k) % tps) for i in range(tps)])  8.59 us
    all_to_all x1, waiting for transfers between devices, of_plane(): lax.all_to_all(copies, 'ctx', 0, 0, tiled=True, axis_index_groups=z_groups)  8.32 us
    all_to_all x1, waiting for transfers between devices, of_pairs(): lax.all_to_all(copies, 'ctx', 0, 0, tiled=True, axis_index_groups=groups)  7.83 us
    all_to_all x1, waiting for transfers between devices, body(): lax.all_to_all(summed_y, 'ctx', 0, 0, tiled=True, axis_index_groups=z_gro...  7.21 us
  transfers between devices with their start and end apart: 24, of which 13 were waited for; matrix products, arithmetic and copies ran while one was open for 12% of the time, Pallas kernels for 0%

profile of v5, /device:TPU:2, one launch (start us, length us, event | category | flops | bytes accessed | tf_op | source)
XLA Modules:
  0.0 143.0 jit_solution(11591869345417059354)
XLA Ops:
  0.7 0.8 fusion.90
  1.5 0.9 convert_multiply_fusion.5
  3.2 1.2 collective-permute-done
  5.2 11.6 %all-to-all-start = ((bf16[32,32,128]{2,1,0:T(8,128)(2,1)}), bf16[32,32,128]{2,1,0:T(8,128)(2,1)S(1)}, u32[]{:S(2)}, u32[]{:S(2)}) async-start(bf16[32,32,128]{2,1,0:T(8,128)(2,1)} %broadcast_in_dim.49), calls=%async_computation | async-start | bytes 524288 | tf_op jit(solution)/shard_map/all_to_all | solution.py:167
  16.9 1.6 %collective-permute-start.3 = (bf16[128,2048]{1,0:T(8,128)(2,1)S(1)}, bf16[128,2048]{1,0:T(8,128)(2,1)S(1)}, u32[]{:S(2)}, u32[]{:S(2)}) collective-permute-start(bf16[128,2048]{1,0:T(8,128)(2,1)S(1)} %copy-done.1), channel_id=1, source_target_pairs={{0,1},{1,2},{2,3},{3,0},{4,5},{5,6},{6,7},{7,4},{8,9},{9,10},{10,1... | collective-permute-start | bytes 1572872 | tf_op jit(solution)/shard_map/ppermute | solution.py:152
  18.4 1.1 collective-permute-start.4
  19.5 2.2 %collective-permute-start.5 = (bf16[128,2048]{1,0:T(8,128)(2,1)S(1)}, bf16[128,2048]{1,0:T(8,128)(2,1)S(1)}, u32[]{:S(2)}, u32[]{:S(2)}) collective-permute-start(bf16[128,2048]{1,0:T(8,128)(2,1)S(1)} %copy-done.1), channel_id=1, source_target_pairs={{0,3},{1,0},{2,1},{3,2},{4,7},{5,4},{6,5},{7,6},{8,11},{9,8},{10,9... | collective-permute-start | bytes 1572872 | tf_op jit(solution)/shard_map/ppermute | solution.py:152
  21.7 7.8 %all-to-all-done = bf16[32,32,128]{2,1,0:T(8,128)(2,1)S(1)} async-done(((bf16[32,32,128]{2,1,0:T(8,128)(2,1)}), bf16[32,32,128]{2,1,0:T(8,128)(2,1)S(1)}, u32[]{:S(2)}, u32[]{:S(2)}) %all-to-all-start) | async-done | bytes 262176 | tf_op jit(solution)/shard_map/all_to_all | solution.py:167
  30.9 0.8 collective-permute-done.3.refs_3_.refs_1_
  31.7 3.0 %collective-permute-done.4.refs_4_.refs_2_ = bf16[128,2048]{1,0:T(8,128)(2,1)S(1)} collective-permute-done((bf16[128,2048]{1,0:T(8,128)(2,1)S(1)}, bf16[128,2048]{1,0:T(8,128)(2,1)S(1)}, u32[]{:S(2)}, u32[]{:S(2)}) %collective-permute-start.4) | collective-permute-done | bytes 524320 | tf_op jit(solution)/shard_map/ppermute | solution.py:152
  34.7 9.2 %collective-permute-done.5.refs_5_.refs_3_ = bf16[128,2048]{1,0:T(8,128)(2,1)S(1)} collective-permute-done((bf16[128,2048]{1,0:T(8,128)(2,1)S(1)}, bf16[128,2048]{1,0:T(8,128)(2,1)S(1)}, u32[]{:S(2)}, u32[]{:S(2)}) %collective-permute-start.5) | collective-permute-done | bytes 524320 | tf_op jit(solution)/shard_map/ppermute | solution.py:152
  48.0 0.8 collective-permute-start.2
  48.9 0.8 collective-permute-done.2.refs_1_
  49.7 2.7 %shard_map.161 = (bf16[8,256,128]{2,1,0:T(8,128)(2,1)S(1)}, bf16[8,256,128]{2,1,0:T(8,128)(2,1)S(1)}, bf16[8,256,128]{2,1,0:T(8,128)(2,1)S(1)}, bf16[8,256,128]{2,1,0:T(8,128)(2,1)S(1)}) custom-call(s32[3]{0:T(128)S(1)} %pad_add_fusion.turns_ref, bf16[128,256]{1,0:T(8,128)(2,1)S(1)} %get-tuple-element.42.refs_0_.result_ref, ...), custom_call_target="tpu_custom_call" | custom-call | tf_op jit(solution)/shard_map/pallas_call | solution.py:80
  52.5 0.8 copy-done.8
  53.3 0.8 copy-done.10
  54.1 0.8 copy-done.11
  54.9 2.6 %shard_map.162 = (f32[128,256]{1,0:T(8,128)S(1)}, bf16[128,2048]{1,0:T(8,128)(2,1)S(1)}, bf16[128,2048]{1,0:T(8,128)(2,1)S(1)}, bf16[128,2048]{1,0:T(8,128)(2,1)S(1)}, bf16[128,2048]{1,0:T(8,128)(2,1)S(1)}) custom-call(s32[3]{0:T(128)S(1)} %pad_add_fusion.turns_ref, bf16[128,256]{1,0:T(8,128)(2,1)S(1)} %get-tuple-element.42.refs_0_.result_ref, ...), custom_call_target="tpu_custom_call" | custom-call | tf_op jit(solution)/shard_map/pallas_call | solution.py:121
  57.6 1.3 fusion.37
  60.0 1.3 fusion.5
  61.3 1.8 %copy.34 = f32[128,256]{1,0:T(8,128)} copy(f32[128,256]{0,1:T(8,128)} %fusion.5) | data formatting | bytes 262144 | tf_op jit(solution)/shard_map/dot_general | solution.py:33
  63.8 2.1 %fusion.3 = (f32[16,256]{1,0:T(8,128)S(1)}, f32[16,256]{1,0:T(8,128)S(1)}, f32[16,256]{1,0:T(8,128)S(1)}, f32[16,256]{1,0:T(8,128)S(1)}) fusion(f32[128,256]{1,0:T(8,128)} %copy.34, f32[16,256]{1,0:T(8,128)S(1)} %exponential_negate_fusion.1, f32[128,256]{1,0:T(8,128)} %copy-done.19), kind=kLoop, calls=%fused_computation.7 | loop fusion | flops 4702208 | bytes 344064 | tf_op jit(solution)/shard_map/reduce_sum | solution.py:281
  66.7 1.3 pad_maximum_fusion
  68.3 1.2 collective-permute-done.13
  72.4 6.7 %all-to-all-start.1 = ((bf16[8,49,128]{2,1,0:T(8,128)(2,1)}), bf16[8,49,128]{2,1,0:T(8,128)(2,1)}, u32[]{:S(2)}, u32[]{:S(2)}) async-start(bf16[8,49,128]{2,1,0:T(8,128)(2,1)} %broadcast_in_dim.86), calls=%async_computation.1 | async-start | bytes 229376 | tf_op jit(solution)/shard_map/all_to_all | solution.py:162
  80.2 8.3 %all-to-all-done.1 = bf16[8,49,128]{2,1,0:T(8,128)(2,1)} async-done(((bf16[8,49,128]{2,1,0:T(8,128)(2,1)}), bf16[8,49,128]{2,1,0:T(8,128)(2,1)}, u32[]{:S(2)}, u32[]{:S(2)}) %all-to-all-start.1) | async-done | bytes 100384 | tf_op jit(solution)/shard_map/all_to_all | solution.py:162
  88.5 0.9 convert_element_type.127
  89.4 1.4 multiply_reduce_fusion.8
  91.4 2.7 %collective-permute-start.14 = (f32[49,128]{1,0:T(8,128)}, f32[49,128]{1,0:T(8,128)}, u32[]{:S(2)}, u32[]{:S(2)}) collective-permute-start(f32[49,128]{1,0:T(8,128)} %pad_maximum_fusion.2), channel_id=1, source_target_pairs={{0,192},{4,196},{8,200},{12,204},{16,208},{20,212},{24,216},{28,22... | collective-permute-start | bytes 75272 | tf_op jit(solution)/shard_map/ppermute | solution.py:156
  94.2 0.8 collective-permute-start.15
  95.0 0.9 collective-permute-start.16
  95.8 1.8 %collective-permute-start.18 = (bf16[8,256,128]{2,1,0:T(8,128)(2,1)}, bf16[8,256,128]{2,1,0:T(8,128)(2,1)S(1)}, u32[]{:S(2)}, u32[]{:S(2)}) collective-permute-start(bf16[8,256,128]{2,1,0:T(8,128)(2,1)} %copy-done.11), channel_id=1, source_target_pairs={{0,64},{4,68},{8,72},{12,76},{16,80},{20,84},{24,88},{28,92},{32,9... | collective-permute-start | bytes 1572872 | tf_op jit(solution)/shard_map/ppermute | solution.py:156
  97.7 2.0 %collective-permute-start.19 = (bf16[8,256,128]{2,1,0:T(8,128)(2,1)}, bf16[8,256,128]{2,1,0:T(8,128)(2,1)S(1)}, u32[]{:S(2)}, u32[]{:S(2)}) collective-permute-start(bf16[8,256,128]{2,1,0:T(8,128)(2,1)} %copy-done.10), channel_id=1, source_target_pairs={{0,128},{4,132},{8,136},{12,140},{16,144},{20,148},{24,152},{28,15... | collective-permute-start | bytes 1572872 | tf_op jit(solution)/shard_map/ppermute | solution.py:156
  100.7 0.8 slice_add_fusion.1
  102.4 2.0 %fusion.24 = f32[256,128]{0,1:T(8,128)} fusion(f32[128,129]{1,0:T(8,128)} %constant.98, f32[258,256]{1,0:T(8,128)} %copy-done.12, f32[258,256]{1,0:T(8,128)S(1)} %fusion.91), kind=kOutput, calls=%fused_computation.46 | convolution fusion | flops 50823936 | bytes 819200 | tf_op jit(solution)/shard_map/dot_general | solution.py:33
  104.4 1.3 collective-permute-start.10
  105.7 1.6 %collective-permute-start.11 = (bf16[128,2048]{1,0:T(8,128)(2,1)S(1)}, bf16[128,2048]{1,0:T(8,128)(2,1)}, u32[]{:S(2)}, u32[]{:S(2)}) collective-permute-start(bf16[128,2048]{1,0:T(8,128)(2,1)S(1)} %copy-done.5), channel_id=1, source_target_pairs={{0,2},{1,3},{2,0},{3,1},{4,6},{5,7},{6,4},{7,5},{8,10},{9,11},{10,... | collective-permute-start | bytes 1572872 | tf_op jit(solution)/shard_map/ppermute | solution.py:152
  107.9 1.4 fusion.72
  109.3 2.2 %collective-permute-done.18 = bf16[8,256,128]{2,1,0:T(8,128)(2,1)S(1)} collective-permute-done((bf16[8,256,128]{2,1,0:T(8,128)(2,1)}, bf16[8,256,128]{2,1,0:T(8,128)(2,1)S(1)}, u32[]{:S(2)}, u32[]{:S(2)}) %collective-permute-start.18) | collective-permute-done | bytes 524320 | tf_op jit(solution)/shard_map/ppermute | solution.py:156
  111.5 0.8 collective-permute-start.12
  112.3 9.1 %collective-permute-done.19 = bf16[8,256,128]{2,1,0:T(8,128)(2,1)S(1)} collective-permute-done((bf16[8,256,128]{2,1,0:T(8,128)(2,1)}, bf16[8,256,128]{2,1,0:T(8,128)(2,1)S(1)}, u32[]{:S(2)}, u32[]{:S(2)}) %collective-permute-start.19) | collective-permute-done | bytes 524320 | tf_op jit(solution)/shard_map/ppermute | solution.py:156
  121.5 1.1 add_convert_fusion
  122.5 3.5 %all-to-all-start.2 = ((bf16[8,256,128]{2,1,0:T(8,128)(2,1)}), bf16[8,256,128]{2,1,0:T(8,128)(2,1)S(1)}, u32[]{:S(2)}, u32[]{:S(2)}) async-start(bf16[8,256,128]{2,1,0:T(8,128)(2,1)} %add_convert_fusion), calls=%async_computation.2 | async-start | bytes 1048576 | tf_op jit(solution)/shard_map/all_to_all | solution.py:315
  126.1 1.1 multiply_reduce_fusion
  127.2 2.2 %fusion.35 = (bf16[128,256]{1,0:T(8,128)(2,1)}, bf16[128,256]{1,0:T(8,128)(2,1)}) fusion(bf16[128,256]{1,0:T(8,128)(2,1)S(1)} %copy-done.14, bf16[128,256]{1,0:T(8,128)(2,1)S(1)} %copy-done.13, f32[128,256]{1,0:T(8,128)} %copy-done.19, f32[256]{0:T(256)S(1)} %copy-done.33, f32[128,256]{1,0:T(8,128)S(1)} %multiply_reduce_fusion, f32[256,128]{0,1:T(8,128)} %fusion.24, ...), kind=kOutput, calls=%fused_computation.57 | convolution fusion | flops 51151616 | bytes 1344512 | tf_op jit(solution)/shard_map/dot_general | solution.py:33
  129.4 3.2 %collective-permute-done.12 = bf16[128,2048]{1,0:T(8,128)(2,1)} collective-permute-done((bf16[128,2048]{1,0:T(8,128)(2,1)S(1)}, bf16[128,2048]{1,0:T(8,128)(2,1)}, u32[]{:S(2)}, u32[]{:S(2)}) %collective-permute-start.12) | collective-permute-done | bytes 524320 | tf_op jit(solution)/shard_map/ppermute | solution.py:152
  132.6 2.5 %add_convert_fusion.1 = bf16[128,2048]{1,0:T(8,128)(2,1)} fusion(bf16[128,2048]{1,0:T(8,128)(2,1)} %collective-permute-done.12, bf16[128,2048]{1,0:T(8,128)(2,1)} %collective-permute-done.11, bf16[128,2048]{1,0:T(8,128)(2,1)} %collective-permute-done.10, bf16[128,2048]{1,0:T(8,128)(2,1)S(1)} %get-tuple-element.43), kind=kLoop, calls=%fused_computation.26 | loop fusion | flops 2097152 | bytes 2621440 | tf_op jit(solution)/shard_map/convert_element_type | solution.py:255
  135.1 7.2 %all-to-all-done.2 = bf16[8,256,128]{2,1,0:T(8,128)(2,1)S(1)} async-done(((bf16[8,256,128]{2,1,0:T(8,128)(2,1)}), bf16[8,256,128]{2,1,0:T(8,128)(2,1)S(1)}, u32[]{:S(2)}, u32[]{:S(2)}) %all-to-all-start.2) | async-done | bytes 524320 | tf_op jit(solution)/shard_map/all_to_all | solution.py:315
  (131 shorter events, 17.7 us)
Async XLA Ops:
  0.6 44.0 %copy-start.22 = (f32[16,256]{1,0:T(8,128)S(1)}, f32[16,256]{1,0:T(8,128)}, u32[]{:S(2)}) copy-start(f32[16,256]{1,0:T(8,128)} %param.14) | copy-start | bytes 49156
  0.6 16.2 %copy-start.1 = (bf16[128,2048]{1,0:T(8,128)(2,1)S(1)}, bf16[128,2048]{1,0:T(8,128)(2,1)}, u32[]{:S(2)}) copy-start(bf16[128,2048]{1,0:T(8,128)(2,1)} %refs_0_.1) | copy-start | bytes 1572868
  3.0 43.5 %copy-start.15 = (f32[258,128]{1,0:T(8,128)S(1)}, f32[258,128]{1,0:T(8,128)}, u32[]{:S(2)}) copy-start(f32[258,128]{1,0:T(8,128)} %constant.96.clone) | copy-start | bytes 396292
  3.1 1.3 collective-permute-start
  4.4 42.5 %copy-start.13 = (bf16[128,256]{1,0:T(8,128)(2,1)S(1)}, bf16[128,256]{1,0:T(8,128)(2,1)}, u32[]{:S(2)}) copy-start(bf16[128,256]{1,0:T(8,128)(2,1)} %param.12) | copy-start | bytes 196612
  4.4 42.5 %copy-start.14 = (bf16[128,256]{1,0:T(8,128)(2,1)S(1)}, bf16[128,256]{1,0:T(8,128)(2,1)}, u32[]{:S(2)}) copy-start(bf16[128,256]{1,0:T(8,128)(2,1)} %param.11) | copy-start | bytes 196612
  5.2 42.1 %copy-start.20 = (f32[128,129]{1,0:T(8,128)S(1)}, f32[128,129]{1,0:T(8,128)}, u32[]{:S(2)}) copy-start(f32[128,129]{1,0:T(8,128)} %constant.98) | copy-start | bytes 198148
  5.2 24.4 %all-to-all-start = ((bf16[32,32,128]{2,1,0:T(8,128)(2,1)}), bf16[32,32,128]{2,1,0:T(8,128)(2,1)S(1)}, u32[]{:S(2)}, u32[]{:S(2)}) async-start(bf16[32,32,128]{2,1,0:T(8,128)(2,1)} %broadcast_in_dim.49), calls=%async_computation | async-start | bytes 524288 | tf_op jit(solution)/shard_map/all_to_all | solution.py:167
  16.9 14.9 %collective-permute-start.3 = (bf16[128,2048]{1,0:T(8,128)(2,1)S(1)}, bf16[128,2048]{1,0:T(8,128)(2,1)S(1)}, u32[]{:S(2)}, u32[]{:S(2)}) collective-permute-start(bf16[128,2048]{1,0:T(8,128)(2,1)S(1)} %copy-done.1), channel_id=1, source_target_pairs={{0,1},{1,2},{2,3},{3,0},{4,5},{5,6},{6,7},{7,4},{8,9},{9,10},{10,1... | collective-permute-start | bytes 1572872 | tf_op jit(solution)/shard_map/ppermute | solution.py:152
  18.4 16.3 %collective-permute-start.4 = (bf16[128,2048]{1,0:T(8,128)(2,1)S(1)}, bf16[128,2048]{1,0:T(8,128)(2,1)S(1)}, u32[]{:S(2)}, u32[]{:S(2)}) collective-permute-start(bf16[128,2048]{1,0:T(8,128)(2,1)S(1)} %copy-done.1), channel_id=1, source_target_pairs={{0,2},{1,3},{2,0},{3,1},{4,6},{5,7},{6,4},{7,5},{8,10},{9,11},{10,... | collective-permute-start | bytes 1572872 | tf_op jit(solution)/shard_map/ppermute | solution.py:152
  19.5 24.4 %collective-permute-start.5 = (bf16[128,2048]{1,0:T(8,128)(2,1)S(1)}, bf16[128,2048]{1,0:T(8,128)(2,1)S(1)}, u32[]{:S(2)}, u32[]{:S(2)}) collective-permute-start(bf16[128,2048]{1,0:T(8,128)(2,1)S(1)} %copy-done.1), channel_id=1, source_target_pairs={{0,3},{1,0},{2,1},{3,2},{4,7},{5,4},{6,5},{7,6},{8,11},{9,8},{10,9... | collective-permute-start | bytes 1572872 | tf_op jit(solution)/shard_map/ppermute | solution.py:152
  21.7 26.0 %copy-start.17 = (f32[128,129]{1,0:T(8,128)S(1)}, f32[128,129]{1,0:T(8,128)}, u32[]{:S(2)}) copy-start(f32[128,129]{1,0:T(8,128)} %constant.99) | copy-start | bytes 198148
  21.7 26.0 %copy-start.23 = (bf16[128,256]{1,0:T(8,128)(2,1)S(1)}, bf16[128,256]{1,0:T(8,128)(2,1)}, u32[]{:S(2)}) copy-start(bf16[128,256]{1,0:T(8,128)(2,1)} %param.10) | copy-start | bytes 196612
  21.7 26.0 %copy-start.32 = (f32[256]{0:T(256)S(1)}, f32[256]{0:T(256)}, u32[]{:S(2)}) copy-start(f32[256]{0:T(256)} %param.15) | copy-start | bytes 3076
  30.4 13.5 %collective-permute-start.1 = (f32[32,128]{1,0:T(8,128)S(1)}, f32[32,128]{1,0:T(8,128)S(1)}, u32[]{:S(2)}, u32[]{:S(2)}) collective-permute-start(f32[32,128]{1,0:T(8,128)S(1)} %pad_maximum_fusion.6), channel_id=1, source_target_pairs={{0,4},{4,0},{8,12},{12,8},{16,20},{20,16},{24,28},{28,24},{32,36},... | collective-permute-start | bytes 49160 | tf_op jit(solution)/shard_map/ppermute | solution.py:149
  30.4 18.5 %collective-permute-start.6 = (bf16[128,2048]{1,0:T(8,128)(2,1)S(1)}, bf16[128,2048]{1,0:T(8,128)(2,1)S(1)}, u32[]{:S(2)}, u32[]{:S(2)}) collective-permute-start(bf16[128,2048]{1,0:T(8,128)(2,1)S(1)} %copy-done.1), channel_id=1, source_target_pairs={{0,4},{4,0},{8,12},{12,8},{16,20},{20,16},{24,28},{28,24},{32,36},... | collective-permute-start | bytes 1572872 | tf_op jit(solution)/shard_map/ppermute | solution.py:149
  31.7 18.0 %collective-permute-start.7 = (bf16[128,2048]{1,0:T(8,128)(2,1)S(1)}, bf16[128,2048]{1,0:T(8,128)(2,1)S(1)}, u32[]{:S(2)}, u32[]{:S(2)}) collective-permute-start(bf16[128,2048]{1,0:T(8,128)(2,1)S(1)} %collective-permute-done.3.refs_3_.refs_1_), channel_id=1, source_target_pairs={{0,4},{4,0},{8,12},{12,8},{16,20},{20,16},{24,28},{28,24},{32,36},... | collective-permute-start | bytes 1572872 | tf_op jit(solution)/shard_map/ppermute | solution.py:149
  34.7 15.0 %collective-permute-start.8 = (bf16[128,2048]{1,0:T(8,128)(2,1)S(1)}, bf16[128,2048]{1,0:T(8,128)(2,1)S(1)}, u32[]{:S(2)}, u32[]{:S(2)}) collective-permute-start(bf16[128,2048]{1,0:T(8,128)(2,1)S(1)} %collective-permute-done.4.refs_4_.refs_2_), channel_id=1, source_target_pairs={{0,4},{4,0},{8,12},{12,8},{16,20},{20,16},{24,28},{28,24},{32,36},... | collective-permute-start | bytes 1572872 | tf_op jit(solution)/shard_map/ppermute | solution.py:149
  43.9 5.8 %collective-permute-start.9 = (bf16[128,2048]{1,0:T(8,128)(2,1)S(1)}, bf16[128,2048]{1,0:T(8,128)(2,1)S(1)}, u32[]{:S(2)}, u32[]{:S(2)}) collective-permute-start(bf16[128,2048]{1,0:T(8,128)(2,1)S(1)} %collective-permute-done.5.refs_5_.refs_3_), channel_id=1, source_target_pairs={{0,4},{4,0},{8,12},{12,8},{16,20},{20,16},{24,28},{28,24},{32,36},... | collective-permute-start | bytes 1572872 | tf_op jit(solution)/shard_map/ppermute | solution.py:149
  48.0 1.7 %collective-permute-start.2 = (bf16[128,256]{1,0:T(8,128)(2,1)S(1)}, bf16[128,256]{1,0:T(8,128)(2,1)S(1)}, u32[]{:S(2)}, u32[]{:S(2)}) collective-permute-start(bf16[128,256]{1,0:T(8,128)(2,1)S(1)} %get-tuple-element.42.refs_0_.result_ref), channel_id=1, source_target_pairs={{0,4},{4,0},{8,12},{12,8},{16,20},{20,16},{24,28},{28,24},{32,36},... | collective-permute-start | bytes 196616 | tf_op jit(solution)/shard_map/ppermute | solution.py:149
  48.9 6.0 %copy-start = (bf16[256,8192]{1,0:T(8,128)(2,1)S(1)}, bf16[256,8192]{1,0:T(8,128)(2,1)}, u32[]{:S(2)}) copy-start(bf16[256,8192]{1,0:T(8,128)(2,1)} %refs_4_.1) | copy-start | bytes 12582916
  54.9 2.7 %copy-start.24 = (bf16[128,256]{1,0:T(8,128)(2,1)S(1)}, bf16[128,256]{1,0:T(8,128)(2,1)}, u32[]{:S(2)}) copy-start(bf16[128,256]{1,0:T(8,128)(2,1)} %param.10) | copy-start | bytes 196612
  54.9 4.1 %copy-start.16 = (f32[258,128]{1,0:T(8,128)S(1)}, f32[258,128]{1,0:T(8,128)}, u32[]{:S(2)}) copy-start(f32[258,128]{1,0:T(8,128)} %constant.96.clone) | copy-start | bytes 396292
  54.9 4.4 %copy-start.21 = (f32[128,129]{1,0:T(8,128)S(1)}, f32[128,129]{1,0:T(8,128)}, u32[]{:S(2)}) copy-start(f32[128,129]{1,0:T(8,128)} %constant.98) | copy-start | bytes 198148
  54.9 5.1 %copy-start.18 = (f32[128,129]{1,0:T(8,128)S(1)}, f32[128,129]{1,0:T(8,128)}, u32[]{:S(2)}) copy-start(f32[128,129]{1,0:T(8,128)} %constant.99) | copy-start | bytes 198148
  57.6 2.4 %copy-start.4 = (bf16[128,2048]{1,0:T(8,128)(2,1)}, bf16[128,2048]{1,0:T(8,128)(2,1)S(1)}, u32[]{:S(2)}) copy-start(bf16[128,2048]{1,0:T(8,128)(2,1)S(1)} %get-tuple-element.45) | copy-start | bytes 1572868
  57.6 2.4 %copy-start.6 = (bf16[128,2048]{1,0:T(8,128)(2,1)}, bf16[128,2048]{1,0:T(8,128)(2,1)S(1)}, u32[]{:S(2)}) copy-start(bf16[128,2048]{1,0:T(8,128)(2,1)S(1)} %get-tuple-element.44) | copy-start | bytes 1572868
  59.3 40.3 %copy-start.9 = (bf16[8,256,128]{2,1,0:T(8,128)(2,1)S(1)}, bf16[8,256,128]{2,1,0:T(8,128)(2,1)}, u32[]{:S(2)}) copy-start(bf16[8,256,128]{2,1,0:T(8,128)(2,1)} %copy-done.8) | copy-start | bytes 1572868
  61.3 43.1 %copy-start.7 = (bf16[128,2048]{1,0:T(8,128)(2,1)S(1)}, bf16[128,2048]{1,0:T(8,128)(2,1)}, u32[]{:S(2)}) copy-start(bf16[128,2048]{1,0:T(8,128)(2,1)} %copy-done.6) | copy-start | bytes 1572868
  61.3 44.4 %copy-start.5 = (bf16[128,2048]{1,0:T(8,128)(2,1)S(1)}, bf16[128,2048]{1,0:T(8,128)(2,1)}, u32[]{:S(2)}) copy-start(bf16[128,2048]{1,0:T(8,128)(2,1)} %copy-done.4) | copy-start | bytes 1572868
  61.3 50.2 %copy-start.3 = (bf16[128,2048]{1,0:T(8,128)(2,1)S(1)}, bf16[128,2048]{1,0:T(8,128)(2,1)}, u32[]{:S(2)}) copy-start(bf16[128,2048]{1,0:T(8,128)(2,1)} %copy-done.2) | copy-start | bytes 1572868
  63.8 4.2 %copy-start.31 = (f32[16,256]{1,0:T(8,128)}, f32[16,256]{1,0:T(8,128)S(1)}, u32[]{:S(2)}) copy-start(f32[16,256]{1,0:T(8,128)S(1)} %exponential_negate_fusion.1) | copy-start | bytes 49156
  68.0 1.6 %collective-permute-start.13 = (f32[49,256]{1,0:T(8,128)}, f32[49,256]{1,0:T(8,128)}, u32[]{:S(2)}, u32[]{:S(2)}) collective-permute-start(f32[49,256]{1,0:T(8,128)} %pad_maximum_fusion), channel_id=1, source_target_pairs={{0,4},{4,0},{8,12},{12,8},{16,20},{20,16},{24,28},{28,24},{32,36},... | collective-permute-start | bytes 150536 | tf_op jit(solution)/shard_map/ppermute | solution.py:149
  72.4 16.0 %all-to-all-start.1 = ((bf16[8,49,128]{2,1,0:T(8,128)(2,1)}), bf16[8,49,128]{2,1,0:T(8,128)(2,1)}, u32[]{:S(2)}, u32[]{:S(2)}) async-start(bf16[8,49,128]{2,1,0:T(8,128)(2,1)} %broadcast_in_dim.86), calls=%async_computation.1 | async-start | bytes 229376 | tf_op jit(solution)/shard_map/all_to_all | solution.py:162
  91.4 8.2 %collective-permute-start.14 = (f32[49,128]{1,0:T(8,128)}, f32[49,128]{1,0:T(8,128)}, u32[]{:S(2)}, u32[]{:S(2)}) collective-permute-start(f32[49,128]{1,0:T(8,128)} %pad_maximum_fusion.2), channel_id=1, source_target_pairs={{0,192},{4,196},{8,200},{12,204},{16,208},{20,212},{24,216},{28,22... | collective-permute-start | bytes 75272 | tf_op jit(solution)/shard_map/ppermute | solution.py:156
  94.2 6.2 %collective-permute-start.15 = (f32[49,128]{1,0:T(8,128)}, f32[49,128]{1,0:T(8,128)}, u32[]{:S(2)}, u32[]{:S(2)}) collective-permute-start(f32[49,128]{1,0:T(8,128)} %pad_maximum_fusion.2), channel_id=1, source_target_pairs={{0,128},{4,132},{8,136},{12,140},{16,144},{20,148},{24,152},{28,15... | collective-permute-start | bytes 75272 | tf_op jit(solution)/shard_map/ppermute | solution.py:156
  95.0 5.8 %collective-permute-start.16 = (f32[49,128]{1,0:T(8,128)}, f32[49,128]{1,0:T(8,128)}, u32[]{:S(2)}, u32[]{:S(2)}) collective-permute-start(f32[49,128]{1,0:T(8,128)} %pad_maximum_fusion.2), channel_id=1, source_target_pairs={{0,64},{4,68},{8,72},{12,76},{16,80},{20,84},{24,88},{28,92},{32,9... | collective-permute-start | bytes 75272 | tf_op jit(solution)/shard_map/ppermute | solution.py:156
  95.8 15.7 %collective-permute-start.18 = (bf16[8,256,128]{2,1,0:T(8,128)(2,1)}, bf16[8,256,128]{2,1,0:T(8,128)(2,1)S(1)}, u32[]{:S(2)}, u32[]{:S(2)}) collective-permute-start(bf16[8,256,128]{2,1,0:T(8,128)(2,1)} %copy-done.11), channel_id=1, source_target_pairs={{0,64},{4,68},{8,72},{12,76},{16,80},{20,84},{24,88},{28,92},{32,9... | collective-permute-start | bytes 1572872 | tf_op jit(solution)/shard_map/ppermute | solution.py:156
  97.7 23.8 %collective-permute-start.19 = (bf16[8,256,128]{2,1,0:T(8,128)(2,1)}, bf16[8,256,128]{2,1,0:T(8,128)(2,1)S(1)}, u32[]{:S(2)}, u32[]{:S(2)}) collective-permute-start(bf16[8,256,128]{2,1,0:T(8,128)(2,1)} %copy-done.10), channel_id=1, source_target_pairs={{0,128},{4,132},{8,136},{12,140},{16,144},{20,148},{24,152},{28,15... | collective-permute-start | bytes 1572872 | tf_op jit(solution)/shard_map/ppermute | solution.py:156
  99.7 21.8 %collective-permute-start.20 = (bf16[8,256,128]{2,1,0:T(8,128)(2,1)S(1)}, bf16[8,256,128]{2,1,0:T(8,128)(2,1)S(1)}, u32[]{:S(2)}, u32[]{:S(2)}) collective-permute-start(bf16[8,256,128]{2,1,0:T(8,128)(2,1)S(1)} %copy-done.9), channel_id=1, source_target_pairs={{0,192},{4,196},{8,200},{12,204},{16,208},{20,212},{24,216},{28,22... | collective-permute-start | bytes 1572872 | tf_op jit(solution)/shard_map/ppermute | solution.py:156
  102.3 3.4 %collective-permute-start.17 = (f32[49,128]{1,0:T(8,128)S(1)}, f32[49,128]{1,0:T(8,128)S(1)}, u32[]{:S(2)}, u32[]{:S(2)}) collective-permute-start(f32[49,128]{1,0:T(8,128)S(1)} %pad_maximum_fusion.3), channel_id=1, source_target_pairs={{0,4},{4,0},{8,12},{12,8},{16,20},{20,16},{24,28},{28,24},{32,36},... | collective-permute-start | bytes 75272 | tf_op jit(solution)/shard_map/ppermute | solution.py:149
  104.4 21.6 %copy-start.35 = (f32[128]{0:T(128)S(1)}, f32[128]{0:T(128)}, u32[]{:S(2)}) copy-start(f32[128]{0:T(128)} %copy-done.34) | copy-start | bytes 1540
  104.4 25.0 %collective-permute-start.10 = (bf16[128,2048]{1,0:T(8,128)(2,1)S(1)}, bf16[128,2048]{1,0:T(8,128)(2,1)}, u32[]{:S(2)}, u32[]{:S(2)}) collective-permute-start(bf16[128,2048]{1,0:T(8,128)(2,1)S(1)} %copy-done.7), channel_id=1, source_target_pairs={{0,1},{1,2},{2,3},{3,0},{4,5},{5,6},{6,7},{7,4},{8,9},{9,10},{10,1... | collective-permute-start | bytes 1572872 | tf_op jit(solution)/shard_map/ppermute | solution.py:152
  105.7 23.7 %collective-permute-start.11 = (bf16[128,2048]{1,0:T(8,128)(2,1)S(1)}, bf16[128,2048]{1,0:T(8,128)(2,1)}, u32[]{:S(2)}, u32[]{:S(2)}) collective-permute-start(bf16[128,2048]{1,0:T(8,128)(2,1)S(1)} %copy-done.5), channel_id=1, source_target_pairs={{0,2},{1,3},{2,0},{3,1},{4,6},{5,7},{6,4},{7,5},{8,10},{9,11},{10,... | collective-permute-start | bytes 1572872 | tf_op jit(solution)/shard_map/ppermute | solution.py:152
  111.5 15.7 %copy-start.33 = (f32[256]{0:T(256)S(1)}, f32[256]{0:T(256)}, u32[]{:S(2)}) copy-start(f32[256]{0:T(256)} %param.15) | copy-start | bytes 3076
  111.5 21.1 %collective-permute-start.12 = (bf16[128,2048]{1,0:T(8,128)(2,1)S(1)}, bf16[128,2048]{1,0:T(8,128)(2,1)}, u32[]{:S(2)}, u32[]{:S(2)}) collective-permute-start(bf16[128,2048]{1,0:T(8,128)(2,1)S(1)} %copy-done.3), channel_id=1, source_target_pairs={{0,3},{1,0},{2,1},{3,2},{4,7},{5,4},{6,5},{7,6},{8,11},{9,8},{10,9... | collective-permute-start | bytes 1572872 | tf_op jit(solution)/shard_map/ppermute | solution.py:152
  121.5 4.6 %copy-start.30 = (f32[16,256]{1,0:T(8,128)S(1)}, f32[16,256]{1,0:T(8,128)}, u32[]{:S(2)}) copy-start(f32[16,256]{1,0:T(8,128)} %get-tuple-element.80) | copy-start | bytes 49156
  122.5 19.7 %all-to-all-start.2 = ((bf16[8,256,128]{2,1,0:T(8,128)(2,1)}), bf16[8,256,128]{2,1,0:T(8,128)(2,1)S(1)}, u32[]{:S(2)}, u32[]{:S(2)}) async-start(bf16[8,256,128]{2,1,0:T(8,128)(2,1)} %add_convert_fusion), calls=%async_computation.2 | async-start | bytes 1048576 | tf_op jit(solution)/shard_map/all_to_all | solution.py:315
  (12 other events, 12.7 us)

commit v6 on v5

--- a/solution.py
+++ b/solution.py
@@ -94,38 +94,52 @@
     )(turns, result, result_other, *blocks, *taken)
 
 
-def projections(turns, result, blocks, weight):
+def gated_gradient(turns, blocks, weight):
     count = len(blocks)
     tokens, feats = blocks[0].shape
-    chans = result.shape[1]
-
-    def kernel(turns_ref, result_ref, *refs):
-        block_refs, weight_ref = refs[:count], refs[count]
-        grad_ref, piece_refs = refs[count + 1], refs[count + 2 :]
+    chans = weight.shape[0]
+
+    def kernel(turns_ref, *refs):
+        weight_ref, grad_ref = refs[count:]
         grad = None
-        for j in range(count):
-            at = pl.multiple_of((turns_ref[2] + j) % count * feats, feats)
-            w = weight_ref[:, pl.ds(at, feats)]
-            piece_refs[j][...] = jnp.dot(result_ref[...], w, preferred_element_type=F32).astype(
-                BF16
-            )
+        for k in range(count):
+            at = pl.multiple_of((turns_ref[2] - k + count) % count * feats, feats)
             term = lax.dot_general(
-                block_refs[-j % count][...],
-                w,
+                refs[k][...],
+                weight_ref[:, pl.ds(at, feats)],
                 (((1,), (1,)), ((), ())),
                 preferred_element_type=F32,
             )
-            grad = term if j == 0 else grad + term
+            grad = term if k == 0 else grad + term
         grad_ref[...] = grad
 
     return pl.pallas_call(
         kernel,
-        out_shape=[jax.ShapeDtypeStruct((tokens, chans), F32)]
-        + [jax.ShapeDtypeStruct((tokens, feats), BF16)] * count,
-        in_specs=[pl.BlockSpec(memory_space=pltpu.SMEM)] + in_vmem(2 + count),
-        out_specs=in_vmem(1 + count),
-        compiler_params=pltpu.CompilerParams(vmem_limit_bytes=24 * 2**20),
-    )(turns, result, *blocks, weight)
+        out_shape=jax.ShapeDtypeStruct((tokens, chans), F32),
+        in_specs=[pl.BlockSpec(memory_space=pltpu.SMEM)] + in_vmem(1 + count),
+        out_specs=in_vmem(1)[0],
+        compiler_params=pltpu.CompilerParams(vmem_limit_bytes=16 * 2**20),
+    )(turns, *blocks, weight)
+
+
+def output_pieces(turns, result, weight, count):
+    tokens = result.shape[0]
+    feats = weight.shape[1] // count
+
+    def kernel(turns_ref, result_ref, weight_ref, *piece_refs):
+        for k in range(count):
+            at = pl.multiple_of((turns_ref[2] + k) % count * feats, feats)
+            piece_refs[k][...] = jnp.dot(
+                result_ref[...], weight_ref[:, pl.ds(at, feats)], preferred_element_type=F32
+            ).astype(BF16)
+
+    return pl.pallas_call(
+        kernel,
+        out_shape=[jax.ShapeDtypeStruct((tokens, feats), BF16)] * count,
+        in_specs=[pl.BlockSpec(memory_space=pltpu.SMEM)] + in_vmem(2),
+        out_specs=in_vmem(count),
+        compiler_params=pltpu.CompilerParams(vmem_limit_bytes=16 * 2**20),
+    )(turns, result, weight)
 
 
 def body(outer_gate, inner_gate, values, residues, log_decay, skip_gain, out_weight, out_grad):
@@ -140,7 +154,6 @@
     nz = ctx // (2 * ny)
     core = dev % 2
     pair = dev // 2
-    zz = pair % nz
     pairs = ctx // 2
     yy = dev // (2 * nz)
     width = feats // (2 * nz)
@@ -156,10 +169,6 @@
         return lax.ppermute(a, "ctx", [(i, (i // per + k) % ny * per + i % per) for i in range(ctx)])
 
     z_groups = [[i * 2 * nz + j * 2 + k for j in range(nz)] for i in range(ny) for k in range(2)]
-
-    def of_plane(a):
-        copies = jnp.broadcast_to(a[None], (nz, *a.shape))
-        return lax.all_to_all(copies, "ctx", 0, 0, tiled=True, axis_index_groups=z_groups)
 
     def of_pairs(a):
         copies = jnp.broadcast_to(a[None], (pairs, *a.shape))
@@ -200,10 +209,8 @@
     total_lag = decay_h * (block * f_h[:modes] + f_h[modes:]) + s_h[modes:]
     to_send = jnp.concatenate([total, total_lag], 0).astype(BF16)
     gathered = of_pairs(to_send).astype(F32)
-    place = jnp.arange(nz, dtype=jnp.int32)
     every = jnp.arange(pairs, dtype=jnp.int32)
     per_pair = 2 * block
-    per_plane = per_pair * nz
 
     def weights(which, gap):
         gap = jnp.where(which, gap, 0).astype(F32)[:, None, None] * per_pair
@@ -239,7 +246,8 @@
     result = row_major((outer_f * gated).astype(BF16))
 
     turns = jnp.stack([core, (tp - yy) % tps, tp]).astype(jnp.int32)
-    taken = [row_major(swap_core(a)) for a in og]
+    taken = [row_major(swap_core(out_grad))]
+    taken = taken + [row_major(swap_core(a)) for a in og[1:]]
     result_other = swap_core(result)
     y_parts = weight_parts(turns, result, result_other, og, taken, width)
     over_y = [y_parts[0]] + [shift_y(y_parts[s], s) for s in range(1, ny)]
@@ -247,7 +255,8 @@
 
     late = lax.optimization_barrier((result, gated, *y_parts))
     result, gated = late[:2]
-    grad_gated, *pieces = projections(turns, result, og, out_weight)
+    grad_gated = gated_gradient(turns, og, out_weight)
+    pieces = output_pieces(turns, result, out_weight, tps)
     mixed = pieces[0].astype(F32)
     for k in range(1, tps):
         piece = shift_tp(pieces[k], k)
@@ -288,18 +297,11 @@
     early_h = jnp.where(core == 0, mine_h[:modes], theirs_h[:modes])
     total_g = early_h + decay_h * my_half(later)
     sent = jnp.concatenate([total_g, mine_h[modes:] + theirs_h[modes:]], 0).astype(BF16)
-    got = of_plane(sent).astype(F32)
-    plane_h = jnp.sum(weights(place >= 0, place)[0] * got[:, :modes], 0)
-    plane_sums = jnp.sum(got[:, modes:], 0)
-    plane_g = jnp.concatenate([plane_h, plane_sums], 0)
-    h_half = jnp.sum(weights(place > zz, place - zz - 1)[0] * got[:, :modes], 0)
-    y_h, sums_half = 0.0, plane_sums
-    for k in range(1, ny):
-        came = shift_y(plane_g, -k)
-        w = jnp.exp(-rate_h * float(per_plane * (k - 1)))
-        y_h = y_h + jnp.where(yy + k < ny, w * came[:modes], 0.0)
-        sums_half = sums_half + came[modes:]
-    h_half = h_half + jnp.exp(-rate_h * (per_pair * (nz - 1 - zz)).astype(F32)) * y_h
+    got = of_pairs(sent)
+    got = got.astype(F32)
+    w = weights(every > pair, every - pair - 1)[0]
+    h_half = jnp.sum(w * got[:, :modes], 0)
+    sums_half = jnp.sum(got[:, modes:], 0)
     final = both_halves(jnp.concatenate([h_half, sums_half], 0))
     h_pair = final[:modes]
     h_in = jnp.where(core == 0, later + fall_block * h_pair, h_pair)

time: 146 us -> 121 us (0.83); the launches traced: 143 us -> 120 us
  waiting for transfers between devices: 54.5 us -> 40.8 us
  other arithmetic: 26.7 us -> 15.2 us
  matrix products: 7.83 us -> 5.81 us
  local copies, waits for them, and re-layouts: 6.29 us -> 7.95 us
    all_to_all x1 -> x0, waiting for transfers between devices: 8.32 us -> none  [of_plane(): lax.all_to_all(copies, 'ctx', 0, 0, tiled=True, axis_index_groups=z_groups)]
    all_to_all x1 -> x2, starting transfers between devices: 11.6 us -> 18.8 us  [of_pairs(): lax.all_to_all(copies, 'ctx', 0, 0, tiled=True, axis_index_groups=groups)]
    all_to_all x1 -> x0, starting transfers between devices: 6.69 us -> none  [of_plane(): lax.all_to_all(copies, 'ctx', 0, 0, tiled=True, axis_index_groups=z_groups)]
    ppermute x6 -> x3, waiting for transfers between devices: 11.7 us -> 7.88 us  [shift_y(): lax.ppermute(a, 'ctx', [(i, (i // per + k) % ny * per + i % per) for i in...]
    ppermute x6 -> x3, starting transfers between devices: 8.93 us -> 5.73 us  [shift_y(): lax.ppermute(a, 'ctx', [(i, (i // per + k) % ny * per + i % per) for i in...]
    unnamed x72 -> x98, local copies, waits for them, and re-layouts: 3.13 us -> 6.28 us
    all_to_all x1, starting transfers between devices: 3.49 us -> 6.62 us  [body(): lax.all_to_all(summed_y, 'ctx', 0, 0, tiled=True, axis_index_groups=z_gro...]
    ppermute x9, waiting for transfers between devices: 3.24 us -> 1.19 us  [swap_core(): return lax.ppermute(a, 'ctx', [(i, i ^ 1) for i in range(ctx)])]
  transfers between devices with their start and end apart: 24 -> 21, of which waited for: 13 -> 8; matrix products, arithmetic and copies ran while one was open for 12% -> 13% of each run, Pallas kernels for 0% -> 3%
where the time goes in v6:
time: 121 us; the launch traced here: 120 us
  starting transfers between devices  42.2 us (35%)
  waiting for transfers between devices  40.8 us (34%)
  other arithmetic  15.2 us (13%)
  local copies, waits for them, and re-layouts  7.95 us (7%)
  Pallas kernels  6.78 us (6%)
  matrix products  5.81 us (5%)
  between operations  1.51 us (1%)
    all_to_all x2, starting transfers between devices, of_pairs(): lax.all_to_all(copies, 'ctx', 0, 0, tiled=True, axis_index_groups=groups)  18.8 us
    ppermute x6, waiting for transfers between devices, shift_tp(): return lax.ppermute(a, 'tp', [(i, (i + k) % tps) for i in range(tps)])  16.6 us
    ppermute x6, starting transfers between devices, shift_tp(): return lax.ppermute(a, 'tp', [(i, (i + k) % tps) for i in range(tps)])  9.32 us
    ppermute x3, waiting for transfers between devices, shift_y(): lax.ppermute(a, 'ctx', [(i, (i // per + k) % ny * per + i % per) for i in...  7.88 us
    all_to_all x2, waiting for transfers between devices, of_pairs(): lax.all_to_all(copies, 'ctx', 0, 0, tiled=True, axis_index_groups=groups)  7.85 us
    all_to_all x1, waiting for transfers between devices, body(): lax.all_to_all(summed_y, 'ctx', 0, 0, tiled=True, axis_index_groups=z_gro...  7.23 us
    all_to_all x1, starting transfers between devices, body(): lax.all_to_all(summed_y, 'ctx', 0, 0, tiled=True, axis_index_groups=z_gro...  6.62 us
    unnamed x98, local copies, waits for them, and re-layouts  6.28 us
  transfers between devices with their start and end apart: 21, of which 8 were waited for; matrix products, arithmetic and copies ran while one was open for 13% of the time, Pallas kernels for 3%

profile of v6, /device:TPU:2, one launch (start us, length us, event | category | flops | bytes accessed | tf_op | source)
XLA Modules:
  0.0 120.2 jit_solution(13073765173564353718)
XLA Ops:
  0.7 0.8 fusion.84
  1.5 0.9 convert_multiply_fusion.5
  2.4 0.7 fusion.4
  3.2 1.2 collective-permute-done
  4.5 0.7 broadcast_in_dim.32
  5.2 11.6 %all-to-all-start = ((bf16[32,32,128]{2,1,0:T(8,128)(2,1)}), bf16[32,32,128]{2,1,0:T(8,128)(2,1)S(1)}, u32[]{:S(2)}, u32[]{:S(2)}) async-start(bf16[32,32,128]{2,1,0:T(8,128)(2,1)} %broadcast_in_dim.32), calls=%async_computation | async-start | bytes 524288 | tf_op jit(solution)/shard_map/all_to_all | solution.py:176
  16.9 1.6 %collective-permute-start.3 = (bf16[128,2048]{1,0:T(8,128)(2,1)S(1)}, bf16[128,2048]{1,0:T(8,128)(2,1)S(1)}, u32[]{:S(2)}, u32[]{:S(2)}) collective-permute-start(bf16[128,2048]{1,0:T(8,128)(2,1)S(1)} %copy-done.2), channel_id=1, source_target_pairs={{0,1},{1,2},{2,3},{3,0},{4,5},{5,6},{6,7},{7,4},{8,9},{9,10},{10,1... | collective-permute-start | bytes 1572872 | tf_op jit(solution)/shard_map/ppermute | solution.py:165
  18.4 1.1 collective-permute-start.4
  19.5 2.2 %collective-permute-start.5 = (bf16[128,2048]{1,0:T(8,128)(2,1)S(1)}, bf16[128,2048]{1,0:T(8,128)(2,1)S(1)}, u32[]{:S(2)}, u32[]{:S(2)}) collective-permute-start(bf16[128,2048]{1,0:T(8,128)(2,1)S(1)} %copy-done.2), channel_id=1, source_target_pairs={{0,3},{1,0},{2,1},{3,2},{4,7},{5,4},{6,5},{7,6},{8,11},{9,8},{10,9... | collective-permute-start | bytes 1572872 | tf_op jit(solution)/shard_map/ppermute | solution.py:165
  21.7 7.8 %all-to-all-done = bf16[32,32,128]{2,1,0:T(8,128)(2,1)S(1)} async-done(((bf16[32,32,128]{2,1,0:T(8,128)(2,1)}), bf16[32,32,128]{2,1,0:T(8,128)(2,1)S(1)}, u32[]{:S(2)}, u32[]{:S(2)}) %all-to-all-start) | async-done | bytes 262176 | tf_op jit(solution)/shard_map/all_to_all | solution.py:176
  30.4 1.3 %collective-permute-done.3.refs_3_.refs_1_ = bf16[128,2048]{1,0:T(8,128)(2,1)S(1)} collective-permute-done((bf16[128,2048]{1,0:T(8,128)(2,1)S(1)}, bf16[128,2048]{1,0:T(8,128)(2,1)S(1)}, u32[]{:S(2)}, u32[]{:S(2)}) %collective-permute-start.3) | collective-permute-done | bytes 524320 | tf_op jit(solution)/shard_map/ppermute | solution.py:165
  31.7 3.0 %collective-permute-done.4.refs_4_.refs_2_ = bf16[128,2048]{1,0:T(8,128)(2,1)S(1)} collective-permute-done((bf16[128,2048]{1,0:T(8,128)(2,1)S(1)}, bf16[128,2048]{1,0:T(8,128)(2,1)S(1)}, u32[]{:S(2)}, u32[]{:S(2)}) %collective-permute-start.4) | collective-permute-done | bytes 524320 | tf_op jit(solution)/shard_map/ppermute | solution.py:165
  34.7 9.2 %collective-permute-done.5.refs_5_.refs_3_ = bf16[128,2048]{1,0:T(8,128)(2,1)S(1)} collective-permute-done((bf16[128,2048]{1,0:T(8,128)(2,1)S(1)}, bf16[128,2048]{1,0:T(8,128)(2,1)S(1)}, u32[]{:S(2)}, u32[]{:S(2)}) %collective-permute-start.5) | collective-permute-done | bytes 524320 | tf_op jit(solution)/shard_map/ppermute | solution.py:165
  43.9 0.6 fusion.74
  46.3 1.2 multiply_convert_fusion.1
  47.5 0.8 collective-permute-start.2
  48.3 2.2 %copy-done = bf16[256,8192]{1,0:T(8,128)(2,1)S(1)} copy-done((bf16[256,8192]{1,0:T(8,128)(2,1)S(1)}, bf16[256,8192]{1,0:T(8,128)(2,1)}, u32[]{:S(2)}) %copy-start) | copy-done | bytes 4194328
  50.5 2.0 %shard_map.163 = f32[128,256]{1,0:T(8,128)S(1)} custom-call(s32[3]{0:T(128)S(1)} %pad_add_fusion.turns_ref, bf16[128,2048]{1,0:T(8,128)(2,1)S(1)} %copy-done.2, bf16[128,2048]{1,0:T(8,128)(2,1)S(1)} %collective-permute-done.3.refs_3_.refs_1_, bf16[128,2048]{1,0:T(8,128)(2,1)S(1)} %collective-permute-done.4.refs_4_.refs_2_, ...), custom_call_target="tpu_custom_call" | custom-call | tf_op jit(solution)/shard_map/pallas_call | solution.py:116
  52.7 2.7 %shard_map.161 = (bf16[8,256,128]{2,1,0:T(8,128)(2,1)S(1)}, bf16[8,256,128]{2,1,0:T(8,128)(2,1)S(1)}, bf16[8,256,128]{2,1,0:T(8,128)(2,1)S(1)}, bf16[8,256,128]{2,1,0:T(8,128)(2,1)S(1)}) custom-call(s32[3]{0:T(128)S(1)} %pad_add_fusion.turns_ref, bf16[128,256]{1,0:T(8,128)(2,1)S(1)} %get-tuple-element.41.refs_0_.result_ref, ...), custom_call_target="tpu_custom_call" | custom-call | tf_op jit(solution)/shard_map/pallas_call | solution.py:80
  55.4 0.8 copy-done.5
  56.2 0.8 copy-done.7
  57.1 0.7 fusion.38
  58.2 0.6 fusion.18
  58.9 0.6 fusion.5
  59.6 1.1 fusion.3
  61.0 1.6 %collective-permute-start.15 = (bf16[8,256,128]{2,1,0:T(8,128)(2,1)S(1)}, bf16[8,256,128]{2,1,0:T(8,128)(2,1)}, u32[]{:S(2)}, u32[]{:S(2)}) collective-permute-start(bf16[8,256,128]{2,1,0:T(8,128)(2,1)S(1)} %copy-done.8), channel_id=1, source_target_pairs={{0,64},{4,68},{8,72},{12,76},{16,80},{20,84},{24,88},{28,92},{32,9... | collective-permute-start | bytes 1572872 | tf_op jit(solution)/shard_map/ppermute | solution.py:169
  62.6 2.7 %collective-permute-start.16 = (bf16[8,256,128]{2,1,0:T(8,128)(2,1)S(1)}, bf16[8,256,128]{2,1,0:T(8,128)(2,1)}, u32[]{:S(2)}, u32[]{:S(2)}) collective-permute-start(bf16[8,256,128]{2,1,0:T(8,128)(2,1)S(1)} %copy-done.6), channel_id=1, source_target_pairs={{0,128},{4,132},{8,136},{12,140},{16,144},{20,148},{24,152},{28,15... | collective-permute-start | bytes 1572872 | tf_op jit(solution)/shard_map/ppermute | solution.py:169
  65.3 1.4 %collective-permute-start.17 = (bf16[8,256,128]{2,1,0:T(8,128)(2,1)S(1)}, bf16[8,256,128]{2,1,0:T(8,128)(2,1)}, u32[]{:S(2)}, u32[]{:S(2)}) collective-permute-start(bf16[8,256,128]{2,1,0:T(8,128)(2,1)S(1)} %copy-done.4), channel_id=1, source_target_pairs={{0,192},{4,196},{8,200},{12,204},{16,208},{20,212},{24,216},{28,22... | collective-permute-start | bytes 1572872 | tf_op jit(solution)/shard_map/ppermute | solution.py:169
  66.8 0.8 broadcast_in_dim.35
  67.7 7.2 %all-to-all-start.1 = ((bf16[32,49,128]{2,1,0:T(8,128)(2,1)}), bf16[32,49,128]{2,1,0:T(8,128)(2,1)}, u32[]{:S(2)}, u32[]{:S(2)}) async-start(bf16[32,49,128]{2,1,0:T(8,128)(2,1)} %broadcast_in_dim.35), calls=%async_computation.1 | async-start | bytes 917504 | tf_op jit(solution)/shard_map/all_to_all | solution.py:176
  74.9 0.5 convert_multiply_fusion.7
  75.9 2.2 %copy-done.1 = bf16[256,8192]{1,0:T(8,128)(2,1)S(1)} copy-done((bf16[256,8192]{1,0:T(8,128)(2,1)S(1)}, bf16[256,8192]{1,0:T(8,128)(2,1)}, u32[]{:S(2)}) %copy-start.1) | copy-done | bytes 4194328
  78.1 2.0 %shard_map.162 = (bf16[128,2048]{1,0:T(8,128)(2,1)S(1)}, bf16[128,2048]{1,0:T(8,128)(2,1)}, bf16[128,2048]{1,0:T(8,128)(2,1)}, bf16[128,2048]{1,0:T(8,128)(2,1)S(1)}) custom-call(s32[3]{0:T(128)S(1)} %pad_add_fusion.turns_ref, bf16[128,256]{1,0:T(8,128)(2,1)S(1)} %get-tuple-element.41.refs_0_.result_ref, bf16[256,8192]{1,0:T(8,128)(2,1)S(1)} %copy-done.1), custom_call_target="tpu_custom_call" | custom-call | tf_op jit(solution)/shard_map/pallas_call | solution.py:136
  80.1 1.3 %collective-permute-start.10 = (bf16[128,2048]{1,0:T(8,128)(2,1)}, bf16[128,2048]{1,0:T(8,128)(2,1)}, u32[]{:S(2)}, u32[]{:S(2)}) collective-permute-start(bf16[128,2048]{1,0:T(8,128)(2,1)} %get-tuple-element.43), channel_id=1, source_target_pairs={{0,1},{1,2},{2,3},{3,0},{4,5},{5,6},{6,7},{7,4},{8,9},{9,10},{10,1... | collective-permute-start | bytes 1572872 | tf_op jit(solution)/shard_map/ppermute | solution.py:165
  81.4 1.9 %collective-permute-start.11 = (bf16[128,2048]{1,0:T(8,128)(2,1)}, bf16[128,2048]{1,0:T(8,128)(2,1)}, u32[]{:S(2)}, u32[]{:S(2)}) collective-permute-start(bf16[128,2048]{1,0:T(8,128)(2,1)} %get-tuple-element.44), channel_id=1, source_target_pairs={{0,2},{1,3},{2,0},{3,1},{4,6},{5,7},{6,4},{7,5},{8,10},{9,11},{10,... | collective-permute-start | bytes 1572872 | tf_op jit(solution)/shard_map/ppermute | solution.py:165
  83.3 1.0 fusion.25
  84.3 1.3 %collective-permute-start.12 = (bf16[128,2048]{1,0:T(8,128)(2,1)S(1)}, bf16[128,2048]{1,0:T(8,128)(2,1)S(1)}, u32[]{:S(2)}, u32[]{:S(2)}) collective-permute-start(bf16[128,2048]{1,0:T(8,128)(2,1)S(1)} %get-tuple-element.45), channel_id=1, source_target_pairs={{0,3},{1,0},{2,1},{3,2},{4,7},{5,4},{6,5},{7,6},{8,11},{9,8},{10,9... | collective-permute-start | bytes 1572872 | tf_op jit(solution)/shard_map/ppermute | solution.py:165
  85.6 7.9 %collective-permute-done.16 = bf16[8,256,128]{2,1,0:T(8,128)(2,1)} collective-permute-done((bf16[8,256,128]{2,1,0:T(8,128)(2,1)S(1)}, bf16[8,256,128]{2,1,0:T(8,128)(2,1)}, u32[]{:S(2)}, u32[]{:S(2)}) %collective-permute-start.16) | collective-permute-done | bytes 524320 | tf_op jit(solution)/shard_map/ppermute | solution.py:169
  93.5 2.4 %add_convert_fusion = bf16[8,256,128]{2,1,0:T(8,128)(2,1)} fusion(bf16[8,256,128]{2,1,0:T(8,128)(2,1)} %collective-permute-done.17, bf16[8,256,128]{2,1,0:T(8,128)(2,1)} %collective-permute-done.16, bf16[8,256,128]{2,1,0:T(8,128)(2,1)} %collective-permute-done.15, bf16[8,256,128]{2,1,0:T(8,128)(2,1)S(1)} %get-tuple-element.37), kind=kLoop, calls=%fused_computation.25 | loop fusion | flops 2097152 | bytes 2621440 | tf_op jit(solution)/shard_map/convert_element_type | solution.py:254
  95.9 6.6 %all-to-all-start.2 = ((bf16[8,256,128]{2,1,0:T(8,128)(2,1)}), bf16[8,256,128]{2,1,0:T(8,128)(2,1)S(1)}, u32[]{:S(2)}, u32[]{:S(2)}) async-start(bf16[8,256,128]{2,1,0:T(8,128)(2,1)} %add_convert_fusion), calls=%async_computation.2 | async-start | bytes 1048576 | tf_op jit(solution)/shard_map/all_to_all | solution.py:317
  102.6 1.1 convert_element_type.117
  104.1 3.1 %collective-permute-done.12 = bf16[128,2048]{1,0:T(8,128)(2,1)S(1)} collective-permute-done((bf16[128,2048]{1,0:T(8,128)(2,1)S(1)}, bf16[128,2048]{1,0:T(8,128)(2,1)S(1)}, u32[]{:S(2)}, u32[]{:S(2)}) %collective-permute-start.12) | collective-permute-done | bytes 524320 | tf_op jit(solution)/shard_map/ppermute | solution.py:165
  107.2 2.3 %add_convert_fusion.1 = bf16[128,2048]{1,0:T(8,128)(2,1)} fusion(bf16[128,2048]{1,0:T(8,128)(2,1)S(1)} %collective-permute-done.12, bf16[128,2048]{1,0:T(8,128)(2,1)} %collective-permute-done.11, bf16[128,2048]{1,0:T(8,128)(2,1)} %collective-permute-done.10, bf16[128,2048]{1,0:T(8,128)(2,1)S(1)} %get-tuple-element.42), kind=kLoop, calls=%fused_computation.26 | loop fusion | flops 2097152 | bytes 2621440 | tf_op jit(solution)/shard_map/convert_element_type | solution.py:264
  109.5 0.6 fusion.82
  110.1 0.7 fusion.73
  111.2 1.0 fusion.36
  112.2 7.2 %all-to-all-done.2 = bf16[8,256,128]{2,1,0:T(8,128)(2,1)S(1)} async-done(((bf16[8,256,128]{2,1,0:T(8,128)(2,1)}), bf16[8,256,128]{2,1,0:T(8,128)(2,1)S(1)}, u32[]{:S(2)}, u32[]{:S(2)}) %all-to-all-start.2) | async-done | bytes 524320 | tf_op jit(solution)/shard_map/all_to_all | solution.py:317
  119.5 0.7 convert_reduce_fusion
  (148 shorter events, 4.9 us)
Async XLA Ops:
  0.6 43.3 %copy-start.27 = (f32[16,256]{1,0:T(8,128)S(1)}, f32[16,256]{1,0:T(8,128)}, u32[]{:S(2)}) copy-start(f32[16,256]{1,0:T(8,128)} %param.14) | copy-start | bytes 49156
  0.6 16.2 %copy-start.2 = (bf16[128,2048]{1,0:T(8,128)(2,1)S(1)}, bf16[128,2048]{1,0:T(8,128)(2,1)}, u32[]{:S(2)}) copy-start(bf16[128,2048]{1,0:T(8,128)(2,1)} %refs_0_.1) | copy-start | bytes 1572868
  0.7 43.9 %copy-start.39 = (f32[16,256]{1,0:T(8,128)S(1)}, f32[16,256]{1,0:T(8,128)}, u32[]{:S(2)}) copy-start(f32[16,256]{1,0:T(8,128)} %param.13) | copy-start | bytes 49156
  1.5 43.7 %copy-start.37 = (f32[16,256]{1,0:T(8,128)}, f32[16,256]{1,0:T(8,128)S(1)}, u32[]{:S(2)}) copy-start(f32[16,256]{1,0:T(8,128)S(1)} %get-tuple-element.88) | copy-start | bytes 49156
  3.1 42.1 %copy-start.16 = (f32[258,128]{1,0:T(8,128)S(1)}, f32[258,128]{1,0:T(8,128)}, u32[]{:S(2)}) copy-start(f32[258,128]{1,0:T(8,128)} %constant.76.clone) | copy-start | bytes 396292
  3.1 1.3 %collective-permute-start = (f32[32,256]{1,0:T(8,128)S(1)}, f32[32,256]{1,0:T(8,128)S(1)}, u32[]{:S(2)}, u32[]{:S(2)}) collective-permute-start(f32[32,256]{1,0:T(8,128)S(1)} %pad_maximum_fusion.1), channel_id=1, source_target_pairs={{0,4},{4,0},{8,12},{12,8},{16,20},{20,16},{24,28},{28,24},{32,36},... | collective-permute-start | bytes 98312 | tf_op jit(solution)/shard_map/ppermute | solution.py:162
  4.4 41.1 %copy-start.12 = (bf16[128,256]{1,0:T(8,128)(2,1)S(1)}, bf16[128,256]{1,0:T(8,128)(2,1)}, u32[]{:S(2)}) copy-start(bf16[128,256]{1,0:T(8,128)(2,1)} %param.12) | copy-start | bytes 196612
  4.4 41.1 %copy-start.13 = (bf16[128,256]{1,0:T(8,128)(2,1)S(1)}, bf16[128,256]{1,0:T(8,128)(2,1)}, u32[]{:S(2)}) copy-start(bf16[128,256]{1,0:T(8,128)(2,1)} %param.11) | copy-start | bytes 196612
  4.5 40.7 %copy-start.35 = (f32[16,128]{1,0:T(8,128)}, f32[16,128]{1,0:T(8,128)S(1)}, u32[]{:S(2)}) copy-start(f32[16,128]{1,0:T(8,128)S(1)} %get-tuple-element.87) | copy-start | bytes 24580
  5.2 40.7 %copy-start.23 = (f32[128,129]{1,0:T(8,128)S(1)}, f32[128,129]{1,0:T(8,128)}, u32[]{:S(2)}) copy-start(f32[128,129]{1,0:T(8,128)} %constant.78) | copy-start | bytes 198148
  5.2 24.4 %all-to-all-start = ((bf16[32,32,128]{2,1,0:T(8,128)(2,1)}), bf16[32,32,128]{2,1,0:T(8,128)(2,1)S(1)}, u32[]{:S(2)}, u32[]{:S(2)}) async-start(bf16[32,32,128]{2,1,0:T(8,128)(2,1)} %broadcast_in_dim.32), calls=%async_computation | async-start | bytes 524288 | tf_op jit(solution)/shard_map/all_to_all | solution.py:176
  16.9 14.9 %collective-permute-start.3 = (bf16[128,2048]{1,0:T(8,128)(2,1)S(1)}, bf16[128,2048]{1,0:T(8,128)(2,1)S(1)}, u32[]{:S(2)}, u32[]{:S(2)}) collective-permute-start(bf16[128,2048]{1,0:T(8,128)(2,1)S(1)} %copy-done.2), channel_id=1, source_target_pairs={{0,1},{1,2},{2,3},{3,0},{4,5},{5,6},{6,7},{7,4},{8,9},{9,10},{10,1... | collective-permute-start | bytes 1572872 | tf_op jit(solution)/shard_map/ppermute | solution.py:165
  18.4 16.3 %collective-permute-start.4 = (bf16[128,2048]{1,0:T(8,128)(2,1)S(1)}, bf16[128,2048]{1,0:T(8,128)(2,1)S(1)}, u32[]{:S(2)}, u32[]{:S(2)}) collective-permute-start(bf16[128,2048]{1,0:T(8,128)(2,1)S(1)} %copy-done.2), channel_id=1, source_target_pairs={{0,2},{1,3},{2,0},{3,1},{4,6},{5,7},{6,4},{7,5},{8,10},{9,11},{10,... | collective-permute-start | bytes 1572872 | tf_op jit(solution)/shard_map/ppermute | solution.py:165
  19.5 24.4 %collective-permute-start.5 = (bf16[128,2048]{1,0:T(8,128)(2,1)S(1)}, bf16[128,2048]{1,0:T(8,128)(2,1)S(1)}, u32[]{:S(2)}, u32[]{:S(2)}) collective-permute-start(bf16[128,2048]{1,0:T(8,128)(2,1)S(1)} %copy-done.2), channel_id=1, source_target_pairs={{0,3},{1,0},{2,1},{3,2},{4,7},{5,4},{6,5},{7,6},{8,11},{9,8},{10,9... | collective-permute-start | bytes 1572872 | tf_op jit(solution)/shard_map/ppermute | solution.py:165
  21.7 24.6 %copy-start.18 = (f32[128,129]{1,0:T(8,128)S(1)}, f32[128,129]{1,0:T(8,128)}, u32[]{:S(2)}) copy-start(f32[128,129]{1,0:T(8,128)} %constant.79) | copy-start | bytes 198148
  21.7 24.6 %copy-start.44 = (f32[256]{0:T(256)S(1)}, f32[256]{0:T(256)}, u32[]{:S(2)}) copy-start(f32[256]{0:T(256)} %param.15) | copy-start | bytes 3076
  29.8 14.1 %collective-permute-start.1 = (f32[32,128]{1,0:T(8,128)S(1)}, f32[32,128]{1,0:T(8,128)S(1)}, u32[]{:S(2)}, u32[]{:S(2)}) collective-permute-start(f32[32,128]{1,0:T(8,128)S(1)} %pad_maximum_fusion.5), channel_id=1, source_target_pairs={{0,4},{4,0},{8,12},{12,8},{16,20},{20,16},{24,28},{28,24},{32,36},... | collective-permute-start | bytes 49160 | tf_op jit(solution)/shard_map/ppermute | solution.py:162
  29.9 22.7 %collective-permute-start.6 = (bf16[128,2048]{1,0:T(8,128)(2,1)S(1)}, bf16[128,2048]{1,0:T(8,128)(2,1)S(1)}, u32[]{:S(2)}, u32[]{:S(2)}) collective-permute-start(bf16[128,2048]{1,0:T(8,128)(2,1)S(1)} %copy-done.2), channel_id=1, source_target_pairs={{0,4},{4,0},{8,12},{12,8},{16,20},{20,16},{24,28},{28,24},{32,36},... | collective-permute-start | bytes 1572872 | tf_op jit(solution)/shard_map/ppermute | solution.py:162
  31.7 20.9 %collective-permute-start.7 = (bf16[128,2048]{1,0:T(8,128)(2,1)S(1)}, bf16[128,2048]{1,0:T(8,128)(2,1)S(1)}, u32[]{:S(2)}, u32[]{:S(2)}) collective-permute-start(bf16[128,2048]{1,0:T(8,128)(2,1)S(1)} %collective-permute-done.3.refs_3_.refs_1_), channel_id=1, source_target_pairs={{0,4},{4,0},{8,12},{12,8},{16,20},{20,16},{24,28},{28,24},{32,36},... | collective-permute-start | bytes 1572872 | tf_op jit(solution)/shard_map/ppermute | solution.py:162
  34.7 17.9 %collective-permute-start.8 = (bf16[128,2048]{1,0:T(8,128)(2,1)S(1)}, bf16[128,2048]{1,0:T(8,128)(2,1)S(1)}, u32[]{:S(2)}, u32[]{:S(2)}) collective-permute-start(bf16[128,2048]{1,0:T(8,128)(2,1)S(1)} %collective-permute-done.4.refs_4_.refs_2_), channel_id=1, source_target_pairs={{0,4},{4,0},{8,12},{12,8},{16,20},{20,16},{24,28},{28,24},{32,36},... | collective-permute-start | bytes 1572872 | tf_op jit(solution)/shard_map/ppermute | solution.py:162
  43.9 8.7 %collective-permute-start.9 = (bf16[128,2048]{1,0:T(8,128)(2,1)S(1)}, bf16[128,2048]{1,0:T(8,128)(2,1)S(1)}, u32[]{:S(2)}, u32[]{:S(2)}) collective-permute-start(bf16[128,2048]{1,0:T(8,128)(2,1)S(1)} %collective-permute-done.5.refs_5_.refs_3_), channel_id=1, source_target_pairs={{0,4},{4,0},{8,12},{12,8},{16,20},{20,16},{24,28},{28,24},{32,36},... | collective-permute-start | bytes 1572872 | tf_op jit(solution)/shard_map/ppermute | solution.py:162
  47.5 5.2 %collective-permute-start.2 = (bf16[128,256]{1,0:T(8,128)(2,1)S(1)}, bf16[128,256]{1,0:T(8,128)(2,1)S(1)}, u32[]{:S(2)}, u32[]{:S(2)}) collective-permute-start(bf16[128,256]{1,0:T(8,128)(2,1)S(1)} %get-tuple-element.41.refs_0_.result_ref), channel_id=1, source_target_pairs={{0,4},{4,0},{8,12},{12,8},{16,20},{20,16},{24,28},{28,24},{32,36},... | collective-permute-start | bytes 196616 | tf_op jit(solution)/shard_map/ppermute | solution.py:162
  57.0 9.7 %copy-start.38 = (f32[16,256]{1,0:T(8,128)S(1)}, f32[16,256]{1,0:T(8,128)}, u32[]{:S(2)}) copy-start(f32[16,256]{1,0:T(8,128)} %copy-done.37) | copy-start | bytes 49156
  57.8 9.8 %copy-start.21 = (f32[128,256]{1,0:T(8,128)}, f32[128,256]{1,0:T(8,128)S(1)}, u32[]{:S(2)}) copy-start(f32[128,256]{1,0:T(8,128)S(1)} %get-tuple-element.67) | copy-start | bytes 393220
  57.8 7.5 %copy-start.4 = (bf16[8,256,128]{2,1,0:T(8,128)(2,1)S(1)}, bf16[8,256,128]{2,1,0:T(8,128)(2,1)}, u32[]{:S(2)}) copy-start(bf16[8,256,128]{2,1,0:T(8,128)(2,1)} %copy-done.3) | copy-start | bytes 1572868
  58.2 9.4 %copy-start.9 = (f32[258,256]{1,0:T(8,128)}, f32[258,256]{1,0:T(8,128)S(1)}, u32[]{:S(2)}) copy-start(f32[258,256]{1,0:T(8,128)S(1)} %fusion.86) | copy-start | bytes 792580
  60.9 5.9 %collective-permute-start.13 = (f32[49,256]{1,0:T(8,128)S(1)}, f32[49,256]{1,0:T(8,128)S(1)}, u32[]{:S(2)}, u32[]{:S(2)}) collective-permute-start(f32[49,256]{1,0:T(8,128)S(1)} %pad_maximum_fusion), channel_id=1, source_target_pairs={{0,4},{4,0},{8,12},{12,8},{16,20},{20,16},{24,28},{28,24},{32,36},... | collective-permute-start | bytes 150536 | tf_op jit(solution)/shard_map/ppermute | solution.py:162
  61.0 23.3 %collective-permute-start.15 = (bf16[8,256,128]{2,1,0:T(8,128)(2,1)S(1)}, bf16[8,256,128]{2,1,0:T(8,128)(2,1)}, u32[]{:S(2)}, u32[]{:S(2)}) collective-permute-start(bf16[8,256,128]{2,1,0:T(8,128)(2,1)S(1)} %copy-done.8), channel_id=1, source_target_pairs={{0,64},{4,68},{8,72},{12,76},{16,80},{20,84},{24,88},{28,92},{32,9... | collective-permute-start | bytes 1572872 | tf_op jit(solution)/shard_map/ppermute | solution.py:169
  62.6 30.9 %collective-permute-start.16 = (bf16[8,256,128]{2,1,0:T(8,128)(2,1)S(1)}, bf16[8,256,128]{2,1,0:T(8,128)(2,1)}, u32[]{:S(2)}, u32[]{:S(2)}) collective-permute-start(bf16[8,256,128]{2,1,0:T(8,128)(2,1)S(1)} %copy-done.6), channel_id=1, source_target_pairs={{0,128},{4,132},{8,136},{12,140},{16,144},{20,148},{24,152},{28,15... | collective-permute-start | bytes 1572872 | tf_op jit(solution)/shard_map/ppermute | solution.py:169
  65.3 28.2 %collective-permute-start.17 = (bf16[8,256,128]{2,1,0:T(8,128)(2,1)S(1)}, bf16[8,256,128]{2,1,0:T(8,128)(2,1)}, u32[]{:S(2)}, u32[]{:S(2)}) collective-permute-start(bf16[8,256,128]{2,1,0:T(8,128)(2,1)S(1)} %copy-done.4), channel_id=1, source_target_pairs={{0,192},{4,196},{8,200},{12,204},{16,208},{20,212},{24,216},{28,22... | collective-permute-start | bytes 1572872 | tf_op jit(solution)/shard_map/ppermute | solution.py:169
  66.7 8.7 %copy-start.33 = (f32[16,256]{1,0:T(8,128)}, f32[16,256]{1,0:T(8,128)S(1)}, u32[]{:S(2)}) copy-start(f32[16,256]{1,0:T(8,128)S(1)} %slice_select_fusion) | copy-start | bytes 49156
  67.7 28.3 %all-to-all-start.1 = ((bf16[32,49,128]{2,1,0:T(8,128)(2,1)}), bf16[32,49,128]{2,1,0:T(8,128)(2,1)}, u32[]{:S(2)}, u32[]{:S(2)}) async-start(bf16[32,49,128]{2,1,0:T(8,128)(2,1)} %broadcast_in_dim.35), calls=%async_computation.1 | async-start | bytes 917504 | tf_op jit(solution)/shard_map/all_to_all | solution.py:176
  80.1 24.0 %collective-permute-start.10 = (bf16[128,2048]{1,0:T(8,128)(2,1)}, bf16[128,2048]{1,0:T(8,128)(2,1)}, u32[]{:S(2)}, u32[]{:S(2)}) collective-permute-start(bf16[128,2048]{1,0:T(8,128)(2,1)} %get-tuple-element.43), channel_id=1, source_target_pairs={{0,1},{1,2},{2,3},{3,0},{4,5},{5,6},{6,7},{7,4},{8,9},{9,10},{10,1... | collective-permute-start | bytes 1572872 | tf_op jit(solution)/shard_map/ppermute | solution.py:165
  81.4 22.7 %collective-permute-start.11 = (bf16[128,2048]{1,0:T(8,128)(2,1)}, bf16[128,2048]{1,0:T(8,128)(2,1)}, u32[]{:S(2)}, u32[]{:S(2)}) collective-permute-start(bf16[128,2048]{1,0:T(8,128)(2,1)} %get-tuple-element.44), channel_id=1, source_target_pairs={{0,2},{1,3},{2,0},{3,1},{4,6},{5,7},{6,4},{7,5},{8,10},{9,11},{10,... | collective-permute-start | bytes 1572872 | tf_op jit(solution)/shard_map/ppermute | solution.py:165
  84.3 19.3 %copy-start.36 = (f32[16,128]{1,0:T(8,128)S(1)}, f32[16,128]{1,0:T(8,128)}, u32[]{:S(2)}) copy-start(f32[16,128]{1,0:T(8,128)} %copy-done.35) | copy-start | bytes 24580
  84.3 19.3 %copy-start.45 = (f32[32]{0:T(128)S(1)}, f32[32]{0:T(128)}, u32[]{:S(2)}) copy-start(f32[32]{0:T(128)} %convert_multiply_fusion.7) | copy-start | bytes 388
  84.3 19.3 %copy-start.46 = (pred[32]{0:T(512)(128)(4,1)S(1)}, pred[32]{0:T(512)(128)(4,1)}, u32[]{:S(2)}) copy-start(pred[32]{0:T(512)(128)(4,1)} %iota_compare_fusion) | copy-start | bytes 100
  84.3 22.9 %collective-permute-start.12 = (bf16[128,2048]{1,0:T(8,128)(2,1)S(1)}, bf16[128,2048]{1,0:T(8,128)(2,1)S(1)}, u32[]{:S(2)}, u32[]{:S(2)}) collective-permute-start(bf16[128,2048]{1,0:T(8,128)(2,1)S(1)} %get-tuple-element.45), channel_id=1, source_target_pairs={{0,3},{1,0},{2,1},{3,2},{4,7},{5,4},{6,5},{7,6},{8,11},{9,8},{10,9... | collective-permute-start | bytes 1572872 | tf_op jit(solution)/shard_map/ppermute | solution.py:165
  95.9 23.5 %all-to-all-start.2 = ((bf16[8,256,128]{2,1,0:T(8,128)(2,1)}), bf16[8,256,128]{2,1,0:T(8,128)(2,1)S(1)}, u32[]{:S(2)}, u32[]{:S(2)}) async-start(bf16[8,256,128]{2,1,0:T(8,128)(2,1)} %add_convert_fusion), calls=%async_computation.2 | async-start | bytes 1048576 | tf_op jit(solution)/shard_map/all_to_all | solution.py:317
  103.7 6.5 %copy-start.29 = (f32[16,256]{1,0:T(8,128)S(1)}, f32[16,256]{1,0:T(8,128)}, u32[]{:S(2)}) copy-start(f32[16,256]{1,0:T(8,128)} %param.14) | copy-start | bytes 49156
  103.7 7.1 %copy-start.43 = (f32[16,256]{1,0:T(8,128)S(1)}, f32[16,256]{1,0:T(8,128)}, u32[]{:S(2)}) copy-start(f32[16,256]{1,0:T(8,128)} %copy-done.42) | copy-start | bytes 49156
  103.7 7.1 %copy-start.48 = (f32[128]{0:T(128)S(1)}, f32[128]{0:T(128)}, u32[]{:S(2)}) copy-start(f32[128]{0:T(128)} %copy-done.47) | copy-start | bytes 1540
  103.9 7.3 %copy-start.11 = (f32[258,256]{1,0:T(8,128)S(1)}, f32[258,256]{1,0:T(8,128)}, u32[]{:S(2)}) copy-start(f32[258,256]{1,0:T(8,128)} %copy-done.9) | copy-start | bytes 792580
  103.9 7.3 %copy-start.15 = (bf16[128,256]{1,0:T(8,128)(2,1)S(1)}, bf16[128,256]{1,0:T(8,128)(2,1)}, u32[]{:S(2)}) copy-start(bf16[128,256]{1,0:T(8,128)(2,1)} %param.11) | copy-start | bytes 196612
  103.9 7.3 %copy-start.20 = (f32[128,129]{1,0:T(8,128)S(1)}, f32[128,129]{1,0:T(8,128)}, u32[]{:S(2)}) copy-start(f32[128,129]{1,0:T(8,128)} %constant.79) | copy-start | bytes 198148
  104.0 7.3 %copy-start.22 = (f32[128,256]{1,0:T(8,128)S(1)}, f32[128,256]{1,0:T(8,128)}, u32[]{:S(2)}) copy-start(f32[128,256]{1,0:T(8,128)} %copy-done.21) | copy-start | bytes 393220
  104.0 7.3 %copy-start.26 = (f32[256,128]{0,1:T(8,128)S(1)}, f32[256,128]{0,1:T(8,128)}, u32[]{:S(2)}) copy-start(f32[256,128]{0,1:T(8,128)} %fusion.25) | copy-start | bytes 393220
  104.0 5.5 %collective-permute-start.14 = (f32[49,128]{1,0:T(8,128)S(1)}, f32[49,128]{1,0:T(8,128)S(1)}, u32[]{:S(2)}, u32[]{:S(2)}) collective-permute-start(f32[49,128]{1,0:T(8,128)S(1)} %pad_maximum_fusion.2), channel_id=1, source_target_pairs={{0,4},{4,0},{8,12},{12,8},{16,20},{20,16},{24,28},{28,24},{32,36},... | collective-permute-start | bytes 75272 | tf_op jit(solution)/shard_map/ppermute | solution.py:162
  (22 other events, 81.2 us)

commit v7 on v5

--- a/solution.py
+++ b/solution.py
@@ -90,7 +90,7 @@
             pltpu.SemaphoreType.DMA((count,)),
             pltpu.SemaphoreType.DMA((count,)),
         ],
-        compiler_params=pltpu.CompilerParams(vmem_limit_bytes=12 * 2**20),
+        compiler_params=pltpu.CompilerParams(vmem_limit_bytes=6 * 2**20),
     )(turns, result, result_other, *blocks, *taken)
 
 
@@ -124,7 +124,7 @@
         + [jax.ShapeDtypeStruct((tokens, feats), BF16)] * count,
         in_specs=[pl.BlockSpec(memory_space=pltpu.SMEM)] + in_vmem(2 + count),
         out_specs=in_vmem(1 + count),
-        compiler_params=pltpu.CompilerParams(vmem_limit_bytes=24 * 2**20),
+        compiler_params=pltpu.CompilerParams(vmem_limit_bytes=6 * 2**20),
     )(turns, result, *blocks, weight)
 
 
@@ -288,7 +288,8 @@
     early_h = jnp.where(core == 0, mine_h[:modes], theirs_h[:modes])
     total_g = early_h + decay_h * my_half(later)
     sent = jnp.concatenate([total_g, mine_h[modes:] + theirs_h[modes:]], 0).astype(BF16)
-    got = of_plane(sent).astype(F32)
+    got = of_plane(sent)
+    got = got.astype(F32)
     plane_h = jnp.sum(weights(place >= 0, place)[0] * got[:, :modes], 0)
     plane_sums = jnp.sum(got[:, modes:], 0)
     plane_g = jnp.concatenate([plane_h, plane_sums], 0)

time: 146 us -> 145 us (level)
  no operation moved by 1% of the time
where the time goes in v7:
time: 145 us; the launch traced here: 142 us
  waiting for transfers between devices  54.4 us (38%)
  starting transfers between devices  41.2 us (28%)
  other arithmetic  26.6 us (18%)
  matrix products  7.83 us (5%)
  local copies, waits for them, and re-layouts  5.5 us (4%)
  Pallas kernels  5.35 us (4%)
    ppermute x6, waiting for transfers between devices, shift_tp(): return lax.ppermute(a, 'tp', [(i, (i + k) % tps) for i in range(tps)])  16.2 us
    ppermute x6, waiting for transfers between devices, shift_y(): lax.ppermute(a, 'ctx', [(i, (i // per + k) % ny * per + i % per) for i in...  11.7 us
    all_to_all x1, starting transfers between devices, of_pairs(): lax.all_to_all(copies, 'ctx', 0, 0, tiled=True, axis_index_groups=groups)  11.6 us
    ppermute x6, starting transfers between devices, shift_y(): lax.ppermute(a, 'ctx', [(i, (i // per + k) % ny * per + i % per) for i in...  8.93 us
    ppermute x6, starting transfers between devices, shift_tp(): return lax.ppermute(a, 'tp', [(i, (i + k) % tps) for i in range(tps)])  8.61 us
    all_to_all x1, waiting for transfers between devices, of_plane(): lax.all_to_all(copies, 'ctx', 0, 0, tiled=True, axis_index_groups=z_groups)  8.31 us
    all_to_all x1, waiting for transfers between devices, of_pairs(): lax.all_to_all(copies, 'ctx', 0, 0, tiled=True, axis_index_groups=groups)  7.83 us
    all_to_all x1, waiting for transfers between devices, body(): lax.all_to_all(summed_y, 'ctx', 0, 0, tiled=True, axis_index_groups=z_gro...  7.2 us
  transfers between devices with their start and end apart: 24, of which 13 were waited for; matrix products, arithmetic and copies ran while one was open for 12% of the time, Pallas kernels for 0%

profile of v7, /device:TPU:2, one launch (start us, length us, event | category | flops | bytes accessed | tf_op | source)
XLA Modules:
  0.0 142.2 jit_solution(17915708420098303869)
XLA Ops:
  0.7 0.8 fusion.90
  1.5 0.9 convert_multiply_fusion.5
  3.2 1.2 collective-permute-done
  5.2 11.6 %all-to-all-start = ((bf16[32,32,128]{2,1,0:T(8,128)(2,1)}), bf16[32,32,128]{2,1,0:T(8,128)(2,1)S(1)}, u32[]{:S(2)}, u32[]{:S(2)}) async-start(bf16[32,32,128]{2,1,0:T(8,128)(2,1)} %broadcast_in_dim.49), calls=%async_computation | async-start | bytes 524288 | tf_op jit(solution)/shard_map/all_to_all | solution.py:167
  16.9 1.6 %collective-permute-start.3 = (bf16[128,2048]{1,0:T(8,128)(2,1)S(1)}, bf16[128,2048]{1,0:T(8,128)(2,1)S(1)}, u32[]{:S(2)}, u32[]{:S(2)}) collective-permute-start(bf16[128,2048]{1,0:T(8,128)(2,1)S(1)} %copy-done.1), channel_id=1, source_target_pairs={{0,1},{1,2},{2,3},{3,0},{4,5},{5,6},{6,7},{7,4},{8,9},{9,10},{10,1... | collective-permute-start | bytes 1572872 | tf_op jit(solution)/shard_map/ppermute | solution.py:152
  18.4 1.1 collective-permute-start.4
  19.5 2.2 %collective-permute-start.5 = (bf16[128,2048]{1,0:T(8,128)(2,1)S(1)}, bf16[128,2048]{1,0:T(8,128)(2,1)S(1)}, u32[]{:S(2)}, u32[]{:S(2)}) collective-permute-start(bf16[128,2048]{1,0:T(8,128)(2,1)S(1)} %copy-done.1), channel_id=1, source_target_pairs={{0,3},{1,0},{2,1},{3,2},{4,7},{5,4},{6,5},{7,6},{8,11},{9,8},{10,9... | collective-permute-start | bytes 1572872 | tf_op jit(solution)/shard_map/ppermute | solution.py:152
  21.7 7.8 %all-to-all-done = bf16[32,32,128]{2,1,0:T(8,128)(2,1)S(1)} async-done(((bf16[32,32,128]{2,1,0:T(8,128)(2,1)}), bf16[32,32,128]{2,1,0:T(8,128)(2,1)S(1)}, u32[]{:S(2)}, u32[]{:S(2)}) %all-to-all-start) | async-done | bytes 262176 | tf_op jit(solution)/shard_map/all_to_all | solution.py:167
  30.9 0.8 collective-permute-done.3.refs_3_.refs_1_
  31.7 3.0 %collective-permute-done.4.refs_4_.refs_2_ = bf16[128,2048]{1,0:T(8,128)(2,1)S(1)} collective-permute-done((bf16[128,2048]{1,0:T(8,128)(2,1)S(1)}, bf16[128,2048]{1,0:T(8,128)(2,1)S(1)}, u32[]{:S(2)}, u32[]{:S(2)}) %collective-permute-start.4) | collective-permute-done | bytes 524320 | tf_op jit(solution)/shard_map/ppermute | solution.py:152
  34.7 9.2 %collective-permute-done.5.refs_5_.refs_3_ = bf16[128,2048]{1,0:T(8,128)(2,1)S(1)} collective-permute-done((bf16[128,2048]{1,0:T(8,128)(2,1)S(1)}, bf16[128,2048]{1,0:T(8,128)(2,1)S(1)}, u32[]{:S(2)}, u32[]{:S(2)}) %collective-permute-start.5) | collective-permute-done | bytes 524320 | tf_op jit(solution)/shard_map/ppermute | solution.py:152
  48.0 0.8 collective-permute-start.2
  48.9 0.8 collective-permute-done.2.refs_1_
  49.7 2.7 %shard_map.161 = (bf16[8,256,128]{2,1,0:T(8,128)(2,1)S(1)}, bf16[8,256,128]{2,1,0:T(8,128)(2,1)S(1)}, bf16[8,256,128]{2,1,0:T(8,128)(2,1)S(1)}, bf16[8,256,128]{2,1,0:T(8,128)(2,1)S(1)}) custom-call(s32[3]{0:T(128)S(1)} %pad_add_fusion.turns_ref, bf16[128,256]{1,0:T(8,128)(2,1)S(1)} %get-tuple-element.42.refs_0_.result_ref, ...), custom_call_target="tpu_custom_call" | custom-call | tf_op jit(solution)/shard_map/pallas_call | solution.py:80
  52.5 0.8 copy-done.10
  53.3 0.8 copy-done.11
  54.1 2.6 %shard_map.162 = (f32[128,256]{1,0:T(8,128)S(1)}, bf16[128,2048]{1,0:T(8,128)(2,1)S(1)}, bf16[128,2048]{1,0:T(8,128)(2,1)S(1)}, bf16[128,2048]{1,0:T(8,128)(2,1)S(1)}, bf16[128,2048]{1,0:T(8,128)(2,1)S(1)}) custom-call(s32[3]{0:T(128)S(1)} %pad_add_fusion.turns_ref, bf16[128,256]{1,0:T(8,128)(2,1)S(1)} %get-tuple-element.42.refs_0_.result_ref, ...), custom_call_target="tpu_custom_call" | custom-call | tf_op jit(solution)/shard_map/pallas_call | solution.py:121
  56.8 1.3 fusion.37
  59.2 1.3 fusion.5
  60.5 1.8 %copy.34 = f32[128,256]{1,0:T(8,128)} copy(f32[128,256]{0,1:T(8,128)} %fusion.5) | data formatting | bytes 262144 | tf_op jit(solution)/shard_map/dot_general | solution.py:33
  63.0 2.1 %fusion.3 = (f32[16,256]{1,0:T(8,128)S(1)}, f32[16,256]{1,0:T(8,128)S(1)}, f32[16,256]{1,0:T(8,128)S(1)}, f32[16,256]{1,0:T(8,128)S(1)}) fusion(f32[128,256]{1,0:T(8,128)} %copy.34, f32[16,256]{1,0:T(8,128)S(1)} %exponential_negate_fusion.1, f32[128,256]{1,0:T(8,128)} %copy-done.19), kind=kLoop, calls=%fused_computation.7 | loop fusion | flops 4702208 | bytes 344064 | tf_op jit(solution)/shard_map/reduce_sum | solution.py:281
  65.9 1.3 pad_maximum_fusion
  67.5 1.2 collective-permute-done.13
  71.6 6.7 %all-to-all-start.1 = ((bf16[8,49,128]{2,1,0:T(8,128)(2,1)}), bf16[8,49,128]{2,1,0:T(8,128)(2,1)}, u32[]{:S(2)}, u32[]{:S(2)}) async-start(bf16[8,49,128]{2,1,0:T(8,128)(2,1)} %broadcast_in_dim.86), calls=%async_computation.1 | async-start | bytes 229376 | tf_op jit(solution)/shard_map/all_to_all | solution.py:162
  79.4 8.3 %all-to-all-done.1 = bf16[8,49,128]{2,1,0:T(8,128)(2,1)} async-done(((bf16[8,49,128]{2,1,0:T(8,128)(2,1)}), bf16[8,49,128]{2,1,0:T(8,128)(2,1)}, u32[]{:S(2)}, u32[]{:S(2)}) %all-to-all-start.1) | async-done | bytes 100384 | tf_op jit(solution)/shard_map/all_to_all | solution.py:162
  87.7 0.9 convert_element_type.127
  88.6 1.4 multiply_reduce_fusion.8
  90.6 2.7 %collective-permute-start.14 = (f32[49,128]{1,0:T(8,128)}, f32[49,128]{1,0:T(8,128)}, u32[]{:S(2)}, u32[]{:S(2)}) collective-permute-start(f32[49,128]{1,0:T(8,128)} %pad_maximum_fusion.2), channel_id=1, source_target_pairs={{0,192},{4,196},{8,200},{12,204},{16,208},{20,212},{24,216},{28,22... | collective-permute-start | bytes 75272 | tf_op jit(solution)/shard_map/ppermute | solution.py:156
  93.4 0.8 collective-permute-start.15
  94.2 0.9 collective-permute-start.16
  95.0 1.8 %collective-permute-start.18 = (bf16[8,256,128]{2,1,0:T(8,128)(2,1)}, bf16[8,256,128]{2,1,0:T(8,128)(2,1)S(1)}, u32[]{:S(2)}, u32[]{:S(2)}) collective-permute-start(bf16[8,256,128]{2,1,0:T(8,128)(2,1)} %copy-done.11), channel_id=1, source_target_pairs={{0,64},{4,68},{8,72},{12,76},{16,80},{20,84},{24,88},{28,92},{32,9... | collective-permute-start | bytes 1572872 | tf_op jit(solution)/shard_map/ppermute | solution.py:156
  96.8 2.0 %collective-permute-start.19 = (bf16[8,256,128]{2,1,0:T(8,128)(2,1)}, bf16[8,256,128]{2,1,0:T(8,128)(2,1)S(1)}, u32[]{:S(2)}, u32[]{:S(2)}) collective-permute-start(bf16[8,256,128]{2,1,0:T(8,128)(2,1)} %copy-done.10), channel_id=1, source_target_pairs={{0,128},{4,132},{8,136},{12,140},{16,144},{20,148},{24,152},{28,15... | collective-permute-start | bytes 1572872 | tf_op jit(solution)/shard_map/ppermute | solution.py:156
  99.9 0.8 slice_add_fusion.1
  100.7 0.8 fusion.79
  101.6 2.0 %fusion.24 = f32[256,128]{0,1:T(8,128)} fusion(f32[128,129]{1,0:T(8,128)} %constant.98, f32[258,256]{1,0:T(8,128)} %copy-done.12, f32[258,256]{1,0:T(8,128)S(1)} %fusion.91), kind=kOutput, calls=%fused_computation.46 | convolution fusion | flops 50823936 | bytes 819200 | tf_op jit(solution)/shard_map/dot_general | solution.py:33
  103.6 1.3 collective-permute-start.10
  104.9 1.6 %collective-permute-start.11 = (bf16[128,2048]{1,0:T(8,128)(2,1)S(1)}, bf16[128,2048]{1,0:T(8,128)(2,1)}, u32[]{:S(2)}, u32[]{:S(2)}) collective-permute-start(bf16[128,2048]{1,0:T(8,128)(2,1)S(1)} %copy-done.5), channel_id=1, source_target_pairs={{0,2},{1,3},{2,0},{3,1},{4,6},{5,7},{6,4},{7,5},{8,10},{9,11},{10,... | collective-permute-start | bytes 1572872 | tf_op jit(solution)/shard_map/ppermute | solution.py:152
  107.1 1.4 fusion.72
  108.5 2.1 %collective-permute-done.18 = bf16[8,256,128]{2,1,0:T(8,128)(2,1)S(1)} collective-permute-done((bf16[8,256,128]{2,1,0:T(8,128)(2,1)}, bf16[8,256,128]{2,1,0:T(8,128)(2,1)S(1)}, u32[]{:S(2)}, u32[]{:S(2)}) %collective-permute-start.18) | collective-permute-done | bytes 524320 | tf_op jit(solution)/shard_map/ppermute | solution.py:156
  110.6 0.9 collective-permute-start.12
  111.5 9.2 %collective-permute-done.19 = bf16[8,256,128]{2,1,0:T(8,128)(2,1)S(1)} collective-permute-done((bf16[8,256,128]{2,1,0:T(8,128)(2,1)}, bf16[8,256,128]{2,1,0:T(8,128)(2,1)S(1)}, u32[]{:S(2)}, u32[]{:S(2)}) %collective-permute-start.19) | collective-permute-done | bytes 524320 | tf_op jit(solution)/shard_map/ppermute | solution.py:156
  120.7 1.1 add_convert_fusion
  121.7 3.5 %all-to-all-start.2 = ((bf16[8,256,128]{2,1,0:T(8,128)(2,1)}), bf16[8,256,128]{2,1,0:T(8,128)(2,1)S(1)}, u32[]{:S(2)}, u32[]{:S(2)}) async-start(bf16[8,256,128]{2,1,0:T(8,128)(2,1)} %add_convert_fusion), calls=%async_computation.2 | async-start | bytes 1048576 | tf_op jit(solution)/shard_map/all_to_all | solution.py:316
  125.3 1.1 multiply_reduce_fusion
  126.4 2.2 %fusion.35 = (bf16[128,256]{1,0:T(8,128)(2,1)}, bf16[128,256]{1,0:T(8,128)(2,1)}) fusion(bf16[128,256]{1,0:T(8,128)(2,1)S(1)} %copy-done.14, bf16[128,256]{1,0:T(8,128)(2,1)S(1)} %copy-done.13, f32[128,256]{1,0:T(8,128)} %copy-done.19, f32[256]{0:T(256)S(1)} %copy-done.33, f32[128,256]{1,0:T(8,128)S(1)} %multiply_reduce_fusion, f32[256,128]{0,1:T(8,128)} %fusion.24, ...), kind=kOutput, calls=%fused_computation.57 | convolution fusion | flops 51151616 | bytes 1344512 | tf_op jit(solution)/shard_map/dot_general | solution.py:33
  128.6 3.2 %collective-permute-done.12 = bf16[128,2048]{1,0:T(8,128)(2,1)} collective-permute-done((bf16[128,2048]{1,0:T(8,128)(2,1)S(1)}, bf16[128,2048]{1,0:T(8,128)(2,1)}, u32[]{:S(2)}, u32[]{:S(2)}) %collective-permute-start.12) | collective-permute-done | bytes 524320 | tf_op jit(solution)/shard_map/ppermute | solution.py:152
  131.8 2.5 %add_convert_fusion.1 = bf16[128,2048]{1,0:T(8,128)(2,1)} fusion(bf16[128,2048]{1,0:T(8,128)(2,1)} %collective-permute-done.12, bf16[128,2048]{1,0:T(8,128)(2,1)} %collective-permute-done.11, bf16[128,2048]{1,0:T(8,128)(2,1)} %collective-permute-done.10, bf16[128,2048]{1,0:T(8,128)(2,1)S(1)} %get-tuple-element.43), kind=kLoop, calls=%fused_computation.26 | loop fusion | flops 2097152 | bytes 2621440 | tf_op jit(solution)/shard_map/convert_element_type | solution.py:255
  134.2 7.2 %all-to-all-done.2 = bf16[8,256,128]{2,1,0:T(8,128)(2,1)S(1)} async-done(((bf16[8,256,128]{2,1,0:T(8,128)(2,1)}), bf16[8,256,128]{2,1,0:T(8,128)(2,1)S(1)}, u32[]{:S(2)}, u32[]{:S(2)}) %all-to-all-start.2) | async-done | bytes 524320 | tf_op jit(solution)/shard_map/all_to_all | solution.py:316
  (131 shorter events, 17.0 us)
Async XLA Ops:
  0.6 44.0 %copy-start.22 = (f32[16,256]{1,0:T(8,128)S(1)}, f32[16,256]{1,0:T(8,128)}, u32[]{:S(2)}) copy-start(f32[16,256]{1,0:T(8,128)} %param.14) | copy-start | bytes 49156
  0.6 16.2 %copy-start.1 = (bf16[128,2048]{1,0:T(8,128)(2,1)S(1)}, bf16[128,2048]{1,0:T(8,128)(2,1)}, u32[]{:S(2)}) copy-start(bf16[128,2048]{1,0:T(8,128)(2,1)} %refs_0_.1) | copy-start | bytes 1572868
  3.0 43.5 %copy-start.15 = (f32[258,128]{1,0:T(8,128)S(1)}, f32[258,128]{1,0:T(8,128)}, u32[]{:S(2)}) copy-start(f32[258,128]{1,0:T(8,128)} %constant.96.clone) | copy-start | bytes 396292
  3.1 1.3 collective-permute-start
  4.4 42.5 %copy-start.13 = (bf16[128,256]{1,0:T(8,128)(2,1)S(1)}, bf16[128,256]{1,0:T(8,128)(2,1)}, u32[]{:S(2)}) copy-start(bf16[128,256]{1,0:T(8,128)(2,1)} %param.12) | copy-start | bytes 196612
  4.4 42.5 %copy-start.14 = (bf16[128,256]{1,0:T(8,128)(2,1)S(1)}, bf16[128,256]{1,0:T(8,128)(2,1)}, u32[]{:S(2)}) copy-start(bf16[128,256]{1,0:T(8,128)(2,1)} %param.11) | copy-start | bytes 196612
  5.2 42.1 %copy-start.20 = (f32[128,129]{1,0:T(8,128)S(1)}, f32[128,129]{1,0:T(8,128)}, u32[]{:S(2)}) copy-start(f32[128,129]{1,0:T(8,128)} %constant.98) | copy-start | bytes 198148
  5.2 24.4 %all-to-all-start = ((bf16[32,32,128]{2,1,0:T(8,128)(2,1)}), bf16[32,32,128]{2,1,0:T(8,128)(2,1)S(1)}, u32[]{:S(2)}, u32[]{:S(2)}) async-start(bf16[32,32,128]{2,1,0:T(8,128)(2,1)} %broadcast_in_dim.49), calls=%async_computation | async-start | bytes 524288 | tf_op jit(solution)/shard_map/all_to_all | solution.py:167
  16.9 14.9 %collective-permute-start.3 = (bf16[128,2048]{1,0:T(8,128)(2,1)S(1)}, bf16[128,2048]{1,0:T(8,128)(2,1)S(1)}, u32[]{:S(2)}, u32[]{:S(2)}) collective-permute-start(bf16[128,2048]{1,0:T(8,128)(2,1)S(1)} %copy-done.1), channel_id=1, source_target_pairs={{0,1},{1,2},{2,3},{3,0},{4,5},{5,6},{6,7},{7,4},{8,9},{9,10},{10,1... | collective-permute-start | bytes 1572872 | tf_op jit(solution)/shard_map/ppermute | solution.py:152
  18.4 16.3 %collective-permute-start.4 = (bf16[128,2048]{1,0:T(8,128)(2,1)S(1)}, bf16[128,2048]{1,0:T(8,128)(2,1)S(1)}, u32[]{:S(2)}, u32[]{:S(2)}) collective-permute-start(bf16[128,2048]{1,0:T(8,128)(2,1)S(1)} %copy-done.1), channel_id=1, source_target_pairs={{0,2},{1,3},{2,0},{3,1},{4,6},{5,7},{6,4},{7,5},{8,10},{9,11},{10,... | collective-permute-start | bytes 1572872 | tf_op jit(solution)/shard_map/ppermute | solution.py:152
  19.5 24.4 %collective-permute-start.5 = (bf16[128,2048]{1,0:T(8,128)(2,1)S(1)}, bf16[128,2048]{1,0:T(8,128)(2,1)S(1)}, u32[]{:S(2)}, u32[]{:S(2)}) collective-permute-start(bf16[128,2048]{1,0:T(8,128)(2,1)S(1)} %copy-done.1), channel_id=1, source_target_pairs={{0,3},{1,0},{2,1},{3,2},{4,7},{5,4},{6,5},{7,6},{8,11},{9,8},{10,9... | collective-permute-start | bytes 1572872 | tf_op jit(solution)/shard_map/ppermute | solution.py:152
  21.7 26.0 %copy-start.17 = (f32[128,129]{1,0:T(8,128)S(1)}, f32[128,129]{1,0:T(8,128)}, u32[]{:S(2)}) copy-start(f32[128,129]{1,0:T(8,128)} %constant.99) | copy-start | bytes 198148
  21.7 26.0 %copy-start.23 = (bf16[128,256]{1,0:T(8,128)(2,1)S(1)}, bf16[128,256]{1,0:T(8,128)(2,1)}, u32[]{:S(2)}) copy-start(bf16[128,256]{1,0:T(8,128)(2,1)} %param.10) | copy-start | bytes 196612
  21.7 26.0 %copy-start.32 = (f32[256]{0:T(256)S(1)}, f32[256]{0:T(256)}, u32[]{:S(2)}) copy-start(f32[256]{0:T(256)} %param.15) | copy-start | bytes 3076
  30.4 13.5 %collective-permute-start.1 = (f32[32,128]{1,0:T(8,128)S(1)}, f32[32,128]{1,0:T(8,128)S(1)}, u32[]{:S(2)}, u32[]{:S(2)}) collective-permute-start(f32[32,128]{1,0:T(8,128)S(1)} %pad_maximum_fusion.6), channel_id=1, source_target_pairs={{0,4},{4,0},{8,12},{12,8},{16,20},{20,16},{24,28},{28,24},{32,36},... | collective-permute-start | bytes 49160 | tf_op jit(solution)/shard_map/ppermute | solution.py:149
  30.4 18.5 %collective-permute-start.6 = (bf16[128,2048]{1,0:T(8,128)(2,1)S(1)}, bf16[128,2048]{1,0:T(8,128)(2,1)S(1)}, u32[]{:S(2)}, u32[]{:S(2)}) collective-permute-start(bf16[128,2048]{1,0:T(8,128)(2,1)S(1)} %copy-done.1), channel_id=1, source_target_pairs={{0,4},{4,0},{8,12},{12,8},{16,20},{20,16},{24,28},{28,24},{32,36},... | collective-permute-start | bytes 1572872 | tf_op jit(solution)/shard_map/ppermute | solution.py:149
  31.7 18.0 %collective-permute-start.7 = (bf16[128,2048]{1,0:T(8,128)(2,1)S(1)}, bf16[128,2048]{1,0:T(8,128)(2,1)S(1)}, u32[]{:S(2)}, u32[]{:S(2)}) collective-permute-start(bf16[128,2048]{1,0:T(8,128)(2,1)S(1)} %collective-permute-done.3.refs_3_.refs_1_), channel_id=1, source_target_pairs={{0,4},{4,0},{8,12},{12,8},{16,20},{20,16},{24,28},{28,24},{32,36},... | collective-permute-start | bytes 1572872 | tf_op jit(solution)/shard_map/ppermute | solution.py:149
  34.7 15.0 %collective-permute-start.8 = (bf16[128,2048]{1,0:T(8,128)(2,1)S(1)}, bf16[128,2048]{1,0:T(8,128)(2,1)S(1)}, u32[]{:S(2)}, u32[]{:S(2)}) collective-permute-start(bf16[128,2048]{1,0:T(8,128)(2,1)S(1)} %collective-permute-done.4.refs_4_.refs_2_), channel_id=1, source_target_pairs={{0,4},{4,0},{8,12},{12,8},{16,20},{20,16},{24,28},{28,24},{32,36},... | collective-permute-start | bytes 1572872 | tf_op jit(solution)/shard_map/ppermute | solution.py:149
  43.9 5.8 %collective-permute-start.9 = (bf16[128,2048]{1,0:T(8,128)(2,1)S(1)}, bf16[128,2048]{1,0:T(8,128)(2,1)S(1)}, u32[]{:S(2)}, u32[]{:S(2)}) collective-permute-start(bf16[128,2048]{1,0:T(8,128)(2,1)S(1)} %collective-permute-done.5.refs_5_.refs_3_), channel_id=1, source_target_pairs={{0,4},{4,0},{8,12},{12,8},{16,20},{20,16},{24,28},{28,24},{32,36},... | collective-permute-start | bytes 1572872 | tf_op jit(solution)/shard_map/ppermute | solution.py:149
  48.0 1.7 %collective-permute-start.2 = (bf16[128,256]{1,0:T(8,128)(2,1)S(1)}, bf16[128,256]{1,0:T(8,128)(2,1)S(1)}, u32[]{:S(2)}, u32[]{:S(2)}) collective-permute-start(bf16[128,256]{1,0:T(8,128)(2,1)S(1)} %get-tuple-element.42.refs_0_.result_ref), channel_id=1, source_target_pairs={{0,4},{4,0},{8,12},{12,8},{16,20},{20,16},{24,28},{28,24},{32,36},... | collective-permute-start | bytes 196616 | tf_op jit(solution)/shard_map/ppermute | solution.py:149
  48.9 5.2 %copy-start = (bf16[256,8192]{1,0:T(8,128)(2,1)S(1)}, bf16[256,8192]{1,0:T(8,128)(2,1)}, u32[]{:S(2)}) copy-start(bf16[256,8192]{1,0:T(8,128)(2,1)} %refs_4_.1) | copy-start | bytes 12582916
  54.1 2.7 %copy-start.8 = (bf16[8,256,128]{2,1,0:T(8,128)(2,1)}, bf16[8,256,128]{2,1,0:T(8,128)(2,1)S(1)}, u32[]{:S(2)}) copy-start(bf16[8,256,128]{2,1,0:T(8,128)(2,1)S(1)} %get-tuple-element.41) | copy-start | bytes 1572868
  54.1 2.7 %copy-start.24 = (bf16[128,256]{1,0:T(8,128)(2,1)S(1)}, bf16[128,256]{1,0:T(8,128)(2,1)}, u32[]{:S(2)}) copy-start(bf16[128,256]{1,0:T(8,128)(2,1)} %param.10) | copy-start | bytes 196612
  54.1 4.0 %copy-start.16 = (f32[258,128]{1,0:T(8,128)S(1)}, f32[258,128]{1,0:T(8,128)}, u32[]{:S(2)}) copy-start(f32[258,128]{1,0:T(8,128)} %constant.96.clone) | copy-start | bytes 396292
  54.1 4.4 %copy-start.21 = (f32[128,129]{1,0:T(8,128)S(1)}, f32[128,129]{1,0:T(8,128)}, u32[]{:S(2)}) copy-start(f32[128,129]{1,0:T(8,128)} %constant.98) | copy-start | bytes 198148
  54.1 5.1 %copy-start.18 = (f32[128,129]{1,0:T(8,128)S(1)}, f32[128,129]{1,0:T(8,128)}, u32[]{:S(2)}) copy-start(f32[128,129]{1,0:T(8,128)} %constant.99) | copy-start | bytes 198148
  56.8 2.4 %copy-start.4 = (bf16[128,2048]{1,0:T(8,128)(2,1)}, bf16[128,2048]{1,0:T(8,128)(2,1)S(1)}, u32[]{:S(2)}) copy-start(bf16[128,2048]{1,0:T(8,128)(2,1)S(1)} %get-tuple-element.45) | copy-start | bytes 1572868
  58.5 40.3 %copy-start.9 = (bf16[8,256,128]{2,1,0:T(8,128)(2,1)S(1)}, bf16[8,256,128]{2,1,0:T(8,128)(2,1)}, u32[]{:S(2)}) copy-start(bf16[8,256,128]{2,1,0:T(8,128)(2,1)} %copy-done.8) | copy-start | bytes 1572868
  60.5 43.1 %copy-start.7 = (bf16[128,2048]{1,0:T(8,128)(2,1)S(1)}, bf16[128,2048]{1,0:T(8,128)(2,1)}, u32[]{:S(2)}) copy-start(bf16[128,2048]{1,0:T(8,128)(2,1)} %copy-done.6) | copy-start | bytes 1572868
  60.5 44.4 %copy-start.5 = (bf16[128,2048]{1,0:T(8,128)(2,1)S(1)}, bf16[128,2048]{1,0:T(8,128)(2,1)}, u32[]{:S(2)}) copy-start(bf16[128,2048]{1,0:T(8,128)(2,1)} %copy-done.4) | copy-start | bytes 1572868
  60.5 50.1 %copy-start.3 = (bf16[128,2048]{1,0:T(8,128)(2,1)S(1)}, bf16[128,2048]{1,0:T(8,128)(2,1)}, u32[]{:S(2)}) copy-start(bf16[128,2048]{1,0:T(8,128)(2,1)} %copy-done.2) | copy-start | bytes 1572868
  63.0 4.2 %copy-start.31 = (f32[16,256]{1,0:T(8,128)}, f32[16,256]{1,0:T(8,128)S(1)}, u32[]{:S(2)}) copy-start(f32[16,256]{1,0:T(8,128)S(1)} %exponential_negate_fusion.1) | copy-start | bytes 49156
  67.2 1.6 %collective-permute-start.13 = (f32[49,256]{1,0:T(8,128)}, f32[49,256]{1,0:T(8,128)}, u32[]{:S(2)}, u32[]{:S(2)}) collective-permute-start(f32[49,256]{1,0:T(8,128)} %pad_maximum_fusion), channel_id=1, source_target_pairs={{0,4},{4,0},{8,12},{12,8},{16,20},{20,16},{24,28},{28,24},{32,36},... | collective-permute-start | bytes 150536 | tf_op jit(solution)/shard_map/ppermute | solution.py:149
  71.6 16.0 %all-to-all-start.1 = ((bf16[8,49,128]{2,1,0:T(8,128)(2,1)}), bf16[8,49,128]{2,1,0:T(8,128)(2,1)}, u32[]{:S(2)}, u32[]{:S(2)}) async-start(bf16[8,49,128]{2,1,0:T(8,128)(2,1)} %broadcast_in_dim.86), calls=%async_computation.1 | async-start | bytes 229376 | tf_op jit(solution)/shard_map/all_to_all | solution.py:162
  90.6 8.2 %collective-permute-start.14 = (f32[49,128]{1,0:T(8,128)}, f32[49,128]{1,0:T(8,128)}, u32[]{:S(2)}, u32[]{:S(2)}) collective-permute-start(f32[49,128]{1,0:T(8,128)} %pad_maximum_fusion.2), channel_id=1, source_target_pairs={{0,192},{4,196},{8,200},{12,204},{16,208},{20,212},{24,216},{28,22... | collective-permute-start | bytes 75272 | tf_op jit(solution)/shard_map/ppermute | solution.py:156
  93.4 6.2 %collective-permute-start.15 = (f32[49,128]{1,0:T(8,128)}, f32[49,128]{1,0:T(8,128)}, u32[]{:S(2)}, u32[]{:S(2)}) collective-permute-start(f32[49,128]{1,0:T(8,128)} %pad_maximum_fusion.2), channel_id=1, source_target_pairs={{0,128},{4,132},{8,136},{12,140},{16,144},{20,148},{24,152},{28,15... | collective-permute-start | bytes 75272 | tf_op jit(solution)/shard_map/ppermute | solution.py:156
  94.2 5.8 %collective-permute-start.16 = (f32[49,128]{1,0:T(8,128)}, f32[49,128]{1,0:T(8,128)}, u32[]{:S(2)}, u32[]{:S(2)}) collective-permute-start(f32[49,128]{1,0:T(8,128)} %pad_maximum_fusion.2), channel_id=1, source_target_pairs={{0,64},{4,68},{8,72},{12,76},{16,80},{20,84},{24,88},{28,92},{32,9... | collective-permute-start | bytes 75272 | tf_op jit(solution)/shard_map/ppermute | solution.py:156
  95.0 15.6 %collective-permute-start.18 = (bf16[8,256,128]{2,1,0:T(8,128)(2,1)}, bf16[8,256,128]{2,1,0:T(8,128)(2,1)S(1)}, u32[]{:S(2)}, u32[]{:S(2)}) collective-permute-start(bf16[8,256,128]{2,1,0:T(8,128)(2,1)} %copy-done.11), channel_id=1, source_target_pairs={{0,64},{4,68},{8,72},{12,76},{16,80},{20,84},{24,88},{28,92},{32,9... | collective-permute-start | bytes 1572872 | tf_op jit(solution)/shard_map/ppermute | solution.py:156
  96.8 23.8 %collective-permute-start.19 = (bf16[8,256,128]{2,1,0:T(8,128)(2,1)}, bf16[8,256,128]{2,1,0:T(8,128)(2,1)S(1)}, u32[]{:S(2)}, u32[]{:S(2)}) collective-permute-start(bf16[8,256,128]{2,1,0:T(8,128)(2,1)} %copy-done.10), channel_id=1, source_target_pairs={{0,128},{4,132},{8,136},{12,140},{16,144},{20,148},{24,152},{28,15... | collective-permute-start | bytes 1572872 | tf_op jit(solution)/shard_map/ppermute | solution.py:156
  98.9 21.8 %collective-permute-start.20 = (bf16[8,256,128]{2,1,0:T(8,128)(2,1)S(1)}, bf16[8,256,128]{2,1,0:T(8,128)(2,1)S(1)}, u32[]{:S(2)}, u32[]{:S(2)}) collective-permute-start(bf16[8,256,128]{2,1,0:T(8,128)(2,1)S(1)} %copy-done.9), channel_id=1, source_target_pairs={{0,192},{4,196},{8,200},{12,204},{16,208},{20,212},{24,216},{28,22... | collective-permute-start | bytes 1572872 | tf_op jit(solution)/shard_map/ppermute | solution.py:156
  101.5 3.4 %collective-permute-start.17 = (f32[49,128]{1,0:T(8,128)S(1)}, f32[49,128]{1,0:T(8,128)S(1)}, u32[]{:S(2)}, u32[]{:S(2)}) collective-permute-start(f32[49,128]{1,0:T(8,128)S(1)} %pad_maximum_fusion.3), channel_id=1, source_target_pairs={{0,4},{4,0},{8,12},{12,8},{16,20},{20,16},{24,28},{28,24},{32,36},... | collective-permute-start | bytes 75272 | tf_op jit(solution)/shard_map/ppermute | solution.py:149
  103.6 21.6 %copy-start.35 = (f32[128]{0:T(128)S(1)}, f32[128]{0:T(128)}, u32[]{:S(2)}) copy-start(f32[128]{0:T(128)} %copy-done.34) | copy-start | bytes 1540
  103.6 25.0 %collective-permute-start.10 = (bf16[128,2048]{1,0:T(8,128)(2,1)S(1)}, bf16[128,2048]{1,0:T(8,128)(2,1)}, u32[]{:S(2)}, u32[]{:S(2)}) collective-permute-start(bf16[128,2048]{1,0:T(8,128)(2,1)S(1)} %copy-done.7), channel_id=1, source_target_pairs={{0,1},{1,2},{2,3},{3,0},{4,5},{5,6},{6,7},{7,4},{8,9},{9,10},{10,1... | collective-permute-start | bytes 1572872 | tf_op jit(solution)/shard_map/ppermute | solution.py:152
  104.9 23.7 %collective-permute-start.11 = (bf16[128,2048]{1,0:T(8,128)(2,1)S(1)}, bf16[128,2048]{1,0:T(8,128)(2,1)}, u32[]{:S(2)}, u32[]{:S(2)}) collective-permute-start(bf16[128,2048]{1,0:T(8,128)(2,1)S(1)} %copy-done.5), channel_id=1, source_target_pairs={{0,2},{1,3},{2,0},{3,1},{4,6},{5,7},{6,4},{7,5},{8,10},{9,11},{10,... | collective-permute-start | bytes 1572872 | tf_op jit(solution)/shard_map/ppermute | solution.py:152
  110.6 15.8 %copy-start.33 = (f32[256]{0:T(256)S(1)}, f32[256]{0:T(256)}, u32[]{:S(2)}) copy-start(f32[256]{0:T(256)} %param.15) | copy-start | bytes 3076
  110.6 21.1 %collective-permute-start.12 = (bf16[128,2048]{1,0:T(8,128)(2,1)S(1)}, bf16[128,2048]{1,0:T(8,128)(2,1)}, u32[]{:S(2)}, u32[]{:S(2)}) collective-permute-start(bf16[128,2048]{1,0:T(8,128)(2,1)S(1)} %copy-done.3), channel_id=1, source_target_pairs={{0,3},{1,0},{2,1},{3,2},{4,7},{5,4},{6,5},{7,6},{8,11},{9,8},{10,9... | collective-permute-start | bytes 1572872 | tf_op jit(solution)/shard_map/ppermute | solution.py:152
  120.7 4.6 %copy-start.30 = (f32[16,256]{1,0:T(8,128)S(1)}, f32[16,256]{1,0:T(8,128)}, u32[]{:S(2)}) copy-start(f32[16,256]{1,0:T(8,128)} %get-tuple-element.80) | copy-start | bytes 49156
  121.7 19.7 %all-to-all-start.2 = ((bf16[8,256,128]{2,1,0:T(8,128)(2,1)}), bf16[8,256,128]{2,1,0:T(8,128)(2,1)S(1)}, u32[]{:S(2)}, u32[]{:S(2)}) async-start(bf16[8,256,128]{2,1,0:T(8,128)(2,1)} %add_convert_fusion), calls=%async_computation.2 | async-start | bytes 1048576 | tf_op jit(solution)/shard_map/all_to_all | solution.py:316
  (12 other events, 14.3 us)

commit v8 on v7

--- a/solution.py
+++ b/solution.py
@@ -140,7 +140,6 @@
     nz = ctx // (2 * ny)
     core = dev % 2
     pair = dev // 2
-    zz = pair % nz
     pairs = ctx // 2
     yy = dev // (2 * nz)
     width = feats // (2 * nz)
@@ -157,9 +156,12 @@
 
     z_groups = [[i * 2 * nz + j * 2 + k for j in range(nz)] for i in range(ny) for k in range(2)]
 
+    per = 2 * nz
+
     def of_plane(a):
-        copies = jnp.broadcast_to(a[None], (nz, *a.shape))
-        return lax.all_to_all(copies, "ctx", 0, 0, tiled=True, axis_index_groups=z_groups)
+        copies = jnp.broadcast_to(a[None], (per, *a.shape))
+        groups = [[i * per + j for j in range(per)] for i in range(ny)]
+        return lax.all_to_all(copies, "ctx", 0, 0, tiled=True, axis_index_groups=groups)
 
     def of_pairs(a):
         copies = jnp.broadcast_to(a[None], (pairs, *a.shape))
@@ -200,10 +202,8 @@
     total_lag = decay_h * (block * f_h[:modes] + f_h[modes:]) + s_h[modes:]
     to_send = jnp.concatenate([total, total_lag], 0).astype(BF16)
     gathered = of_pairs(to_send).astype(F32)
-    place = jnp.arange(nz, dtype=jnp.int32)
     every = jnp.arange(pairs, dtype=jnp.int32)
     per_pair = 2 * block
-    per_plane = per_pair * nz
 
     def weights(which, gap):
         gap = jnp.where(which, gap, 0).astype(F32)[:, None, None] * per_pair
@@ -267,7 +267,6 @@
     gain = residues * norm
     fall = jnp.exp(-rate[:, None, :] * rows)
     rise = jnp.exp(-rate[:, None, :] * (block - rows))
-    fall_block = jnp.exp(-rate * block)
     gc = grad_gated * outer_f
     grad_outer = (grad_gated * gated).astype(BF16)
 
@@ -281,31 +280,28 @@
     sum_a = g_st * x_in + jnp.sum(fl, 1)
     sum_b = g_lag * x_in + g_st * x_lag + jnp.sum(fl * rows, 1)
     sum_skip = jnp.sum(gc * u, 0, keepdims=True)
-    mine_g = jnp.concatenate([g_st, sum_a, sum_b, sum_skip], 0)
-    theirs_g = swap_core(mine_g)
-    later = jnp.where(core == 0, theirs_g[:modes], mine_g[:modes])
-    mine_h, theirs_h = my_half(mine_g), my_half(theirs_g)
-    early_h = jnp.where(core == 0, mine_h[:modes], theirs_h[:modes])
-    total_g = early_h + decay_h * my_half(later)
-    sent = jnp.concatenate([total_g, mine_h[modes:] + theirs_h[modes:]], 0).astype(BF16)
+    sent = jnp.concatenate([g_st, sum_a, sum_b, sum_skip], 0).astype(BF16)
     got = of_plane(sent)
+    slot = dev % per
+    slots = jnp.arange(per, dtype=jnp.int32)
+
+    def falls(which, steps):
+        steps = jnp.where(which, steps, 0).astype(F32)[:, None, None] * block
+        return jnp.where(which[:, None, None], jnp.exp(-rate[None] * steps), 0.0)
+
     got = got.astype(F32)
-    plane_h = jnp.sum(weights(place >= 0, place)[0] * got[:, :modes], 0)
-    plane_sums = jnp.sum(got[:, modes:], 0)
-    plane_g = jnp.concatenate([plane_h, plane_sums], 0)
-    h_half = jnp.sum(weights(place > zz, place - zz - 1)[0] * got[:, :modes], 0)
-    y_h, sums_half = 0.0, plane_sums
+    h_in = jnp.sum(falls(slots > slot, slots - slot - 1) * got[:, :modes], 0)
+    plane_h = jnp.sum(falls(slots >= 0, slots) * got[:, :modes], 0)
+    sums = jnp.sum(got[:, modes:], 0)
+    plane_g = jnp.concatenate([plane_h, sums], 0)
+    y_h = 0.0
     for k in range(1, ny):
         came = shift_y(plane_g, -k)
-        w = jnp.exp(-rate_h * float(per_plane * (k - 1)))
+        w = jnp.exp(-rate * float(block * per * (k - 1)))
         y_h = y_h + jnp.where(yy + k < ny, w * came[:modes], 0.0)
-        sums_half = sums_half + came[modes:]
-    h_half = h_half + jnp.exp(-rate_h * (per_pair * (nz - 1 - zz)).astype(F32)) * y_h
-    final = both_halves(jnp.concatenate([h_half, sums_half], 0))
-    h_pair = final[:modes]
-    h_in = jnp.where(core == 0, later + fall_block * h_pair, h_pair)
-    tot_a, tot_b = final[modes : 2 * modes], final[2 * modes : 3 * modes]
-    grad_skip = final[3 * modes]
+        sums = sums + came[modes:]
+    h_in = h_in + jnp.exp(-rate * (block * (per - 1 - slot)).astype(F32)) * y_h
+    tot_a, tot_b, grad_skip = sums[:modes], sums[modes : 2 * modes], sums[2 * modes]
     grad_residues = norm * tot_a
     grad_decay = rate * residues * (jnp.exp(-2.0 * rate) / norm * tot_a - norm * tot_b)
     corr_in = corr_local + jnp.sum((gain * h_in)[:, None, :] * rise, 0)

time: 145 us -> 114 us (0.79)
  waiting for transfers between devices: 54.4 us -> 37 us
  other arithmetic: 26.6 us -> 15.4 us
    ppermute x6, waiting for transfers between devices: 11.7 us -> 1.59 us  [shift_y(): lax.ppermute(a, 'ctx', [(i, (i // per + k) % ny * per + i % per) for i in...]
    all_to_all x1, waiting for transfers between devices: 8.31 us -> 4.41 us  [of_plane(): lax.all_to_all(copies, 'ctx', 0, 0, tiled=True, axis_index_groups=groups)]
    concatenate x5 -> x2, other arithmetic: 2.51 us -> 0.02 us  [the longest x1 0.01 us: body(): sent = jnp.concatenate([g_st, sum_a, sum_b, sum_skip], 0).astype(BF16)]
    add x3 -> x1, other arithmetic: 2.3 us -> 0.02 us  [body(): sums = sums + came[modes:]]
    all_to_all x1, waiting for transfers between devices: 7.2 us -> 5.03 us  [body(): lax.all_to_all(summed_y, 'ctx', 0, 0, tiled=True, axis_index_groups=z_gro...]
    unnamed x72 -> x66, local copies, waits for them, and re-layouts: 2.34 us -> 0.25 us
    another operation x4 -> x2, other arithmetic: 1.52 us -> 0.03 us
    ppermute x9 -> x7, waiting for transfers between devices: 3.24 us -> 2.01 us  [swap_core(): return lax.ppermute(a, 'ctx', [(i, i ^ 1) for i in range(ctx)])]
  transfers between devices with their start and end apart: 24 -> 22, of which waited for: 13 -> 11; matrix products, arithmetic and copies ran while one was open for 12% -> 19% of each run, Pallas kernels for 0% -> 2%
where the time goes in v8:
time: 114 us; the launch traced here: 112 us
  starting transfers between devices  42.1 us (37%)
  waiting for transfers between devices  37 us (32%)
  other arithmetic  15.4 us (14%)
  matrix products  6.54 us (6%)
  Pallas kernels  5.75 us (5%)
  local copies, waits for them, and re-layouts  4.09 us (4%)
  between operations  1.32 us (1%)
    ppermute x6, waiting for transfers between devices, shift_tp(): return lax.ppermute(a, 'tp', [(i, (i + k) % tps) for i in range(tps)])  16.2 us
    all_to_all x1, starting transfers between devices, of_pairs(): lax.all_to_all(copies, 'ctx', 0, 0, tiled=True, axis_index_groups=groups)  11.6 us
    ppermute x6, starting transfers between devices, shift_tp(): return lax.ppermute(a, 'tp', [(i, (i + k) % tps) for i in range(tps)])  9.32 us
    ppermute x6, starting transfers between devices, shift_y(): lax.ppermute(a, 'ctx', [(i, (i // per + k) % ny * per + i % per) for i in...  9.19 us
    all_to_all x1, waiting for transfers between devices, of_pairs(): lax.all_to_all(copies, 'ctx', 0, 0, tiled=True, axis_index_groups=groups)  7.84 us
    all_to_all x1, starting transfers between devices, of_plane(): lax.all_to_all(copies, 'ctx', 0, 0, tiled=True, axis_index_groups=groups)  6.81 us
    dot_general x6, matrix products, back(): jnp.dot(inverse, jnp.concatenate([real_part, imag_part], 0), precision=EX...  5.43 us
    all_to_all x1, waiting for transfers between devices, body(): lax.all_to_all(summed_y, 'ctx', 0, 0, tiled=True, axis_index_groups=z_gro...  5.03 us
  transfers between devices with their start and end apart: 22, of which 11 were waited for; matrix products, arithmetic and copies ran while one was open for 19% of the time, Pallas kernels for 2%

profile of v8, /device:TPU:2, one launch (start us, length us, event | category | flops | bytes accessed | tf_op | source)
XLA Modules:
  0.0 112.2 jit_solution(3913715660970809118)
XLA Ops:
  0.7 0.8 fusion.84
  1.5 0.9 convert_multiply_fusion.5
  2.4 0.7 fusion.4
  3.2 1.2 %collective-permute-done = f32[32,256]{1,0:T(8,128)S(1)} collective-permute-done((f32[32,256]{1,0:T(8,128)S(1)}, f32[32,256]{1,0:T(8,128)S(1)}, u32[]{:S(2)}, u32[]{:S(2)}) %collective-permute-start) | collective-permute-done | bytes 32800 | tf_op jit(solution)/shard_map/ppermute | solution.py:148
  4.5 0.7 broadcast_in_dim.47
  5.2 11.6 %all-to-all-start = ((bf16[32,32,128]{2,1,0:T(8,128)(2,1)}), bf16[32,32,128]{2,1,0:T(8,128)(2,1)S(1)}, u32[]{:S(2)}, u32[]{:S(2)}) async-start(bf16[32,32,128]{2,1,0:T(8,128)(2,1)} %broadcast_in_dim.47), calls=%async_computation | async-start | bytes 524288 | tf_op jit(solution)/shard_map/all_to_all | solution.py:169
  16.8 1.6 %collective-permute-start.3 = (bf16[128,2048]{1,0:T(8,128)(2,1)S(1)}, bf16[128,2048]{1,0:T(8,128)(2,1)S(1)}, u32[]{:S(2)}, u32[]{:S(2)}) collective-permute-start(bf16[128,2048]{1,0:T(8,128)(2,1)S(1)} %copy-done.1), channel_id=1, source_target_pairs={{0,1},{1,2},{2,3},{3,0},{4,5},{5,6},{6,7},{7,4},{8,9},{9,10},{10,1... | collective-permute-start | bytes 1572872 | tf_op jit(solution)/shard_map/ppermute | solution.py:151
  18.4 1.1 collective-permute-start.4
  19.5 2.2 %collective-permute-start.5 = (bf16[128,2048]{1,0:T(8,128)(2,1)S(1)}, bf16[128,2048]{1,0:T(8,128)(2,1)S(1)}, u32[]{:S(2)}, u32[]{:S(2)}) collective-permute-start(bf16[128,2048]{1,0:T(8,128)(2,1)S(1)} %copy-done.1), channel_id=1, source_target_pairs={{0,3},{1,0},{2,1},{3,2},{4,7},{5,4},{6,5},{7,6},{8,11},{9,8},{10,9... | collective-permute-start | bytes 1572872 | tf_op jit(solution)/shard_map/ppermute | solution.py:151
  21.7 7.8 %all-to-all-done = bf16[32,32,128]{2,1,0:T(8,128)(2,1)S(1)} async-done(((bf16[32,32,128]{2,1,0:T(8,128)(2,1)}), bf16[32,32,128]{2,1,0:T(8,128)(2,1)S(1)}, u32[]{:S(2)}, u32[]{:S(2)}) %all-to-all-start) | async-done | bytes 262176 | tf_op jit(solution)/shard_map/all_to_all | solution.py:169
  30.4 1.3 %collective-permute-done.3.refs_3_.refs_1_ = bf16[128,2048]{1,0:T(8,128)(2,1)S(1)} collective-permute-done((bf16[128,2048]{1,0:T(8,128)(2,1)S(1)}, bf16[128,2048]{1,0:T(8,128)(2,1)S(1)}, u32[]{:S(2)}, u32[]{:S(2)}) %collective-permute-start.3) | collective-permute-done | bytes 524320 | tf_op jit(solution)/shard_map/ppermute | solution.py:151
  31.7 3.0 %collective-permute-done.4.refs_4_.refs_2_ = bf16[128,2048]{1,0:T(8,128)(2,1)S(1)} collective-permute-done((bf16[128,2048]{1,0:T(8,128)(2,1)S(1)}, bf16[128,2048]{1,0:T(8,128)(2,1)S(1)}, u32[]{:S(2)}, u32[]{:S(2)}) %collective-permute-start.4) | collective-permute-done | bytes 524320 | tf_op jit(solution)/shard_map/ppermute | solution.py:151
  34.7 9.2 %collective-permute-done.5.refs_5_.refs_3_ = bf16[128,2048]{1,0:T(8,128)(2,1)S(1)} collective-permute-done((bf16[128,2048]{1,0:T(8,128)(2,1)S(1)}, bf16[128,2048]{1,0:T(8,128)(2,1)S(1)}, u32[]{:S(2)}, u32[]{:S(2)}) %collective-permute-start.5) | collective-permute-done | bytes 524320 | tf_op jit(solution)/shard_map/ppermute | solution.py:151
  43.9 0.6 fusion.77
  44.6 0.8 fusion.83
  47.3 0.6 collective-permute-start.2
  48.0 0.8 collective-permute-done.2.refs_1_
  48.9 3.1 %shard_map.161 = (bf16[8,256,128]{2,1,0:T(8,128)(2,1)S(1)}, bf16[8,256,128]{2,1,0:T(8,128)(2,1)}, bf16[8,256,128]{2,1,0:T(8,128)(2,1)}, bf16[8,256,128]{2,1,0:T(8,128)(2,1)}) custom-call(s32[3]{0:T(128)S(1)} %pad_add_fusion.turns_ref, bf16[128,256]{1,0:T(8,128)(2,1)S(1)} %get-tuple-element.42.refs_0_.result_ref, ...), custom_call_target="tpu_custom_call" | custom-call | tf_op jit(solution)/shard_map/pallas_call | solution.py:80
  52.0 2.8 %collective-permute-start.18 = (bf16[8,256,128]{2,1,0:T(8,128)(2,1)}, bf16[8,256,128]{2,1,0:T(8,128)(2,1)}, u32[]{:S(2)}, u32[]{:S(2)}) collective-permute-start(bf16[8,256,128]{2,1,0:T(8,128)(2,1)} %get-tuple-element.41), channel_id=1, source_target_pairs={{0,192},{4,196},{8,200},{12,204},{16,208},{20,212},{24,216},{28,22... | collective-permute-start | bytes 1572872 | tf_op jit(solution)/shard_map/ppermute | solution.py:155
  54.8 0.8 collective-permute-start.17
  55.6 0.9 collective-permute-start.16
  56.5 2.6 %shard_map.162 = (f32[128,256]{1,0:T(8,128)S(1)}, bf16[128,2048]{1,0:T(8,128)(2,1)S(1)}, bf16[128,2048]{1,0:T(8,128)(2,1)S(1)}, bf16[128,2048]{1,0:T(8,128)(2,1)S(1)}, bf16[128,2048]{1,0:T(8,128)(2,1)S(1)}) custom-call(s32[3]{0:T(128)S(1)} %pad_add_fusion.turns_ref, bf16[128,256]{1,0:T(8,128)(2,1)S(1)} %get-tuple-element.42.refs_0_.result_ref, ...), custom_call_target="tpu_custom_call" | custom-call | tf_op jit(solution)/shard_map/pallas_call | solution.py:121
  59.2 0.7 fusion.37
  60.4 0.6 fusion.17
  61.1 1.3 %fusion.5 = f32[128,256]{0,1:T(8,128)} fusion(f32[256,128]{1,0:T(8,128)S(1)} %fusion.17, f32[128,129]{1,0:T(8,128)S(1)} %copy-done.13, f32[258,256]{1,0:T(8,128)S(1)} %fusion.86, f32[258,256]{1,0:T(8,128)S(1)} %fusion.39), kind=kOutput, calls=%fused_computation.15 | convolution fusion | flops 50856704 | bytes 950272 | tf_op jit(solution)/shard_map/dot_general | solution.py:33
  62.3 1.7 %copy.34 = f32[128,256]{1,0:T(8,128)} copy(f32[128,256]{0,1:T(8,128)} %fusion.5) | data formatting | bytes 262144 | tf_op jit(solution)/shard_map/dot_general | solution.py:33
  64.1 2.0 %fusion.3 = (f32[16,256]{1,0:T(8,128)S(1)}, f32[16,256]{1,0:T(8,128)S(1)}, f32[16,256]{1,0:T(8,128)S(1)}, f32[16,256]{1,0:T(8,128)S(1)}) fusion(f32[128,256]{1,0:T(8,128)} %copy.34, f32[16,256]{1,0:T(8,128)S(1)} %exponential_negate_fusion.1, f32[128,256]{1,0:T(8,128)S(1)} %get-tuple-element.71), kind=kLoop, calls=%fused_computation.7 | loop fusion | flops 4702208 | bytes 344064 | tf_op jit(solution)/shard_map/reduce_sum | solution.py:280
  66.2 0.8 broadcast_in_dim.52
  67.0 6.8 %all-to-all-start.1 = ((bf16[16,49,256]{2,1,0:T(8,128)(2,1)}), bf16[16,49,256]{2,1,0:T(8,128)(2,1)}, u32[]{:S(2)}, u32[]{:S(2)}) async-start(bf16[16,49,256]{2,1,0:T(8,128)(2,1)} %broadcast_in_dim.52), calls=%async_computation.1 | async-start | bytes 917504 | tf_op jit(solution)/shard_map/all_to_all | solution.py:164
  73.8 1.1 collective-permute-start.12
  75.0 1.7 %collective-permute-start.11 = (bf16[128,2048]{1,0:T(8,128)(2,1)S(1)}, bf16[128,2048]{1,0:T(8,128)(2,1)}, u32[]{:S(2)}, u32[]{:S(2)}) collective-permute-start(bf16[128,2048]{1,0:T(8,128)(2,1)S(1)} %copy-done.5), channel_id=1, source_target_pairs={{0,2},{1,3},{2,0},{3,1},{4,6},{5,7},{6,4},{7,5},{8,10},{9,11},{10,... | collective-permute-start | bytes 1572872 | tf_op jit(solution)/shard_map/ppermute | solution.py:151
  76.7 1.9 %fusion.24 = f32[256,128]{0,1:T(8,128)} fusion(f32[128,129]{1,0:T(8,128)} %constant.96, f32[258,256]{1,0:T(8,128)S(1)} %fusion.86, f32[258,256]{1,0:T(8,128)S(1)} %fusion.85), kind=kOutput, calls=%fused_computation.48 | convolution fusion | flops 50823936 | bytes 754176 | tf_op jit(solution)/shard_map/dot_general | solution.py:33
  78.5 1.7 %collective-permute-start.10 = (bf16[128,2048]{1,0:T(8,128)(2,1)S(1)}, bf16[128,2048]{1,0:T(8,128)(2,1)}, u32[]{:S(2)}, u32[]{:S(2)}) collective-permute-start(bf16[128,2048]{1,0:T(8,128)(2,1)S(1)} %copy-done.3), channel_id=1, source_target_pairs={{0,1},{1,2},{2,3},{3,0},{4,5},{5,6},{6,7},{7,4},{8,9},{9,10},{10,1... | collective-permute-start | bytes 1572872 | tf_op jit(solution)/shard_map/ppermute | solution.py:151
  80.2 1.6 %collective-permute-done.16 = bf16[8,256,128]{2,1,0:T(8,128)(2,1)} collective-permute-done((bf16[8,256,128]{2,1,0:T(8,128)(2,1)}, bf16[8,256,128]{2,1,0:T(8,128)(2,1)}, u32[]{:S(2)}, u32[]{:S(2)}) %collective-permute-start.16) | collective-permute-done | bytes 524320 | tf_op jit(solution)/shard_map/ppermute | solution.py:155
  81.8 2.4 %add_convert_fusion = bf16[8,256,128]{2,1,0:T(8,128)(2,1)} fusion(bf16[8,256,128]{2,1,0:T(8,128)(2,1)} %collective-permute-done.18, bf16[8,256,128]{2,1,0:T(8,128)(2,1)} %collective-permute-done.17, bf16[8,256,128]{2,1,0:T(8,128)(2,1)} %collective-permute-done.16, bf16[8,256,128]{2,1,0:T(8,128)(2,1)S(1)} %get-tuple-element.38), kind=kLoop, calls=%fused_computation.25 | loop fusion | flops 2097152 | bytes 2621440 | tf_op jit(solution)/shard_map/convert_element_type | solution.py:246
  84.2 4.4 %all-to-all-done.1 = bf16[16,49,256]{2,1,0:T(8,128)(2,1)} async-done(((bf16[16,49,256]{2,1,0:T(8,128)(2,1)}), bf16[16,49,256]{2,1,0:T(8,128)(2,1)}, u32[]{:S(2)}, u32[]{:S(2)}) %all-to-all-start.1) | async-done | bytes 401440 | tf_op jit(solution)/shard_map/all_to_all | solution.py:164
  88.6 3.9 %all-to-all-start.2 = ((bf16[8,256,128]{2,1,0:T(8,128)(2,1)}), bf16[8,256,128]{2,1,0:T(8,128)(2,1)S(1)}, u32[]{:S(2)}, u32[]{:S(2)}) async-start(bf16[8,256,128]{2,1,0:T(8,128)(2,1)} %add_convert_fusion), calls=%async_computation.2 | async-start | bytes 1048576 | tf_op jit(solution)/shard_map/all_to_all | solution.py:312
  92.5 1.1 convert_element_type.127
  93.9 1.9 %collective-permute-start.15 = (f32[49,256]{1,0:T(8,128)S(1)}, f32[49,256]{1,0:T(8,128)S(1)}, u32[]{:S(2)}, u32[]{:S(2)}) collective-permute-start(f32[49,256]{1,0:T(8,128)S(1)} %pad_maximum_fusion), channel_id=1, source_target_pairs={{0,64},{4,68},{8,72},{12,76},{16,80},{20,84},{24,88},{28,92},{32,9... | collective-permute-start | bytes 150536 | tf_op jit(solution)/shard_map/ppermute | solution.py:155
  95.8 2.0 %collective-permute-start.14 = (f32[49,256]{1,0:T(8,128)S(1)}, f32[49,256]{1,0:T(8,128)S(1)}, u32[]{:S(2)}, u32[]{:S(2)}) collective-permute-start(f32[49,256]{1,0:T(8,128)S(1)} %pad_maximum_fusion), channel_id=1, source_target_pairs={{0,128},{4,132},{8,136},{12,140},{16,144},{20,148},{24,152},{28,15... | collective-permute-start | bytes 150536 | tf_op jit(solution)/shard_map/ppermute | solution.py:155
  97.8 0.8 collective-permute-start.13
  98.6 1.5 %collective-permute-done.11 = bf16[128,2048]{1,0:T(8,128)(2,1)} collective-permute-done((bf16[128,2048]{1,0:T(8,128)(2,1)S(1)}, bf16[128,2048]{1,0:T(8,128)(2,1)}, u32[]{:S(2)}, u32[]{:S(2)}) %collective-permute-start.11) | collective-permute-done | bytes 524320 | tf_op jit(solution)/shard_map/ppermute | solution.py:151
  100.2 1.1 %collective-permute-done.10 = bf16[128,2048]{1,0:T(8,128)(2,1)} collective-permute-done((bf16[128,2048]{1,0:T(8,128)(2,1)S(1)}, bf16[128,2048]{1,0:T(8,128)(2,1)}, u32[]{:S(2)}, u32[]{:S(2)}) %collective-permute-start.10) | collective-permute-done | bytes 524320 | tf_op jit(solution)/shard_map/ppermute | solution.py:151
  101.3 2.5 %add_convert_fusion.1 = bf16[128,2048]{1,0:T(8,128)(2,1)} fusion(bf16[128,2048]{1,0:T(8,128)(2,1)} %collective-permute-done.12, bf16[128,2048]{1,0:T(8,128)(2,1)} %collective-permute-done.11, bf16[128,2048]{1,0:T(8,128)(2,1)} %collective-permute-done.10, bf16[128,2048]{1,0:T(8,128)(2,1)S(1)} %get-tuple-element.43), kind=kLoop, calls=%fused_computation.26 | loop fusion | flops 2097152 | bytes 2621440 | tf_op jit(solution)/shard_map/convert_element_type | solution.py:255
  104.4 0.7 fusion.68
  105.5 1.0 fusion.35
  106.5 5.0 %all-to-all-done.2 = bf16[8,256,128]{2,1,0:T(8,128)(2,1)S(1)} async-done(((bf16[8,256,128]{2,1,0:T(8,128)(2,1)}), bf16[8,256,128]{2,1,0:T(8,128)(2,1)S(1)}, u32[]{:S(2)}, u32[]{:S(2)}) %all-to-all-start.2) | async-done | bytes 524320 | tf_op jit(solution)/shard_map/all_to_all | solution.py:312
  111.5 0.7 convert_reduce_fusion
  (114 shorter events, 4.8 us)
Async XLA Ops:
  0.6 43.3 %copy-start.20 = (f32[16,256]{1,0:T(8,128)S(1)}, f32[16,256]{1,0:T(8,128)}, u32[]{:S(2)}) copy-start(f32[16,256]{1,0:T(8,128)} %param.14) | copy-start | bytes 49156
  0.6 16.2 %copy-start.1 = (bf16[128,2048]{1,0:T(8,128)(2,1)S(1)}, bf16[128,2048]{1,0:T(8,128)(2,1)}, u32[]{:S(2)}) copy-start(bf16[128,2048]{1,0:T(8,128)(2,1)} %refs_0_.1) | copy-start | bytes 1572868
  3.0 42.8 %copy-start.10 = (f32[258,128]{1,0:T(8,128)S(1)}, f32[258,128]{1,0:T(8,128)}, u32[]{:S(2)}) copy-start(f32[258,128]{1,0:T(8,128)} %constant.94.clone) | copy-start | bytes 396292
  3.1 1.3 %collective-permute-start = (f32[32,256]{1,0:T(8,128)S(1)}, f32[32,256]{1,0:T(8,128)S(1)}, u32[]{:S(2)}, u32[]{:S(2)}) collective-permute-start(f32[32,256]{1,0:T(8,128)S(1)} %pad_maximum_fusion.1), channel_id=1, source_target_pairs={{0,4},{4,0},{8,12},{12,8},{16,20},{20,16},{24,28},{28,24},{32,36},... | collective-permute-start | bytes 98312 | tf_op jit(solution)/shard_map/ppermute | solution.py:148
  4.4 41.8 %copy-start.8 = (bf16[128,256]{1,0:T(8,128)(2,1)S(1)}, bf16[128,256]{1,0:T(8,128)(2,1)}, u32[]{:S(2)}) copy-start(bf16[128,256]{1,0:T(8,128)(2,1)} %param.12) | copy-start | bytes 196612
  4.4 41.8 %copy-start.9 = (bf16[128,256]{1,0:T(8,128)(2,1)S(1)}, bf16[128,256]{1,0:T(8,128)(2,1)}, u32[]{:S(2)}) copy-start(bf16[128,256]{1,0:T(8,128)(2,1)} %param.11) | copy-start | bytes 196612
  5.2 41.4 %copy-start.17 = (f32[128,129]{1,0:T(8,128)S(1)}, f32[128,129]{1,0:T(8,128)}, u32[]{:S(2)}) copy-start(f32[128,129]{1,0:T(8,128)} %constant.96) | copy-start | bytes 198148
  5.2 24.4 %all-to-all-start = ((bf16[32,32,128]{2,1,0:T(8,128)(2,1)}), bf16[32,32,128]{2,1,0:T(8,128)(2,1)S(1)}, u32[]{:S(2)}, u32[]{:S(2)}) async-start(bf16[32,32,128]{2,1,0:T(8,128)(2,1)} %broadcast_in_dim.47), calls=%async_computation | async-start | bytes 524288 | tf_op jit(solution)/shard_map/all_to_all | solution.py:169
  16.8 14.9 %collective-permute-start.3 = (bf16[128,2048]{1,0:T(8,128)(2,1)S(1)}, bf16[128,2048]{1,0:T(8,128)(2,1)S(1)}, u32[]{:S(2)}, u32[]{:S(2)}) collective-permute-start(bf16[128,2048]{1,0:T(8,128)(2,1)S(1)} %copy-done.1), channel_id=1, source_target_pairs={{0,1},{1,2},{2,3},{3,0},{4,5},{5,6},{6,7},{7,4},{8,9},{9,10},{10,1... | collective-permute-start | bytes 1572872 | tf_op jit(solution)/shard_map/ppermute | solution.py:151
  18.4 16.3 %collective-permute-start.4 = (bf16[128,2048]{1,0:T(8,128)(2,1)S(1)}, bf16[128,2048]{1,0:T(8,128)(2,1)S(1)}, u32[]{:S(2)}, u32[]{:S(2)}) collective-permute-start(bf16[128,2048]{1,0:T(8,128)(2,1)S(1)} %copy-done.1), channel_id=1, source_target_pairs={{0,2},{1,3},{2,0},{3,1},{4,6},{5,7},{6,4},{7,5},{8,10},{9,11},{10,... | collective-permute-start | bytes 1572872 | tf_op jit(solution)/shard_map/ppermute | solution.py:151
  19.5 24.4 %collective-permute-start.5 = (bf16[128,2048]{1,0:T(8,128)(2,1)S(1)}, bf16[128,2048]{1,0:T(8,128)(2,1)S(1)}, u32[]{:S(2)}, u32[]{:S(2)}) collective-permute-start(bf16[128,2048]{1,0:T(8,128)(2,1)S(1)} %copy-done.1), channel_id=1, source_target_pairs={{0,3},{1,0},{2,1},{3,2},{4,7},{5,4},{6,5},{7,6},{8,11},{9,8},{10,9... | collective-permute-start | bytes 1572872 | tf_op jit(solution)/shard_map/ppermute | solution.py:151
  21.7 25.3 %copy-start.12 = (f32[128,129]{1,0:T(8,128)S(1)}, f32[128,129]{1,0:T(8,128)}, u32[]{:S(2)}) copy-start(f32[128,129]{1,0:T(8,128)} %constant.97) | copy-start | bytes 198148
  21.7 25.3 %copy-start.22 = (bf16[128,256]{1,0:T(8,128)(2,1)S(1)}, bf16[128,256]{1,0:T(8,128)(2,1)}, u32[]{:S(2)}) copy-start(bf16[128,256]{1,0:T(8,128)(2,1)} %param.10) | copy-start | bytes 196612
  21.7 25.3 %copy-start.30 = (f32[256]{0:T(256)S(1)}, f32[256]{0:T(256)}, u32[]{:S(2)}) copy-start(f32[256]{0:T(256)} %param.15) | copy-start | bytes 3076
  29.8 14.1 %collective-permute-start.1 = (f32[32,128]{1,0:T(8,128)S(1)}, f32[32,128]{1,0:T(8,128)S(1)}, u32[]{:S(2)}, u32[]{:S(2)}) collective-permute-start(f32[32,128]{1,0:T(8,128)S(1)} %pad_maximum_fusion.4), channel_id=1, source_target_pairs={{0,4},{4,0},{8,12},{12,8},{16,20},{20,16},{24,28},{28,24},{32,36},... | collective-permute-start | bytes 49160 | tf_op jit(solution)/shard_map/ppermute | solution.py:148
  29.9 18.1 %collective-permute-start.6 = (bf16[128,2048]{1,0:T(8,128)(2,1)S(1)}, bf16[128,2048]{1,0:T(8,128)(2,1)S(1)}, u32[]{:S(2)}, u32[]{:S(2)}) collective-permute-start(bf16[128,2048]{1,0:T(8,128)(2,1)S(1)} %copy-done.1), channel_id=1, source_target_pairs={{0,4},{4,0},{8,12},{12,8},{16,20},{20,16},{24,28},{28,24},{32,36},... | collective-permute-start | bytes 1572872 | tf_op jit(solution)/shard_map/ppermute | solution.py:148
  31.7 17.1 %collective-permute-start.7 = (bf16[128,2048]{1,0:T(8,128)(2,1)S(1)}, bf16[128,2048]{1,0:T(8,128)(2,1)S(1)}, u32[]{:S(2)}, u32[]{:S(2)}) collective-permute-start(bf16[128,2048]{1,0:T(8,128)(2,1)S(1)} %collective-permute-done.3.refs_3_.refs_1_), channel_id=1, source_target_pairs={{0,4},{4,0},{8,12},{12,8},{16,20},{20,16},{24,28},{28,24},{32,36},... | collective-permute-start | bytes 1572872 | tf_op jit(solution)/shard_map/ppermute | solution.py:148
  34.7 14.1 %collective-permute-start.8 = (bf16[128,2048]{1,0:T(8,128)(2,1)S(1)}, bf16[128,2048]{1,0:T(8,128)(2,1)S(1)}, u32[]{:S(2)}, u32[]{:S(2)}) collective-permute-start(bf16[128,2048]{1,0:T(8,128)(2,1)S(1)} %collective-permute-done.4.refs_4_.refs_2_), channel_id=1, source_target_pairs={{0,4},{4,0},{8,12},{12,8},{16,20},{20,16},{24,28},{28,24},{32,36},... | collective-permute-start | bytes 1572872 | tf_op jit(solution)/shard_map/ppermute | solution.py:148
  43.9 5.0 %collective-permute-start.9 = (bf16[128,2048]{1,0:T(8,128)(2,1)S(1)}, bf16[128,2048]{1,0:T(8,128)(2,1)S(1)}, u32[]{:S(2)}, u32[]{:S(2)}) collective-permute-start(bf16[128,2048]{1,0:T(8,128)(2,1)S(1)} %collective-permute-done.5.refs_5_.refs_3_), channel_id=1, source_target_pairs={{0,4},{4,0},{8,12},{12,8},{16,20},{20,16},{24,28},{28,24},{32,36},... | collective-permute-start | bytes 1572872 | tf_op jit(solution)/shard_map/ppermute | solution.py:148
  47.3 1.5 %collective-permute-start.2 = (bf16[128,256]{1,0:T(8,128)(2,1)S(1)}, bf16[128,256]{1,0:T(8,128)(2,1)S(1)}, u32[]{:S(2)}, u32[]{:S(2)}) collective-permute-start(bf16[128,256]{1,0:T(8,128)(2,1)S(1)} %get-tuple-element.42.refs_0_.result_ref), channel_id=1, source_target_pairs={{0,4},{4,0},{8,12},{12,8},{16,20},{20,16},{24,28},{28,24},{32,36},... | collective-permute-start | bytes 196616 | tf_op jit(solution)/shard_map/ppermute | solution.py:148
  48.0 8.5 %copy-start = (bf16[256,8192]{1,0:T(8,128)(2,1)S(1)}, bf16[256,8192]{1,0:T(8,128)(2,1)}, u32[]{:S(2)}) copy-start(bf16[256,8192]{1,0:T(8,128)(2,1)} %refs_4_.1) | copy-start | bytes 12582916
  52.0 26.5 %collective-permute-start.18 = (bf16[8,256,128]{2,1,0:T(8,128)(2,1)}, bf16[8,256,128]{2,1,0:T(8,128)(2,1)}, u32[]{:S(2)}, u32[]{:S(2)}) collective-permute-start(bf16[8,256,128]{2,1,0:T(8,128)(2,1)} %get-tuple-element.41), channel_id=1, source_target_pairs={{0,192},{4,196},{8,200},{12,204},{16,208},{20,212},{24,216},{28,22... | collective-permute-start | bytes 1572872 | tf_op jit(solution)/shard_map/ppermute | solution.py:155
  54.8 25.4 %collective-permute-start.17 = (bf16[8,256,128]{2,1,0:T(8,128)(2,1)}, bf16[8,256,128]{2,1,0:T(8,128)(2,1)}, u32[]{:S(2)}, u32[]{:S(2)}) collective-permute-start(bf16[8,256,128]{2,1,0:T(8,128)(2,1)} %get-tuple-element.40), channel_id=1, source_target_pairs={{0,128},{4,132},{8,136},{12,140},{16,144},{20,148},{24,152},{28,15... | collective-permute-start | bytes 1572872 | tf_op jit(solution)/shard_map/ppermute | solution.py:155
  55.6 26.1 %collective-permute-start.16 = (bf16[8,256,128]{2,1,0:T(8,128)(2,1)}, bf16[8,256,128]{2,1,0:T(8,128)(2,1)}, u32[]{:S(2)}, u32[]{:S(2)}) collective-permute-start(bf16[8,256,128]{2,1,0:T(8,128)(2,1)} %get-tuple-element.39), channel_id=1, source_target_pairs={{0,64},{4,68},{8,72},{12,76},{16,80},{20,84},{24,88},{28,92},{32,9... | collective-permute-start | bytes 1572872 | tf_op jit(solution)/shard_map/ppermute | solution.py:155
  56.5 3.9 %copy-start.18 = (f32[128,129]{1,0:T(8,128)S(1)}, f32[128,129]{1,0:T(8,128)}, u32[]{:S(2)}) copy-start(f32[128,129]{1,0:T(8,128)} %constant.96) | copy-start | bytes 198148
  56.5 4.5 %copy-start.13 = (f32[128,129]{1,0:T(8,128)S(1)}, f32[128,129]{1,0:T(8,128)}, u32[]{:S(2)}) copy-start(f32[128,129]{1,0:T(8,128)} %constant.97) | copy-start | bytes 198148
  59.2 4.9 %copy-start.21 = (f32[16,256]{1,0:T(8,128)S(1)}, f32[16,256]{1,0:T(8,128)}, u32[]{:S(2)}) copy-start(f32[16,256]{1,0:T(8,128)} %param.14) | copy-start | bytes 49156
  59.2 6.9 %copy-start.25 = (f32[16,256]{1,0:T(8,128)S(1)}, f32[16,256]{1,0:T(8,128)}, u32[]{:S(2)}) copy-start(f32[16,256]{1,0:T(8,128)} %copy-done.24) | copy-start | bytes 49156
  59.2 6.9 %copy-start.26 = (f32[16,256]{1,0:T(8,128)S(1)}, f32[16,256]{1,0:T(8,128)}, u32[]{:S(2)}) copy-start(f32[16,256]{1,0:T(8,128)} %get-tuple-element.53) | copy-start | bytes 49156
  60.0 7.0 %copy-start.15 = (f32[128,256]{1,0:T(8,128)}, f32[128,256]{1,0:T(8,128)S(1)}, u32[]{:S(2)}) copy-start(f32[128,256]{1,0:T(8,128)S(1)} %get-tuple-element.71) | copy-start | bytes 393220
  61.0 13.9 %copy-start.5 = (bf16[128,2048]{1,0:T(8,128)(2,1)S(1)}, bf16[128,2048]{1,0:T(8,128)(2,1)}, u32[]{:S(2)}) copy-start(bf16[128,2048]{1,0:T(8,128)(2,1)} %copy-done.4) | copy-start | bytes 1572868
  61.1 17.5 %copy-start.3 = (bf16[128,2048]{1,0:T(8,128)(2,1)S(1)}, bf16[128,2048]{1,0:T(8,128)(2,1)}, u32[]{:S(2)}) copy-start(bf16[128,2048]{1,0:T(8,128)(2,1)} %copy-done.2) | copy-start | bytes 1572868
  62.3 11.5 %copy-start.7 = (bf16[128,2048]{1,0:T(8,128)(2,1)S(1)}, bf16[128,2048]{1,0:T(8,128)(2,1)}, u32[]{:S(2)}) copy-start(bf16[128,2048]{1,0:T(8,128)(2,1)} %copy-done.6) | copy-start | bytes 1572868
  64.1 29.6 %copy-start.27 = (f32[16,256]{1,0:T(8,128)}, f32[16,256]{1,0:T(8,128)S(1)}, u32[]{:S(2)}) copy-start(f32[16,256]{1,0:T(8,128)S(1)} %exponential_negate_fusion.1) | copy-start | bytes 49156
  67.0 21.6 %all-to-all-start.1 = ((bf16[16,49,256]{2,1,0:T(8,128)(2,1)}), bf16[16,49,256]{2,1,0:T(8,128)(2,1)}, u32[]{:S(2)}, u32[]{:S(2)}) async-start(bf16[16,49,256]{2,1,0:T(8,128)(2,1)} %broadcast_in_dim.52), calls=%async_computation.1 | async-start | bytes 917504 | tf_op jit(solution)/shard_map/all_to_all | solution.py:164
  73.8 24.0 %collective-permute-start.12 = (bf16[128,2048]{1,0:T(8,128)(2,1)S(1)}, bf16[128,2048]{1,0:T(8,128)(2,1)}, u32[]{:S(2)}, u32[]{:S(2)}) collective-permute-start(bf16[128,2048]{1,0:T(8,128)(2,1)S(1)} %copy-done.7), channel_id=1, source_target_pairs={{0,3},{1,0},{2,1},{3,2},{4,7},{5,4},{6,5},{7,6},{8,11},{9,8},{10,9... | collective-permute-start | bytes 1572872 | tf_op jit(solution)/shard_map/ppermute | solution.py:151
  75.0 25.2 %collective-permute-start.11 = (bf16[128,2048]{1,0:T(8,128)(2,1)S(1)}, bf16[128,2048]{1,0:T(8,128)(2,1)}, u32[]{:S(2)}, u32[]{:S(2)}) collective-permute-start(bf16[128,2048]{1,0:T(8,128)(2,1)S(1)} %copy-done.5), channel_id=1, source_target_pairs={{0,2},{1,3},{2,0},{3,1},{4,6},{5,7},{6,4},{7,5},{8,10},{9,11},{10,... | collective-permute-start | bytes 1572872 | tf_op jit(solution)/shard_map/ppermute | solution.py:151
  78.5 22.7 %collective-permute-start.10 = (bf16[128,2048]{1,0:T(8,128)(2,1)S(1)}, bf16[128,2048]{1,0:T(8,128)(2,1)}, u32[]{:S(2)}, u32[]{:S(2)}) collective-permute-start(bf16[128,2048]{1,0:T(8,128)(2,1)S(1)} %copy-done.3), channel_id=1, source_target_pairs={{0,1},{1,2},{2,3},{3,0},{4,5},{5,6},{6,7},{7,4},{8,9},{9,10},{10,1... | collective-permute-start | bytes 1572872 | tf_op jit(solution)/shard_map/ppermute | solution.py:151
  88.6 22.9 %all-to-all-start.2 = ((bf16[8,256,128]{2,1,0:T(8,128)(2,1)}), bf16[8,256,128]{2,1,0:T(8,128)(2,1)S(1)}, u32[]{:S(2)}, u32[]{:S(2)}) async-start(bf16[8,256,128]{2,1,0:T(8,128)(2,1)} %add_convert_fusion), calls=%async_computation.2 | async-start | bytes 1048576 | tf_op jit(solution)/shard_map/all_to_all | solution.py:312
  93.6 10.7 %copy-start.29 = (f32[16,256]{1,0:T(8,128)S(1)}, f32[16,256]{1,0:T(8,128)}, u32[]{:S(2)}) copy-start(f32[16,256]{1,0:T(8,128)} %param.13) | copy-start | bytes 49156
  93.6 11.4 %copy-start.32 = (f32[128]{0:T(128)S(1)}, f32[128]{0:T(128)}, u32[]{:S(2)}) copy-start(f32[128]{0:T(128)} %copy-done.31) | copy-start | bytes 1540
  93.8 11.2 %copy-start.28 = (f32[16,256]{1,0:T(8,128)S(1)}, f32[16,256]{1,0:T(8,128)}, u32[]{:S(2)}) copy-start(f32[16,256]{1,0:T(8,128)} %copy-done.27) | copy-start | bytes 49156
  93.9 11.5 %copy-start.14 = (f32[128,129]{1,0:T(8,128)S(1)}, f32[128,129]{1,0:T(8,128)}, u32[]{:S(2)}) copy-start(f32[128,129]{1,0:T(8,128)} %constant.97) | copy-start | bytes 198148
  93.9 11.5 %copy-start.16 = (f32[128,256]{1,0:T(8,128)S(1)}, f32[128,256]{1,0:T(8,128)}, u32[]{:S(2)}) copy-start(f32[128,256]{1,0:T(8,128)} %copy-done.15) | copy-start | bytes 393220
  93.9 11.5 %copy-start.19 = (f32[256,128]{0,1:T(8,128)S(1)}, f32[256,128]{0,1:T(8,128)}, u32[]{:S(2)}) copy-start(f32[256,128]{0,1:T(8,128)} %fusion.24) | copy-start | bytes 393220
  93.9 9.8 %collective-permute-start.15 = (f32[49,256]{1,0:T(8,128)S(1)}, f32[49,256]{1,0:T(8,128)S(1)}, u32[]{:S(2)}, u32[]{:S(2)}) collective-permute-start(f32[49,256]{1,0:T(8,128)S(1)} %pad_maximum_fusion), channel_id=1, source_target_pairs={{0,64},{4,68},{8,72},{12,76},{16,80},{20,84},{24,88},{28,92},{32,9... | collective-permute-start | bytes 150536 | tf_op jit(solution)/shard_map/ppermute | solution.py:155
  95.8 7.9 %collective-permute-start.14 = (f32[49,256]{1,0:T(8,128)S(1)}, f32[49,256]{1,0:T(8,128)S(1)}, u32[]{:S(2)}, u32[]{:S(2)}) collective-permute-start(f32[49,256]{1,0:T(8,128)S(1)} %pad_maximum_fusion), channel_id=1, source_target_pairs={{0,128},{4,132},{8,136},{12,140},{16,144},{20,148},{24,152},{28,15... | collective-permute-start | bytes 150536 | tf_op jit(solution)/shard_map/ppermute | solution.py:155
  97.8 5.9 %collective-permute-start.13 = (f32[49,256]{1,0:T(8,128)S(1)}, f32[49,256]{1,0:T(8,128)S(1)}, u32[]{:S(2)}, u32[]{:S(2)}) collective-permute-start(f32[49,256]{1,0:T(8,128)S(1)} %pad_maximum_fusion), channel_id=1, source_target_pairs={{0,192},{4,196},{8,200},{12,204},{16,208},{20,212},{24,216},{28,22... | collective-permute-start | bytes 150536 | tf_op jit(solution)/shard_map/ppermute | solution.py:155
  (7 other events, 13.8 us)

commit v9 on v7

--- a/solution.py
+++ b/solution.py
@@ -9,7 +9,7 @@
 
 F32 = jnp.float32
 BF16 = jnp.bfloat16
-EXACT = lax.Precision.HIGHEST
+FINE = lax.Precision.HIGH
 
 
 def dft_tables(block):
@@ -24,14 +24,14 @@
 
 
 def spectrum(forward, rows):
-    both = jnp.dot(forward, rows, precision=EXACT, preferred_element_type=F32)
+    both = jnp.dot(forward, rows, precision=FINE, preferred_element_type=F32)
     half = both.shape[0] // 2
     return both[:half], both[half:]
 
 
 def back(inverse, real_part, imag_part):
     return jnp.dot(
-        inverse, jnp.concatenate([real_part, imag_part], 0), precision=EXACT, preferred_element_type=F32
+        inverse, jnp.concatenate([real_part, imag_part], 0), precision=FINE, preferred_element_type=F32
     )
 
 
@@ -292,11 +292,11 @@
     got = got.astype(F32)
     plane_h = jnp.sum(weights(place >= 0, place)[0] * got[:, :modes], 0)
     plane_sums = jnp.sum(got[:, modes:], 0)
-    plane_g = jnp.concatenate([plane_h, plane_sums], 0)
+    plane_g = jnp.concatenate([plane_h, plane_sums], 0).astype(BF16)
     h_half = jnp.sum(weights(place > zz, place - zz - 1)[0] * got[:, :modes], 0)
     y_h, sums_half = 0.0, plane_sums
     for k in range(1, ny):
-        came = shift_y(plane_g, -k)
+        came = shift_y(plane_g, -k).astype(F32)
         w = jnp.exp(-rate_h * float(per_plane * (k - 1)))
         y_h = y_h + jnp.where(yy + k < ny, w * came[:modes], 0.0)
         sums_half = sums_half + came[modes:]

time: 145 us -> 144 us (level)
  waiting for transfers between devices: 54.4 us -> 52.8 us
  other arithmetic: 26.6 us -> 28.1 us
    ppermute x6, waiting for transfers between devices: 16.2 us -> 18.7 us  [shift_tp(): return lax.ppermute(a, 'tp', [(i, (i + k) % tps) for i in range(tps)])]
    ppermute x6, waiting for transfers between devices: 11.7 us -> 9.2 us  [shift_y(): lax.ppermute(a, 'ctx', [(i, (i // per + k) % ny * per + i % per) for i in...]
    convert_element_type x0 -> x3, other arithmetic: none -> 2.15 us  [body(): came = shift_y(plane_g, -k).astype(F32)]
    all_to_all x1, waiting for transfers between devices: 7.2 us -> 5.6 us  [body(): lax.all_to_all(summed_y, 'ctx', 0, 0, tiled=True, axis_index_groups=z_gro...]
  transfers between devices with their start and end apart: 24 -> 24, of which waited for: 13 -> 12; matrix products, arithmetic and copies ran while one was open for 12% -> 13% of each run, Pallas kernels for 0% -> 0%
where the time goes in v9:
time: 144 us; the launch traced here: 141 us
  waiting for transfers between devices  52.8 us (37%)
  starting transfers between devices  41.5 us (29%)
  other arithmetic  28.1 us (20%)
  matrix products  6.77 us (5%)
  Pallas kernels  5.34 us (4%)
  local copies, waits for them, and re-layouts  5.15 us (4%)
    ppermute x6, waiting for transfers between devices, shift_tp(): return lax.ppermute(a, 'tp', [(i, (i + k) % tps) for i in range(tps)])  18.7 us
    all_to_all x1, starting transfers between devices, of_pairs(): lax.all_to_all(copies, 'ctx', 0, 0, tiled=True, axis_index_groups=groups)  11.6 us
    ppermute x6, waiting for transfers between devices, shift_y(): lax.ppermute(a, 'ctx', [(i, (i // per + k) % ny * per + i % per) for i in...  9.2 us
    ppermute x6, starting transfers between devices, shift_y(): lax.ppermute(a, 'ctx', [(i, (i // per + k) % ny * per + i % per) for i in...  8.93 us
    ppermute x6, starting transfers between devices, shift_tp(): return lax.ppermute(a, 'tp', [(i, (i + k) % tps) for i in range(tps)])  8.81 us
    all_to_all x1, waiting for transfers between devices, of_plane(): lax.all_to_all(copies, 'ctx', 0, 0, tiled=True, axis_index_groups=z_groups)  8.26 us
    all_to_all x1, waiting for transfers between devices, of_pairs(): lax.all_to_all(copies, 'ctx', 0, 0, tiled=True, axis_index_groups=groups)  7.83 us
    all_to_all x1, starting transfers between devices, of_plane(): lax.all_to_all(copies, 'ctx', 0, 0, tiled=True, axis_index_groups=z_groups)  6.69 us
  transfers between devices with their start and end apart: 24, of which 12 were waited for; matrix products, arithmetic and copies ran while one was open for 13% of the time, Pallas kernels for 0%

profile of v9, /device:TPU:2, one launch (start us, length us, event | category | flops | bytes accessed | tf_op | source)
XLA Modules:
  0.0 140.9 jit_solution(3317466306374699472)
XLA Ops:
  0.7 0.8 fusion.90
  1.5 0.9 convert_multiply_fusion.5
  3.2 1.2 collective-permute-done
  5.2 11.6 %all-to-all-start = ((bf16[32,32,128]{2,1,0:T(8,128)(2,1)}), bf16[32,32,128]{2,1,0:T(8,128)(2,1)S(1)}, u32[]{:S(2)}, u32[]{:S(2)}) async-start(bf16[32,32,128]{2,1,0:T(8,128)(2,1)} %broadcast_in_dim.49), calls=%async_computation | async-start | bytes 524288 | tf_op jit(solution)/shard_map/all_to_all | solution.py:167
  16.9 1.6 %collective-permute-start.3 = (bf16[128,2048]{1,0:T(8,128)(2,1)S(1)}, bf16[128,2048]{1,0:T(8,128)(2,1)S(1)}, u32[]{:S(2)}, u32[]{:S(2)}) collective-permute-start(bf16[128,2048]{1,0:T(8,128)(2,1)S(1)} %copy-done.1), channel_id=1, source_target_pairs={{0,1},{1,2},{2,3},{3,0},{4,5},{5,6},{6,7},{7,4},{8,9},{9,10},{10,1... | collective-permute-start | bytes 1572872 | tf_op jit(solution)/shard_map/ppermute | solution.py:152
  18.4 1.1 collective-permute-start.4
  19.5 2.2 %collective-permute-start.5 = (bf16[128,2048]{1,0:T(8,128)(2,1)S(1)}, bf16[128,2048]{1,0:T(8,128)(2,1)S(1)}, u32[]{:S(2)}, u32[]{:S(2)}) collective-permute-start(bf16[128,2048]{1,0:T(8,128)(2,1)S(1)} %copy-done.1), channel_id=1, source_target_pairs={{0,3},{1,0},{2,1},{3,2},{4,7},{5,4},{6,5},{7,6},{8,11},{9,8},{10,9... | collective-permute-start | bytes 1572872 | tf_op jit(solution)/shard_map/ppermute | solution.py:152
  21.7 7.8 %all-to-all-done = bf16[32,32,128]{2,1,0:T(8,128)(2,1)S(1)} async-done(((bf16[32,32,128]{2,1,0:T(8,128)(2,1)}), bf16[32,32,128]{2,1,0:T(8,128)(2,1)S(1)}, u32[]{:S(2)}, u32[]{:S(2)}) %all-to-all-start) | async-done | bytes 262176 | tf_op jit(solution)/shard_map/all_to_all | solution.py:167
  30.4 1.3 collective-permute-done.3.refs_3_.refs_1_
  31.7 3.0 %collective-permute-done.4.refs_4_.refs_2_ = bf16[128,2048]{1,0:T(8,128)(2,1)S(1)} collective-permute-done((bf16[128,2048]{1,0:T(8,128)(2,1)S(1)}, bf16[128,2048]{1,0:T(8,128)(2,1)S(1)}, u32[]{:S(2)}, u32[]{:S(2)}) %collective-permute-start.4) | collective-permute-done | bytes 524320 | tf_op jit(solution)/shard_map/ppermute | solution.py:152
  34.7 9.2 %collective-permute-done.5.refs_5_.refs_3_ = bf16[128,2048]{1,0:T(8,128)(2,1)S(1)} collective-permute-done((bf16[128,2048]{1,0:T(8,128)(2,1)S(1)}, bf16[128,2048]{1,0:T(8,128)(2,1)S(1)}, u32[]{:S(2)}, u32[]{:S(2)}) %collective-permute-start.5) | collective-permute-done | bytes 524320 | tf_op jit(solution)/shard_map/ppermute | solution.py:152
  44.6 0.8 fusion.89
  47.0 0.8 collective-permute-start.2
  47.8 0.8 collective-permute-done.2.refs_1_
  48.7 2.7 %shard_map.161 = (bf16[8,256,128]{2,1,0:T(8,128)(2,1)S(1)}, bf16[8,256,128]{2,1,0:T(8,128)(2,1)S(1)}, bf16[8,256,128]{2,1,0:T(8,128)(2,1)S(1)}, bf16[8,256,128]{2,1,0:T(8,128)(2,1)S(1)}) custom-call(s32[3]{0:T(128)S(1)} %pad_add_fusion.turns_ref, bf16[128,256]{1,0:T(8,128)(2,1)S(1)} %get-tuple-element.42.refs_0_.result_ref, ...), custom_call_target="tpu_custom_call" | custom-call | tf_op jit(solution)/shard_map/pallas_call | solution.py:80
  51.4 0.8 copy-done.10
  52.2 0.8 copy-done.11
  53.1 2.6 %shard_map.162 = (f32[128,256]{1,0:T(8,128)S(1)}, bf16[128,2048]{1,0:T(8,128)(2,1)S(1)}, bf16[128,2048]{1,0:T(8,128)(2,1)S(1)}, bf16[128,2048]{1,0:T(8,128)(2,1)S(1)}, bf16[128,2048]{1,0:T(8,128)(2,1)S(1)}) custom-call(s32[3]{0:T(128)S(1)} %pad_add_fusion.turns_ref, bf16[128,256]{1,0:T(8,128)(2,1)S(1)} %get-tuple-element.42.refs_0_.result_ref, ...), custom_call_target="tpu_custom_call" | custom-call | tf_op jit(solution)/shard_map/pallas_call | solution.py:121
  55.7 1.3 fusion.37
  58.0 1.1 fusion.5
  59.1 1.8 %copy.34 = f32[128,256]{1,0:T(8,128)} copy(f32[128,256]{0,1:T(8,128)} %fusion.5) | data formatting | bytes 262144 | tf_op jit(solution)/shard_map/dot_general | solution.py:33
  61.6 2.1 %fusion.3 = (f32[16,256]{1,0:T(8,128)S(1)}, f32[16,256]{1,0:T(8,128)S(1)}, f32[16,256]{1,0:T(8,128)S(1)}, f32[16,256]{1,0:T(8,128)S(1)}) fusion(f32[128,256]{1,0:T(8,128)} %copy.34, f32[16,256]{1,0:T(8,128)S(1)} %exponential_negate_fusion.1, f32[128,256]{1,0:T(8,128)} %copy-done.19), kind=kLoop, calls=%fused_computation.7 | loop fusion | flops 4702208 | bytes 344064 | tf_op jit(solution)/shard_map/reduce_sum | solution.py:281
  63.7 0.7 multiply_add_fusion
  64.5 1.3 pad_maximum_fusion
  66.2 1.2 collective-permute-done.13
  68.1 0.8 fusion.64
  70.3 6.7 %all-to-all-start.1 = ((bf16[8,49,128]{2,1,0:T(8,128)(2,1)}), bf16[8,49,128]{2,1,0:T(8,128)(2,1)}, u32[]{:S(2)}, u32[]{:S(2)}) async-start(bf16[8,49,128]{2,1,0:T(8,128)(2,1)} %broadcast_in_dim.86), calls=%async_computation.1 | async-start | bytes 229376 | tf_op jit(solution)/shard_map/all_to_all | solution.py:162
  78.1 8.3 %all-to-all-done.1 = bf16[8,49,128]{2,1,0:T(8,128)(2,1)} async-done(((bf16[8,49,128]{2,1,0:T(8,128)(2,1)}), bf16[8,49,128]{2,1,0:T(8,128)(2,1)}, u32[]{:S(2)}, u32[]{:S(2)}) %all-to-all-start.1) | async-done | bytes 100384 | tf_op jit(solution)/shard_map/all_to_all | solution.py:162
  86.3 0.9 convert_element_type.137
  87.3 1.4 multiply_reduce_fusion.8
  89.3 2.7 %collective-permute-start.14 = (bf16[49,128]{1,0:T(8,128)(2,1)}, bf16[49,128]{1,0:T(8,128)(2,1)}, u32[]{:S(2)}, u32[]{:S(2)}) collective-permute-start(bf16[49,128]{1,0:T(8,128)(2,1)} %pad_maximum_fusion.7), channel_id=1, source_target_pairs={{0,192},{4,196},{8,200},{12,204},{16,208},{20,212},{24,216},{28,22... | collective-permute-start | bytes 37640 | tf_op jit(solution)/shard_map/ppermute | solution.py:156
  92.0 0.8 collective-permute-start.15
  92.8 0.9 collective-permute-start.16
  93.7 1.8 %collective-permute-start.18 = (bf16[8,256,128]{2,1,0:T(8,128)(2,1)}, bf16[8,256,128]{2,1,0:T(8,128)(2,1)S(1)}, u32[]{:S(2)}, u32[]{:S(2)}) collective-permute-start(bf16[8,256,128]{2,1,0:T(8,128)(2,1)} %copy-done.11), channel_id=1, source_target_pairs={{0,64},{4,68},{8,72},{12,76},{16,80},{20,84},{24,88},{28,92},{32,9... | collective-permute-start | bytes 1572872 | tf_op jit(solution)/shard_map/ppermute | solution.py:156
  95.5 2.0 %collective-permute-start.19 = (bf16[8,256,128]{2,1,0:T(8,128)(2,1)}, bf16[8,256,128]{2,1,0:T(8,128)(2,1)S(1)}, u32[]{:S(2)}, u32[]{:S(2)}) collective-permute-start(bf16[8,256,128]{2,1,0:T(8,128)(2,1)} %copy-done.10), channel_id=1, source_target_pairs={{0,128},{4,132},{8,136},{12,140},{16,144},{20,148},{24,152},{28,15... | collective-permute-start | bytes 1572872 | tf_op jit(solution)/shard_map/ppermute | solution.py:156
  101.9 1.9 %fusion.24 = f32[256,128]{0,1:T(8,128)} fusion(f32[128,129]{1,0:T(8,128)} %constant.98, f32[258,256]{1,0:T(8,128)} %copy-done.12, f32[258,256]{1,0:T(8,128)S(1)} %fusion.91), kind=kOutput, calls=%fused_computation.46 | convolution fusion | flops 25461504 | bytes 819200 | tf_op jit(solution)/shard_map/dot_general | solution.py:33
  103.9 1.3 collective-permute-start.10
  105.2 1.6 %collective-permute-start.11 = (bf16[128,2048]{1,0:T(8,128)(2,1)S(1)}, bf16[128,2048]{1,0:T(8,128)(2,1)}, u32[]{:S(2)}, u32[]{:S(2)}) collective-permute-start(bf16[128,2048]{1,0:T(8,128)(2,1)S(1)} %copy-done.5), channel_id=1, source_target_pairs={{0,2},{1,3},{2,0},{3,1},{4,6},{5,7},{6,4},{7,5},{8,10},{9,11},{10,... | collective-permute-start | bytes 1572872 | tf_op jit(solution)/shard_map/ppermute | solution.py:152
  107.4 1.4 fusion.72
  109.3 1.1 collective-permute-start.12
  110.4 8.7 %collective-permute-done.19 = bf16[8,256,128]{2,1,0:T(8,128)(2,1)S(1)} collective-permute-done((bf16[8,256,128]{2,1,0:T(8,128)(2,1)}, bf16[8,256,128]{2,1,0:T(8,128)(2,1)S(1)}, u32[]{:S(2)}, u32[]{:S(2)}) %collective-permute-start.19) | collective-permute-done | bytes 524320 | tf_op jit(solution)/shard_map/ppermute | solution.py:156
  119.0 1.1 add_convert_fusion
  120.1 3.5 %all-to-all-start.2 = ((bf16[8,256,128]{2,1,0:T(8,128)(2,1)}), bf16[8,256,128]{2,1,0:T(8,128)(2,1)S(1)}, u32[]{:S(2)}, u32[]{:S(2)}) async-start(bf16[8,256,128]{2,1,0:T(8,128)(2,1)} %add_convert_fusion), calls=%async_computation.2 | async-start | bytes 1048576 | tf_op jit(solution)/shard_map/all_to_all | solution.py:316
  123.6 1.1 multiply_reduce_fusion
  124.8 2.1 %fusion.35 = (bf16[128,256]{1,0:T(8,128)(2,1)}, bf16[128,256]{1,0:T(8,128)(2,1)}) fusion(bf16[128,256]{1,0:T(8,128)(2,1)S(1)} %copy-done.14, bf16[128,256]{1,0:T(8,128)(2,1)S(1)} %copy-done.13, f32[128,256]{1,0:T(8,128)} %copy-done.19, f32[256]{0:T(256)S(1)} %copy-done.32, f32[128,256]{1,0:T(8,128)S(1)} %multiply_reduce_fusion, f32[256,128]{0,1:T(8,128)} %fusion.24, ...), kind=kOutput, calls=%fused_computation.57 | convolution fusion | flops 25789184 | bytes 1344512 | tf_op jit(solution)/shard_map/dot_general | solution.py:33
  126.9 5.2 %collective-permute-done.12 = bf16[128,2048]{1,0:T(8,128)(2,1)} collective-permute-done((bf16[128,2048]{1,0:T(8,128)(2,1)S(1)}, bf16[128,2048]{1,0:T(8,128)(2,1)}, u32[]{:S(2)}, u32[]{:S(2)}) %collective-permute-start.12) | collective-permute-done | bytes 524320 | tf_op jit(solution)/shard_map/ppermute | solution.py:152
  132.0 2.5 %add_convert_fusion.1 = bf16[128,2048]{1,0:T(8,128)(2,1)} fusion(bf16[128,2048]{1,0:T(8,128)(2,1)} %collective-permute-done.12, bf16[128,2048]{1,0:T(8,128)(2,1)} %collective-permute-done.11, bf16[128,2048]{1,0:T(8,128)(2,1)} %collective-permute-done.10, bf16[128,2048]{1,0:T(8,128)(2,1)S(1)} %get-tuple-element.43), kind=kLoop, calls=%fused_computation.26 | loop fusion | flops 2097152 | bytes 2621440 | tf_op jit(solution)/shard_map/convert_element_type | solution.py:255
  134.5 5.6 %all-to-all-done.2 = bf16[8,256,128]{2,1,0:T(8,128)(2,1)S(1)} async-done(((bf16[8,256,128]{2,1,0:T(8,128)(2,1)}), bf16[8,256,128]{2,1,0:T(8,128)(2,1)S(1)}, u32[]{:S(2)}, u32[]{:S(2)}) %all-to-all-start.2) | async-done | bytes 524320 | tf_op jit(solution)/shard_map/all_to_all | solution.py:316
  (133 shorter events, 16.9 us)
Async XLA Ops:
  0.6 43.3 %copy-start.22 = (f32[16,256]{1,0:T(8,128)S(1)}, f32[16,256]{1,0:T(8,128)}, u32[]{:S(2)}) copy-start(f32[16,256]{1,0:T(8,128)} %param.14) | copy-start | bytes 49156
  0.6 16.2 %copy-start.1 = (bf16[128,2048]{1,0:T(8,128)(2,1)S(1)}, bf16[128,2048]{1,0:T(8,128)(2,1)}, u32[]{:S(2)}) copy-start(bf16[128,2048]{1,0:T(8,128)(2,1)} %refs_0_.1) | copy-start | bytes 1572868
  0.7 2.4 %copy-start.33 = (f32[128]{0:T(128)}, f32[128]{0:T(128)S(1)}, u32[]{:S(2)}) copy-start(f32[128]{0:T(128)S(1)} %iota_subtract_fusion) | copy-start | bytes 1540
  3.0 42.8 %copy-start.15 = (f32[258,128]{1,0:T(8,128)S(1)}, f32[258,128]{1,0:T(8,128)}, u32[]{:S(2)}) copy-start(f32[258,128]{1,0:T(8,128)} %constant.96.clone) | copy-start | bytes 396292
  3.1 1.3 collective-permute-start
  4.4 41.8 %copy-start.13 = (bf16[128,256]{1,0:T(8,128)(2,1)S(1)}, bf16[128,256]{1,0:T(8,128)(2,1)}, u32[]{:S(2)}) copy-start(bf16[128,256]{1,0:T(8,128)(2,1)} %param.12) | copy-start | bytes 196612
  4.4 41.8 %copy-start.14 = (bf16[128,256]{1,0:T(8,128)(2,1)S(1)}, bf16[128,256]{1,0:T(8,128)(2,1)}, u32[]{:S(2)}) copy-start(bf16[128,256]{1,0:T(8,128)(2,1)} %param.11) | copy-start | bytes 196612
  5.2 41.2 %copy-start.20 = (f32[128,129]{1,0:T(8,128)S(1)}, f32[128,129]{1,0:T(8,128)}, u32[]{:S(2)}) copy-start(f32[128,129]{1,0:T(8,128)} %constant.98) | copy-start | bytes 198148
  5.2 24.4 %all-to-all-start = ((bf16[32,32,128]{2,1,0:T(8,128)(2,1)}), bf16[32,32,128]{2,1,0:T(8,128)(2,1)S(1)}, u32[]{:S(2)}, u32[]{:S(2)}) async-start(bf16[32,32,128]{2,1,0:T(8,128)(2,1)} %broadcast_in_dim.49), calls=%async_computation | async-start | bytes 524288 | tf_op jit(solution)/shard_map/all_to_all | solution.py:167
  16.9 14.9 %collective-permute-start.3 = (bf16[128,2048]{1,0:T(8,128)(2,1)S(1)}, bf16[128,2048]{1,0:T(8,128)(2,1)S(1)}, u32[]{:S(2)}, u32[]{:S(2)}) collective-permute-start(bf16[128,2048]{1,0:T(8,128)(2,1)S(1)} %copy-done.1), channel_id=1, source_target_pairs={{0,1},{1,2},{2,3},{3,0},{4,5},{5,6},{6,7},{7,4},{8,9},{9,10},{10,1... | collective-permute-start | bytes 1572872 | tf_op jit(solution)/shard_map/ppermute | solution.py:152
  18.4 16.3 %collective-permute-start.4 = (bf16[128,2048]{1,0:T(8,128)(2,1)S(1)}, bf16[128,2048]{1,0:T(8,128)(2,1)S(1)}, u32[]{:S(2)}, u32[]{:S(2)}) collective-permute-start(bf16[128,2048]{1,0:T(8,128)(2,1)S(1)} %copy-done.1), channel_id=1, source_target_pairs={{0,2},{1,3},{2,0},{3,1},{4,6},{5,7},{6,4},{7,5},{8,10},{9,11},{10,... | collective-permute-start | bytes 1572872 | tf_op jit(solution)/shard_map/ppermute | solution.py:152
  19.5 24.4 %collective-permute-start.5 = (bf16[128,2048]{1,0:T(8,128)(2,1)S(1)}, bf16[128,2048]{1,0:T(8,128)(2,1)S(1)}, u32[]{:S(2)}, u32[]{:S(2)}) collective-permute-start(bf16[128,2048]{1,0:T(8,128)(2,1)S(1)} %copy-done.1), channel_id=1, source_target_pairs={{0,3},{1,0},{2,1},{3,2},{4,7},{5,4},{6,5},{7,6},{8,11},{9,8},{10,9... | collective-permute-start | bytes 1572872 | tf_op jit(solution)/shard_map/ppermute | solution.py:152
  21.7 25.0 %copy-start.17 = (f32[128,129]{1,0:T(8,128)S(1)}, f32[128,129]{1,0:T(8,128)}, u32[]{:S(2)}) copy-start(f32[128,129]{1,0:T(8,128)} %constant.99) | copy-start | bytes 198148
  21.7 25.0 %copy-start.23 = (bf16[128,256]{1,0:T(8,128)(2,1)S(1)}, bf16[128,256]{1,0:T(8,128)(2,1)}, u32[]{:S(2)}) copy-start(bf16[128,256]{1,0:T(8,128)(2,1)} %param.10) | copy-start | bytes 196612
  21.7 25.0 %copy-start.31 = (f32[256]{0:T(256)S(1)}, f32[256]{0:T(256)}, u32[]{:S(2)}) copy-start(f32[256]{0:T(256)} %param.15) | copy-start | bytes 3076
  29.8 14.1 %collective-permute-start.1 = (f32[32,128]{1,0:T(8,128)S(1)}, f32[32,128]{1,0:T(8,128)S(1)}, u32[]{:S(2)}, u32[]{:S(2)}) collective-permute-start(f32[32,128]{1,0:T(8,128)S(1)} %pad_maximum_fusion.5), channel_id=1, source_target_pairs={{0,4},{4,0},{8,12},{12,8},{16,20},{20,16},{24,28},{28,24},{32,36},... | collective-permute-start | bytes 49160 | tf_op jit(solution)/shard_map/ppermute | solution.py:149
  29.9 17.9 %collective-permute-start.6 = (bf16[128,2048]{1,0:T(8,128)(2,1)S(1)}, bf16[128,2048]{1,0:T(8,128)(2,1)S(1)}, u32[]{:S(2)}, u32[]{:S(2)}) collective-permute-start(bf16[128,2048]{1,0:T(8,128)(2,1)S(1)} %copy-done.1), channel_id=1, source_target_pairs={{0,4},{4,0},{8,12},{12,8},{16,20},{20,16},{24,28},{28,24},{32,36},... | collective-permute-start | bytes 1572872 | tf_op jit(solution)/shard_map/ppermute | solution.py:149
  31.7 16.9 %collective-permute-start.7 = (bf16[128,2048]{1,0:T(8,128)(2,1)S(1)}, bf16[128,2048]{1,0:T(8,128)(2,1)S(1)}, u32[]{:S(2)}, u32[]{:S(2)}) collective-permute-start(bf16[128,2048]{1,0:T(8,128)(2,1)S(1)} %collective-permute-done.3.refs_3_.refs_1_), channel_id=1, source_target_pairs={{0,4},{4,0},{8,12},{12,8},{16,20},{20,16},{24,28},{28,24},{32,36},... | collective-permute-start | bytes 1572872 | tf_op jit(solution)/shard_map/ppermute | solution.py:149
  34.7 13.9 %collective-permute-start.8 = (bf16[128,2048]{1,0:T(8,128)(2,1)S(1)}, bf16[128,2048]{1,0:T(8,128)(2,1)S(1)}, u32[]{:S(2)}, u32[]{:S(2)}) collective-permute-start(bf16[128,2048]{1,0:T(8,128)(2,1)S(1)} %collective-permute-done.4.refs_4_.refs_2_), channel_id=1, source_target_pairs={{0,4},{4,0},{8,12},{12,8},{16,20},{20,16},{24,28},{28,24},{32,36},... | collective-permute-start | bytes 1572872 | tf_op jit(solution)/shard_map/ppermute | solution.py:149
  43.9 4.8 %collective-permute-start.9 = (bf16[128,2048]{1,0:T(8,128)(2,1)S(1)}, bf16[128,2048]{1,0:T(8,128)(2,1)S(1)}, u32[]{:S(2)}, u32[]{:S(2)}) collective-permute-start(bf16[128,2048]{1,0:T(8,128)(2,1)S(1)} %collective-permute-done.5.refs_5_.refs_3_), channel_id=1, source_target_pairs={{0,4},{4,0},{8,12},{12,8},{16,20},{20,16},{24,28},{28,24},{32,36},... | collective-permute-start | bytes 1572872 | tf_op jit(solution)/shard_map/ppermute | solution.py:149
  47.0 1.7 %collective-permute-start.2 = (bf16[128,256]{1,0:T(8,128)(2,1)S(1)}, bf16[128,256]{1,0:T(8,128)(2,1)S(1)}, u32[]{:S(2)}, u32[]{:S(2)}) collective-permute-start(bf16[128,256]{1,0:T(8,128)(2,1)S(1)} %get-tuple-element.42.refs_0_.result_ref), channel_id=1, source_target_pairs={{0,4},{4,0},{8,12},{12,8},{16,20},{20,16},{24,28},{28,24},{32,36},... | collective-permute-start | bytes 196616 | tf_op jit(solution)/shard_map/ppermute | solution.py:149
  47.8 5.2 %copy-start = (bf16[256,8192]{1,0:T(8,128)(2,1)S(1)}, bf16[256,8192]{1,0:T(8,128)(2,1)}, u32[]{:S(2)}) copy-start(bf16[256,8192]{1,0:T(8,128)(2,1)} %refs_4_.1) | copy-start | bytes 12582916
  53.0 2.7 %copy-start.8 = (bf16[8,256,128]{2,1,0:T(8,128)(2,1)}, bf16[8,256,128]{2,1,0:T(8,128)(2,1)S(1)}, u32[]{:S(2)}) copy-start(bf16[8,256,128]{2,1,0:T(8,128)(2,1)S(1)} %get-tuple-element.41) | copy-start | bytes 1572868
  53.0 2.7 %copy-start.24 = (bf16[128,256]{1,0:T(8,128)(2,1)S(1)}, bf16[128,256]{1,0:T(8,128)(2,1)}, u32[]{:S(2)}) copy-start(bf16[128,256]{1,0:T(8,128)(2,1)} %param.10) | copy-start | bytes 196612
  53.0 4.0 %copy-start.16 = (f32[258,128]{1,0:T(8,128)S(1)}, f32[258,128]{1,0:T(8,128)}, u32[]{:S(2)}) copy-start(f32[258,128]{1,0:T(8,128)} %constant.96.clone) | copy-start | bytes 396292
  53.0 4.3 %copy-start.21 = (f32[128,129]{1,0:T(8,128)S(1)}, f32[128,129]{1,0:T(8,128)}, u32[]{:S(2)}) copy-start(f32[128,129]{1,0:T(8,128)} %constant.98) | copy-start | bytes 198148
  53.0 5.0 %copy-start.18 = (f32[128,129]{1,0:T(8,128)S(1)}, f32[128,129]{1,0:T(8,128)}, u32[]{:S(2)}) copy-start(f32[128,129]{1,0:T(8,128)} %constant.99) | copy-start | bytes 198148
  57.4 40.2 %copy-start.9 = (bf16[8,256,128]{2,1,0:T(8,128)(2,1)S(1)}, bf16[8,256,128]{2,1,0:T(8,128)(2,1)}, u32[]{:S(2)}) copy-start(bf16[8,256,128]{2,1,0:T(8,128)(2,1)} %copy-done.8) | copy-start | bytes 1572868
  59.1 44.8 %copy-start.7 = (bf16[128,2048]{1,0:T(8,128)(2,1)S(1)}, bf16[128,2048]{1,0:T(8,128)(2,1)}, u32[]{:S(2)}) copy-start(bf16[128,2048]{1,0:T(8,128)(2,1)} %copy-done.6) | copy-start | bytes 1572868
  59.1 46.0 %copy-start.5 = (bf16[128,2048]{1,0:T(8,128)(2,1)S(1)}, bf16[128,2048]{1,0:T(8,128)(2,1)}, u32[]{:S(2)}) copy-start(bf16[128,2048]{1,0:T(8,128)(2,1)} %copy-done.4) | copy-start | bytes 1572868
  59.1 50.2 %copy-start.3 = (bf16[128,2048]{1,0:T(8,128)(2,1)S(1)}, bf16[128,2048]{1,0:T(8,128)(2,1)}, u32[]{:S(2)}) copy-start(bf16[128,2048]{1,0:T(8,128)(2,1)} %copy-done.2) | copy-start | bytes 1572868
  61.6 4.2 %copy-start.30 = (f32[16,256]{1,0:T(8,128)}, f32[16,256]{1,0:T(8,128)S(1)}, u32[]{:S(2)}) copy-start(f32[16,256]{1,0:T(8,128)S(1)} %exponential_negate_fusion.1) | copy-start | bytes 49156
  65.8 1.6 %collective-permute-start.13 = (f32[49,256]{1,0:T(8,128)}, f32[49,256]{1,0:T(8,128)}, u32[]{:S(2)}, u32[]{:S(2)}) collective-permute-start(f32[49,256]{1,0:T(8,128)} %pad_maximum_fusion), channel_id=1, source_target_pairs={{0,4},{4,0},{8,12},{12,8},{16,20},{20,16},{24,28},{28,24},{32,36},... | collective-permute-start | bytes 150536 | tf_op jit(solution)/shard_map/ppermute | solution.py:149
  70.3 16.1 %all-to-all-start.1 = ((bf16[8,49,128]{2,1,0:T(8,128)(2,1)}), bf16[8,49,128]{2,1,0:T(8,128)(2,1)}, u32[]{:S(2)}, u32[]{:S(2)}) async-start(bf16[8,49,128]{2,1,0:T(8,128)(2,1)} %broadcast_in_dim.86), calls=%async_computation.1 | async-start | bytes 229376 | tf_op jit(solution)/shard_map/all_to_all | solution.py:162
  89.3 8.2 %collective-permute-start.14 = (bf16[49,128]{1,0:T(8,128)(2,1)}, bf16[49,128]{1,0:T(8,128)(2,1)}, u32[]{:S(2)}, u32[]{:S(2)}) collective-permute-start(bf16[49,128]{1,0:T(8,128)(2,1)} %pad_maximum_fusion.7), channel_id=1, source_target_pairs={{0,192},{4,196},{8,200},{12,204},{16,208},{20,212},{24,216},{28,22... | collective-permute-start | bytes 37640 | tf_op jit(solution)/shard_map/ppermute | solution.py:156
  92.0 6.9 %collective-permute-start.15 = (bf16[49,128]{1,0:T(8,128)(2,1)}, bf16[49,128]{1,0:T(8,128)(2,1)}, u32[]{:S(2)}, u32[]{:S(2)}) collective-permute-start(bf16[49,128]{1,0:T(8,128)(2,1)} %pad_maximum_fusion.7), channel_id=1, source_target_pairs={{0,128},{4,132},{8,136},{12,140},{16,144},{20,148},{24,152},{28,15... | collective-permute-start | bytes 37640 | tf_op jit(solution)/shard_map/ppermute | solution.py:156
  92.8 6.8 %collective-permute-start.16 = (bf16[49,128]{1,0:T(8,128)(2,1)}, bf16[49,128]{1,0:T(8,128)(2,1)}, u32[]{:S(2)}, u32[]{:S(2)}) collective-permute-start(bf16[49,128]{1,0:T(8,128)(2,1)} %pad_maximum_fusion.7), channel_id=1, source_target_pairs={{0,64},{4,68},{8,72},{12,76},{16,80},{20,84},{24,88},{28,92},{32,9... | collective-permute-start | bytes 37640 | tf_op jit(solution)/shard_map/ppermute | solution.py:156
  93.7 15.6 %collective-permute-start.18 = (bf16[8,256,128]{2,1,0:T(8,128)(2,1)}, bf16[8,256,128]{2,1,0:T(8,128)(2,1)S(1)}, u32[]{:S(2)}, u32[]{:S(2)}) collective-permute-start(bf16[8,256,128]{2,1,0:T(8,128)(2,1)} %copy-done.11), channel_id=1, source_target_pairs={{0,64},{4,68},{8,72},{12,76},{16,80},{20,84},{24,88},{28,92},{32,9... | collective-permute-start | bytes 1572872 | tf_op jit(solution)/shard_map/ppermute | solution.py:156
  95.5 23.5 %collective-permute-start.19 = (bf16[8,256,128]{2,1,0:T(8,128)(2,1)}, bf16[8,256,128]{2,1,0:T(8,128)(2,1)S(1)}, u32[]{:S(2)}, u32[]{:S(2)}) collective-permute-start(bf16[8,256,128]{2,1,0:T(8,128)(2,1)} %copy-done.10), channel_id=1, source_target_pairs={{0,128},{4,132},{8,136},{12,140},{16,144},{20,148},{24,152},{28,15... | collective-permute-start | bytes 1572872 | tf_op jit(solution)/shard_map/ppermute | solution.py:156
  97.5 21.5 %collective-permute-start.20 = (bf16[8,256,128]{2,1,0:T(8,128)(2,1)S(1)}, bf16[8,256,128]{2,1,0:T(8,128)(2,1)S(1)}, u32[]{:S(2)}, u32[]{:S(2)}) collective-permute-start(bf16[8,256,128]{2,1,0:T(8,128)(2,1)S(1)} %copy-done.9), channel_id=1, source_target_pairs={{0,192},{4,196},{8,200},{12,204},{16,208},{20,212},{24,216},{28,22... | collective-permute-start | bytes 1572872 | tf_op jit(solution)/shard_map/ppermute | solution.py:156
  101.8 3.3 %collective-permute-start.17 = (f32[49,128]{1,0:T(8,128)S(1)}, f32[49,128]{1,0:T(8,128)S(1)}, u32[]{:S(2)}, u32[]{:S(2)}) collective-permute-start(f32[49,128]{1,0:T(8,128)S(1)} %pad_maximum_fusion.2), channel_id=1, source_target_pairs={{0,4},{4,0},{8,12},{12,8},{16,20},{20,16},{24,28},{28,24},{32,36},... | collective-permute-start | bytes 75272 | tf_op jit(solution)/shard_map/ppermute | solution.py:149
  103.9 19.7 %copy-start.34 = (f32[128]{0:T(128)S(1)}, f32[128]{0:T(128)}, u32[]{:S(2)}) copy-start(f32[128]{0:T(128)} %copy-done.33) | copy-start | bytes 1540
  103.9 23.0 %collective-permute-start.10 = (bf16[128,2048]{1,0:T(8,128)(2,1)S(1)}, bf16[128,2048]{1,0:T(8,128)(2,1)}, u32[]{:S(2)}, u32[]{:S(2)}) collective-permute-start(bf16[128,2048]{1,0:T(8,128)(2,1)S(1)} %copy-done.7), channel_id=1, source_target_pairs={{0,1},{1,2},{2,3},{3,0},{4,5},{5,6},{6,7},{7,4},{8,9},{9,10},{10,1... | collective-permute-start | bytes 1572872 | tf_op jit(solution)/shard_map/ppermute | solution.py:152
  105.2 21.7 %collective-permute-start.11 = (bf16[128,2048]{1,0:T(8,128)(2,1)S(1)}, bf16[128,2048]{1,0:T(8,128)(2,1)}, u32[]{:S(2)}, u32[]{:S(2)}) collective-permute-start(bf16[128,2048]{1,0:T(8,128)(2,1)S(1)} %copy-done.5), channel_id=1, source_target_pairs={{0,2},{1,3},{2,0},{3,1},{4,6},{5,7},{6,4},{7,5},{8,10},{9,11},{10,... | collective-permute-start | bytes 1572872 | tf_op jit(solution)/shard_map/ppermute | solution.py:152
  109.3 15.5 %copy-start.32 = (f32[256]{0:T(256)S(1)}, f32[256]{0:T(256)}, u32[]{:S(2)}) copy-start(f32[256]{0:T(256)} %param.15) | copy-start | bytes 3076
  109.3 22.7 %collective-permute-start.12 = (bf16[128,2048]{1,0:T(8,128)(2,1)S(1)}, bf16[128,2048]{1,0:T(8,128)(2,1)}, u32[]{:S(2)}, u32[]{:S(2)}) collective-permute-start(bf16[128,2048]{1,0:T(8,128)(2,1)S(1)} %copy-done.3), channel_id=1, source_target_pairs={{0,3},{1,0},{2,1},{3,2},{4,7},{5,4},{6,5},{7,6},{8,11},{9,8},{10,9... | collective-permute-start | bytes 1572872 | tf_op jit(solution)/shard_map/ppermute | solution.py:152
  119.0 4.6 %copy-start.29 = (f32[16,256]{1,0:T(8,128)S(1)}, f32[16,256]{1,0:T(8,128)}, u32[]{:S(2)}) copy-start(f32[16,256]{1,0:T(8,128)} %get-tuple-element.80) | copy-start | bytes 49156
  120.1 20.0 %all-to-all-start.2 = ((bf16[8,256,128]{2,1,0:T(8,128)(2,1)}), bf16[8,256,128]{2,1,0:T(8,128)(2,1)S(1)}, u32[]{:S(2)}, u32[]{:S(2)}) async-start(bf16[8,256,128]{2,1,0:T(8,128)(2,1)} %add_convert_fusion), calls=%async_computation.2 | async-start | bytes 1048576 | tf_op jit(solution)/shard_map/all_to_all | solution.py:316
  (11 other events, 12.3 us)

commit v10 on v9

--- a/solution.py
+++ b/solution.py
@@ -43,52 +43,45 @@
     return [pl.BlockSpec(memory_space=pltpu.VMEM)] * count
 
 
-def weight_parts(turns, result, result_other, blocks, taken, width):
+def weight_part(step, turns, result, result_other, blocks, taken, width):
     count = len(blocks)
     tokens, chans = result.shape
     tiles = blocks[0].shape[1] // (2 * width)
 
-    def kernel(turns_ref, *refs):
-        mine_ref, other_ref = refs[:2]
-        block_refs, taken_refs = refs[2 : 2 + count], refs[2 + count : 2 + 2 * count]
-        out_refs = refs[2 + 2 * count : 2 + 3 * count]
-        all_ref, part_ref, in_sems, out_sems = refs[2 + 3 * count :]
+    def kernel(turns_ref, mine_ref, other_ref, *refs):
+        block_refs, taken_refs = refs[:count], refs[count : 2 * count]
+        out_ref, rows_ref, sem = refs[2 * count :]
         core = turns_ref[0]
+        chosen = (turns_ref[1] - step + count) % count
         for k in range(count):
-            for i in range(tiles):
-                at = pl.multiple_of((2 * i + core) * width, width)
-                lanes = pl.ds(i * width, width)
-                for half, source in enumerate((block_refs[k], taken_refs[k])):
-                    pltpu.make_async_copy(
-                        source.at[:, pl.ds(at, width)],
-                        all_ref.at[k, pl.ds(half * tokens, tokens), lanes],
-                        in_sems.at[k],
-                    ).start()
+
+            @pl.when(chosen == k)
+            def _():
+                for i in range(tiles):
+                    at = pl.multiple_of((2 * i + core) * width, width)
+                    for half, source in enumerate((block_refs[k], taken_refs[k])):
+                        pltpu.make_async_copy(
+                            source.at[:, pl.ds(at, width)],
+                            rows_ref.at[pl.ds(half * tokens, tokens), pl.ds(i * width, width)],
+                            sem,
+                        ).start()
+
         left = jnp.concatenate([mine_ref[...], other_ref[...]], 0).T
-        for k in range(count):
-            pltpu.make_async_copy(all_ref.at[k], all_ref.at[k], in_sems.at[k]).wait()
-        for s in range(count):
-            part = jnp.dot(
-                left, all_ref[(turns_ref[1] - s + count) % count], preferred_element_type=F32
-            ).astype(BF16)
-            for i in range(tiles):
-                part_ref[s, i] = part[:, i * width : (i + 1) * width]
-            pltpu.make_async_copy(part_ref.at[s], out_refs[s], out_sems.at[s]).start()
-        for s in range(count):
-            pltpu.make_async_copy(part_ref.at[s], out_refs[s], out_sems.at[s]).wait()
+        pltpu.make_async_copy(rows_ref, rows_ref, sem).wait()
+        part = jnp.dot(left, rows_ref[...], preferred_element_type=F32).astype(BF16)
+        for i in range(tiles):
+            out_ref[i] = part[:, i * width : (i + 1) * width]
 
     return pl.pallas_call(
         kernel,
-        out_shape=[jax.ShapeDtypeStruct((tiles, chans, width), BF16)] * count,
+        out_shape=jax.ShapeDtypeStruct((tiles, chans, width), BF16),
         in_specs=[pl.BlockSpec(memory_space=pltpu.SMEM)]
         + in_vmem(2)
         + [pl.BlockSpec(memory_space=pl.ANY)] * (2 * count),
-        out_specs=[pl.BlockSpec(memory_space=pl.ANY)] * count,
+        out_specs=in_vmem(1)[0],
         scratch_shapes=[
-            pltpu.VMEM((count, 2 * tokens, tiles * width), BF16),
-            pltpu.VMEM((count, tiles, chans, width), BF16),
-            pltpu.SemaphoreType.DMA((count,)),
-            pltpu.SemaphoreType.DMA((count,)),
+            pltpu.VMEM((2 * tokens, tiles * width), BF16),
+            pltpu.SemaphoreType.DMA,
         ],
         compiler_params=pltpu.CompilerParams(vmem_limit_bytes=6 * 2**20),
     )(turns, result, result_other, *blocks, *taken)
@@ -241,8 +234,10 @@
     turns = jnp.stack([core, (tp - yy) % tps, tp]).astype(jnp.int32)
     taken = [row_major(swap_core(a)) for a in og]
     result_other = swap_core(result)
-    y_parts = weight_parts(turns, result, result_other, og, taken, width)
-    over_y = [y_parts[0]] + [shift_y(y_parts[s], s) for s in range(1, ny)]
+    y_parts, over_y = [None] * ny, [None] * ny
+    for s in (2, 1, 3, 0):
+        y_parts[s] = weight_part(s, turns, result, result_other, og, taken, width)
+        over_y[s] = shift_y(y_parts[s], s) if s else y_parts[s]
     summed_y = sum(a.astype(F32) for a in over_y).astype(BF16)
 
     late = lax.optimization_barrier((result, gated, *y_parts))

time: 144 us -> 150 us (1.042)
  waiting for transfers between devices: 52.8 us -> 57.2 us
  Pallas kernels: 5.34 us -> 7.32 us
  local copies, waits for them, and re-layouts: 5.15 us -> 6.87 us
  starting transfers between devices: 41.5 us -> 39.9 us
    ppermute x6, waiting for transfers between devices: 18.7 us -> 24.2 us  [shift_tp(): return lax.ppermute(a, 'tp', [(i, (i + k) % tps) for i in range(tps)])]
    all_to_all x1, waiting for transfers between devices: 5.6 us -> 1.64 us  [body(): lax.all_to_all(summed_y, 'ctx', 0, 0, tiled=True, axis_index_groups=z_gro...]
    ppermute x6, waiting for transfers between devices: 9.2 us -> 11.9 us  [shift_y(): lax.ppermute(a, 'ctx', [(i, (i // per + k) % ny * per + i % per) for i in...]
    pallas_call x1 -> x4, Pallas kernels: 2.73 us -> 4.7 us  [weight_part(): pl.pallas_call(kernel, out_shape=jax.ShapeDtypeStruct((tiles, chans, widt...]
    unnamed x70 -> x74, local copies, waits for them, and re-layouts: 1.98 us -> 3.77 us
  transfers between devices with their start and end apart: 24 -> 24, of which waited for: 12 -> 14; matrix products, arithmetic and copies ran while one was open for 13% -> 12% of each run, Pallas kernels for 0% -> 0%
where the time goes in v10:
time: 150 us; the launch traced here: 147 us
  waiting for transfers between devices  57.2 us (38%)
  starting transfers between devices  39.9 us (27%)
  other arithmetic  28 us (19%)
  Pallas kernels  7.32 us (5%)
  local copies, waits for them, and re-layouts  6.87 us (5%)
  matrix products  6.6 us (4%)
    ppermute x6, waiting for transfers between devices, shift_tp(): return lax.ppermute(a, 'tp', [(i, (i + k) % tps) for i in range(tps)])  24.2 us
    ppermute x6, waiting for transfers between devices, shift_y(): lax.ppermute(a, 'ctx', [(i, (i // per + k) % ny * per + i % per) for i in...  11.9 us
    all_to_all x1, starting transfers between devices, of_pairs(): lax.all_to_all(copies, 'ctx', 0, 0, tiled=True, axis_index_groups=groups)  11.6 us
    all_to_all x1, waiting for transfers between devices, of_plane(): lax.all_to_all(copies, 'ctx', 0, 0, tiled=True, axis_index_groups=z_groups)  8.32 us
    ppermute x6, starting transfers between devices, shift_y(): lax.ppermute(a, 'ctx', [(i, (i // per + k) % ny * per + i % per) for i in...  8.31 us
    ppermute x6, starting transfers between devices, shift_tp(): return lax.ppermute(a, 'tp', [(i, (i + k) % tps) for i in range(tps)])  8.08 us
    all_to_all x1, waiting for transfers between devices, of_pairs(): lax.all_to_all(copies, 'ctx', 0, 0, tiled=True, axis_index_groups=groups)  7.83 us
    all_to_all x1, starting transfers between devices, of_plane(): lax.all_to_all(copies, 'ctx', 0, 0, tiled=True, axis_index_groups=z_groups)  6.69 us
  transfers between devices with their start and end apart: 24, of which 14 were waited for; matrix products, arithmetic and copies ran while one was open for 12% of the time, Pallas kernels for 0%

profile of v10, /device:TPU:2, one launch (start us, length us, event | category | flops | bytes accessed | tf_op | source)
XLA Modules:
  0.0 147.2 jit_solution(1233584659055623730)
XLA Ops:
  1.5 0.9 convert_multiply_fusion.5
  3.2 1.2 collective-permute-done
  5.2 11.6 %all-to-all-start = ((bf16[32,32,128]{2,1,0:T(8,128)(2,1)}), bf16[32,32,128]{2,1,0:T(8,128)(2,1)S(1)}, u32[]{:S(2)}, u32[]{:S(2)}) async-start(bf16[32,32,128]{2,1,0:T(8,128)(2,1)} %broadcast_in_dim.49), calls=%async_computation | async-start | bytes 524288 | tf_op jit(solution)/shard_map/all_to_all | solution.py:160
  16.9 1.6 %collective-permute-start.3 = (bf16[128,2048]{1,0:T(8,128)(2,1)S(1)}, bf16[128,2048]{1,0:T(8,128)(2,1)S(1)}, u32[]{:S(2)}, u32[]{:S(2)}) collective-permute-start(bf16[128,2048]{1,0:T(8,128)(2,1)S(1)} %copy-done), channel_id=1, source_target_pairs={{0,1},{1,2},{2,3},{3,0},{4,5},{5,6},{6,7},{7,4},{8,9},{9,10},{10,1... | collective-permute-start | bytes 1572872 | tf_op jit(solution)/shard_map/ppermute | solution.py:145
  18.4 1.1 collective-permute-start.4
  19.5 2.2 %collective-permute-start.5 = (bf16[128,2048]{1,0:T(8,128)(2,1)S(1)}, bf16[128,2048]{1,0:T(8,128)(2,1)S(1)}, u32[]{:S(2)}, u32[]{:S(2)}) collective-permute-start(bf16[128,2048]{1,0:T(8,128)(2,1)S(1)} %copy-done), channel_id=1, source_target_pairs={{0,3},{1,0},{2,1},{3,2},{4,7},{5,4},{6,5},{7,6},{8,11},{9,8},{10,9... | collective-permute-start | bytes 1572872 | tf_op jit(solution)/shard_map/ppermute | solution.py:145
  21.7 7.8 %all-to-all-done = bf16[32,32,128]{2,1,0:T(8,128)(2,1)S(1)} async-done(((bf16[32,32,128]{2,1,0:T(8,128)(2,1)}), bf16[32,32,128]{2,1,0:T(8,128)(2,1)S(1)}, u32[]{:S(2)}, u32[]{:S(2)}) %all-to-all-start) | async-done | bytes 262176 | tf_op jit(solution)/shard_map/all_to_all | solution.py:160
  30.4 1.3 collective-permute-done.3.refs_1_
  31.7 3.0 %collective-permute-done.4.refs_2_ = bf16[128,2048]{1,0:T(8,128)(2,1)S(1)} collective-permute-done((bf16[128,2048]{1,0:T(8,128)(2,1)S(1)}, bf16[128,2048]{1,0:T(8,128)(2,1)S(1)}, u32[]{:S(2)}, u32[]{:S(2)}) %collective-permute-start.4) | collective-permute-done | bytes 524320 | tf_op jit(solution)/shard_map/ppermute | solution.py:145
  34.7 9.2 %collective-permute-done.5.refs_3_ = bf16[128,2048]{1,0:T(8,128)(2,1)S(1)} collective-permute-done((bf16[128,2048]{1,0:T(8,128)(2,1)S(1)}, bf16[128,2048]{1,0:T(8,128)(2,1)S(1)}, u32[]{:S(2)}, u32[]{:S(2)}) %collective-permute-start.5) | collective-permute-done | bytes 524320 | tf_op jit(solution)/shard_map/ppermute | solution.py:145
  47.7 0.8 collective-permute-done.2.other_ref
  48.5 1.1 shard_map.164
  49.6 0.8 copy-done.6
  50.4 1.1 shard_map.163
  52.4 1.1 shard_map.162
  53.5 1.3 shard_map.161
  54.9 1.0 copy-done.1
  55.9 2.6 %shard_map.165 = (f32[128,256]{1,0:T(8,128)S(1)}, bf16[128,2048]{1,0:T(8,128)(2,1)S(1)}, bf16[128,2048]{1,0:T(8,128)(2,1)S(1)}, bf16[128,2048]{1,0:T(8,128)(2,1)S(1)}, bf16[128,2048]{1,0:T(8,128)(2,1)S(1)}) custom-call(s32[3]{0:T(128)S(1)} %pad_add_fusion.turns_ref, bf16[128,256]{1,0:T(8,128)(2,1)S(1)} %get-tuple-element.34.mine_ref.result_ref, ...), custom_call_target="tpu_custom_call" | custom-call | tf_op jit(solution)/shard_map/pallas_call | solution.py:114
  58.5 0.8 copy-done.11
  59.3 1.3 fusion.37
  61.7 1.1 fusion.5
  62.7 1.7 %copy.34 = f32[128,256]{1,0:T(8,128)} copy(f32[128,256]{0,1:T(8,128)} %fusion.5) | data formatting | bytes 262144 | tf_op jit(solution)/shard_map/dot_general | solution.py:33
  65.2 2.1 %fusion.3 = (f32[16,256]{1,0:T(8,128)S(1)}, f32[16,256]{1,0:T(8,128)S(1)}, f32[16,256]{1,0:T(8,128)S(1)}, f32[16,256]{1,0:T(8,128)S(1)}) fusion(f32[128,256]{1,0:T(8,128)} %copy.34, f32[16,256]{1,0:T(8,128)S(1)} %exponential_negate_fusion.1, f32[128,256]{1,0:T(8,128)} %copy-done.21), kind=kLoop, calls=%fused_computation.7 | loop fusion | flops 4702208 | bytes 344064 | tf_op jit(solution)/shard_map/reduce_sum | solution.py:276
  68.0 1.3 pad_maximum_fusion
  69.7 1.2 collective-permute-done.13
  73.8 6.7 %all-to-all-start.1 = ((bf16[8,49,128]{2,1,0:T(8,128)(2,1)}), bf16[8,49,128]{2,1,0:T(8,128)(2,1)}, u32[]{:S(2)}, u32[]{:S(2)}) async-start(bf16[8,49,128]{2,1,0:T(8,128)(2,1)} %broadcast_in_dim.86), calls=%async_computation.1 | async-start | bytes 229376 | tf_op jit(solution)/shard_map/all_to_all | solution.py:155
  81.5 8.3 %all-to-all-done.1 = bf16[8,49,128]{2,1,0:T(8,128)(2,1)} async-done(((bf16[8,49,128]{2,1,0:T(8,128)(2,1)}), bf16[8,49,128]{2,1,0:T(8,128)(2,1)}, u32[]{:S(2)}, u32[]{:S(2)}) %all-to-all-start.1) | async-done | bytes 100384 | tf_op jit(solution)/shard_map/all_to_all | solution.py:155
  89.8 0.9 convert_element_type.137
  90.8 1.4 multiply_reduce_fusion.8
  92.8 2.7 %collective-permute-start.14 = (bf16[49,128]{1,0:T(8,128)(2,1)}, bf16[49,128]{1,0:T(8,128)(2,1)}, u32[]{:S(2)}, u32[]{:S(2)}) collective-permute-start(bf16[49,128]{1,0:T(8,128)(2,1)} %pad_maximum_fusion.7), channel_id=1, source_target_pairs={{0,192},{4,196},{8,200},{12,204},{16,208},{20,212},{24,216},{28,22... | collective-permute-start | bytes 37640 | tf_op jit(solution)/shard_map/ppermute | solution.py:149
  95.5 0.8 collective-permute-start.15
  96.3 0.9 collective-permute-start.16
  97.2 2.4 %collective-permute-start.20 = (bf16[8,256,128]{2,1,0:T(8,128)(2,1)S(1)}, bf16[8,256,128]{2,1,0:T(8,128)(2,1)S(1)}, u32[]{:S(2)}, u32[]{:S(2)}) collective-permute-start(bf16[8,256,128]{2,1,0:T(8,128)(2,1)S(1)} %copy-done.7), channel_id=1, source_target_pairs={{0,192},{4,196},{8,200},{12,204},{16,208},{20,212},{24,216},{28,22... | collective-permute-start | bytes 1572872 | tf_op jit(solution)/shard_map/ppermute | solution.py:149
  99.6 1.5 %collective-permute-start.19 = (bf16[8,256,128]{2,1,0:T(8,128)(2,1)S(1)}, bf16[8,256,128]{2,1,0:T(8,128)(2,1)S(1)}, u32[]{:S(2)}, u32[]{:S(2)}) collective-permute-start(bf16[8,256,128]{2,1,0:T(8,128)(2,1)S(1)} %copy-done.5), channel_id=1, source_target_pairs={{0,128},{4,132},{8,136},{12,140},{16,144},{20,148},{24,152},{28,15... | collective-permute-start | bytes 1572872 | tf_op jit(solution)/shard_map/ppermute | solution.py:149
  102.6 7.2 %collective-permute-done.16 = bf16[49,128]{1,0:T(8,128)(2,1)} collective-permute-done((bf16[49,128]{1,0:T(8,128)(2,1)}, bf16[49,128]{1,0:T(8,128)(2,1)}, u32[]{:S(2)}, u32[]{:S(2)}) %collective-permute-start.16) | collective-permute-done | bytes 12576 | tf_op jit(solution)/shard_map/ppermute | solution.py:149
  112.0 1.9 %fusion.24 = f32[256,128]{0,1:T(8,128)} fusion(f32[128,129]{1,0:T(8,128)} %constant.98, f32[258,256]{1,0:T(8,128)} %copy-done.12, f32[258,256]{1,0:T(8,128)S(1)} %fusion.91), kind=kOutput, calls=%fused_computation.46 | convolution fusion | flops 25461504 | bytes 819200 | tf_op jit(solution)/shard_map/dot_general | solution.py:33
  113.9 1.3 collective-permute-start.10
  115.2 1.4 collective-permute-start.11
  117.2 1.4 fusion.72
  118.6 1.7 %collective-permute-done.20 = bf16[8,256,128]{2,1,0:T(8,128)(2,1)S(1)} collective-permute-done((bf16[8,256,128]{2,1,0:T(8,128)(2,1)S(1)}, bf16[8,256,128]{2,1,0:T(8,128)(2,1)S(1)}, u32[]{:S(2)}, u32[]{:S(2)}) %collective-permute-start.20) | collective-permute-done | bytes 524320 | tf_op jit(solution)/shard_map/ppermute | solution.py:149
  120.9 3.0 %collective-permute-done.18 = bf16[8,256,128]{2,1,0:T(8,128)(2,1)S(1)} collective-permute-done((bf16[8,256,128]{2,1,0:T(8,128)(2,1)S(1)}, bf16[8,256,128]{2,1,0:T(8,128)(2,1)S(1)}, u32[]{:S(2)}, u32[]{:S(2)}) %collective-permute-start.18) | collective-permute-done | bytes 524320 | tf_op jit(solution)/shard_map/ppermute | solution.py:149
  123.9 1.1 add_convert_fusion
  125.0 3.5 %all-to-all-start.2 = ((bf16[8,256,128]{2,1,0:T(8,128)(2,1)}), bf16[8,256,128]{2,1,0:T(8,128)(2,1)S(1)}, u32[]{:S(2)}, u32[]{:S(2)}) async-start(bf16[8,256,128]{2,1,0:T(8,128)(2,1)} %add_convert_fusion), calls=%async_computation.2 | async-start | bytes 1048576 | tf_op jit(solution)/shard_map/all_to_all | solution.py:311
  128.5 1.1 multiply_reduce_fusion
  129.7 1.9 %fusion.35 = (bf16[128,256]{1,0:T(8,128)(2,1)}, bf16[128,256]{1,0:T(8,128)(2,1)}) fusion(bf16[128,256]{1,0:T(8,128)(2,1)S(1)} %copy-done.15, bf16[128,256]{1,0:T(8,128)(2,1)S(1)} %copy-done.14, f32[128,256]{1,0:T(8,128)} %copy-done.21, f32[256]{0:T(256)S(1)} %copy-done.34, f32[128,256]{1,0:T(8,128)S(1)} %multiply_reduce_fusion, f32[256,128]{0,1:T(8,128)} %fusion.24, ...), kind=kOutput, calls=%fused_computation.57 | convolution fusion | flops 25789184 | bytes 1344512 | tf_op jit(solution)/shard_map/dot_general | solution.py:33
  131.9 10.4 %collective-permute-done.12 = bf16[128,2048]{1,0:T(8,128)(2,1)} collective-permute-done((bf16[128,2048]{1,0:T(8,128)(2,1)S(1)}, bf16[128,2048]{1,0:T(8,128)(2,1)}, u32[]{:S(2)}, u32[]{:S(2)}) %collective-permute-start.12) | collective-permute-done | bytes 524320 | tf_op jit(solution)/shard_map/ppermute | solution.py:145
  142.3 2.5 %add_convert_fusion.1 = bf16[128,2048]{1,0:T(8,128)(2,1)} fusion(bf16[128,2048]{1,0:T(8,128)(2,1)} %collective-permute-done.12, bf16[128,2048]{1,0:T(8,128)(2,1)} %collective-permute-done.11, bf16[128,2048]{1,0:T(8,128)(2,1)} %collective-permute-done.10, bf16[128,2048]{1,0:T(8,128)(2,1)S(1)} %get-tuple-element.35), kind=kLoop, calls=%fused_computation.26 | loop fusion | flops 2097152 | bytes 2621440 | tf_op jit(solution)/shard_map/convert_element_type | solution.py:250
  144.8 1.6 %all-to-all-done.2 = bf16[8,256,128]{2,1,0:T(8,128)(2,1)S(1)} async-done(((bf16[8,256,128]{2,1,0:T(8,128)(2,1)}), bf16[8,256,128]{2,1,0:T(8,128)(2,1)S(1)}, u32[]{:S(2)}, u32[]{:S(2)}) %all-to-all-start.2) | async-done | bytes 524320 | tf_op jit(solution)/shard_map/all_to_all | solution.py:311
  (140 shorter events, 20.9 us)
Async XLA Ops:
  0.6 43.3 %copy-start.24 = (f32[16,256]{1,0:T(8,128)S(1)}, f32[16,256]{1,0:T(8,128)}, u32[]{:S(2)}) copy-start(f32[16,256]{1,0:T(8,128)} %param.14) | copy-start | bytes 49156
  0.6 16.2 %copy-start = (bf16[128,2048]{1,0:T(8,128)(2,1)S(1)}, bf16[128,2048]{1,0:T(8,128)(2,1)}, u32[]{:S(2)}) copy-start(bf16[128,2048]{1,0:T(8,128)(2,1)} %refs_0_.9) | copy-start | bytes 1572868
  0.7 2.4 %copy-start.35 = (f32[128]{0:T(128)}, f32[128]{0:T(128)S(1)}, u32[]{:S(2)}) copy-start(f32[128]{0:T(128)S(1)} %iota_subtract_fusion) | copy-start | bytes 1540
  3.0 42.8 %copy-start.16 = (f32[258,128]{1,0:T(8,128)S(1)}, f32[258,128]{1,0:T(8,128)}, u32[]{:S(2)}) copy-start(f32[258,128]{1,0:T(8,128)} %constant.96.clone) | copy-start | bytes 396292
  3.1 1.3 collective-permute-start
  4.4 41.8 %copy-start.14 = (bf16[128,256]{1,0:T(8,128)(2,1)S(1)}, bf16[128,256]{1,0:T(8,128)(2,1)}, u32[]{:S(2)}) copy-start(bf16[128,256]{1,0:T(8,128)(2,1)} %param.12) | copy-start | bytes 196612
  4.4 41.8 %copy-start.15 = (bf16[128,256]{1,0:T(8,128)(2,1)S(1)}, bf16[128,256]{1,0:T(8,128)(2,1)}, u32[]{:S(2)}) copy-start(bf16[128,256]{1,0:T(8,128)(2,1)} %param.11) | copy-start | bytes 196612
  5.2 41.2 %copy-start.22 = (f32[128,129]{1,0:T(8,128)S(1)}, f32[128,129]{1,0:T(8,128)}, u32[]{:S(2)}) copy-start(f32[128,129]{1,0:T(8,128)} %constant.98) | copy-start | bytes 198148
  5.2 24.4 %all-to-all-start = ((bf16[32,32,128]{2,1,0:T(8,128)(2,1)}), bf16[32,32,128]{2,1,0:T(8,128)(2,1)S(1)}, u32[]{:S(2)}, u32[]{:S(2)}) async-start(bf16[32,32,128]{2,1,0:T(8,128)(2,1)} %broadcast_in_dim.49), calls=%async_computation | async-start | bytes 524288 | tf_op jit(solution)/shard_map/all_to_all | solution.py:160
  16.9 14.9 %collective-permute-start.3 = (bf16[128,2048]{1,0:T(8,128)(2,1)S(1)}, bf16[128,2048]{1,0:T(8,128)(2,1)S(1)}, u32[]{:S(2)}, u32[]{:S(2)}) collective-permute-start(bf16[128,2048]{1,0:T(8,128)(2,1)S(1)} %copy-done), channel_id=1, source_target_pairs={{0,1},{1,2},{2,3},{3,0},{4,5},{5,6},{6,7},{7,4},{8,9},{9,10},{10,1... | collective-permute-start | bytes 1572872 | tf_op jit(solution)/shard_map/ppermute | solution.py:145
  18.4 16.3 %collective-permute-start.4 = (bf16[128,2048]{1,0:T(8,128)(2,1)S(1)}, bf16[128,2048]{1,0:T(8,128)(2,1)S(1)}, u32[]{:S(2)}, u32[]{:S(2)}) collective-permute-start(bf16[128,2048]{1,0:T(8,128)(2,1)S(1)} %copy-done), channel_id=1, source_target_pairs={{0,2},{1,3},{2,0},{3,1},{4,6},{5,7},{6,4},{7,5},{8,10},{9,11},{10,... | collective-permute-start | bytes 1572872 | tf_op jit(solution)/shard_map/ppermute | solution.py:145
  19.5 24.4 %collective-permute-start.5 = (bf16[128,2048]{1,0:T(8,128)(2,1)S(1)}, bf16[128,2048]{1,0:T(8,128)(2,1)S(1)}, u32[]{:S(2)}, u32[]{:S(2)}) collective-permute-start(bf16[128,2048]{1,0:T(8,128)(2,1)S(1)} %copy-done), channel_id=1, source_target_pairs={{0,3},{1,0},{2,1},{3,2},{4,7},{5,4},{6,5},{7,6},{8,11},{9,8},{10,9... | collective-permute-start | bytes 1572872 | tf_op jit(solution)/shard_map/ppermute | solution.py:145
  21.7 25.0 %copy-start.18 = (f32[128,129]{1,0:T(8,128)S(1)}, f32[128,129]{1,0:T(8,128)}, u32[]{:S(2)}) copy-start(f32[128,129]{1,0:T(8,128)} %constant.99) | copy-start | bytes 198148
  21.7 25.0 %copy-start.25 = (bf16[128,256]{1,0:T(8,128)(2,1)S(1)}, bf16[128,256]{1,0:T(8,128)(2,1)}, u32[]{:S(2)}) copy-start(bf16[128,256]{1,0:T(8,128)(2,1)} %param.10) | copy-start | bytes 196612
  21.7 25.0 %copy-start.33 = (f32[256]{0:T(256)S(1)}, f32[256]{0:T(256)}, u32[]{:S(2)}) copy-start(f32[256]{0:T(256)} %param.15) | copy-start | bytes 3076
  29.8 14.1 %collective-permute-start.1 = (f32[32,128]{1,0:T(8,128)S(1)}, f32[32,128]{1,0:T(8,128)S(1)}, u32[]{:S(2)}, u32[]{:S(2)}) collective-permute-start(f32[32,128]{1,0:T(8,128)S(1)} %pad_maximum_fusion.5), channel_id=1, source_target_pairs={{0,4},{4,0},{8,12},{12,8},{16,20},{20,16},{24,28},{28,24},{32,36},... | collective-permute-start | bytes 49160 | tf_op jit(solution)/shard_map/ppermute | solution.py:142
  29.9 17.7 %collective-permute-start.6 = (bf16[128,2048]{1,0:T(8,128)(2,1)S(1)}, bf16[128,2048]{1,0:T(8,128)(2,1)S(1)}, u32[]{:S(2)}, u32[]{:S(2)}) collective-permute-start(bf16[128,2048]{1,0:T(8,128)(2,1)S(1)} %copy-done), channel_id=1, source_target_pairs={{0,4},{4,0},{8,12},{12,8},{16,20},{20,16},{24,28},{28,24},{32,36},... | collective-permute-start | bytes 1572872 | tf_op jit(solution)/shard_map/ppermute | solution.py:142
  31.7 16.8 %collective-permute-start.7 = (bf16[128,2048]{1,0:T(8,128)(2,1)S(1)}, bf16[128,2048]{1,0:T(8,128)(2,1)S(1)}, u32[]{:S(2)}, u32[]{:S(2)}) collective-permute-start(bf16[128,2048]{1,0:T(8,128)(2,1)S(1)} %collective-permute-done.3.refs_1_), channel_id=1, source_target_pairs={{0,4},{4,0},{8,12},{12,8},{16,20},{20,16},{24,28},{28,24},{32,36},... | collective-permute-start | bytes 1572872 | tf_op jit(solution)/shard_map/ppermute | solution.py:142
  34.7 13.8 %collective-permute-start.8 = (bf16[128,2048]{1,0:T(8,128)(2,1)S(1)}, bf16[128,2048]{1,0:T(8,128)(2,1)S(1)}, u32[]{:S(2)}, u32[]{:S(2)}) collective-permute-start(bf16[128,2048]{1,0:T(8,128)(2,1)S(1)} %collective-permute-done.4.refs_2_), channel_id=1, source_target_pairs={{0,4},{4,0},{8,12},{12,8},{16,20},{20,16},{24,28},{28,24},{32,36},... | collective-permute-start | bytes 1572872 | tf_op jit(solution)/shard_map/ppermute | solution.py:142
  43.9 4.6 %collective-permute-start.9 = (bf16[128,2048]{1,0:T(8,128)(2,1)S(1)}, bf16[128,2048]{1,0:T(8,128)(2,1)S(1)}, u32[]{:S(2)}, u32[]{:S(2)}) collective-permute-start(bf16[128,2048]{1,0:T(8,128)(2,1)S(1)} %collective-permute-done.5.refs_3_), channel_id=1, source_target_pairs={{0,4},{4,0},{8,12},{12,8},{16,20},{20,16},{24,28},{28,24},{32,36},... | collective-permute-start | bytes 1572872 | tf_op jit(solution)/shard_map/ppermute | solution.py:142
  47.0 1.5 %collective-permute-start.2 = (bf16[128,256]{1,0:T(8,128)(2,1)S(1)}, bf16[128,256]{1,0:T(8,128)(2,1)S(1)}, u32[]{:S(2)}, u32[]{:S(2)}) collective-permute-start(bf16[128,256]{1,0:T(8,128)(2,1)S(1)} %get-tuple-element.34.mine_ref.result_ref), channel_id=1, source_target_pairs={{0,4},{4,0},{8,12},{12,8},{16,20},{20,16},{24,28},{28,24},{32,36},... | collective-permute-start | bytes 196616 | tf_op jit(solution)/shard_map/ppermute | solution.py:142
  55.9 3.4 %copy-start.26 = (bf16[128,256]{1,0:T(8,128)(2,1)S(1)}, bf16[128,256]{1,0:T(8,128)(2,1)}, u32[]{:S(2)}) copy-start(bf16[128,256]{1,0:T(8,128)(2,1)} %param.10) | copy-start | bytes 196612
  55.9 4.8 %copy-start.17 = (f32[258,128]{1,0:T(8,128)S(1)}, f32[258,128]{1,0:T(8,128)}, u32[]{:S(2)}) copy-start(f32[258,128]{1,0:T(8,128)} %constant.96.clone) | copy-start | bytes 396292
  55.9 5.0 %copy-start.23 = (f32[128,129]{1,0:T(8,128)S(1)}, f32[128,129]{1,0:T(8,128)}, u32[]{:S(2)}) copy-start(f32[128,129]{1,0:T(8,128)} %constant.98) | copy-start | bytes 198148
  55.9 5.8 %copy-start.19 = (f32[128,129]{1,0:T(8,128)S(1)}, f32[128,129]{1,0:T(8,128)}, u32[]{:S(2)}) copy-start(f32[128,129]{1,0:T(8,128)} %constant.99) | copy-start | bytes 198148
  61.0 36.2 %copy-start.7 = (bf16[8,256,128]{2,1,0:T(8,128)(2,1)S(1)}, bf16[8,256,128]{2,1,0:T(8,128)(2,1)}, u32[]{:S(2)}) copy-start(bf16[8,256,128]{2,1,0:T(8,128)(2,1)} %copy-done.6) | copy-start | bytes 1572868
  61.0 38.6 %copy-start.5 = (bf16[8,256,128]{2,1,0:T(8,128)(2,1)S(1)}, bf16[8,256,128]{2,1,0:T(8,128)(2,1)}, u32[]{:S(2)}) copy-start(bf16[8,256,128]{2,1,0:T(8,128)(2,1)} %copy-done.4) | copy-start | bytes 1572868
  61.0 40.1 %copy-start.3 = (bf16[8,256,128]{2,1,0:T(8,128)(2,1)S(1)}, bf16[8,256,128]{2,1,0:T(8,128)(2,1)}, u32[]{:S(2)}) copy-start(bf16[8,256,128]{2,1,0:T(8,128)(2,1)} %copy-done.2) | copy-start | bytes 1572868
  62.7 57.6 %copy-start.9 = (bf16[128,2048]{1,0:T(8,128)(2,1)S(1)}, bf16[128,2048]{1,0:T(8,128)(2,1)}, u32[]{:S(2)}) copy-start(bf16[128,2048]{1,0:T(8,128)(2,1)} %copy-done.8) | copy-start | bytes 1572868
  65.2 4.2 %copy-start.32 = (f32[16,256]{1,0:T(8,128)}, f32[16,256]{1,0:T(8,128)S(1)}, u32[]{:S(2)}) copy-start(f32[16,256]{1,0:T(8,128)S(1)} %exponential_negate_fusion.1) | copy-start | bytes 49156
  69.3 1.6 %collective-permute-start.13 = (f32[49,256]{1,0:T(8,128)}, f32[49,256]{1,0:T(8,128)}, u32[]{:S(2)}, u32[]{:S(2)}) collective-permute-start(f32[49,256]{1,0:T(8,128)} %pad_maximum_fusion), channel_id=1, source_target_pairs={{0,4},{4,0},{8,12},{12,8},{16,20},{20,16},{24,28},{28,24},{32,36},... | collective-permute-start | bytes 150536 | tf_op jit(solution)/shard_map/ppermute | solution.py:142
  73.8 16.0 %all-to-all-start.1 = ((bf16[8,49,128]{2,1,0:T(8,128)(2,1)}), bf16[8,49,128]{2,1,0:T(8,128)(2,1)}, u32[]{:S(2)}, u32[]{:S(2)}) async-start(bf16[8,49,128]{2,1,0:T(8,128)(2,1)} %broadcast_in_dim.86), calls=%async_computation.1 | async-start | bytes 229376 | tf_op jit(solution)/shard_map/all_to_all | solution.py:155
  92.8 8.3 %collective-permute-start.14 = (bf16[49,128]{1,0:T(8,128)(2,1)}, bf16[49,128]{1,0:T(8,128)(2,1)}, u32[]{:S(2)}, u32[]{:S(2)}) collective-permute-start(bf16[49,128]{1,0:T(8,128)(2,1)} %pad_maximum_fusion.7), channel_id=1, source_target_pairs={{0,192},{4,196},{8,200},{12,204},{16,208},{20,212},{24,216},{28,22... | collective-permute-start | bytes 37640 | tf_op jit(solution)/shard_map/ppermute | solution.py:149
  95.5 6.3 %collective-permute-start.15 = (bf16[49,128]{1,0:T(8,128)(2,1)}, bf16[49,128]{1,0:T(8,128)(2,1)}, u32[]{:S(2)}, u32[]{:S(2)}) collective-permute-start(bf16[49,128]{1,0:T(8,128)(2,1)} %pad_maximum_fusion.7), channel_id=1, source_target_pairs={{0,128},{4,132},{8,136},{12,140},{16,144},{20,148},{24,152},{28,15... | collective-permute-start | bytes 37640 | tf_op jit(solution)/shard_map/ppermute | solution.py:149
  96.3 13.4 %collective-permute-start.16 = (bf16[49,128]{1,0:T(8,128)(2,1)}, bf16[49,128]{1,0:T(8,128)(2,1)}, u32[]{:S(2)}, u32[]{:S(2)}) collective-permute-start(bf16[49,128]{1,0:T(8,128)(2,1)} %pad_maximum_fusion.7), channel_id=1, source_target_pairs={{0,64},{4,68},{8,72},{12,76},{16,80},{20,84},{24,88},{28,92},{32,9... | collective-permute-start | bytes 37640 | tf_op jit(solution)/shard_map/ppermute | solution.py:149
  97.2 23.1 %collective-permute-start.20 = (bf16[8,256,128]{2,1,0:T(8,128)(2,1)S(1)}, bf16[8,256,128]{2,1,0:T(8,128)(2,1)S(1)}, u32[]{:S(2)}, u32[]{:S(2)}) collective-permute-start(bf16[8,256,128]{2,1,0:T(8,128)(2,1)S(1)} %copy-done.7), channel_id=1, source_target_pairs={{0,192},{4,196},{8,200},{12,204},{16,208},{20,212},{24,216},{28,22... | collective-permute-start | bytes 1572872 | tf_op jit(solution)/shard_map/ppermute | solution.py:149
  99.6 21.3 %collective-permute-start.19 = (bf16[8,256,128]{2,1,0:T(8,128)(2,1)S(1)}, bf16[8,256,128]{2,1,0:T(8,128)(2,1)S(1)}, u32[]{:S(2)}, u32[]{:S(2)}) collective-permute-start(bf16[8,256,128]{2,1,0:T(8,128)(2,1)S(1)} %copy-done.5), channel_id=1, source_target_pairs={{0,128},{4,132},{8,136},{12,140},{16,144},{20,148},{24,152},{28,15... | collective-permute-start | bytes 1572872 | tf_op jit(solution)/shard_map/ppermute | solution.py:149
  101.1 22.8 %collective-permute-start.18 = (bf16[8,256,128]{2,1,0:T(8,128)(2,1)S(1)}, bf16[8,256,128]{2,1,0:T(8,128)(2,1)S(1)}, u32[]{:S(2)}, u32[]{:S(2)}) collective-permute-start(bf16[8,256,128]{2,1,0:T(8,128)(2,1)S(1)} %copy-done.3), channel_id=1, source_target_pairs={{0,64},{4,68},{8,72},{12,76},{16,80},{20,84},{24,88},{28,92},{32,9... | collective-permute-start | bytes 1572872 | tf_op jit(solution)/shard_map/ppermute | solution.py:149
  111.9 3.3 %collective-permute-start.17 = (f32[49,128]{1,0:T(8,128)S(1)}, f32[49,128]{1,0:T(8,128)S(1)}, u32[]{:S(2)}, u32[]{:S(2)}) collective-permute-start(f32[49,128]{1,0:T(8,128)S(1)} %pad_maximum_fusion.2), channel_id=1, source_target_pairs={{0,4},{4,0},{8,12},{12,8},{16,20},{20,16},{24,28},{28,24},{32,36},... | collective-permute-start | bytes 75272 | tf_op jit(solution)/shard_map/ppermute | solution.py:142
  113.9 14.6 %copy-start.36 = (f32[128]{0:T(128)S(1)}, f32[128]{0:T(128)}, u32[]{:S(2)}) copy-start(f32[128]{0:T(128)} %copy-done.35) | copy-start | bytes 1540
  113.9 17.7 %collective-permute-start.10 = (bf16[128,2048]{1,0:T(8,128)(2,1)}, bf16[128,2048]{1,0:T(8,128)(2,1)}, u32[]{:S(2)}, u32[]{:S(2)}) collective-permute-start(bf16[128,2048]{1,0:T(8,128)(2,1)} %copy-done.11), channel_id=1, source_target_pairs={{0,1},{1,2},{2,3},{3,0},{4,5},{5,6},{6,7},{7,4},{8,9},{9,10},{10,1... | collective-permute-start | bytes 1572872 | tf_op jit(solution)/shard_map/ppermute | solution.py:145
  115.2 16.7 %collective-permute-start.11 = (bf16[128,2048]{1,0:T(8,128)(2,1)}, bf16[128,2048]{1,0:T(8,128)(2,1)}, u32[]{:S(2)}, u32[]{:S(2)}) collective-permute-start(bf16[128,2048]{1,0:T(8,128)(2,1)} %copy-done.10), channel_id=1, source_target_pairs={{0,2},{1,3},{2,0},{3,1},{4,6},{5,7},{6,4},{7,5},{8,10},{9,11},{10,... | collective-permute-start | bytes 1572872 | tf_op jit(solution)/shard_map/ppermute | solution.py:145
  120.3 8.2 %copy-start.31 = (f32[16,256]{1,0:T(8,128)S(1)}, f32[16,256]{1,0:T(8,128)}, u32[]{:S(2)}) copy-start(f32[16,256]{1,0:T(8,128)} %get-tuple-element.72) | copy-start | bytes 49156
  120.3 9.4 %copy-start.13 = (f32[258,256]{1,0:T(8,128)S(1)}, f32[258,256]{1,0:T(8,128)}, u32[]{:S(2)}) copy-start(f32[258,256]{1,0:T(8,128)} %copy-done.12) | copy-start | bytes 792580
  120.3 9.4 %copy-start.20 = (f32[128,129]{1,0:T(8,128)S(1)}, f32[128,129]{1,0:T(8,128)}, u32[]{:S(2)}) copy-start(f32[128,129]{1,0:T(8,128)} %constant.99) | copy-start | bytes 198148
  120.3 9.4 %copy-start.34 = (f32[256]{0:T(256)S(1)}, f32[256]{0:T(256)}, u32[]{:S(2)}) copy-start(f32[256]{0:T(256)} %param.15) | copy-start | bytes 3076
  120.3 22.0 %collective-permute-start.12 = (bf16[128,2048]{1,0:T(8,128)(2,1)S(1)}, bf16[128,2048]{1,0:T(8,128)(2,1)}, u32[]{:S(2)}, u32[]{:S(2)}) collective-permute-start(bf16[128,2048]{1,0:T(8,128)(2,1)S(1)} %copy-done.9), channel_id=1, source_target_pairs={{0,3},{1,0},{2,1},{3,2},{4,7},{5,4},{6,5},{7,6},{8,11},{9,8},{10,9... | collective-permute-start | bytes 1572872 | tf_op jit(solution)/shard_map/ppermute | solution.py:145
  125.0 21.4 %all-to-all-start.2 = ((bf16[8,256,128]{2,1,0:T(8,128)(2,1)}), bf16[8,256,128]{2,1,0:T(8,128)(2,1)S(1)}, u32[]{:S(2)}, u32[]{:S(2)}) async-start(bf16[8,256,128]{2,1,0:T(8,128)(2,1)} %add_convert_fusion), calls=%async_computation.2 | async-start | bytes 1048576 | tf_op jit(solution)/shard_map/all_to_all | solution.py:311
  (13 other events, 14.7 us)

commit v11 on v9

--- a/solution.py
+++ b/solution.py
@@ -128,6 +128,39 @@
     )(turns, result, *blocks, weight)
 
 
+def first_states(inner_gate, values, log_decay):
+    block, chans = inner_gate.shape
+    modes = log_decay.shape[0]
+    sub = 8
+
+    def kernel(inner_ref, values_ref, decay_ref, out_ref):
+        u = inner_ref[...].astype(F32) * values_ref[...].astype(F32)
+        row = lax.broadcasted_iota(jnp.int32, (sub, 1), 0).astype(F32)
+        groups = block // sub
+        for n in range(modes):
+            rate = jnp.exp(decay_ref[n : n + 1, :])
+            near = jnp.exp(-rate * (sub - row))
+            step = jnp.exp(-rate * float(sub))
+            base = jnp.zeros((sub, chans), F32)
+            lagged = jnp.zeros((sub, chans), F32)
+            for b in range(groups):
+                base_old = base
+                base = u[b * sub : (b + 1) * sub] + step * base_old
+                lagged = step * (lagged + float(sub) * base_old)
+            st = jnp.sum(near * base, 0, keepdims=True)
+            lag = jnp.sum(near * ((sub - row) * base + lagged), 0, keepdims=True)
+            out_ref[n : n + 1, :] = st
+            out_ref[modes + n : modes + n + 1, :] = lag
+
+    return pl.pallas_call(
+        kernel,
+        out_shape=jax.ShapeDtypeStruct((2 * modes, chans), F32),
+        in_specs=in_vmem(3),
+        out_specs=in_vmem(1)[0],
+        compiler_params=pltpu.CompilerParams(vmem_limit_bytes=4 * 2**20),
+    )(inner_gate, values, log_decay)
+
+
 def body(outer_gate, inner_gate, values, residues, log_decay, skip_gain, out_weight, out_grad):
     ctx = lax.axis_size("ctx")
     tps = lax.axis_size("tp")
@@ -175,10 +208,7 @@
     rise = jnp.exp(-rate3 * (block - rows))
     fall_block = jnp.exp(-rate * block)
 
-    lead = rise * u[None]
-    st = jnp.sum(lead, 1)
-    st_lag = jnp.sum(lead * (block - rows), 1)
-    mine = jnp.concatenate([st, st_lag], 0)
+    mine = first_states(inner_gate, values, log_decay)
     theirs = swap_core(mine)
     first = jnp.where(core == 0, mine, theirs)
     second = jnp.where(core == 0, theirs, mine)

time: 144 us -> 141 us (0.979)
  other arithmetic: 28.1 us -> 19.2 us
  local copies, waits for them, and re-layouts: 5.15 us -> 8.87 us
  waiting for transfers between devices: 52.8 us -> 55.4 us
    unnamed x70 -> x74, local copies, waits for them, and re-layouts: 1.98 us -> 6 us
    ppermute x6, waiting for transfers between devices: 9.2 us -> 12.1 us  [shift_y(): lax.ppermute(a, 'ctx', [(i, (i // per + k) % ny * per + i % per) for i in...]
    all_to_all x1, waiting for transfers between devices: 5.6 us -> 8.3 us  [body(): lax.all_to_all(summed_y, 'ctx', 0, 0, tiled=True, axis_index_groups=z_gro...]
    ppermute x6, waiting for transfers between devices: 18.7 us -> 16.2 us  [shift_tp(): return lax.ppermute(a, 'tp', [(i, (i + k) % tps) for i in range(tps)])]
  transfers between devices with their start and end apart: 24 -> 24, of which waited for: 12 -> 12; matrix products, arithmetic and copies ran while one was open for 13% -> 12% of each run, Pallas kernels for 0% -> 0%
where the time goes in v11:
time: 141 us; the launch traced here: 139 us
  waiting for transfers between devices  55.4 us (39%)
  starting transfers between devices  41.1 us (29%)
  other arithmetic  19.2 us (14%)
  local copies, waits for them, and re-layouts  8.87 us (6%)
  matrix products  7.12 us (5%)
  Pallas kernels  5.82 us (4%)
    ppermute x6, waiting for transfers between devices, shift_tp(): return lax.ppermute(a, 'tp', [(i, (i + k) % tps) for i in range(tps)])  16.2 us
    ppermute x6, waiting for transfers between devices, shift_y(): lax.ppermute(a, 'ctx', [(i, (i // per + k) % ny * per + i % per) for i in...  12.1 us
    all_to_all x1, starting transfers between devices, of_pairs(): lax.all_to_all(copies, 'ctx', 0, 0, tiled=True, axis_index_groups=groups)  11.5 us
    ppermute x6, starting transfers between devices, shift_y(): lax.ppermute(a, 'ctx', [(i, (i // per + k) % ny * per + i % per) for i in...  8.9 us
    all_to_all x1, waiting for transfers between devices, of_plane(): lax.all_to_all(copies, 'ctx', 0, 0, tiled=True, axis_index_groups=z_groups)  8.71 us
    ppermute x6, starting transfers between devices, shift_tp(): return lax.ppermute(a, 'tp', [(i, (i + k) % tps) for i in range(tps)])  8.61 us
    all_to_all x1, waiting for transfers between devices, body(): lax.all_to_all(summed_y, 'ctx', 0, 0, tiled=True, axis_index_groups=z_gro...  8.3 us
    all_to_all x1, waiting for transfers between devices, of_pairs(): lax.all_to_all(copies, 'ctx', 0, 0, tiled=True, axis_index_groups=groups)  7.84 us
  transfers between devices with their start and end apart: 24, of which 12 were waited for; matrix products, arithmetic and copies ran while one was open for 12% of the time, Pallas kernels for 0%

profile of v11, /device:TPU:2, one launch (start us, length us, event | category | flops | bytes accessed | tf_op | source)
XLA Modules:
  0.0 138.7 jit_solution(6010478190047130385)
XLA Ops:
  0.7 0.9 copy-done.2
  1.5 0.8 copy-done.4
  5.0 0.7 broadcast_in_dim.50
  5.8 11.5 %all-to-all-start = ((bf16[32,32,128]{2,1,0:T(8,128)(2,1)}), bf16[32,32,128]{2,1,0:T(8,128)(2,1)S(1)}, u32[]{:S(2)}, u32[]{:S(2)}) async-start(bf16[32,32,128]{2,1,0:T(8,128)(2,1)} %broadcast_in_dim.50), calls=%async_computation | async-start | bytes 524288 | tf_op jit(solution)/shard_map/all_to_all | solution.py:200
  17.2 1.6 %collective-permute-start.3 = (bf16[128,2048]{1,0:T(8,128)(2,1)}, bf16[128,2048]{1,0:T(8,128)(2,1)S(1)}, u32[]{:S(2)}, u32[]{:S(2)}) collective-permute-start(bf16[128,2048]{1,0:T(8,128)(2,1)} %refs_0_.1), channel_id=1, source_target_pairs={{0,1},{1,2},{2,3},{3,0},{4,5},{5,6},{6,7},{7,4},{8,9},{9,10},{10,1... | collective-permute-start | bytes 1572872 | tf_op jit(solution)/shard_map/ppermute | solution.py:185
  18.8 1.1 collective-permute-start.4
  19.9 2.2 %collective-permute-start.5 = (bf16[128,2048]{1,0:T(8,128)(2,1)}, bf16[128,2048]{1,0:T(8,128)(2,1)S(1)}, u32[]{:S(2)}, u32[]{:S(2)}) collective-permute-start(bf16[128,2048]{1,0:T(8,128)(2,1)} %refs_0_.1), channel_id=1, source_target_pairs={{0,3},{1,0},{2,1},{3,2},{4,7},{5,4},{6,5},{7,6},{8,11},{9,8},{10,9... | collective-permute-start | bytes 1572872 | tf_op jit(solution)/shard_map/ppermute | solution.py:185
  22.1 7.8 %all-to-all-done = bf16[32,32,128]{2,1,0:T(8,128)(2,1)S(1)} async-done(((bf16[32,32,128]{2,1,0:T(8,128)(2,1)}), bf16[32,32,128]{2,1,0:T(8,128)(2,1)S(1)}, u32[]{:S(2)}, u32[]{:S(2)}) %all-to-all-start) | async-done | bytes 262176 | tf_op jit(solution)/shard_map/all_to_all | solution.py:200
  30.8 1.5 %collective-permute-done.3.refs_3_.refs_1_ = bf16[128,2048]{1,0:T(8,128)(2,1)S(1)} collective-permute-done((bf16[128,2048]{1,0:T(8,128)(2,1)}, bf16[128,2048]{1,0:T(8,128)(2,1)S(1)}, u32[]{:S(2)}, u32[]{:S(2)}) %collective-permute-start.3) | collective-permute-done | bytes 524320 | tf_op jit(solution)/shard_map/ppermute | solution.py:185
  32.3 3.0 %collective-permute-done.4.refs_4_.refs_2_ = bf16[128,2048]{1,0:T(8,128)(2,1)S(1)} collective-permute-done((bf16[128,2048]{1,0:T(8,128)(2,1)}, bf16[128,2048]{1,0:T(8,128)(2,1)S(1)}, u32[]{:S(2)}, u32[]{:S(2)}) %collective-permute-start.4) | collective-permute-done | bytes 524320 | tf_op jit(solution)/shard_map/ppermute | solution.py:185
  35.3 9.2 %collective-permute-done.5.refs_5_.refs_3_ = bf16[128,2048]{1,0:T(8,128)(2,1)S(1)} collective-permute-done((bf16[128,2048]{1,0:T(8,128)(2,1)}, bf16[128,2048]{1,0:T(8,128)(2,1)S(1)}, u32[]{:S(2)}, u32[]{:S(2)}) %collective-permute-start.5) | collective-permute-done | bytes 524320 | tf_op jit(solution)/shard_map/ppermute | solution.py:185
  46.3 1.2 fusion.30
  47.8 0.8 collective-permute-start.2
  48.6 0.8 collective-permute-done.2.refs_1_
  49.5 2.7 %shard_map.162 = (bf16[8,256,128]{2,1,0:T(8,128)(2,1)S(1)}, bf16[8,256,128]{2,1,0:T(8,128)(2,1)S(1)}, bf16[8,256,128]{2,1,0:T(8,128)(2,1)S(1)}, bf16[8,256,128]{2,1,0:T(8,128)(2,1)S(1)}) custom-call(s32[3]{0:T(128)S(1)} %pad_add_fusion.turns_ref, bf16[128,256]{1,0:T(8,128)(2,1)S(1)} %get-tuple-element.42.refs_0_.result_ref, ...), custom_call_target="tpu_custom_call" | custom-call | tf_op jit(solution)/shard_map/pallas_call | solution.py:80
  52.2 0.8 copy-done.16
  53.0 0.8 copy-done.17
  53.8 2.6 %shard_map.163 = (f32[128,256]{1,0:T(8,128)S(1)}, bf16[128,2048]{1,0:T(8,128)(2,1)S(1)}, bf16[128,2048]{1,0:T(8,128)(2,1)S(1)}, bf16[128,2048]{1,0:T(8,128)(2,1)S(1)}, bf16[128,2048]{1,0:T(8,128)(2,1)S(1)}) custom-call(s32[3]{0:T(128)S(1)} %pad_add_fusion.turns_ref, bf16[128,256]{1,0:T(8,128)(2,1)S(1)} %get-tuple-element.42.refs_0_.result_ref, ...), custom_call_target="tpu_custom_call" | custom-call | tf_op jit(solution)/shard_map/pallas_call | solution.py:121
  56.5 0.8 copy-done.8
  57.3 0.8 copy-done.12
  58.1 1.3 fusion.36
  60.8 0.7 copy.34
  61.6 2.1 %fusion.3 = (f32[16,256]{1,0:T(8,128)S(1)}, f32[16,256]{1,0:T(8,128)S(1)}, f32[16,256]{1,0:T(8,128)S(1)}, f32[16,256]{1,0:T(8,128)S(1)}) fusion(f32[128,256]{1,0:T(8,128)} %copy.34, f32[16,256]{1,0:T(8,128)S(1)} %exponential_negate_fusion.1, f32[128,256]{1,0:T(8,128)} %copy-done.24), kind=kLoop, calls=%fused_computation.7 | loop fusion | flops 4702208 | bytes 344064 | tf_op jit(solution)/shard_map/reduce_sum | solution.py:311
  63.7 0.7 multiply_add_fusion
  65.5 1.0 collective-permute-done.13
  67.2 0.7 fusion.63
  69.3 6.7 %all-to-all-start.1 = ((bf16[8,49,128]{2,1,0:T(8,128)(2,1)}), bf16[8,49,128]{2,1,0:T(8,128)(2,1)S(1)}, u32[]{:S(2)}, u32[]{:S(2)}) async-start(bf16[8,49,128]{2,1,0:T(8,128)(2,1)} %broadcast_in_dim.84), calls=%async_computation.1 | async-start | bytes 229376 | tf_op jit(solution)/shard_map/all_to_all | solution.py:195
  76.6 8.7 %all-to-all-done.1 = bf16[8,49,128]{2,1,0:T(8,128)(2,1)S(1)} async-done(((bf16[8,49,128]{2,1,0:T(8,128)(2,1)}), bf16[8,49,128]{2,1,0:T(8,128)(2,1)S(1)}, u32[]{:S(2)}, u32[]{:S(2)}) %all-to-all-start.1) | async-done | bytes 100384 | tf_op jit(solution)/shard_map/all_to_all | solution.py:195
  85.3 0.8 multiply_reduce_fusion.7
  86.7 2.7 %collective-permute-start.14 = (bf16[49,128]{1,0:T(8,128)(2,1)}, bf16[49,128]{1,0:T(8,128)(2,1)S(1)}, u32[]{:S(2)}, u32[]{:S(2)}) collective-permute-start(bf16[49,128]{1,0:T(8,128)(2,1)} %pad_maximum_fusion.6), channel_id=1, source_target_pairs={{0,192},{4,196},{8,200},{12,204},{16,208},{20,212},{24,216},{28,22... | collective-permute-start | bytes 37640 | tf_op jit(solution)/shard_map/ppermute | solution.py:189
  89.5 0.8 collective-permute-start.15
  90.2 0.9 collective-permute-start.16
  91.6 1.8 %collective-permute-start.18 = (bf16[8,256,128]{2,1,0:T(8,128)(2,1)}, bf16[8,256,128]{2,1,0:T(8,128)(2,1)S(1)}, u32[]{:S(2)}, u32[]{:S(2)}) collective-permute-start(bf16[8,256,128]{2,1,0:T(8,128)(2,1)} %copy-done.17), channel_id=1, source_target_pairs={{0,64},{4,68},{8,72},{12,76},{16,80},{20,84},{24,88},{28,92},{32,9... | collective-permute-start | bytes 1572872 | tf_op jit(solution)/shard_map/ppermute | solution.py:189
  93.5 2.0 %collective-permute-start.19 = (bf16[8,256,128]{2,1,0:T(8,128)(2,1)}, bf16[8,256,128]{2,1,0:T(8,128)(2,1)S(1)}, u32[]{:S(2)}, u32[]{:S(2)}) collective-permute-start(bf16[8,256,128]{2,1,0:T(8,128)(2,1)} %copy-done.16), channel_id=1, source_target_pairs={{0,128},{4,132},{8,136},{12,140},{16,144},{20,148},{24,152},{28,15... | collective-permute-start | bytes 1572872 | tf_op jit(solution)/shard_map/ppermute | solution.py:189
  97.1 2.0 %fusion.23 = f32[256,128]{0,1:T(8,128)} fusion(f32[128,129]{1,0:T(8,128)S(1)} %copy-done.27, f32[258,256]{1,0:T(8,128)} %copy-done.19, f32[258,256]{1,0:T(8,128)} %copy-done.18), kind=kOutput, calls=%fused_computation.43 | convolution fusion | flops 25461504 | bytes 754176 | tf_op jit(solution)/shard_map/dot_general | solution.py:33
  99.1 1.3 collective-permute-start.10
  100.4 1.6 %collective-permute-start.11 = (bf16[128,2048]{1,0:T(8,128)(2,1)S(1)}, bf16[128,2048]{1,0:T(8,128)(2,1)}, u32[]{:S(2)}, u32[]{:S(2)}) collective-permute-start(bf16[128,2048]{1,0:T(8,128)(2,1)S(1)} %copy-done.11), channel_id=1, source_target_pairs={{0,2},{1,3},{2,0},{3,1},{4,6},{5,7},{6,4},{7,5},{8,10},{9,11},{10,... | collective-permute-start | bytes 1572872 | tf_op jit(solution)/shard_map/ppermute | solution.py:185
  102.6 1.4 fusion.69
  104.0 3.3 %collective-permute-done.18 = bf16[8,256,128]{2,1,0:T(8,128)(2,1)S(1)} collective-permute-done((bf16[8,256,128]{2,1,0:T(8,128)(2,1)}, bf16[8,256,128]{2,1,0:T(8,128)(2,1)S(1)}, u32[]{:S(2)}, u32[]{:S(2)}) %collective-permute-start.18) | collective-permute-done | bytes 524320 | tf_op jit(solution)/shard_map/ppermute | solution.py:189
  107.3 0.8 collective-permute-start.12
  108.1 8.8 %collective-permute-done.19 = bf16[8,256,128]{2,1,0:T(8,128)(2,1)S(1)} collective-permute-done((bf16[8,256,128]{2,1,0:T(8,128)(2,1)}, bf16[8,256,128]{2,1,0:T(8,128)(2,1)S(1)}, u32[]{:S(2)}, u32[]{:S(2)}) %collective-permute-start.19) | collective-permute-done | bytes 524320 | tf_op jit(solution)/shard_map/ppermute | solution.py:189
  116.9 1.1 add_convert_fusion
  118.0 3.5 %all-to-all-start.2 = ((bf16[8,256,128]{2,1,0:T(8,128)(2,1)}), bf16[8,256,128]{2,1,0:T(8,128)(2,1)S(1)}, u32[]{:S(2)}, u32[]{:S(2)}) async-start(bf16[8,256,128]{2,1,0:T(8,128)(2,1)} %add_convert_fusion), calls=%async_computation.2 | async-start | bytes 1048576 | tf_op jit(solution)/shard_map/all_to_all | solution.py:346
  121.5 1.1 multiply_reduce_fusion
  122.7 2.1 %fusion.34 = (bf16[128,256]{1,0:T(8,128)(2,1)}, bf16[128,256]{1,0:T(8,128)(2,1)}) fusion(bf16[128,256]{1,0:T(8,128)(2,1)S(1)} %copy-done.5, bf16[128,256]{1,0:T(8,128)(2,1)S(1)} %copy-done.3, f32[128,256]{1,0:T(8,128)S(1)} %copy-done.25, f32[256]{0:T(256)} %param.15, f32[128,256]{1,0:T(8,128)S(1)} %multiply_reduce_fusion, f32[256,128]{0,1:T(8,128)} %fusion.23, ...), kind=kOutput, calls=%fused_computation.54 | convolution fusion | flops 25789184 | bytes 1279488 | tf_op jit(solution)/shard_map/dot_general | solution.py:33
  124.8 2.4 %collective-permute-done.12 = bf16[128,2048]{1,0:T(8,128)(2,1)} collective-permute-done((bf16[128,2048]{1,0:T(8,128)(2,1)S(1)}, bf16[128,2048]{1,0:T(8,128)(2,1)}, u32[]{:S(2)}, u32[]{:S(2)}) %collective-permute-start.12) | collective-permute-done | bytes 524320 | tf_op jit(solution)/shard_map/ppermute | solution.py:185
  127.2 2.5 %add_convert_fusion.1 = bf16[128,2048]{1,0:T(8,128)(2,1)} fusion(bf16[128,2048]{1,0:T(8,128)(2,1)} %collective-permute-done.12, bf16[128,2048]{1,0:T(8,128)(2,1)} %collective-permute-done.11, bf16[128,2048]{1,0:T(8,128)(2,1)} %collective-permute-done.10, bf16[128,2048]{1,0:T(8,128)(2,1)S(1)} %get-tuple-element.43), kind=kLoop, calls=%fused_computation.23 | loop fusion | flops 2097152 | bytes 2621440 | tf_op jit(solution)/shard_map/convert_element_type | solution.py:285
  129.7 8.3 %all-to-all-done.2 = bf16[8,256,128]{2,1,0:T(8,128)(2,1)S(1)} async-done(((bf16[8,256,128]{2,1,0:T(8,128)(2,1)}), bf16[8,256,128]{2,1,0:T(8,128)(2,1)S(1)}, u32[]{:S(2)}, u32[]{:S(2)}) %all-to-all-start.2) | async-done | bytes 524320 | tf_op jit(solution)/shard_map/all_to_all | solution.py:346
  (135 shorter events, 14.6 us)
Async XLA Ops:
  0.6 29.7 %copy-start.1 = (bf16[128,2048]{1,0:T(8,128)(2,1)S(1)}, bf16[128,2048]{1,0:T(8,128)(2,1)}, u32[]{:S(2)}) copy-start(bf16[128,2048]{1,0:T(8,128)(2,1)} %refs_0_.1) | copy-start | bytes 1572868
  3.1 41.4 %copy-start.7 = (f32[16,256]{1,0:T(8,128)S(1)}, f32[16,256]{1,0:T(8,128)}, u32[]{:S(2)}) copy-start(f32[16,256]{1,0:T(8,128)} %decay_ref.1) | copy-start | bytes 49156
  3.1 42.1 %copy-start.33 = (f32[16,256]{1,0:T(8,128)S(1)}, f32[16,256]{1,0:T(8,128)}, u32[]{:S(2)}) copy-start(f32[16,256]{1,0:T(8,128)} %param.13) | copy-start | bytes 49156
  3.1 42.6 %copy-start.20 = (f32[258,128]{1,0:T(8,128)S(1)}, f32[258,128]{1,0:T(8,128)}, u32[]{:S(2)}) copy-start(f32[258,128]{1,0:T(8,128)} %constant.96.clone) | copy-start | bytes 396292
  3.6 1.3 collective-permute-start
  4.9 41.1 %copy-start.3 = (bf16[128,256]{1,0:T(8,128)(2,1)S(1)}, bf16[128,256]{1,0:T(8,128)(2,1)}, u32[]{:S(2)}) copy-start(bf16[128,256]{1,0:T(8,128)(2,1)} %values_ref.1) | copy-start | bytes 196612
  4.9 41.1 %copy-start.5 = (bf16[128,256]{1,0:T(8,128)(2,1)S(1)}, bf16[128,256]{1,0:T(8,128)(2,1)}, u32[]{:S(2)}) copy-start(bf16[128,256]{1,0:T(8,128)(2,1)} %inner_ref.1) | copy-start | bytes 196612
  5.0 40.8 %copy-start.28 = (f32[16,128]{1,0:T(8,128)}, f32[16,128]{1,0:T(8,128)S(1)}, u32[]{:S(2)}) copy-start(f32[16,128]{1,0:T(8,128)S(1)} %get-tuple-element.73) | copy-start | bytes 24580
  5.8 24.2 %all-to-all-start = ((bf16[32,32,128]{2,1,0:T(8,128)(2,1)}), bf16[32,32,128]{2,1,0:T(8,128)(2,1)S(1)}, u32[]{:S(2)}, u32[]{:S(2)}) async-start(bf16[32,32,128]{2,1,0:T(8,128)(2,1)} %broadcast_in_dim.50), calls=%async_computation | async-start | bytes 524288 | tf_op jit(solution)/shard_map/all_to_all | solution.py:200
  17.2 15.1 %collective-permute-start.3 = (bf16[128,2048]{1,0:T(8,128)(2,1)}, bf16[128,2048]{1,0:T(8,128)(2,1)S(1)}, u32[]{:S(2)}, u32[]{:S(2)}) collective-permute-start(bf16[128,2048]{1,0:T(8,128)(2,1)} %refs_0_.1), channel_id=1, source_target_pairs={{0,1},{1,2},{2,3},{3,0},{4,5},{5,6},{6,7},{7,4},{8,9},{9,10},{10,1... | collective-permute-start | bytes 1572872 | tf_op jit(solution)/shard_map/ppermute | solution.py:185
  18.8 16.5 %collective-permute-start.4 = (bf16[128,2048]{1,0:T(8,128)(2,1)}, bf16[128,2048]{1,0:T(8,128)(2,1)S(1)}, u32[]{:S(2)}, u32[]{:S(2)}) collective-permute-start(bf16[128,2048]{1,0:T(8,128)(2,1)} %refs_0_.1), channel_id=1, source_target_pairs={{0,2},{1,3},{2,0},{3,1},{4,6},{5,7},{6,4},{7,5},{8,10},{9,11},{10,... | collective-permute-start | bytes 1572872 | tf_op jit(solution)/shard_map/ppermute | solution.py:185
  19.9 24.6 %collective-permute-start.5 = (bf16[128,2048]{1,0:T(8,128)(2,1)}, bf16[128,2048]{1,0:T(8,128)(2,1)S(1)}, u32[]{:S(2)}, u32[]{:S(2)}) collective-permute-start(bf16[128,2048]{1,0:T(8,128)(2,1)} %refs_0_.1), channel_id=1, source_target_pairs={{0,3},{1,0},{2,1},{3,2},{4,7},{5,4},{6,5},{7,6},{8,11},{9,8},{10,9... | collective-permute-start | bytes 1572872 | tf_op jit(solution)/shard_map/ppermute | solution.py:185
  22.1 25.4 %copy-start.21 = (f32[128,129]{1,0:T(8,128)S(1)}, f32[128,129]{1,0:T(8,128)}, u32[]{:S(2)}) copy-start(f32[128,129]{1,0:T(8,128)} %constant.99) | copy-start | bytes 198148
  22.1 25.4 %copy-start.30 = (bf16[128,256]{1,0:T(8,128)(2,1)S(1)}, bf16[128,256]{1,0:T(8,128)(2,1)}, u32[]{:S(2)}) copy-start(bf16[128,256]{1,0:T(8,128)(2,1)} %param.10) | copy-start | bytes 196612
  22.1 25.4 %copy-start.36 = (f32[256]{0:T(256)S(1)}, f32[256]{0:T(256)}, u32[]{:S(2)}) copy-start(f32[256]{0:T(256)} %param.15) | copy-start | bytes 3076
  30.2 14.3 %collective-permute-start.1 = (f32[32,128]{1,0:T(8,128)S(1)}, f32[32,128]{1,0:T(8,128)S(1)}, u32[]{:S(2)}, u32[]{:S(2)}) collective-permute-start(f32[32,128]{1,0:T(8,128)S(1)} %pad_maximum_fusion.4), channel_id=1, source_target_pairs={{0,4},{4,0},{8,12},{12,8},{16,20},{20,16},{24,28},{28,24},{32,36},... | collective-permute-start | bytes 49160 | tf_op jit(solution)/shard_map/ppermute | solution.py:182
  30.3 18.3 %collective-permute-start.6 = (bf16[128,2048]{1,0:T(8,128)(2,1)S(1)}, bf16[128,2048]{1,0:T(8,128)(2,1)S(1)}, u32[]{:S(2)}, u32[]{:S(2)}) collective-permute-start(bf16[128,2048]{1,0:T(8,128)(2,1)S(1)} %copy-done.1), channel_id=1, source_target_pairs={{0,4},{4,0},{8,12},{12,8},{16,20},{20,16},{24,28},{28,24},{32,36},... | collective-permute-start | bytes 1572872 | tf_op jit(solution)/shard_map/ppermute | solution.py:182
  32.3 17.1 %collective-permute-start.7 = (bf16[128,2048]{1,0:T(8,128)(2,1)S(1)}, bf16[128,2048]{1,0:T(8,128)(2,1)S(1)}, u32[]{:S(2)}, u32[]{:S(2)}) collective-permute-start(bf16[128,2048]{1,0:T(8,128)(2,1)S(1)} %collective-permute-done.3.refs_3_.refs_1_), channel_id=1, source_target_pairs={{0,4},{4,0},{8,12},{12,8},{16,20},{20,16},{24,28},{28,24},{32,36},... | collective-permute-start | bytes 1572872 | tf_op jit(solution)/shard_map/ppermute | solution.py:182
  35.3 14.1 %collective-permute-start.8 = (bf16[128,2048]{1,0:T(8,128)(2,1)S(1)}, bf16[128,2048]{1,0:T(8,128)(2,1)S(1)}, u32[]{:S(2)}, u32[]{:S(2)}) collective-permute-start(bf16[128,2048]{1,0:T(8,128)(2,1)S(1)} %collective-permute-done.4.refs_4_.refs_2_), channel_id=1, source_target_pairs={{0,4},{4,0},{8,12},{12,8},{16,20},{20,16},{24,28},{28,24},{32,36},... | collective-permute-start | bytes 1572872 | tf_op jit(solution)/shard_map/ppermute | solution.py:182
  44.5 5.0 %collective-permute-start.9 = (bf16[128,2048]{1,0:T(8,128)(2,1)S(1)}, bf16[128,2048]{1,0:T(8,128)(2,1)S(1)}, u32[]{:S(2)}, u32[]{:S(2)}) collective-permute-start(bf16[128,2048]{1,0:T(8,128)(2,1)S(1)} %collective-permute-done.5.refs_5_.refs_3_), channel_id=1, source_target_pairs={{0,4},{4,0},{8,12},{12,8},{16,20},{20,16},{24,28},{28,24},{32,36},... | collective-permute-start | bytes 1572872 | tf_op jit(solution)/shard_map/ppermute | solution.py:182
  45.2 4.3 %copy-start.31 = (f32[16,256]{1,0:T(8,128)}, f32[16,256]{1,0:T(8,128)S(1)}, u32[]{:S(2)}) copy-start(f32[16,256]{1,0:T(8,128)S(1)} %get-tuple-element.37) | copy-start | bytes 49156
  46.0 3.4 %copy-start.18 = (f32[258,256]{1,0:T(8,128)}, f32[258,256]{1,0:T(8,128)S(1)}, u32[]{:S(2)}) copy-start(f32[258,256]{1,0:T(8,128)S(1)} %fusion.87) | copy-start | bytes 792580
  47.8 1.7 %collective-permute-start.2 = (bf16[128,256]{1,0:T(8,128)(2,1)S(1)}, bf16[128,256]{1,0:T(8,128)(2,1)S(1)}, u32[]{:S(2)}, u32[]{:S(2)}) collective-permute-start(bf16[128,256]{1,0:T(8,128)(2,1)S(1)} %get-tuple-element.42.refs_0_.result_ref), channel_id=1, source_target_pairs={{0,4},{4,0},{8,12},{12,8},{16,20},{20,16},{24,28},{28,24},{32,36},... | collective-permute-start | bytes 196616 | tf_op jit(solution)/shard_map/ppermute | solution.py:182
  48.6 5.2 %copy-start = (bf16[256,8192]{1,0:T(8,128)(2,1)S(1)}, bf16[256,8192]{1,0:T(8,128)(2,1)}, u32[]{:S(2)}) copy-start(bf16[256,8192]{1,0:T(8,128)(2,1)} %refs_4_.1) | copy-start | bytes 12582916
  53.8 5.8 %copy-start.26 = (f32[128,129]{1,0:T(8,128)S(1)}, f32[128,129]{1,0:T(8,128)}, u32[]{:S(2)}) copy-start(f32[128,129]{1,0:T(8,128)} %constant.98) | copy-start | bytes 198148
  53.8 6.5 %copy-start.22 = (f32[128,129]{1,0:T(8,128)S(1)}, f32[128,129]{1,0:T(8,128)}, u32[]{:S(2)}) copy-start(f32[128,129]{1,0:T(8,128)} %constant.99) | copy-start | bytes 198148
  59.7 35.8 %copy-start.15 = (bf16[8,256,128]{2,1,0:T(8,128)(2,1)S(1)}, bf16[8,256,128]{2,1,0:T(8,128)(2,1)}, u32[]{:S(2)}) copy-start(bf16[8,256,128]{2,1,0:T(8,128)(2,1)} %copy-done.14) | copy-start | bytes 1572868
  59.7 37.4 %copy-start.27 = (f32[128,129]{1,0:T(8,128)S(1)}, f32[128,129]{1,0:T(8,128)}, u32[]{:S(2)}) copy-start(f32[128,129]{1,0:T(8,128)} %constant.98) | copy-start | bytes 198148
  60.4 38.7 %copy-start.13 = (bf16[128,2048]{1,0:T(8,128)(2,1)S(1)}, bf16[128,2048]{1,0:T(8,128)(2,1)}, u32[]{:S(2)}) copy-start(bf16[128,2048]{1,0:T(8,128)(2,1)} %copy-done.12) | copy-start | bytes 1572868
  60.8 39.6 %copy-start.11 = (bf16[128,2048]{1,0:T(8,128)(2,1)S(1)}, bf16[128,2048]{1,0:T(8,128)(2,1)}, u32[]{:S(2)}) copy-start(bf16[128,2048]{1,0:T(8,128)(2,1)} %copy-done.10) | copy-start | bytes 1572868
  60.8 46.5 %copy-start.9 = (bf16[128,2048]{1,0:T(8,128)(2,1)S(1)}, bf16[128,2048]{1,0:T(8,128)(2,1)}, u32[]{:S(2)}) copy-start(bf16[128,2048]{1,0:T(8,128)(2,1)} %copy-done.8) | copy-start | bytes 1572868
  61.5 23.8 %copy-start.29 = (f32[16,128]{1,0:T(8,128)S(1)}, f32[16,128]{1,0:T(8,128)}, u32[]{:S(2)}) copy-start(f32[16,128]{1,0:T(8,128)} %copy-done.28) | copy-start | bytes 24580
  65.1 1.4 collective-permute-start.13
  69.3 15.9 %all-to-all-start.1 = ((bf16[8,49,128]{2,1,0:T(8,128)(2,1)}), bf16[8,49,128]{2,1,0:T(8,128)(2,1)S(1)}, u32[]{:S(2)}, u32[]{:S(2)}) async-start(bf16[8,49,128]{2,1,0:T(8,128)(2,1)} %broadcast_in_dim.84), calls=%async_computation.1 | async-start | bytes 229376 | tf_op jit(solution)/shard_map/all_to_all | solution.py:195
  86.7 8.8 %collective-permute-start.14 = (bf16[49,128]{1,0:T(8,128)(2,1)}, bf16[49,128]{1,0:T(8,128)(2,1)S(1)}, u32[]{:S(2)}, u32[]{:S(2)}) collective-permute-start(bf16[49,128]{1,0:T(8,128)(2,1)} %pad_maximum_fusion.6), channel_id=1, source_target_pairs={{0,192},{4,196},{8,200},{12,204},{16,208},{20,212},{24,216},{28,22... | collective-permute-start | bytes 37640 | tf_op jit(solution)/shard_map/ppermute | solution.py:189
  89.5 6.7 %collective-permute-start.15 = (bf16[49,128]{1,0:T(8,128)(2,1)}, bf16[49,128]{1,0:T(8,128)(2,1)}, u32[]{:S(2)}, u32[]{:S(2)}) collective-permute-start(bf16[49,128]{1,0:T(8,128)(2,1)} %pad_maximum_fusion.6), channel_id=1, source_target_pairs={{0,128},{4,132},{8,136},{12,140},{16,144},{20,148},{24,152},{28,15... | collective-permute-start | bytes 37640 | tf_op jit(solution)/shard_map/ppermute | solution.py:189
  90.2 6.6 %collective-permute-start.16 = (bf16[49,128]{1,0:T(8,128)(2,1)}, bf16[49,128]{1,0:T(8,128)(2,1)S(1)}, u32[]{:S(2)}, u32[]{:S(2)}) collective-permute-start(bf16[49,128]{1,0:T(8,128)(2,1)} %pad_maximum_fusion.6), channel_id=1, source_target_pairs={{0,64},{4,68},{8,72},{12,76},{16,80},{20,84},{24,88},{28,92},{32,9... | collective-permute-start | bytes 37640 | tf_op jit(solution)/shard_map/ppermute | solution.py:189
  91.6 15.6 %collective-permute-start.18 = (bf16[8,256,128]{2,1,0:T(8,128)(2,1)}, bf16[8,256,128]{2,1,0:T(8,128)(2,1)S(1)}, u32[]{:S(2)}, u32[]{:S(2)}) collective-permute-start(bf16[8,256,128]{2,1,0:T(8,128)(2,1)} %copy-done.17), channel_id=1, source_target_pairs={{0,64},{4,68},{8,72},{12,76},{16,80},{20,84},{24,88},{28,92},{32,9... | collective-permute-start | bytes 1572872 | tf_op jit(solution)/shard_map/ppermute | solution.py:189
  93.5 23.5 %collective-permute-start.19 = (bf16[8,256,128]{2,1,0:T(8,128)(2,1)}, bf16[8,256,128]{2,1,0:T(8,128)(2,1)S(1)}, u32[]{:S(2)}, u32[]{:S(2)}) collective-permute-start(bf16[8,256,128]{2,1,0:T(8,128)(2,1)} %copy-done.16), channel_id=1, source_target_pairs={{0,128},{4,132},{8,136},{12,140},{16,144},{20,148},{24,152},{28,15... | collective-permute-start | bytes 1572872 | tf_op jit(solution)/shard_map/ppermute | solution.py:189
  95.5 21.5 %collective-permute-start.20 = (bf16[8,256,128]{2,1,0:T(8,128)(2,1)S(1)}, bf16[8,256,128]{2,1,0:T(8,128)(2,1)S(1)}, u32[]{:S(2)}, u32[]{:S(2)}) collective-permute-start(bf16[8,256,128]{2,1,0:T(8,128)(2,1)S(1)} %copy-done.15), channel_id=1, source_target_pairs={{0,192},{4,196},{8,200},{12,204},{16,208},{20,212},{24,216},{28,22... | collective-permute-start | bytes 1572872 | tf_op jit(solution)/shard_map/ppermute | solution.py:189
  96.9 3.4 %collective-permute-start.17 = (f32[49,128]{1,0:T(8,128)S(1)}, f32[49,128]{1,0:T(8,128)S(1)}, u32[]{:S(2)}, u32[]{:S(2)}) collective-permute-start(f32[49,128]{1,0:T(8,128)S(1)} %pad_maximum_fusion.1), channel_id=1, source_target_pairs={{0,4},{4,0},{8,12},{12,8},{16,20},{20,16},{24,28},{28,24},{32,36},... | collective-permute-start | bytes 75272 | tf_op jit(solution)/shard_map/ppermute | solution.py:182
  99.1 25.7 %collective-permute-start.10 = (bf16[128,2048]{1,0:T(8,128)(2,1)S(1)}, bf16[128,2048]{1,0:T(8,128)(2,1)}, u32[]{:S(2)}, u32[]{:S(2)}) collective-permute-start(bf16[128,2048]{1,0:T(8,128)(2,1)S(1)} %copy-done.13), channel_id=1, source_target_pairs={{0,1},{1,2},{2,3},{3,0},{4,5},{5,6},{6,7},{7,4},{8,9},{9,10},{10,1... | collective-permute-start | bytes 1572872 | tf_op jit(solution)/shard_map/ppermute | solution.py:185
  100.4 24.4 %collective-permute-start.11 = (bf16[128,2048]{1,0:T(8,128)(2,1)S(1)}, bf16[128,2048]{1,0:T(8,128)(2,1)}, u32[]{:S(2)}, u32[]{:S(2)}) collective-permute-start(bf16[128,2048]{1,0:T(8,128)(2,1)S(1)} %copy-done.11), channel_id=1, source_target_pairs={{0,2},{1,3},{2,0},{3,1},{4,6},{5,7},{6,4},{7,5},{8,10},{9,11},{10,... | collective-permute-start | bytes 1572872 | tf_op jit(solution)/shard_map/ppermute | solution.py:185
  104.0 17.5 %copy-start.34 = (f32[16,256]{1,0:T(8,128)S(1)}, f32[16,256]{1,0:T(8,128)}, u32[]{:S(2)}) copy-start(f32[16,256]{1,0:T(8,128)} %get-tuple-element.78) | copy-start | bytes 49156
  107.3 15.4 %copy-start.23 = (f32[128,129]{1,0:T(8,128)S(1)}, f32[128,129]{1,0:T(8,128)}, u32[]{:S(2)}) copy-start(f32[128,129]{1,0:T(8,128)} %constant.99) | copy-start | bytes 198148
  107.3 15.4 %copy-start.25 = (f32[128,256]{1,0:T(8,128)S(1)}, f32[128,256]{1,0:T(8,128)}, u32[]{:S(2)}) copy-start(f32[128,256]{1,0:T(8,128)} %copy-done.24) | copy-start | bytes 393220
  107.3 20.0 %collective-permute-start.12 = (bf16[128,2048]{1,0:T(8,128)(2,1)S(1)}, bf16[128,2048]{1,0:T(8,128)(2,1)}, u32[]{:S(2)}, u32[]{:S(2)}) collective-permute-start(bf16[128,2048]{1,0:T(8,128)(2,1)S(1)} %copy-done.9), channel_id=1, source_target_pairs={{0,3},{1,0},{2,1},{3,2},{4,7},{5,4},{6,5},{7,6},{8,11},{9,8},{10,9... | collective-permute-start | bytes 1572872 | tf_op jit(solution)/shard_map/ppermute | solution.py:185
  118.0 20.0 %all-to-all-start.2 = ((bf16[8,256,128]{2,1,0:T(8,128)(2,1)}), bf16[8,256,128]{2,1,0:T(8,128)(2,1)S(1)}, u32[]{:S(2)}, u32[]{:S(2)}) async-start(bf16[8,256,128]{2,1,0:T(8,128)(2,1)} %add_convert_fusion), calls=%async_computation.2 | async-start | bytes 1048576 | tf_op jit(solution)/shard_map/all_to_all | solution.py:346
  (13 other events, 16.8 us)

commit v12 on v11

--- a/solution.py
+++ b/solution.py
@@ -152,12 +152,16 @@
             out_ref[n : n + 1, :] = st
             out_ref[modes + n : modes + n + 1, :] = lag
 
+    def whole(shape):
+        return pl.BlockSpec(shape, lambda i: (0, 0))
+
     return pl.pallas_call(
         kernel,
         out_shape=jax.ShapeDtypeStruct((2 * modes, chans), F32),
-        in_specs=in_vmem(3),
-        out_specs=in_vmem(1)[0],
-        compiler_params=pltpu.CompilerParams(vmem_limit_bytes=4 * 2**20),
+        grid=(1,),
+        in_specs=[whole((block, chans)), whole((block, chans)), whole((modes, chans))],
+        out_specs=whole((2 * modes, chans)),
+        compiler_params=pltpu.CompilerParams(vmem_limit_bytes=60 * 2**20),
     )(inner_gate, values, log_decay)
 
 

time: 141 us -> 146 us (1.035)
  other arithmetic: 19.2 us -> 28.3 us
  waiting for transfers between devices: 55.4 us -> 51.4 us
  local copies, waits for them, and re-layouts: 8.87 us -> 6.44 us
  Pallas kernels: 5.82 us -> 7.38 us
    unnamed x74 -> x70, local copies, waits for them, and re-layouts: 6 us -> 2.55 us
    ppermute x6, waiting for transfers between devices: 12.1 us -> 9.23 us  [shift_y(): lax.ppermute(a, 'ctx', [(i, (i // per + k) % ny * per + i % per) for i in...]
    all_to_all x1, waiting for transfers between devices: 8.3 us -> 5.6 us  [body(): lax.all_to_all(summed_y, 'ctx', 0, 0, tiled=True, axis_index_groups=z_gro...]
    ppermute x6, waiting for transfers between devices: 16.2 us -> 18.4 us  [shift_tp(): return lax.ppermute(a, 'tp', [(i, (i + k) % tps) for i in range(tps)])]
    pallas_call x1, Pallas kernels: 0.49 us -> 2.04 us  [first_states(): pl.pallas_call(kernel, out_shape=jax.ShapeDtypeStruct((2 * modes, chans),...]
  transfers between devices with their start and end apart: 24 -> 24, of which waited for: 12 -> 12; matrix products, arithmetic and copies ran while one was open for 12% -> 14% of each run, Pallas kernels for 0% -> 0%
where the time goes in v12:
time: 146 us; the launch traced here: 143 us
  waiting for transfers between devices  51.4 us (35%)
  starting transfers between devices  41.2 us (28%)
  other arithmetic  28.3 us (19%)
  Pallas kernels  7.38 us (5%)
  matrix products  6.78 us (5%)
  local copies, waits for them, and re-layouts  6.44 us (4%)
    ppermute x6, waiting for transfers between devices, shift_tp(): return lax.ppermute(a, 'tp', [(i, (i + k) % tps) for i in range(tps)])  18.4 us
    all_to_all x1, starting transfers between devices, of_pairs(): lax.all_to_all(copies, 'ctx', 0, 0, tiled=True, axis_index_groups=groups)  11.6 us
    ppermute x6, waiting for transfers between devices, shift_y(): lax.ppermute(a, 'ctx', [(i, (i // per + k) % ny * per + i % per) for i in...  9.23 us
    ppermute x6, starting transfers between devices, shift_y(): lax.ppermute(a, 'ctx', [(i, (i // per + k) % ny * per + i % per) for i in...  8.9 us
    ppermute x6, starting transfers between devices, shift_tp(): return lax.ppermute(a, 'tp', [(i, (i + k) % tps) for i in range(tps)])  8.79 us
    all_to_all x1, waiting for transfers between devices, of_plane(): lax.all_to_all(copies, 'ctx', 0, 0, tiled=True, axis_index_groups=z_groups)  8.35 us
    all_to_all x1, waiting for transfers between devices, of_pairs(): lax.all_to_all(copies, 'ctx', 0, 0, tiled=True, axis_index_groups=groups)  7.07 us
    all_to_all x1, starting transfers between devices, of_plane(): lax.all_to_all(copies, 'ctx', 0, 0, tiled=True, axis_index_groups=z_groups)  6.7 us
  transfers between devices with their start and end apart: 24, of which 12 were waited for; matrix products, arithmetic and copies ran while one was open for 14% of the time, Pallas kernels for 0%

profile of v12, /device:TPU:2, one launch (start us, length us, event | category | flops | bytes accessed | tf_op | source)
XLA Modules:
  0.0 142.7 jit_solution(11545610434691255421)
XLA Ops:
  0.7 2.0 %shard_map.161 = f32[32,256]{1,0:T(8,128)} custom-call(bf16[128,256]{1,0:T(8,128)(2,1)} %inner_ref.1, bf16[128,256]{1,0:T(8,128)(2,1)} %values_ref.1, f32[16,256]{1,0:T(8,128)} %decay_ref.1), custom_call_target="tpu_custom_call" | custom-call | tf_op jit(solution)/shard_map/pallas_call | solution.py:158
  4.1 0.8 broadcast_select_fusion
  4.9 0.8 dynamic-slice_select_fusion
  6.5 11.6 %all-to-all-start = ((bf16[32,32,128]{2,1,0:T(8,128)(2,1)}), bf16[32,32,128]{2,1,0:T(8,128)(2,1)S(1)}, u32[]{:S(2)}, u32[]{:S(2)}) async-start(bf16[32,32,128]{2,1,0:T(8,128)(2,1)} %broadcast_in_dim.50), calls=%async_computation | async-start | bytes 524288 | tf_op jit(solution)/shard_map/all_to_all | solution.py:204
  18.1 1.6 %collective-permute-start.3 = (bf16[128,2048]{1,0:T(8,128)(2,1)}, bf16[128,2048]{1,0:T(8,128)(2,1)S(1)}, u32[]{:S(2)}, u32[]{:S(2)}) collective-permute-start(bf16[128,2048]{1,0:T(8,128)(2,1)} %refs_0_.1), channel_id=1, source_target_pairs={{0,1},{1,2},{2,3},{3,0},{4,5},{5,6},{6,7},{7,4},{8,9},{9,10},{10,1... | collective-permute-start | bytes 1572872 | tf_op jit(solution)/shard_map/ppermute | solution.py:189
  19.6 1.1 collective-permute-start.4
  20.8 2.2 %collective-permute-start.5 = (bf16[128,2048]{1,0:T(8,128)(2,1)}, bf16[128,2048]{1,0:T(8,128)(2,1)S(1)}, u32[]{:S(2)}, u32[]{:S(2)}) collective-permute-start(bf16[128,2048]{1,0:T(8,128)(2,1)} %refs_0_.1), channel_id=1, source_target_pairs={{0,3},{1,0},{2,1},{3,2},{4,7},{5,4},{6,5},{7,6},{8,11},{9,8},{10,9... | collective-permute-start | bytes 1572872 | tf_op jit(solution)/shard_map/ppermute | solution.py:189
  23.0 7.1 %all-to-all-done = bf16[32,32,128]{2,1,0:T(8,128)(2,1)S(1)} async-done(((bf16[32,32,128]{2,1,0:T(8,128)(2,1)}), bf16[32,32,128]{2,1,0:T(8,128)(2,1)S(1)}, u32[]{:S(2)}, u32[]{:S(2)}) %all-to-all-start) | async-done | bytes 262176 | tf_op jit(solution)/shard_map/all_to_all | solution.py:204
  31.4 1.8 %collective-permute-done.3.refs_3_.refs_1_ = bf16[128,2048]{1,0:T(8,128)(2,1)S(1)} collective-permute-done((bf16[128,2048]{1,0:T(8,128)(2,1)}, bf16[128,2048]{1,0:T(8,128)(2,1)S(1)}, u32[]{:S(2)}, u32[]{:S(2)}) %collective-permute-start.3) | collective-permute-done | bytes 524320 | tf_op jit(solution)/shard_map/ppermute | solution.py:189
  33.2 3.0 %collective-permute-done.4.refs_4_.refs_2_ = bf16[128,2048]{1,0:T(8,128)(2,1)S(1)} collective-permute-done((bf16[128,2048]{1,0:T(8,128)(2,1)}, bf16[128,2048]{1,0:T(8,128)(2,1)S(1)}, u32[]{:S(2)}, u32[]{:S(2)}) %collective-permute-start.4) | collective-permute-done | bytes 524320 | tf_op jit(solution)/shard_map/ppermute | solution.py:189
  36.2 8.5 %collective-permute-done.5.refs_5_.refs_3_ = bf16[128,2048]{1,0:T(8,128)(2,1)S(1)} collective-permute-done((bf16[128,2048]{1,0:T(8,128)(2,1)}, bf16[128,2048]{1,0:T(8,128)(2,1)S(1)}, u32[]{:S(2)}, u32[]{:S(2)}) %collective-permute-start.5) | collective-permute-done | bytes 524320 | tf_op jit(solution)/shard_map/ppermute | solution.py:189
  46.0 0.8 fusion.86
  48.4 0.8 collective-permute-start.2
  49.2 0.8 collective-permute-done.2.refs_1_
  50.1 2.7 %shard_map.162 = (bf16[8,256,128]{2,1,0:T(8,128)(2,1)S(1)}, bf16[8,256,128]{2,1,0:T(8,128)(2,1)S(1)}, bf16[8,256,128]{2,1,0:T(8,128)(2,1)S(1)}, bf16[8,256,128]{2,1,0:T(8,128)(2,1)S(1)}) custom-call(s32[3]{0:T(128)S(1)} %pad_add_fusion.turns_ref, bf16[128,256]{1,0:T(8,128)(2,1)S(1)} %get-tuple-element.42.refs_0_.result_ref, ...), custom_call_target="tpu_custom_call" | custom-call | tf_op jit(solution)/shard_map/pallas_call | solution.py:80
  52.8 0.8 copy-done.10
  53.6 0.8 copy-done.11
  54.4 2.6 %shard_map.163 = (f32[128,256]{1,0:T(8,128)S(1)}, bf16[128,2048]{1,0:T(8,128)(2,1)S(1)}, bf16[128,2048]{1,0:T(8,128)(2,1)S(1)}, bf16[128,2048]{1,0:T(8,128)(2,1)S(1)}, bf16[128,2048]{1,0:T(8,128)(2,1)S(1)}) custom-call(s32[3]{0:T(128)S(1)} %pad_add_fusion.turns_ref, bf16[128,256]{1,0:T(8,128)(2,1)S(1)} %get-tuple-element.42.refs_0_.result_ref, ...), custom_call_target="tpu_custom_call" | custom-call | tf_op jit(solution)/shard_map/pallas_call | solution.py:121
  57.1 1.3 fusion.36
  59.4 1.1 fusion.4
  60.5 1.8 %copy.34 = f32[128,256]{1,0:T(8,128)} copy(f32[128,256]{0,1:T(8,128)} %fusion.4) | data formatting | bytes 262144 | tf_op jit(solution)/shard_map/dot_general | solution.py:33
  63.0 2.1 %fusion.3 = (f32[16,256]{1,0:T(8,128)S(1)}, f32[16,256]{1,0:T(8,128)S(1)}, f32[16,256]{1,0:T(8,128)S(1)}, f32[16,256]{1,0:T(8,128)S(1)}) fusion(f32[128,256]{1,0:T(8,128)} %copy.34, f32[16,256]{1,0:T(8,128)S(1)} %exponential_negate_fusion.1, f32[128,256]{1,0:T(8,128)} %copy-done.19), kind=kLoop, calls=%fused_computation.7 | loop fusion | flops 4702208 | bytes 344064 | tf_op jit(solution)/shard_map/reduce_sum | solution.py:315
  65.1 0.7 multiply_add_fusion
  65.9 1.3 pad_maximum_fusion
  67.5 1.2 collective-permute-done.13
  69.5 0.8 fusion.63
  71.6 6.7 %all-to-all-start.1 = ((bf16[8,49,128]{2,1,0:T(8,128)(2,1)}), bf16[8,49,128]{2,1,0:T(8,128)(2,1)}, u32[]{:S(2)}, u32[]{:S(2)}) async-start(bf16[8,49,128]{2,1,0:T(8,128)(2,1)} %broadcast_in_dim.84), calls=%async_computation.1 | async-start | bytes 229376 | tf_op jit(solution)/shard_map/all_to_all | solution.py:199
  79.3 8.4 %all-to-all-done.1 = bf16[8,49,128]{2,1,0:T(8,128)(2,1)} async-done(((bf16[8,49,128]{2,1,0:T(8,128)(2,1)}), bf16[8,49,128]{2,1,0:T(8,128)(2,1)}, u32[]{:S(2)}, u32[]{:S(2)}) %all-to-all-start.1) | async-done | bytes 100384 | tf_op jit(solution)/shard_map/all_to_all | solution.py:199
  87.7 0.9 convert_element_type.129
  88.7 1.4 multiply_reduce_fusion.7
  90.6 2.7 %collective-permute-start.14 = (bf16[49,128]{1,0:T(8,128)(2,1)}, bf16[49,128]{1,0:T(8,128)(2,1)}, u32[]{:S(2)}, u32[]{:S(2)}) collective-permute-start(bf16[49,128]{1,0:T(8,128)(2,1)} %pad_maximum_fusion.6), channel_id=1, source_target_pairs={{0,192},{4,196},{8,200},{12,204},{16,208},{20,212},{24,216},{28,22... | collective-permute-start | bytes 37640 | tf_op jit(solution)/shard_map/ppermute | solution.py:193
  93.4 0.8 collective-permute-start.15
  94.2 0.9 collective-permute-start.16
  95.5 1.8 %collective-permute-start.18 = (bf16[8,256,128]{2,1,0:T(8,128)(2,1)}, bf16[8,256,128]{2,1,0:T(8,128)(2,1)S(1)}, u32[]{:S(2)}, u32[]{:S(2)}) collective-permute-start(bf16[8,256,128]{2,1,0:T(8,128)(2,1)} %copy-done.11), channel_id=1, source_target_pairs={{0,64},{4,68},{8,72},{12,76},{16,80},{20,84},{24,88},{28,92},{32,9... | collective-permute-start | bytes 1572872 | tf_op jit(solution)/shard_map/ppermute | solution.py:193
  97.4 2.0 %collective-permute-start.19 = (bf16[8,256,128]{2,1,0:T(8,128)(2,1)}, bf16[8,256,128]{2,1,0:T(8,128)(2,1)S(1)}, u32[]{:S(2)}, u32[]{:S(2)}) collective-permute-start(bf16[8,256,128]{2,1,0:T(8,128)(2,1)} %copy-done.10), channel_id=1, source_target_pairs={{0,128},{4,132},{8,136},{12,140},{16,144},{20,148},{24,152},{28,15... | collective-permute-start | bytes 1572872 | tf_op jit(solution)/shard_map/ppermute | solution.py:193
  103.8 1.9 %fusion.23 = f32[256,128]{0,1:T(8,128)} fusion(f32[128,129]{1,0:T(8,128)} %constant.98, f32[258,256]{1,0:T(8,128)} %copy-done.12, f32[258,256]{1,0:T(8,128)S(1)} %fusion.87), kind=kOutput, calls=%fused_computation.43 | convolution fusion | flops 25461504 | bytes 819200 | tf_op jit(solution)/shard_map/dot_general | solution.py:33
  105.7 1.3 collective-permute-start.10
  107.0 1.6 %collective-permute-start.11 = (bf16[128,2048]{1,0:T(8,128)(2,1)S(1)}, bf16[128,2048]{1,0:T(8,128)(2,1)}, u32[]{:S(2)}, u32[]{:S(2)}) collective-permute-start(bf16[128,2048]{1,0:T(8,128)(2,1)S(1)} %copy-done.5), channel_id=1, source_target_pairs={{0,2},{1,3},{2,0},{3,1},{4,6},{5,7},{6,4},{7,5},{8,10},{9,11},{10,... | collective-permute-start | bytes 1572872 | tf_op jit(solution)/shard_map/ppermute | solution.py:189
  109.2 1.4 fusion.69
  111.2 1.0 collective-permute-start.12
  112.2 8.7 %collective-permute-done.19 = bf16[8,256,128]{2,1,0:T(8,128)(2,1)S(1)} collective-permute-done((bf16[8,256,128]{2,1,0:T(8,128)(2,1)}, bf16[8,256,128]{2,1,0:T(8,128)(2,1)S(1)}, u32[]{:S(2)}, u32[]{:S(2)}) %collective-permute-start.19) | collective-permute-done | bytes 524320 | tf_op jit(solution)/shard_map/ppermute | solution.py:193
  120.9 1.1 add_convert_fusion
  121.9 3.5 %all-to-all-start.2 = ((bf16[8,256,128]{2,1,0:T(8,128)(2,1)}), bf16[8,256,128]{2,1,0:T(8,128)(2,1)S(1)}, u32[]{:S(2)}, u32[]{:S(2)}) async-start(bf16[8,256,128]{2,1,0:T(8,128)(2,1)} %add_convert_fusion), calls=%async_computation.2 | async-start | bytes 1048576 | tf_op jit(solution)/shard_map/all_to_all | solution.py:350
  125.5 1.1 multiply_reduce_fusion
  126.6 2.1 %fusion.34 = (bf16[128,256]{1,0:T(8,128)(2,1)}, bf16[128,256]{1,0:T(8,128)(2,1)}) fusion(bf16[128,256]{1,0:T(8,128)(2,1)S(1)} %copy-done.14, bf16[128,256]{1,0:T(8,128)(2,1)S(1)} %copy-done.13, f32[128,256]{1,0:T(8,128)} %copy-done.19, f32[256]{0:T(256)S(1)} %copy-done.33, f32[128,256]{1,0:T(8,128)S(1)} %multiply_reduce_fusion, f32[256,128]{0,1:T(8,128)} %fusion.23, ...), kind=kOutput, calls=%fused_computation.54 | convolution fusion | flops 25789184 | bytes 1344512 | tf_op jit(solution)/shard_map/dot_general | solution.py:33
  128.7 5.2 %collective-permute-done.12 = bf16[128,2048]{1,0:T(8,128)(2,1)} collective-permute-done((bf16[128,2048]{1,0:T(8,128)(2,1)S(1)}, bf16[128,2048]{1,0:T(8,128)(2,1)}, u32[]{:S(2)}, u32[]{:S(2)}) %collective-permute-start.12) | collective-permute-done | bytes 524320 | tf_op jit(solution)/shard_map/ppermute | solution.py:189
  133.9 2.5 %add_convert_fusion.1 = bf16[128,2048]{1,0:T(8,128)(2,1)} fusion(bf16[128,2048]{1,0:T(8,128)(2,1)} %collective-permute-done.12, bf16[128,2048]{1,0:T(8,128)(2,1)} %collective-permute-done.11, bf16[128,2048]{1,0:T(8,128)(2,1)} %collective-permute-done.10, bf16[128,2048]{1,0:T(8,128)(2,1)S(1)} %get-tuple-element.43), kind=kLoop, calls=%fused_computation.23 | loop fusion | flops 2097152 | bytes 2621440 | tf_op jit(solution)/shard_map/convert_element_type | solution.py:289
  136.4 5.6 %all-to-all-done.2 = bf16[8,256,128]{2,1,0:T(8,128)(2,1)S(1)} async-done(((bf16[8,256,128]{2,1,0:T(8,128)(2,1)}), bf16[8,256,128]{2,1,0:T(8,128)(2,1)S(1)}, u32[]{:S(2)}, u32[]{:S(2)}) %all-to-all-start.2) | async-done | bytes 524320 | tf_op jit(solution)/shard_map/all_to_all | solution.py:350
  (131 shorter events, 19.1 us)
Async XLA Ops:
  0.6 46.6 %copy-start.15 = (f32[258,128]{1,0:T(8,128)S(1)}, f32[258,128]{1,0:T(8,128)}, u32[]{:S(2)}) copy-start(f32[258,128]{1,0:T(8,128)} %constant.96.clone) | copy-start | bytes 396292
  0.6 44.7 %copy-start.22 = (f32[16,256]{1,0:T(8,128)S(1)}, f32[16,256]{1,0:T(8,128)}, u32[]{:S(2)}) copy-start(f32[16,256]{1,0:T(8,128)} %decay_ref.1) | copy-start | bytes 49156
  0.7 30.2 %copy-start.1 = (bf16[128,2048]{1,0:T(8,128)(2,1)S(1)}, bf16[128,2048]{1,0:T(8,128)(2,1)}, u32[]{:S(2)}) copy-start(bf16[128,2048]{1,0:T(8,128)(2,1)} %refs_0_.1) | copy-start | bytes 1572868
  2.7 1.4 collective-permute-start
  4.9 42.6 %copy-start.13 = (bf16[128,256]{1,0:T(8,128)(2,1)S(1)}, bf16[128,256]{1,0:T(8,128)(2,1)}, u32[]{:S(2)}) copy-start(bf16[128,256]{1,0:T(8,128)(2,1)} %values_ref.1) | copy-start | bytes 196612
  4.9 42.6 %copy-start.14 = (bf16[128,256]{1,0:T(8,128)(2,1)S(1)}, bf16[128,256]{1,0:T(8,128)(2,1)}, u32[]{:S(2)}) copy-start(bf16[128,256]{1,0:T(8,128)(2,1)} %inner_ref.1) | copy-start | bytes 196612
  6.5 41.4 %copy-start.20 = (f32[128,129]{1,0:T(8,128)S(1)}, f32[128,129]{1,0:T(8,128)}, u32[]{:S(2)}) copy-start(f32[128,129]{1,0:T(8,128)} %constant.98) | copy-start | bytes 198148
  6.5 23.6 %all-to-all-start = ((bf16[32,32,128]{2,1,0:T(8,128)(2,1)}), bf16[32,32,128]{2,1,0:T(8,128)(2,1)S(1)}, u32[]{:S(2)}, u32[]{:S(2)}) async-start(bf16[32,32,128]{2,1,0:T(8,128)(2,1)} %broadcast_in_dim.50), calls=%async_computation | async-start | bytes 524288 | tf_op jit(solution)/shard_map/all_to_all | solution.py:204
  18.1 15.1 %collective-permute-start.3 = (bf16[128,2048]{1,0:T(8,128)(2,1)}, bf16[128,2048]{1,0:T(8,128)(2,1)S(1)}, u32[]{:S(2)}, u32[]{:S(2)}) collective-permute-start(bf16[128,2048]{1,0:T(8,128)(2,1)} %refs_0_.1), channel_id=1, source_target_pairs={{0,1},{1,2},{2,3},{3,0},{4,5},{5,6},{6,7},{7,4},{8,9},{9,10},{10,1... | collective-permute-start | bytes 1572872 | tf_op jit(solution)/shard_map/ppermute | solution.py:189
  19.6 16.5 %collective-permute-start.4 = (bf16[128,2048]{1,0:T(8,128)(2,1)}, bf16[128,2048]{1,0:T(8,128)(2,1)S(1)}, u32[]{:S(2)}, u32[]{:S(2)}) collective-permute-start(bf16[128,2048]{1,0:T(8,128)(2,1)} %refs_0_.1), channel_id=1, source_target_pairs={{0,2},{1,3},{2,0},{3,1},{4,6},{5,7},{6,4},{7,5},{8,10},{9,11},{10,... | collective-permute-start | bytes 1572872 | tf_op jit(solution)/shard_map/ppermute | solution.py:189
  20.8 23.9 %collective-permute-start.5 = (bf16[128,2048]{1,0:T(8,128)(2,1)}, bf16[128,2048]{1,0:T(8,128)(2,1)S(1)}, u32[]{:S(2)}, u32[]{:S(2)}) collective-permute-start(bf16[128,2048]{1,0:T(8,128)(2,1)} %refs_0_.1), channel_id=1, source_target_pairs={{0,3},{1,0},{2,1},{3,2},{4,7},{5,4},{6,5},{7,6},{8,11},{9,8},{10,9... | collective-permute-start | bytes 1572872 | tf_op jit(solution)/shard_map/ppermute | solution.py:189
  22.9 25.2 %copy-start.17 = (f32[128,129]{1,0:T(8,128)S(1)}, f32[128,129]{1,0:T(8,128)}, u32[]{:S(2)}) copy-start(f32[128,129]{1,0:T(8,128)} %constant.99) | copy-start | bytes 198148
  22.9 25.1 %copy-start.23 = (bf16[128,256]{1,0:T(8,128)(2,1)S(1)}, bf16[128,256]{1,0:T(8,128)(2,1)}, u32[]{:S(2)}) copy-start(bf16[128,256]{1,0:T(8,128)(2,1)} %param.10) | copy-start | bytes 196612
  23.0 25.1 %copy-start.32 = (f32[256]{0:T(256)S(1)}, f32[256]{0:T(256)}, u32[]{:S(2)}) copy-start(f32[256]{0:T(256)} %param.15) | copy-start | bytes 3076
  30.9 13.8 %collective-permute-start.1 = (f32[32,128]{1,0:T(8,128)S(1)}, f32[32,128]{1,0:T(8,128)S(1)}, u32[]{:S(2)}, u32[]{:S(2)}) collective-permute-start(f32[32,128]{1,0:T(8,128)S(1)} %pad_maximum_fusion.4), channel_id=1, source_target_pairs={{0,4},{4,0},{8,12},{12,8},{16,20},{20,16},{24,28},{28,24},{32,36},... | collective-permute-start | bytes 49160 | tf_op jit(solution)/shard_map/ppermute | solution.py:186
  30.9 18.4 %collective-permute-start.6 = (bf16[128,2048]{1,0:T(8,128)(2,1)S(1)}, bf16[128,2048]{1,0:T(8,128)(2,1)S(1)}, u32[]{:S(2)}, u32[]{:S(2)}) collective-permute-start(bf16[128,2048]{1,0:T(8,128)(2,1)S(1)} %copy-done.1), channel_id=1, source_target_pairs={{0,4},{4,0},{8,12},{12,8},{16,20},{20,16},{24,28},{28,24},{32,36},... | collective-permute-start | bytes 1572872 | tf_op jit(solution)/shard_map/ppermute | solution.py:186
  33.2 16.9 %collective-permute-start.7 = (bf16[128,2048]{1,0:T(8,128)(2,1)S(1)}, bf16[128,2048]{1,0:T(8,128)(2,1)S(1)}, u32[]{:S(2)}, u32[]{:S(2)}) collective-permute-start(bf16[128,2048]{1,0:T(8,128)(2,1)S(1)} %collective-permute-done.3.refs_3_.refs_1_), channel_id=1, source_target_pairs={{0,4},{4,0},{8,12},{12,8},{16,20},{20,16},{24,28},{28,24},{32,36},... | collective-permute-start | bytes 1572872 | tf_op jit(solution)/shard_map/ppermute | solution.py:186
  36.2 13.9 %collective-permute-start.8 = (bf16[128,2048]{1,0:T(8,128)(2,1)S(1)}, bf16[128,2048]{1,0:T(8,128)(2,1)S(1)}, u32[]{:S(2)}, u32[]{:S(2)}) collective-permute-start(bf16[128,2048]{1,0:T(8,128)(2,1)S(1)} %collective-permute-done.4.refs_4_.refs_2_), channel_id=1, source_target_pairs={{0,4},{4,0},{8,12},{12,8},{16,20},{20,16},{24,28},{28,24},{32,36},... | collective-permute-start | bytes 1572872 | tf_op jit(solution)/shard_map/ppermute | solution.py:186
  44.6 5.4 %collective-permute-start.9 = (bf16[128,2048]{1,0:T(8,128)(2,1)S(1)}, bf16[128,2048]{1,0:T(8,128)(2,1)S(1)}, u32[]{:S(2)}, u32[]{:S(2)}) collective-permute-start(bf16[128,2048]{1,0:T(8,128)(2,1)S(1)} %collective-permute-done.5.refs_5_.refs_3_), channel_id=1, source_target_pairs={{0,4},{4,0},{8,12},{12,8},{16,20},{20,16},{24,28},{28,24},{32,36},... | collective-permute-start | bytes 1572872 | tf_op jit(solution)/shard_map/ppermute | solution.py:186
  48.4 1.7 %collective-permute-start.2 = (bf16[128,256]{1,0:T(8,128)(2,1)S(1)}, bf16[128,256]{1,0:T(8,128)(2,1)S(1)}, u32[]{:S(2)}, u32[]{:S(2)}) collective-permute-start(bf16[128,256]{1,0:T(8,128)(2,1)S(1)} %get-tuple-element.42.refs_0_.result_ref), channel_id=1, source_target_pairs={{0,4},{4,0},{8,12},{12,8},{16,20},{20,16},{24,28},{28,24},{32,36},... | collective-permute-start | bytes 196616 | tf_op jit(solution)/shard_map/ppermute | solution.py:186
  49.2 5.2 %copy-start = (bf16[256,8192]{1,0:T(8,128)(2,1)S(1)}, bf16[256,8192]{1,0:T(8,128)(2,1)}, u32[]{:S(2)}) copy-start(bf16[256,8192]{1,0:T(8,128)(2,1)} %refs_4_.1) | copy-start | bytes 12582916
  54.4 2.7 %copy-start.8 = (bf16[8,256,128]{2,1,0:T(8,128)(2,1)}, bf16[8,256,128]{2,1,0:T(8,128)(2,1)S(1)}, u32[]{:S(2)}) copy-start(bf16[8,256,128]{2,1,0:T(8,128)(2,1)S(1)} %get-tuple-element.41) | copy-start | bytes 1572868
  54.4 2.7 %copy-start.24 = (bf16[128,256]{1,0:T(8,128)(2,1)S(1)}, bf16[128,256]{1,0:T(8,128)(2,1)}, u32[]{:S(2)}) copy-start(bf16[128,256]{1,0:T(8,128)(2,1)} %param.10) | copy-start | bytes 196612
  54.4 4.0 %copy-start.16 = (f32[258,128]{1,0:T(8,128)S(1)}, f32[258,128]{1,0:T(8,128)}, u32[]{:S(2)}) copy-start(f32[258,128]{1,0:T(8,128)} %constant.96.clone) | copy-start | bytes 396292
  54.4 4.3 %copy-start.21 = (f32[128,129]{1,0:T(8,128)S(1)}, f32[128,129]{1,0:T(8,128)}, u32[]{:S(2)}) copy-start(f32[128,129]{1,0:T(8,128)} %constant.98) | copy-start | bytes 198148
  54.4 5.0 %copy-start.18 = (f32[128,129]{1,0:T(8,128)S(1)}, f32[128,129]{1,0:T(8,128)}, u32[]{:S(2)}) copy-start(f32[128,129]{1,0:T(8,128)} %constant.99) | copy-start | bytes 198148
  57.1 2.1 %copy-start.4 = (bf16[128,2048]{1,0:T(8,128)(2,1)}, bf16[128,2048]{1,0:T(8,128)(2,1)S(1)}, u32[]{:S(2)}) copy-start(bf16[128,2048]{1,0:T(8,128)(2,1)S(1)} %get-tuple-element.45) | copy-start | bytes 1572868
  58.7 40.6 %copy-start.9 = (bf16[8,256,128]{2,1,0:T(8,128)(2,1)S(1)}, bf16[8,256,128]{2,1,0:T(8,128)(2,1)}, u32[]{:S(2)}) copy-start(bf16[8,256,128]{2,1,0:T(8,128)(2,1)} %copy-done.8) | copy-start | bytes 1572868
  60.5 45.2 %copy-start.7 = (bf16[128,2048]{1,0:T(8,128)(2,1)S(1)}, bf16[128,2048]{1,0:T(8,128)(2,1)}, u32[]{:S(2)}) copy-start(bf16[128,2048]{1,0:T(8,128)(2,1)} %copy-done.6) | copy-start | bytes 1572868
  60.5 46.5 %copy-start.5 = (bf16[128,2048]{1,0:T(8,128)(2,1)S(1)}, bf16[128,2048]{1,0:T(8,128)(2,1)}, u32[]{:S(2)}) copy-start(bf16[128,2048]{1,0:T(8,128)(2,1)} %copy-done.4) | copy-start | bytes 1572868
  60.5 50.7 %copy-start.3 = (bf16[128,2048]{1,0:T(8,128)(2,1)S(1)}, bf16[128,2048]{1,0:T(8,128)(2,1)}, u32[]{:S(2)}) copy-start(bf16[128,2048]{1,0:T(8,128)(2,1)} %copy-done.2) | copy-start | bytes 1572868
  63.0 4.2 %copy-start.31 = (f32[16,256]{1,0:T(8,128)}, f32[16,256]{1,0:T(8,128)S(1)}, u32[]{:S(2)}) copy-start(f32[16,256]{1,0:T(8,128)S(1)} %exponential_negate_fusion.1) | copy-start | bytes 49156
  67.2 1.6 %collective-permute-start.13 = (f32[49,256]{1,0:T(8,128)}, f32[49,256]{1,0:T(8,128)}, u32[]{:S(2)}, u32[]{:S(2)}) collective-permute-start(f32[49,256]{1,0:T(8,128)} %pad_maximum_fusion), channel_id=1, source_target_pairs={{0,4},{4,0},{8,12},{12,8},{16,20},{20,16},{24,28},{28,24},{32,36},... | collective-permute-start | bytes 150536 | tf_op jit(solution)/shard_map/ppermute | solution.py:186
  71.6 16.1 %all-to-all-start.1 = ((bf16[8,49,128]{2,1,0:T(8,128)(2,1)}), bf16[8,49,128]{2,1,0:T(8,128)(2,1)}, u32[]{:S(2)}, u32[]{:S(2)}) async-start(bf16[8,49,128]{2,1,0:T(8,128)(2,1)} %broadcast_in_dim.84), calls=%async_computation.1 | async-start | bytes 229376 | tf_op jit(solution)/shard_map/all_to_all | solution.py:199
  90.6 8.7 %collective-permute-start.14 = (bf16[49,128]{1,0:T(8,128)(2,1)}, bf16[49,128]{1,0:T(8,128)(2,1)}, u32[]{:S(2)}, u32[]{:S(2)}) collective-permute-start(bf16[49,128]{1,0:T(8,128)(2,1)} %pad_maximum_fusion.6), channel_id=1, source_target_pairs={{0,192},{4,196},{8,200},{12,204},{16,208},{20,212},{24,216},{28,22... | collective-permute-start | bytes 37640 | tf_op jit(solution)/shard_map/ppermute | solution.py:193
  93.4 7.4 %collective-permute-start.15 = (bf16[49,128]{1,0:T(8,128)(2,1)}, bf16[49,128]{1,0:T(8,128)(2,1)}, u32[]{:S(2)}, u32[]{:S(2)}) collective-permute-start(bf16[49,128]{1,0:T(8,128)(2,1)} %pad_maximum_fusion.6), channel_id=1, source_target_pairs={{0,128},{4,132},{8,136},{12,140},{16,144},{20,148},{24,152},{28,15... | collective-permute-start | bytes 37640 | tf_op jit(solution)/shard_map/ppermute | solution.py:193
  94.2 7.3 %collective-permute-start.16 = (bf16[49,128]{1,0:T(8,128)(2,1)}, bf16[49,128]{1,0:T(8,128)(2,1)}, u32[]{:S(2)}, u32[]{:S(2)}) collective-permute-start(bf16[49,128]{1,0:T(8,128)(2,1)} %pad_maximum_fusion.6), channel_id=1, source_target_pairs={{0,64},{4,68},{8,72},{12,76},{16,80},{20,84},{24,88},{28,92},{32,9... | collective-permute-start | bytes 37640 | tf_op jit(solution)/shard_map/ppermute | solution.py:193
  95.5 15.6 %collective-permute-start.18 = (bf16[8,256,128]{2,1,0:T(8,128)(2,1)}, bf16[8,256,128]{2,1,0:T(8,128)(2,1)S(1)}, u32[]{:S(2)}, u32[]{:S(2)}) collective-permute-start(bf16[8,256,128]{2,1,0:T(8,128)(2,1)} %copy-done.11), channel_id=1, source_target_pairs={{0,64},{4,68},{8,72},{12,76},{16,80},{20,84},{24,88},{28,92},{32,9... | collective-permute-start | bytes 1572872 | tf_op jit(solution)/shard_map/ppermute | solution.py:193
  97.4 23.5 %collective-permute-start.19 = (bf16[8,256,128]{2,1,0:T(8,128)(2,1)}, bf16[8,256,128]{2,1,0:T(8,128)(2,1)S(1)}, u32[]{:S(2)}, u32[]{:S(2)}) collective-permute-start(bf16[8,256,128]{2,1,0:T(8,128)(2,1)} %copy-done.10), channel_id=1, source_target_pairs={{0,128},{4,132},{8,136},{12,140},{16,144},{20,148},{24,152},{28,15... | collective-permute-start | bytes 1572872 | tf_op jit(solution)/shard_map/ppermute | solution.py:193
  99.4 21.5 %collective-permute-start.20 = (bf16[8,256,128]{2,1,0:T(8,128)(2,1)S(1)}, bf16[8,256,128]{2,1,0:T(8,128)(2,1)S(1)}, u32[]{:S(2)}, u32[]{:S(2)}) collective-permute-start(bf16[8,256,128]{2,1,0:T(8,128)(2,1)S(1)} %copy-done.9), channel_id=1, source_target_pairs={{0,192},{4,196},{8,200},{12,204},{16,208},{20,212},{24,216},{28,22... | collective-permute-start | bytes 1572872 | tf_op jit(solution)/shard_map/ppermute | solution.py:193
  103.7 3.3 %collective-permute-start.17 = (f32[49,128]{1,0:T(8,128)S(1)}, f32[49,128]{1,0:T(8,128)S(1)}, u32[]{:S(2)}, u32[]{:S(2)}) collective-permute-start(f32[49,128]{1,0:T(8,128)S(1)} %pad_maximum_fusion.1), channel_id=1, source_target_pairs={{0,4},{4,0},{8,12},{12,8},{16,20},{20,16},{24,28},{28,24},{32,36},... | collective-permute-start | bytes 75272 | tf_op jit(solution)/shard_map/ppermute | solution.py:186
  105.7 19.7 %copy-start.34 = (f32[128]{0:T(128)S(1)}, f32[128]{0:T(128)}, u32[]{:S(2)}) copy-start(f32[128]{0:T(128)} %iota_subtract_fusion) | copy-start | bytes 1540
  105.7 23.0 %collective-permute-start.10 = (bf16[128,2048]{1,0:T(8,128)(2,1)S(1)}, bf16[128,2048]{1,0:T(8,128)(2,1)}, u32[]{:S(2)}, u32[]{:S(2)}) collective-permute-start(bf16[128,2048]{1,0:T(8,128)(2,1)S(1)} %copy-done.7), channel_id=1, source_target_pairs={{0,1},{1,2},{2,3},{3,0},{4,5},{5,6},{6,7},{7,4},{8,9},{9,10},{10,1... | collective-permute-start | bytes 1572872 | tf_op jit(solution)/shard_map/ppermute | solution.py:189
  107.0 21.7 %collective-permute-start.11 = (bf16[128,2048]{1,0:T(8,128)(2,1)S(1)}, bf16[128,2048]{1,0:T(8,128)(2,1)}, u32[]{:S(2)}, u32[]{:S(2)}) collective-permute-start(bf16[128,2048]{1,0:T(8,128)(2,1)S(1)} %copy-done.5), channel_id=1, source_target_pairs={{0,2},{1,3},{2,0},{3,1},{4,6},{5,7},{6,4},{7,5},{8,10},{9,11},{10,... | collective-permute-start | bytes 1572872 | tf_op jit(solution)/shard_map/ppermute | solution.py:189
  111.2 15.4 %copy-start.33 = (f32[256]{0:T(256)S(1)}, f32[256]{0:T(256)}, u32[]{:S(2)}) copy-start(f32[256]{0:T(256)} %param.15) | copy-start | bytes 3076
  111.2 22.7 %collective-permute-start.12 = (bf16[128,2048]{1,0:T(8,128)(2,1)S(1)}, bf16[128,2048]{1,0:T(8,128)(2,1)}, u32[]{:S(2)}, u32[]{:S(2)}) collective-permute-start(bf16[128,2048]{1,0:T(8,128)(2,1)S(1)} %copy-done.3), channel_id=1, source_target_pairs={{0,3},{1,0},{2,1},{3,2},{4,7},{5,4},{6,5},{7,6},{8,11},{9,8},{10,9... | collective-permute-start | bytes 1572872 | tf_op jit(solution)/shard_map/ppermute | solution.py:189
  120.9 4.6 %copy-start.30 = (f32[16,256]{1,0:T(8,128)S(1)}, f32[16,256]{1,0:T(8,128)}, u32[]{:S(2)}) copy-start(f32[16,256]{1,0:T(8,128)} %get-tuple-element.78) | copy-start | bytes 49156
  121.9 20.0 %all-to-all-start.2 = ((bf16[8,256,128]{2,1,0:T(8,128)(2,1)}), bf16[8,256,128]{2,1,0:T(8,128)(2,1)S(1)}, u32[]{:S(2)}, u32[]{:S(2)}) async-start(bf16[8,256,128]{2,1,0:T(8,128)(2,1)} %add_convert_fusion), calls=%async_computation.2 | async-start | bytes 1048576 | tf_op jit(solution)/shard_map/all_to_all | solution.py:350
  (11 other events, 11.3 us)
